TPU v7x, 32 devices: a whole 2x2x4 slice. The times are simulated.
32 devices in a mesh: pool: 2 (over core), ep: 4 (over z), half: 4 (over y, x).
Axes of the slice: x: 2, y: 2, z: 4, core: 2. Of those that a mesh axis runs over, the one named last changes fastest.
Arguments:
- tokens: bfloat16 [2, 256, 4096], P('pool', 'ep'), may hold values from -6 to 6
- routes: int32 [2, 256, 8], P('pool', 'ep'), may hold values from 0 to 31, all different within a row; in each aligned block of 64 rows (0 to 63, 64 to 127, ..., all dimensions but the last counted through in order) at most 32 rows name the same one
- router: bfloat16 [4096, 32], replicated, may hold values from -0.03125 to 0.03125
- w_gate: bfloat16 [32, 4096, 1536], P('ep', None, 'half'), may hold values from -0.09375 to 0.09375
- w_up: bfloat16 [32, 4096, 1536], P('ep', None, 'half'), may hold values from -0.09375 to 0.09375
- w_down: bfloat16 [32, 1536, 4096], P('ep', 'half'), may hold values from -0.625 to 0.625
- norm_gain: float32 [4096], replicated, may hold values from 0.1 to 1.9
- w_kv: bfloat16 [4096, 2048], P('ep', 'half'), may hold values from -0.09375 to 0.09375
- lengths: int32 [2, 4, 2], P(None, 'ep'), may hold values from 1 to 48, 64 in all within a row
- queries: bfloat16 [2, 1024, 2048], P('pool', 'ep', 'half'), may hold values from -150 to 150
- new_keys: bfloat16 [2, 1024, 1024], P('pool', 'ep', 'half'), may hold values from -5 to 5
- new_values: bfloat16 [2, 1024, 1024], P('pool', 'ep', 'half'), may hold values from -6 to 6
- w_out: bfloat16 [2048, 2048], P('half'), may hold values from -0.125 to 0.125
Outputs:
- decoded: bfloat16 [2, 1024, 2048], P('pool', ('ep', 'half'))
Inputs may be any that keep to these rules, and one draw needn't show every extreme that they name: `routes`: each token names 8 different experts; within each aligned block of 64 tokens no expert is named by more than 32 tokens. The 2 lengths of a group sum to 64.
All inputs are finite; a program needn't handle non-finite values.
Results may differ from a plain program's by a relative error of at most 0.022.
Values may be sent and summed in bfloat16 or wider, within the bound.
No kernel may reach another device: no remote copies, remote signals or barrier semaphores. Data moves between devices by JAX's collectives and lax.ppermute only.
A program may use at most 192 MiB of HBM per device.

v0:
```python
import functools
import math

import jax
import jax.numpy as jnp
from jax import lax
from jax.experimental import pallas as pl
from jax.experimental.pallas import tpu as pltpu
from jax.sharding import PartitionSpec as P


HEAD = 128
SAMPLES = 128
LANES = 128
F32 = jnp.float32
BF16 = jnp.bfloat16
WHOLE = pl.BlockSpec(memory_space=pltpu.VMEM)


def swap(shard, axis, bits):
    return lax.ppermute(shard, axis, [(i, i ^ bits) for i in range(lax.axis_size(axis))])


def shift(shard, axis, distance):
    count = lax.axis_size(axis)
    return lax.ppermute(shard, axis, [(i, (i + distance) % count) for i in range(count)])


def params(steps, mebibytes):
    return pltpu.CompilerParams(
        dimension_semantics=("arbitrary",) * steps, vmem_limit_bytes=mebibytes * 1024 * 1024
    )


def in_vmem(array):
    return pltpu.with_memory_space_constraint(array, pltpu.VMEM)


def in_hbm(array):
    return pltpu.with_memory_space_constraint(array, pltpu.HBM)


def columns_of(piece, width):
    return pl.ds(pl.multiple_of(piece * width, width), width)


def router_logits(rows, router, columns):
    return lax.dot_general(
        rows, router[:, columns], (((1,), (1,)), ((), ())), preferred_element_type=F32
    )


def take_rows(quarters, place, own, nears, router, rows):
    local = own.shape[0]
    width = nears[0].shape[1]
    logits = 0.0
    for i, (k, near) in enumerate(zip(quarters, nears)):
        columns = columns_of(place[0] ^ k, width)
        rows[:local, i * width : (i + 1) * width] = own[:, columns]
        rows[local:, i * width : (i + 1) * width] = near[...]
        logits += router_logits(rows[:, i * width : (i + 1) * width], router, columns)
    return logits


def both(rows, w_gates, w_ups, i):
    width = w_gates[0].shape[1]
    value = 0.0
    for j, (w_gate, w_up) in enumerate(zip(w_gates, w_ups)):
        weight = jnp.concatenate([w_gate[i], w_up[i]], axis=1)
        value += jnp.dot(
            rows[:, j * width : (j + 1) * width], weight, preferred_element_type=F32
        )
    return value


def gather_kernel(quarters, first, place, own, router, *refs):
    count = len(quarters)
    nears, w_gates, w_ups, refs = (
        refs[:count],
        refs[count : 2 * count],
        refs[2 * count : 3 * count],
        refs[3 * count :],
    )
    totals, refs = ((None,) * 2, refs) if first else (refs[:2], refs[2:])
    out, logits_out, rows = refs
    step, each = pl.program_id(0), w_gates[0].shape[0]

    @pl.when(step == 0)
    def _():
        logits = take_rows(quarters, place, own, nears, router, rows)
        logits_out[...] = logits if first else logits + totals[1][...]

    for i in range(each):
        value = both(rows, w_gates, w_ups, i)
        out[step * each + i] = value if first else value + totals[0][step * each + i]


def finish_kernel(quarters, top, place, own, router, *refs):
    count = len(quarters)
    nears, w_gates, w_ups, refs = (
        refs[:count],
        refs[count : 2 * count],
        refs[2 * count : 3 * count],
        refs[3 * count :],
    )
    total, logits_total, tags, hidden, rows, weights = refs
    step, each, units = pl.program_id(0), w_gates[0].shape[0], w_gates[0].shape[2]
    expert = lax.broadcasted_iota(jnp.int32, weights.shape, 1)

    @pl.when(step == 0)
    def _():
        logits = logits_total[...] + take_rows(quarters, place, own, nears, router, rows)
        named = tags[...].astype(F32).astype(jnp.int32)
        picked = named[:, 0:1] == expert
        for j in range(1, top):
            picked = jnp.logical_or(picked, named[:, j : j + 1] == expert)
        most = jnp.max(jnp.where(picked, logits, -1e30), axis=1, keepdims=True)
        spread = jnp.where(picked, jnp.exp(logits - most), 0.0)
        weights[...] = spread / jnp.sum(spread, axis=1, keepdims=True)

    for i in range(each):
        value = total[step * each + i] + both(rows, w_gates, w_ups, i)
        gate, up = value[:, :units], value[:, units:]
        mine = expert == (place[1] * pl.num_programs(0) + step) * each + i
        scale = jnp.sum(jnp.where(mine, weights[...], 0.0), axis=1, keepdims=True)
        hidden[:, i * units : (i + 1) * units] = (
            gate / (1.0 + jnp.exp(-gate)) * up * scale
        ).astype(BF16)


def expand(quarters, place, own, nears, router, w_gate, w_up, totals, tags, top):
    count = len(quarters)
    local, _ = own.shape
    tokens = local + nears[0].shape[0]
    experts, units = w_gate.shape[0], w_gate.shape[2]
    each = math.gcd(experts, 4 // count)
    width = nears[0].shape[1]
    last = tags is not None
    weight = [
        pl.BlockSpec((each, width, units), lambda e, place, k=k: (e, place[0] ^ k, 0))
        for k in quarters
    ]
    operands = [own, router] + [in_vmem(near) for near in nears]
    operands += [in_hbm(w_gate)] * count + [in_hbm(w_up)] * count
    operands += [in_vmem(t) for t in totals]
    scratch = [pltpu.VMEM((tokens, count * width), BF16)]
    if last:
        operands.append(tags)
        kernel = functools.partial(finish_kernel, quarters, top)
        scratch.append(pltpu.VMEM((tokens, router.shape[0]), F32))
        out_shape = pltpu.VMEM((tokens, experts * units), BF16)
        out_specs = pl.BlockSpec((tokens, each * units), lambda e, place: (0, e))
        aliases = {}
    else:
        kernel = functools.partial(gather_kernel, quarters, not totals)
        out_shape = [
            pltpu.VMEM((experts, tokens, 2 * units), F32),
            pltpu.VMEM((tokens, router.shape[0]), F32),
        ]
        out_specs = [WHOLE] * 2
        aliases = {3 + 3 * count + i: i for i in range(len(totals))}
    return pl.pallas_call(
        kernel,
        out_shape=out_shape,
        grid_spec=pltpu.PrefetchScalarGridSpec(
            num_scalar_prefetch=1,
            grid=(experts // each,),
            in_specs=[WHOLE] * (2 + count)
            + weight * 2
            + [WHOLE] * (len(operands) - 2 - 3 * count),
            out_specs=out_specs,
            scratch_shapes=scratch,
        ),
        input_output_aliases=aliases,
        compiler_params=params(1, 24 if tokens <= 1024 else 40),
        cost_estimate=pl.CostEstimate(
            flops=4 * tokens * width * experts * units * count,
            transcendentals=0,
            bytes_accessed=4 * experts * width * units * count,
        ),
        name="expand",
    )(place, *operands)


def reduce_kernel(place, hidden, w_down, out):
    weight = w_down[...].reshape(-1, w_down.shape[2])
    out[...] = jnp.dot(hidden[...], weight, preferred_element_type=F32).astype(BF16)


def reduce(k, place, hidden, w_down, width, block):
    experts, units, _ = w_down.shape
    steps = width // block
    tokens = hidden.shape[0]
    return pl.pallas_call(
        reduce_kernel,
        out_shape=jax.ShapeDtypeStruct((tokens, width), BF16),
        grid_spec=pltpu.PrefetchScalarGridSpec(
            num_scalar_prefetch=1,
            grid=(steps,),
            in_specs=[
                WHOLE,
                pl.BlockSpec(
                    (experts, units, block),
                    lambda i, place: (0, 0, (place[0] ^ k) * steps + i),
                ),
            ],
            out_specs=pl.BlockSpec((tokens, block), lambda i, place: (0, i)),
        ),
        compiler_params=params(1, 16),
        cost_estimate=pl.CostEstimate(
            flops=2 * tokens * width * experts * units,
            transcendentals=0,
            bytes_accessed=2 * experts * width * units,
        ),
        name="reduce",
    )(place, in_vmem(hidden), in_hbm(w_down))


def project_kernel(parts, eps, place, own, *refs):
    moe, refs = refs[:parts], refs[parts:]
    gain, home, refs = refs[0], refs[1], refs[2:]
    mine, theirs, out, mixed, normed = refs
    half, ep, pool = place[0], place[1], place[2]
    width = moe[0].shape[1]
    square = jnp.zeros((own.shape[0], 1), F32)
    for k in range(parts):
        columns = columns_of(half ^ k, width)
        value = own[:, columns].astype(F32) + moe[k][...].astype(F32)
        mixed[:, columns] = value
        square += jnp.sum(value * value, axis=1, keepdims=True)
    factor = lax.rsqrt(square / mixed.shape[1] + 1e-06)
    normed[...] = (mixed[...] * factor * gain[...]).astype(BF16)
    depth, narrow = home.shape[0], mine.shape[1]
    for side, pieces in ((pool, mine), (1 - pool, theirs)):
        kept = columns_of(side, narrow)
        total = jnp.dot(
            normed[:, columns_of(ep, depth)], home[:, kept], preferred_element_type=F32
        )
        for d in range(1, eps):
            origin = lax.rem(ep + eps - d, eps)
            total += jnp.dot(
                normed[:, columns_of(origin, depth)],
                pieces[(d - 1) * depth : d * depth, :],
                preferred_element_type=F32,
            )
        out[:, kept] = total.astype(BF16)


def project(place, own, moe, gain, home, mine, theirs, eps):
    return pl.pallas_call(
        functools.partial(project_kernel, len(moe), eps),
        out_shape=jax.ShapeDtypeStruct((own.shape[0], home.shape[1]), BF16),
        grid_spec=pltpu.PrefetchScalarGridSpec(
            num_scalar_prefetch=1,
            grid=(),
            in_specs=[WHOLE] * (len(moe) + 5),
            out_specs=WHOLE,
            scratch_shapes=[pltpu.VMEM(own.shape, F32), pltpu.VMEM(own.shape, BF16)],
        ),
        compiler_params=params(0, 12),
        name="project",
    )(place, own, *moe, gain, home, mine, theirs)


def attend_kernel(k, prompts, place, block, query, fresh_key, fresh_value, w_out, out):
    rows = query.shape[0]
    group_tok = block.shape[0]
    kv_heads = fresh_key.shape[1] // HEAD
    per_head = query.shape[1] // HEAD // kv_heads
    heads = kv_heads * per_head
    position = lax.broadcasted_iota(jnp.int32, (rows, group_tok), 1)
    row = (place[0] ^ k) * rows + lax.broadcasted_iota(jnp.int32, (rows, group_tok), 0)
    segment = jnp.zeros((rows, group_tok), jnp.int32)
    end = jnp.int32(0)
    for p in range(prompts):
        end = end + place[3 + p]
        segment += (position >= end).astype(jnp.int32)
    allowed = jnp.where(segment == row // SAMPLES, 1.0, 0.0)
    allowed = jnp.concatenate([allowed] * heads, axis=0) > 0.5
    scale = 1.0 / math.sqrt(HEAD)
    scores, owns = [], []
    for kv in range(kv_heads):
        key = block[:, 2 * kv * HEAD : (2 * kv + 1) * HEAD]
        new_key = fresh_key[:, kv * HEAD : (kv + 1) * HEAD].astype(F32)
        first = kv * per_head * HEAD
        asked = [query[:, first + j * HEAD : first + (j + 1) * HEAD] for j in range(per_head)]
        scores.append(
            lax.dot_general(
                jnp.concatenate(asked, axis=0),
                key,
                (((1,), (1,)), ((), ())),
                preferred_element_type=F32,
            )
        )
        owns += [jnp.sum(q.astype(F32) * new_key, axis=1, keepdims=True) for q in asked]
    scores = jnp.where(allowed, jnp.concatenate(scores, axis=0) * scale, -1e30)
    own = jnp.concatenate(owns, axis=0) * scale
    top = jnp.maximum(jnp.max(scores, axis=1, keepdims=True), own)
    spread = jnp.where(allowed, jnp.exp(scores - top), 0.0)
    self_weight = jnp.exp(own - top)
    total = jnp.sum(spread, axis=1, keepdims=True) + self_weight
    probs = (spread / total).astype(BF16)
    self_prob = (self_weight / total).astype(BF16).astype(F32)
    mixed = []
    for kv in range(kv_heads):
        value = block[:, (2 * kv + 1) * HEAD : (2 * kv + 2) * HEAD]
        new_value = fresh_value[:, kv * HEAD : (kv + 1) * HEAD].astype(F32)
        lower = kv * per_head * rows
        summed = jnp.dot(
            probs[lower : lower + per_head * rows], value, preferred_element_type=F32
        )
        for j in range(per_head):
            at = slice(j * rows, (j + 1) * rows)
            own_part = self_prob[lower + j * rows : lower + (j + 1) * rows] * new_value
            mixed.append((summed[at] + own_part).astype(BF16))
    attention = jnp.concatenate(mixed, axis=1)
    out[...] = jnp.dot(attention, w_out[...], preferred_element_type=F32).astype(BF16)


def attend(k, prompts, place, block, query, fresh_key, fresh_value, w_out, rows):
    def cut(array):
        return pl.BlockSpec((rows, array.shape[1]), lambda i, place: (place[0] ^ k, 0))

    return pl.pallas_call(
        functools.partial(attend_kernel, k, prompts),
        out_shape=jax.ShapeDtypeStruct((rows, w_out.shape[1]), BF16),
        grid_spec=pltpu.PrefetchScalarGridSpec(
            num_scalar_prefetch=1,
            grid=(1,),
            in_specs=[WHOLE, cut(query), cut(fresh_key), cut(fresh_value), WHOLE],
            out_specs=pl.BlockSpec((rows, w_out.shape[1]), lambda i, place: (0, 0)),
        ),
        compiler_params=params(1, 8),
        cost_estimate=pl.CostEstimate(
            flops=4 * rows * w_out.shape[0] * w_out.shape[1],
            transcendentals=0,
            bytes_accessed=2 * w_out.size,
        ),
        name="attend",
    )(place, block, query, fresh_key, fresh_value, w_out)


def total_of(first, rest):
    value = first.astype(F32)
    for other in rest:
        value = value + other.astype(F32)
    return value


def on_device(
    tokens,
    routes,
    router,
    w_gate,
    w_up,
    w_down,
    norm_gain,
    w_kv,
    lengths,
    queries,
    new_keys,
    new_values,
    w_out,
):
    own = tokens[0]
    chosen = routes[0]
    local, model = own.shape
    top = chosen.shape[1]
    eps = lax.axis_size("ep")
    parts = lax.axis_size("half")
    half, ep, pool = lax.axis_index("half"), lax.axis_index("ep"), lax.axis_index("pool")
    width = model // parts

    prompt_lengths = lax.dynamic_index_in_dim(lengths, 1 - pool, 0, keepdims=False)[0]
    place = jnp.concatenate([jnp.stack([half, ep, pool]), prompt_lengths])

    narrow = w_kv.shape[1] // 2
    tags = jnp.pad(chosen.astype(BF16), ((0, 0), (0, LANES - top)))
    quarter = lax.dynamic_slice_in_dim(own, half * width, width, axis=1)
    parcel = jnp.concatenate([quarter, tags], axis=1)
    piece, parcel = lax.optimization_barrier(
        (lax.dynamic_slice_in_dim(w_kv, pool * narrow, narrow, axis=1), parcel)
    )
    arrived = [shift(parcel, "ep", d) for d in range(1, eps)]
    near = jnp.concatenate([a[:, :width] for a in arrived], axis=0)
    all_tags = jnp.concatenate([tags] + [a[:, width:] for a in arrived], axis=0)
    order = sorted(range(1, parts), key=lambda k: bin(k).count("1"))
    far = order[::-1]
    others = {k: swap(near, "half", k) for k in order}
    others[0] = near
    pieces = [shift(piece, "ep", d) for d in range(1, eps)]

    totals = ()
    batches = [[0], order[:-1], order[-1:]]
    for quarters in batches:
        totals = expand(
            quarters,
            place,
            own,
            [others[k] for k in quarters],
            router.T,
            w_gate,
            w_up,
            totals,
            all_tags if quarters is batches[-1] else None,
            top,
        )
    hidden = totals
    partial = {}
    for k in far + [0]:
        partial[k] = reduce(k, place, hidden, w_down, width, width // 2)
    gathered = []
    for k in far:
        gathered.append(swap(partial[k], "half", k))
    pieces, partial[0] = lax.optimization_barrier((pieces, partial[0]))
    mine = jnp.concatenate(pieces, axis=0)
    theirs = swap(mine, "pool", 1)
    summed = total_of(partial[0], gathered)
    returned = [
        shift(summed[d * local : (d + 1) * local].astype(BF16), "ep", -d) for d in range(1, eps)
    ]
    moe_quarter = total_of(summed[:local], returned).astype(BF16)
    moe = [moe_quarter] + [None] * (parts - 1)
    for k in order:
        moe[k] = swap(moe_quarter, "half", k)
    keyvals = project(place, own, moe, norm_gain[None], w_kv, mine, theirs, eps)
    block = swap(keyvals, "pool", 1)

    rows = queries.shape[1] // parts
    decoded = {}
    for k in far + [0]:
        decoded[k] = attend(
            k,
            lengths.shape[2],
            place,
            block,
            queries[0],
            new_keys[0],
            new_values[0],
            w_out,
            rows,
        )
    sent = []
    for k in far:
        sent.append(swap(decoded[k], "half", k))
    return total_of(decoded[0], sent).astype(BF16)[None]


def solution(mesh):
    in_specs = (
        P("pool", "ep", None),
        P("pool", "ep", None),
        P(),
        P("ep", None, "half"),
        P("ep", None, "half"),
        P("ep", "half", None),
        P(),
        P("ep", "half"),
        P(None, "ep", None),
        P("pool", "ep", "half"),
        P("pool", "ep", "half"),
        P("pool", "ep", "half"),
        P("half", None),
    )
    out_specs = P("pool", ("ep", "half"), None)
    return jax.shard_map(
        on_device, mesh=mesh, in_specs=in_specs, out_specs=out_specs, check_vma=False
    )
```

profile of v0, /device:TPU:0, one launch (start us, length us, event | category | flops | bytes accessed | tf_op | source)
XLA Modules:
  0.0 161.0 jit_solution(11217818671294345456)
XLA Ops:
  2.9 3.1 %collective-permute-start.3 = (bf16[64,1152]{1,0:T(8,128)(2,1)S(1)}, bf16[64,1152]{1,0:T(8,128)(2,1)S(1)}, u32[]{:S(2)}, u32[]{:S(2)}) collective-permute-start(bf16[64,1152]{1,0:T(8,128)(2,1)S(1)} %pad_maximum_fusion.1), channel_id=1, source_target_pairs={{0,4},{4,8},{8,12},{12,0},{1,5},{5,9},{9,13},{13,1},{2,6},{6,10},{... | collective-permute-start | bytes 442376 | tf_op jit(solution)/shard_map/ppermute | solution.py:26
  6.0 2.6 %collective-permute-start.4 = (bf16[64,1152]{1,0:T(8,128)(2,1)S(1)}, bf16[64,1152]{1,0:T(8,128)(2,1)S(1)}, u32[]{:S(2)}, u32[]{:S(2)}) collective-permute-start(bf16[64,1152]{1,0:T(8,128)(2,1)S(1)} %pad_maximum_fusion.1), channel_id=1, source_target_pairs={{0,8},{4,12},{8,0},{12,4},{1,9},{5,13},{9,1},{13,5},{2,10},{6,14},... | collective-permute-start | bytes 442376 | tf_op jit(solution)/shard_map/ppermute | solution.py:26
  11.1 1.8 %collective-permute-done.3 = bf16[64,1152]{1,0:T(8,128)(2,1)S(1)} collective-permute-done((bf16[64,1152]{1,0:T(8,128)(2,1)S(1)}, bf16[64,1152]{1,0:T(8,128)(2,1)S(1)}, u32[]{:S(2)}, u32[]{:S(2)}) %collective-permute-start.3) | collective-permute-done | bytes 147488 | tf_op jit(solution)/shard_map/ppermute | solution.py:26
  12.9 2.5 %collective-permute-start.2 = (bf16[1024,256]{1,0:T(8,128)(2,1)S(1)}, bf16[1024,256]{1,0:T(8,128)(2,1)S(1)}, u32[]{:S(2)}, u32[]{:S(2)}) collective-permute-start(bf16[1024,256]{1,0:T(8,128)(2,1)S(1)} %constant_dynamic-slice_fusion), channel_id=1, source_target_pairs={{0,12},{4,0},{8,4},{12,8},{1,13},{5,1},{9,5},{13,9},{2,14},{6,2},{... | collective-permute-start | bytes 1572872 | tf_op jit(solution)/shard_map/ppermute | solution.py:26
  15.4 3.9 %collective-permute-done.4 = bf16[64,1152]{1,0:T(8,128)(2,1)S(1)} collective-permute-done((bf16[64,1152]{1,0:T(8,128)(2,1)S(1)}, bf16[64,1152]{1,0:T(8,128)(2,1)S(1)}, u32[]{:S(2)}, u32[]{:S(2)}) %collective-permute-start.4) | collective-permute-done | bytes 147488 | tf_op jit(solution)/shard_map/ppermute | solution.py:26
  19.2 10.3 %collective-permute-done.5 = bf16[64,1152]{1,0:T(8,128)(2,1)S(1)} collective-permute-done((bf16[64,1152]{1,0:T(8,128)(2,1)S(1)}, bf16[64,1152]{1,0:T(8,128)(2,1)S(1)}, u32[]{:S(2)}, u32[]{:S(2)}) %collective-permute-start.5) | collective-permute-done | bytes 147488 | tf_op jit(solution)/shard_map/ppermute | solution.py:26
  29.5 1.6 collective-permute-start.7
  31.1 1.5 collective-permute-start.8
  32.7 7.3 %expand.3 = (f32[8,256,768]{2,1,0:T(8,128)S(1)}, f32[256,32]{1,0:T(8,128)S(1)}) custom-call(s32[5]{0:T(128)S(1)} %pad_add_fusion.place, bf16[64,4096]{1,0:T(8,128)(2,1)S(1)} %bitcast.17, bf16[32,4096]{1,0:T(8,128)(2,1)S(1)} %bitcast.25, bf16[192,1024]{1,0:T(8,128)(2,1)S(1)} %pad_maximum_fusion.refs_0_, bf16[8,4096,384]{2,1,0:T(8,128)(2,1)} %refs_1_.3, ...), custom_call_target="tpu_custom_call" | custom-call | flops 3221225472 | bytes 12582912 | tf_op jit(solution)/shard_map/expand/pallas_call | solution.py:162
  40.3 1.5 collective-permute-start.6
  41.8 12.5 %expand.4 = (f32[8,256,768]{2,1,0:T(8,128)S(1)}, f32[256,32]{1,0:T(8,128)S(1)}) custom-call(s32[5]{0:T(128)S(1)} %pad_add_fusion.place, bf16[64,4096]{1,0:T(8,128)(2,1)S(1)} %bitcast.18, bf16[32,4096]{1,0:T(8,128)(2,1)S(1)} %bitcast.26, bf16[192,1024]{1,0:T(8,128)(2,1)S(1)} %collective-permute-done.7.refs_0_, ...), custom_call_target="tpu_custom_call", output_to_operand_aliasing={{0}: (9, {}), {1}: (10, {})} | custom-call | flops 6442450944 | bytes 25165824 | tf_op jit(solution)/shard_map/expand/pallas_call | solution.py:162
  54.2 8.1 %expand.5.hidden = bf16[256,3072]{1,0:T(8,128)(2,1)S(1)} custom-call(s32[5]{0:T(128)S(1)} %pad_add_fusion.place, bf16[64,4096]{1,0:T(8,128)(2,1)S(1)} %bitcast.19, bf16[32,4096]{1,0:T(8,128)(2,1)S(1)} %bitcast.27, bf16[192,1024]{1,0:T(8,128)(2,1)S(1)} %collective-permute-done.6.refs_0_, bf16[8,4096,384]{2,1,0:T(8,128)(2,1)} %refs_1_.3, ...), custom_call_target="tpu_custom_call" | custom-call | flops 3221225472 | bytes 12582912 | tf_op jit(solution)/shard_map/expand/pallas_call | solution.py:162
  62.4 4.5 %reduce.4 = bf16[256,1024]{1,0:T(8,128)(2,1)S(1)} custom-call(s32[5]{0:T(128)S(1)} %pad_add_fusion.place, bf16[256,3072]{1,0:T(8,128)(2,1)S(1)} %expand.5.hidden, bf16[8,384,4096]{2,1,0:T(8,128)(2,1)} %w_down.7), custom_call_target="tpu_custom_call" | custom-call | flops 1610612736 | bytes 6291456 | tf_op jit(solution)/shard_map/reduce/pallas_call | solution.py:194
  66.9 4.5 %reduce.6 = bf16[256,1024]{1,0:T(8,128)(2,1)S(1)} custom-call(s32[5]{0:T(128)S(1)} %pad_add_fusion.place, bf16[256,3072]{1,0:T(8,128)(2,1)S(1)} %expand.5.hidden, bf16[8,384,4096]{2,1,0:T(8,128)(2,1)} %w_down.7), custom_call_target="tpu_custom_call" | custom-call | flops 1610612736 | bytes 6291456 | tf_op jit(solution)/shard_map/reduce/pallas_call | solution.py:194
  71.4 4.5 %reduce.5 = bf16[256,1024]{1,0:T(8,128)(2,1)S(1)} custom-call(s32[5]{0:T(128)S(1)} %pad_add_fusion.place, bf16[256,3072]{1,0:T(8,128)(2,1)S(1)} %expand.5.hidden, bf16[8,384,4096]{2,1,0:T(8,128)(2,1)} %w_down.7), custom_call_target="tpu_custom_call" | custom-call | flops 1610612736 | bytes 6291456 | tf_op jit(solution)/shard_map/reduce/pallas_call | solution.py:194
  75.8 4.5 %reduce.7 = bf16[256,1024]{1,0:T(8,128)(2,1)S(1)} custom-call(s32[5]{0:T(128)S(1)} %pad_add_fusion.place, bf16[256,3072]{1,0:T(8,128)(2,1)S(1)} %expand.5.hidden, bf16[8,384,4096]{2,1,0:T(8,128)(2,1)} %w_down.7), custom_call_target="tpu_custom_call" | custom-call | flops 1610612736 | bytes 6291456 | tf_op jit(solution)/shard_map/reduce/pallas_call | solution.py:194
  81.2 2.2 %collective-permute-start.9 = (bf16[256,1024]{1,0:T(8,128)(2,1)S(1)}, bf16[256,1024]{1,0:T(8,128)(2,1)S(1)}, u32[]{:S(2)}, u32[]{:S(2)}) collective-permute-start(bf16[256,1024]{1,0:T(8,128)(2,1)S(1)} %reduce.5), channel_id=1, source_target_pairs={{0,3},{1,2},{2,1},{3,0},{4,7},{5,6},{6,5},{7,4},{8,11},{9,10},{10,... | collective-permute-start | bytes 1572872 | tf_op jit(solution)/shard_map/ppermute | solution.py:21
  84.1 11.1 %collective-permute-done.10 = bf16[256,1024]{1,0:T(8,128)(2,1)S(1)} collective-permute-done((bf16[256,1024]{1,0:T(8,128)(2,1)S(1)}, bf16[256,1024]{1,0:T(8,128)(2,1)S(1)}, u32[]{:S(2)}, u32[]{:S(2)}) %collective-permute-start.10) | collective-permute-done | bytes 524320 | tf_op jit(solution)/shard_map/ppermute | solution.py:21
  95.3 1.5 collective-permute-done.11
  97.9 26.0 %collective-permute-start.13 = (bf16[64,1024]{1,0:T(8,128)(2,1)S(1)}, bf16[64,1024]{1,0:T(8,128)(2,1)S(1)}, u32[]{:S(2)}, u32[]{:S(2)}) collective-permute-start(bf16[64,1024]{1,0:T(8,128)(2,1)S(1)} %get-tuple-element.29), channel_id=1, source_target_pairs={{0,8},{4,12},{8,0},{12,4},{1,9},{5,13},{9,1},{13,5},{2,10},{6,14},... | collective-permute-start | bytes 393224 | tf_op jit(solution)/shard_map/ppermute | solution.py:26
  123.9 2.9 %collective-permute-done.12 = bf16[64,1024]{1,0:T(8,128)(2,1)S(1)} collective-permute-done((bf16[64,1024]{1,0:T(8,128)(2,1)S(1)}, bf16[64,1024]{1,0:T(8,128)(2,1)S(1)}, u32[]{:S(2)}, u32[]{:S(2)}) %collective-permute-start.12) | collective-permute-done | bytes 131104 | tf_op jit(solution)/shard_map/ppermute | solution.py:26
  126.8 6.6 %collective-permute-done.13 = bf16[64,1024]{1,0:T(8,128)(2,1)S(1)} collective-permute-done((bf16[64,1024]{1,0:T(8,128)(2,1)S(1)}, bf16[64,1024]{1,0:T(8,128)(2,1)S(1)}, u32[]{:S(2)}, u32[]{:S(2)}) %collective-permute-start.13) | collective-permute-done | bytes 131104 | tf_op jit(solution)/shard_map/ppermute | solution.py:26
  134.6 2.4 %collective-permute-start.17 = (bf16[64,1024]{1,0:T(8,128)(2,1)S(1)}, bf16[64,1024]{1,0:T(8,128)(2,1)S(1)}, u32[]{:S(2)}, u32[]{:S(2)}) collective-permute-start(bf16[64,1024]{1,0:T(8,128)(2,1)S(1)} %fusion.3.refs_0_), channel_id=1, source_target_pairs={{0,3},{1,2},{2,1},{3,0},{4,7},{5,6},{6,5},{7,4},{8,11},{9,10},{10,... | collective-permute-start | bytes 393224 | tf_op jit(solution)/shard_map/ppermute | solution.py:21
  137.0 1.5 collective-permute-done.15.refs_1_
  139.0 1.4 collective-permute-done.17.refs_3_
  140.5 1.7 %project.1 = bf16[64,512]{1,0:T(8,128)(2,1)S(1)} custom-call(s32[5]{0:T(128)S(1)} %pad_add_fusion.place, bf16[64,4096]{1,0:T(8,128)(2,1)S(1)} %bitcast.20, bf16[64,1024]{1,0:T(8,128)(2,1)S(1)} %fusion.3.refs_0_, bf16[64,1024]{1,0:T(8,128)(2,1)S(1)} %collective-permute-done.15.refs_1_, bf16[64,1024]{1,0:T(8,128)(2,1)S(1)} %collective-permute-done.16.refs_2_, ...), custom_call_target="tpu_custom_call" | custom-call | tf_op jit(solution)/shard_map/project/pallas_call | solution.py:250
  143.5 1.6 %attend.5 = bf16[64,2048]{1,0:T(8,128)(2,1)S(1)} custom-call(s32[5]{0:T(128)S(1)} %pad_add_fusion.place, bf16[64,512]{1,0:T(8,128)(2,1)S(1)} %collective-permute-done.19.block, bf16[256,512]{1,0:T(8,128)(2,1)S(1)} %bitcast.21, bf16[256,256]{1,0:T(8,128)(2,1)S(1)} %bitcast.28, bf16[256,256]{1,0:T(8,128)(2,1)S(1)} %bitcast.32, bf16[512,2048]{1,0:T(8,128)(2,1)S(1)} %copy-done.2), custom_call_target="tpu_custom_call" | custom-call | flops 268435456 | bytes 2097152 | tf_op jit(solution)/shard_map/attend/pallas_call | solution.py:324
  145.1 2.5 %collective-permute-start.20 = (bf16[64,2048]{1,0:T(8,128)(2,1)S(1)}, bf16[64,2048]{1,0:T(8,128)(2,1)S(1)}, u32[]{:S(2)}, u32[]{:S(2)}) collective-permute-start(bf16[64,2048]{1,0:T(8,128)(2,1)S(1)} %attend.5), channel_id=1, source_target_pairs={{0,3},{1,2},{2,1},{3,0},{4,7},{5,6},{6,5},{7,4},{8,11},{9,10},{10,... | collective-permute-start | bytes 786440 | tf_op jit(solution)/shard_map/ppermute | solution.py:21
  147.6 1.6 %attend.6 = bf16[64,2048]{1,0:T(8,128)(2,1)S(1)} custom-call(s32[5]{0:T(128)S(1)} %pad_add_fusion.place, bf16[64,512]{1,0:T(8,128)(2,1)S(1)} %collective-permute-done.19.block, bf16[256,512]{1,0:T(8,128)(2,1)S(1)} %bitcast.22, bf16[256,256]{1,0:T(8,128)(2,1)S(1)} %bitcast.29, bf16[256,256]{1,0:T(8,128)(2,1)S(1)} %bitcast.33, bf16[512,2048]{1,0:T(8,128)(2,1)S(1)} %copy-done.2), custom_call_target="tpu_custom_call" | custom-call | flops 268435456 | bytes 2097152 | tf_op jit(solution)/shard_map/attend/pallas_call | solution.py:324
  149.8 1.6 %attend.7 = bf16[64,2048]{1,0:T(8,128)(2,1)S(1)} custom-call(s32[5]{0:T(128)S(1)} %pad_add_fusion.place, bf16[64,512]{1,0:T(8,128)(2,1)S(1)} %collective-permute-done.19.block, bf16[256,512]{1,0:T(8,128)(2,1)S(1)} %bitcast.23, bf16[256,256]{1,0:T(8,128)(2,1)S(1)} %bitcast.30, bf16[256,256]{1,0:T(8,128)(2,1)S(1)} %bitcast.34, bf16[512,2048]{1,0:T(8,128)(2,1)S(1)} %copy-done.2), custom_call_target="tpu_custom_call" | custom-call | flops 268435456 | bytes 2097152 | tf_op jit(solution)/shard_map/attend/pallas_call | solution.py:324
  152.1 1.6 %attend.4 = bf16[64,2048]{1,0:T(8,128)(2,1)S(1)} custom-call(s32[5]{0:T(128)S(1)} %pad_add_fusion.place, bf16[64,512]{1,0:T(8,128)(2,1)S(1)} %collective-permute-done.19.block, bf16[256,512]{1,0:T(8,128)(2,1)S(1)} %bitcast.24, bf16[256,256]{1,0:T(8,128)(2,1)S(1)} %bitcast.31, bf16[256,256]{1,0:T(8,128)(2,1)S(1)} %bitcast.35, bf16[512,2048]{1,0:T(8,128)(2,1)S(1)} %copy-done.2), custom_call_target="tpu_custom_call" | custom-call | flops 268435456 | bytes 2097152 | tf_op jit(solution)/shard_map/attend/pallas_call | solution.py:324
  154.6 5.5 %collective-permute-done.21 = bf16[64,2048]{1,0:T(8,128)(2,1)S(1)} collective-permute-done((bf16[64,2048]{1,0:T(8,128)(2,1)S(1)}, bf16[64,2048]{1,0:T(8,128)(2,1)S(1)}, u32[]{:S(2)}, u32[]{:S(2)}) %collective-permute-start.21) | collective-permute-done | bytes 262176 | tf_op jit(solution)/shard_map/ppermute | solution.py:21
  (69 shorter events, 14.3 us)
Async XLA Ops:
  0.0 11.0 %copy-start = (s32[2,1,2]{2,1,0:T(1,128)S(1)}, s32[2,1,2]{2,1,0:T(1,128)}, u32[]{:S(2)}) copy-start(s32[2,1,2]{2,1,0:T(1,128)} %param.21) | copy-start | bytes 52
  0.8 31.9 %copy-start.3 = (bf16[1,64,4096]{2,1,0:T(8,128)(2,1)S(1)}, bf16[1,64,4096]{2,1,0:T(8,128)(2,1)}, u32[]{:S(2)}) copy-start(bf16[1,64,4096]{2,1,0:T(8,128)(2,1)} %param.13) | copy-start | bytes 1572868
  0.8 31.9 %copy-start.5 = (bf16[4096,32]{0,1:T(8,128)(2,1)S(1)}, bf16[4096,32]{0,1:T(8,128)(2,1)}, u32[]{:S(2)}) copy-start(bf16[4096,32]{0,1:T(8,128)(2,1)} %param.15) | copy-start | bytes 786436
  2.9 9.9 %collective-permute-start.3 = (bf16[64,1152]{1,0:T(8,128)(2,1)S(1)}, bf16[64,1152]{1,0:T(8,128)(2,1)S(1)}, u32[]{:S(2)}, u32[]{:S(2)}) collective-permute-start(bf16[64,1152]{1,0:T(8,128)(2,1)S(1)} %pad_maximum_fusion.1), channel_id=1, source_target_pairs={{0,4},{4,8},{8,12},{12,0},{1,5},{5,9},{9,13},{13,1},{2,6},{6,10},{... | collective-permute-start | bytes 442376 | tf_op jit(solution)/shard_map/ppermute | solution.py:26
  6.0 13.2 %collective-permute-start.4 = (bf16[64,1152]{1,0:T(8,128)(2,1)S(1)}, bf16[64,1152]{1,0:T(8,128)(2,1)S(1)}, u32[]{:S(2)}, u32[]{:S(2)}) collective-permute-start(bf16[64,1152]{1,0:T(8,128)(2,1)S(1)} %pad_maximum_fusion.1), channel_id=1, source_target_pairs={{0,8},{4,12},{8,0},{12,4},{1,9},{5,13},{9,1},{13,5},{2,10},{6,14},... | collective-permute-start | bytes 442376 | tf_op jit(solution)/shard_map/ppermute | solution.py:26
  8.6 20.9 %collective-permute-start.5 = (bf16[64,1152]{1,0:T(8,128)(2,1)S(1)}, bf16[64,1152]{1,0:T(8,128)(2,1)S(1)}, u32[]{:S(2)}, u32[]{:S(2)}) collective-permute-start(bf16[64,1152]{1,0:T(8,128)(2,1)S(1)} %pad_maximum_fusion.1), channel_id=1, source_target_pairs={{0,12},{4,0},{8,4},{12,8},{1,13},{5,1},{9,5},{13,9},{2,14},{6,2},{... | collective-permute-start | bytes 442376 | tf_op jit(solution)/shard_map/ppermute | solution.py:26
  10.0 70.4 %collective-permute-start = (bf16[1024,256]{1,0:T(8,128)(2,1)S(1)}, bf16[1024,256]{1,0:T(8,128)(2,1)S(1)}, u32[]{:S(2)}, u32[]{:S(2)}) collective-permute-start(bf16[1024,256]{1,0:T(8,128)(2,1)S(1)} %constant_dynamic-slice_fusion), channel_id=1, source_target_pairs={{0,4},{4,8},{8,12},{12,0},{1,5},{5,9},{9,13},{13,1},{2,6},{6,10},{... | collective-permute-start | bytes 1572872 | tf_op jit(solution)/shard_map/ppermute | solution.py:26
  10.7 69.7 %collective-permute-start.1 = (bf16[1024,256]{1,0:T(8,128)(2,1)S(1)}, bf16[1024,256]{1,0:T(8,128)(2,1)S(1)}, u32[]{:S(2)}, u32[]{:S(2)}) collective-permute-start(bf16[1024,256]{1,0:T(8,128)(2,1)S(1)} %constant_dynamic-slice_fusion), channel_id=1, source_target_pairs={{0,8},{4,12},{8,0},{12,4},{1,9},{5,13},{9,1},{13,5},{2,10},{6,14},... | collective-permute-start | bytes 1572872 | tf_op jit(solution)/shard_map/ppermute | solution.py:26
  12.9 67.5 %collective-permute-start.2 = (bf16[1024,256]{1,0:T(8,128)(2,1)S(1)}, bf16[1024,256]{1,0:T(8,128)(2,1)S(1)}, u32[]{:S(2)}, u32[]{:S(2)}) collective-permute-start(bf16[1024,256]{1,0:T(8,128)(2,1)S(1)} %constant_dynamic-slice_fusion), channel_id=1, source_target_pairs={{0,12},{4,0},{8,4},{12,8},{1,13},{5,1},{9,5},{13,9},{2,14},{6,2},{... | collective-permute-start | bytes 1572872 | tf_op jit(solution)/shard_map/ppermute | solution.py:26
  29.5 10.7 %collective-permute-start.7 = (bf16[192,1024]{1,0:T(8,128)(2,1)S(1)}, bf16[192,1024]{1,0:T(8,128)(2,1)S(1)}, u32[]{:S(2)}, u32[]{:S(2)}) collective-permute-start(bf16[192,1024]{1,0:T(8,128)(2,1)S(1)} %pad_maximum_fusion.refs_0_), channel_id=1, source_target_pairs={{0,1},{1,0},{2,3},{3,2},{4,5},{5,4},{6,7},{7,6},{8,9},{9,8},{10,11... | collective-permute-start | bytes 1179656 | tf_op jit(solution)/shard_map/ppermute | solution.py:21
  31.1 10.7 %collective-permute-start.8 = (bf16[192,1024]{1,0:T(8,128)(2,1)S(1)}, bf16[192,1024]{1,0:T(8,128)(2,1)S(1)}, u32[]{:S(2)}, u32[]{:S(2)}) collective-permute-start(bf16[192,1024]{1,0:T(8,128)(2,1)S(1)} %pad_maximum_fusion.refs_0_), channel_id=1, source_target_pairs={{0,2},{1,3},{2,0},{3,1},{4,6},{5,7},{6,4},{7,5},{8,10},{9,11},{10,... | collective-permute-start | bytes 1179656 | tf_op jit(solution)/shard_map/ppermute | solution.py:21
  40.3 14.0 %collective-permute-start.6 = (bf16[192,1024]{1,0:T(8,128)(2,1)S(1)}, bf16[192,1024]{1,0:T(8,128)(2,1)S(1)}, u32[]{:S(2)}, u32[]{:S(2)}) collective-permute-start(bf16[192,1024]{1,0:T(8,128)(2,1)S(1)} %pad_maximum_fusion.refs_0_), channel_id=1, source_target_pairs={{0,3},{1,2},{2,1},{3,0},{4,7},{5,6},{6,5},{7,4},{8,11},{9,10},{10,... | collective-permute-start | bytes 1179656 | tf_op jit(solution)/shard_map/ppermute | solution.py:21
  80.4 14.9 %collective-permute-start.10 = (bf16[256,1024]{1,0:T(8,128)(2,1)S(1)}, bf16[256,1024]{1,0:T(8,128)(2,1)S(1)}, u32[]{:S(2)}, u32[]{:S(2)}) collective-permute-start(bf16[256,1024]{1,0:T(8,128)(2,1)S(1)} %reduce.6), channel_id=1, source_target_pairs={{0,2},{1,3},{2,0},{3,1},{4,6},{5,7},{6,4},{7,5},{8,10},{9,11},{10,... | collective-permute-start | bytes 1572872 | tf_op jit(solution)/shard_map/ppermute | solution.py:21
  81.2 14.0 %collective-permute-start.9 = (bf16[256,1024]{1,0:T(8,128)(2,1)S(1)}, bf16[256,1024]{1,0:T(8,128)(2,1)S(1)}, u32[]{:S(2)}, u32[]{:S(2)}) collective-permute-start(bf16[256,1024]{1,0:T(8,128)(2,1)S(1)} %reduce.5), channel_id=1, source_target_pairs={{0,3},{1,2},{2,1},{3,0},{4,7},{5,6},{6,5},{7,4},{8,11},{9,10},{10,... | collective-permute-start | bytes 1572872 | tf_op jit(solution)/shard_map/ppermute | solution.py:21
  83.5 13.3 %collective-permute-start.11 = (bf16[256,1024]{1,0:T(8,128)(2,1)S(1)}, bf16[256,1024]{1,0:T(8,128)(2,1)S(1)}, u32[]{:S(2)}, u32[]{:S(2)}) collective-permute-start(bf16[256,1024]{1,0:T(8,128)(2,1)S(1)} %reduce.7), channel_id=1, source_target_pairs={{0,1},{1,0},{2,3},{3,2},{4,5},{5,4},{6,7},{7,6},{8,9},{9,8},{10,11... | collective-permute-start | bytes 1572872 | tf_op jit(solution)/shard_map/ppermute | solution.py:21
  84.1 56.4 %collective-permute-start.18 = (bf16[3072,256]{1,0:T(8,128)(2,1)S(1)}, bf16[3072,256]{1,0:T(8,128)(2,1)S(1)}, u32[]{:S(2)}, u32[]{:S(2)}) collective-permute-start(bf16[3072,256]{1,0:T(8,128)(2,1)S(1)} %constant_dynamic-update-slice_fusion.refs_6_), channel_id=1, source_target_pairs={{0,16},{16,0},{1,17},{17,1},{2,18},{18,2},{3,19},{19,3},{4,20},{20... | collective-permute-start | bytes 4718600 | tf_op jit(solution)/shard_map/ppermute | solution.py:21
  97.2 43.2 %copy-start.6 = (bf16[1024,512]{1,0:T(8,128)(2,1)S(1)}, bf16[1024,512]{1,0:T(8,128)(2,1)}, u32[]{:S(2)}) copy-start(bf16[1024,512]{1,0:T(8,128)(2,1)} %refs_5_.3) | copy-start | bytes 3145732
  97.2 43.2 %copy-start.9 = (f32[4096]{0:T(1024)S(1)}, f32[4096]{0:T(1024)}, u32[]{:S(2)}) copy-start(f32[4096]{0:T(1024)} %param.19) | copy-start | bytes 49156
  97.3 29.5 %collective-permute-start.12 = (bf16[64,1024]{1,0:T(8,128)(2,1)S(1)}, bf16[64,1024]{1,0:T(8,128)(2,1)S(1)}, u32[]{:S(2)}, u32[]{:S(2)}) collective-permute-start(bf16[64,1024]{1,0:T(8,128)(2,1)S(1)} %get-tuple-element.27), channel_id=1, source_target_pairs={{0,12},{4,0},{8,4},{12,8},{1,13},{5,1},{9,5},{13,9},{2,14},{6,2},{... | collective-permute-start | bytes 393224 | tf_op jit(solution)/shard_map/ppermute | solution.py:26
  97.9 35.5 %collective-permute-start.13 = (bf16[64,1024]{1,0:T(8,128)(2,1)S(1)}, bf16[64,1024]{1,0:T(8,128)(2,1)S(1)}, u32[]{:S(2)}, u32[]{:S(2)}) collective-permute-start(bf16[64,1024]{1,0:T(8,128)(2,1)S(1)} %get-tuple-element.29), channel_id=1, source_target_pairs={{0,8},{4,12},{8,0},{12,4},{1,9},{5,13},{9,1},{13,5},{2,10},{6,14},... | collective-permute-start | bytes 393224 | tf_op jit(solution)/shard_map/ppermute | solution.py:26
  123.9 9.5 %collective-permute-start.14 = (bf16[64,1024]{1,0:T(8,128)(2,1)S(1)}, bf16[64,1024]{1,0:T(8,128)(2,1)S(1)}, u32[]{:S(2)}, u32[]{:S(2)}) collective-permute-start(bf16[64,1024]{1,0:T(8,128)(2,1)S(1)} %get-tuple-element.28), channel_id=1, source_target_pairs={{0,4},{4,8},{8,12},{12,0},{1,5},{5,9},{9,13},{13,1},{2,6},{6,10},{... | collective-permute-start | bytes 393224 | tf_op jit(solution)/shard_map/ppermute | solution.py:26
  133.5 5.0 %collective-permute-start.15 = (bf16[64,1024]{1,0:T(8,128)(2,1)S(1)}, bf16[64,1024]{1,0:T(8,128)(2,1)S(1)}, u32[]{:S(2)}, u32[]{:S(2)}) collective-permute-start(bf16[64,1024]{1,0:T(8,128)(2,1)S(1)} %fusion.3.refs_0_), channel_id=1, source_target_pairs={{0,1},{1,0},{2,3},{3,2},{4,5},{5,4},{6,7},{7,6},{8,9},{9,8},{10,11... | collective-permute-start | bytes 393224 | tf_op jit(solution)/shard_map/ppermute | solution.py:21
  134.0 5.0 %collective-permute-start.16 = (bf16[64,1024]{1,0:T(8,128)(2,1)S(1)}, bf16[64,1024]{1,0:T(8,128)(2,1)S(1)}, u32[]{:S(2)}, u32[]{:S(2)}) collective-permute-start(bf16[64,1024]{1,0:T(8,128)(2,1)S(1)} %fusion.3.refs_0_), channel_id=1, source_target_pairs={{0,2},{1,3},{2,0},{3,1},{4,6},{5,7},{6,4},{7,5},{8,10},{9,11},{10,... | collective-permute-start | bytes 393224 | tf_op jit(solution)/shard_map/ppermute | solution.py:21
  134.6 5.9 %collective-permute-start.17 = (bf16[64,1024]{1,0:T(8,128)(2,1)S(1)}, bf16[64,1024]{1,0:T(8,128)(2,1)S(1)}, u32[]{:S(2)}, u32[]{:S(2)}) collective-permute-start(bf16[64,1024]{1,0:T(8,128)(2,1)S(1)} %fusion.3.refs_0_), channel_id=1, source_target_pairs={{0,3},{1,2},{2,1},{3,0},{4,7},{5,6},{6,5},{7,4},{8,11},{9,10},{10,... | collective-permute-start | bytes 393224 | tf_op jit(solution)/shard_map/ppermute | solution.py:21
  140.4 3.0 %copy-start.2 = (bf16[512,2048]{1,0:T(8,128)(2,1)S(1)}, bf16[512,2048]{1,0:T(8,128)(2,1)}, u32[]{:S(2)}) copy-start(bf16[512,2048]{1,0:T(8,128)(2,1)} %w_out.7) | copy-start | bytes 6291460
  140.5 3.0 %copy-start.4 = (bf16[1,256,512]{2,1,0:T(8,128)(2,1)S(1)}, bf16[1,256,512]{2,1,0:T(8,128)(2,1)}, u32[]{:S(2)}) copy-start(bf16[1,256,512]{2,1,0:T(8,128)(2,1)} %param.22) | copy-start | bytes 786436
  140.5 3.0 %copy-start.7 = (bf16[1,256,256]{2,1,0:T(8,128)(2,1)S(1)}, bf16[1,256,256]{2,1,0:T(8,128)(2,1)}, u32[]{:S(2)}) copy-start(bf16[1,256,256]{2,1,0:T(8,128)(2,1)} %param.23) | copy-start | bytes 393220
  142.2 1.3 collective-permute-start.19
  145.1 9.4 %collective-permute-start.20 = (bf16[64,2048]{1,0:T(8,128)(2,1)S(1)}, bf16[64,2048]{1,0:T(8,128)(2,1)S(1)}, u32[]{:S(2)}, u32[]{:S(2)}) collective-permute-start(bf16[64,2048]{1,0:T(8,128)(2,1)S(1)} %attend.5), channel_id=1, source_target_pairs={{0,3},{1,2},{2,1},{3,0},{4,7},{5,6},{6,5},{7,4},{8,11},{9,10},{10,... | collective-permute-start | bytes 786440 | tf_op jit(solution)/shard_map/ppermute | solution.py:21
  149.3 10.8 %collective-permute-start.21 = (bf16[64,2048]{1,0:T(8,128)(2,1)S(1)}, bf16[64,2048]{1,0:T(8,128)(2,1)S(1)}, u32[]{:S(2)}, u32[]{:S(2)}) collective-permute-start(bf16[64,2048]{1,0:T(8,128)(2,1)S(1)} %attend.6), channel_id=1, source_target_pairs={{0,2},{1,3},{2,0},{3,1},{4,6},{5,7},{6,4},{7,5},{8,10},{9,11},{10,... | collective-permute-start | bytes 786440 | tf_op jit(solution)/shard_map/ppermute | solution.py:21
  149.8 11.2 %copy-start.1 = (s32[2,1,2]{2,1,0:T(1,128)S(1)}, s32[2,1,2]{2,1,0:T(1,128)}, u32[]{:S(2)}) copy-start(s32[2,1,2]{2,1,0:T(1,128)} %param.21) | copy-start | bytes 52
  151.5 8.7 %collective-permute-start.22 = (bf16[64,2048]{1,0:T(8,128)(2,1)S(1)}, bf16[64,2048]{1,0:T(8,128)(2,1)S(1)}, u32[]{:S(2)}, u32[]{:S(2)}) collective-permute-start(bf16[64,2048]{1,0:T(8,128)(2,1)S(1)} %attend.7), channel_id=1, source_target_pairs={{0,1},{1,0},{2,3},{3,2},{4,5},{5,4},{6,7},{7,6},{8,9},{9,8},{10,11... | collective-permute-start | bytes 786440 | tf_op jit(solution)/shard_map/ppermute | solution.py:21
  (1 other events, 3.0 us)
where the time goes:
time: 161 us
  Pallas kernels  54 us (34%)
  starting transfers between devices  52.6 us (33%)
  waiting for transfers between devices  49.5 us (31%)
  local copies, waits for them, and re-layouts  3.09 us (2%)
    ppermute x9, starting transfers between devices, shift(): lax.ppermute(shard, axis, [(i, (i + distance) % count) for i in range(cou...  37.2 us
    pallas_call x3, Pallas kernels, expand(): pl.pallas_call(kernel, out_shape=out_shape, grid_spec=pltpu.PrefetchScala...  27.9 us
    ppermute x9, waiting for transfers between devices, shift(): lax.ppermute(shard, axis, [(i, (i + distance) % count) for i in range(cou...  25.4 us
    ppermute x14, waiting for transfers between devices, swap(): lax.ppermute(shard, axis, [(i, i ^ bits) for i in range(lax.axis_size(axi...  24.1 us
    pallas_call x4, Pallas kernels, reduce(): pl.pallas_call(reduce_kernel, out_shape=jax.ShapeDtypeStruct((tokens, wid...  18 us
    ppermute x14, starting transfers between devices, swap(): lax.ppermute(shard, axis, [(i, i ^ bits) for i in range(lax.axis_size(axi...  15.5 us
    pallas_call x4, Pallas kernels, attend(): pl.pallas_call(functools.partial(attend_kernel, k, prompts), out_shape=ja...  6.49 us
  transfers between devices with their start and end apart: 23, of which 15 were waited for; matrix products, arithmetic and copies ran while one was open for 0% of the time, Pallas kernels for 32%

commit v1 on v0

--- a/solution.py
+++ b/solution.py
@@ -216,10 +216,9 @@
     )(place, in_vmem(hidden), in_hbm(w_down))
 
 
-def project_kernel(parts, eps, place, own, *refs):
+def project_kernel(parts, origins, place, own, *refs):
     moe, refs = refs[:parts], refs[parts:]
-    gain, home, refs = refs[0], refs[1], refs[2:]
-    mine, theirs, out, mixed, normed = refs
+    gain, mine, theirs, out, mixed, normed = refs
     half, ep, pool = place[0], place[1], place[2]
     width = moe[0].shape[1]
     square = jnp.zeros((own.shape[0], 1), F32)
@@ -230,36 +229,32 @@
         square += jnp.sum(value * value, axis=1, keepdims=True)
     factor = lax.rsqrt(square / mixed.shape[1] + 1e-06)
     normed[...] = (mixed[...] * factor * gain[...]).astype(BF16)
-    depth, narrow = home.shape[0], mine.shape[1]
+    depth, narrow = mine.shape[0] // len(origins), mine.shape[1]
     for side, pieces in ((pool, mine), (1 - pool, theirs)):
-        kept = columns_of(side, narrow)
-        total = jnp.dot(
-            normed[:, columns_of(ep, depth)], home[:, kept], preferred_element_type=F32
-        )
-        for d in range(1, eps):
-            origin = lax.rem(ep + eps - d, eps)
+        total = 0.0
+        for i, origin in enumerate(origins):
             total += jnp.dot(
-                normed[:, columns_of(origin, depth)],
-                pieces[(d - 1) * depth : d * depth, :],
+                normed[:, columns_of(ep ^ origin, depth)],
+                pieces[i * depth : (i + 1) * depth, :],
                 preferred_element_type=F32,
             )
-        out[:, kept] = total.astype(BF16)
-
-
-def project(place, own, moe, gain, home, mine, theirs, eps):
+        out[:, columns_of(side, narrow)] = total.astype(BF16)
+
+
+def project(place, own, moe, gain, mine, theirs, origins):
     return pl.pallas_call(
-        functools.partial(project_kernel, len(moe), eps),
-        out_shape=jax.ShapeDtypeStruct((own.shape[0], home.shape[1]), BF16),
+        functools.partial(project_kernel, len(moe), origins),
+        out_shape=jax.ShapeDtypeStruct((own.shape[0], 2 * mine.shape[1]), BF16),
         grid_spec=pltpu.PrefetchScalarGridSpec(
             num_scalar_prefetch=1,
             grid=(),
-            in_specs=[WHOLE] * (len(moe) + 5),
+            in_specs=[WHOLE] * (len(moe) + 4),
             out_specs=WHOLE,
             scratch_shapes=[pltpu.VMEM(own.shape, F32), pltpu.VMEM(own.shape, BF16)],
         ),
         compiler_params=params(0, 12),
         name="project",
-    )(place, own, *moe, gain, home, mine, theirs)
+    )(place, own, *moe, gain, mine, theirs)
 
 
 def attend_kernel(k, prompts, place, block, query, fresh_key, fresh_value, w_out, out):
@@ -378,17 +373,22 @@
     tags = jnp.pad(chosen.astype(BF16), ((0, 0), (0, LANES - top)))
     quarter = lax.dynamic_slice_in_dim(own, half * width, width, axis=1)
     parcel = jnp.concatenate([quarter, tags], axis=1)
-    piece, parcel = lax.optimization_barrier(
-        (lax.dynamic_slice_in_dim(w_kv, pool * narrow, narrow, axis=1), parcel)
-    )
     arrived = [shift(parcel, "ep", d) for d in range(1, eps)]
     near = jnp.concatenate([a[:, :width] for a in arrived], axis=0)
     all_tags = jnp.concatenate([tags] + [a[:, width:] for a in arrived], axis=0)
     order = sorted(range(1, parts), key=lambda k: bin(k).count("1"))
     far = order[::-1]
-    others = {k: swap(near, "half", k) for k in order}
+    others = {k: swap(near, "half", k) for k in order[:-1]}
+    others[order[-1]] = swap(near, "half", order[-1])
+    mine, near = lax.optimization_barrier(
+        (lax.dynamic_slice_in_dim(w_kv, pool * narrow, narrow, axis=1), near)
+    )
     others[0] = near
-    pieces = [shift(piece, "ep", d) for d in range(1, eps)]
+    origins = [0]
+    for i in range(eps.bit_length() - 1):
+        bit = eps >> i + 1
+        mine = jnp.concatenate([mine, swap(mine, "ep", bit)], axis=0)
+        origins += [origin ^ bit for origin in origins]
 
     totals = ()
     batches = [[0], order[:-1], order[-1:]]
@@ -412,8 +412,7 @@
     gathered = []
     for k in far:
         gathered.append(swap(partial[k], "half", k))
-    pieces, partial[0] = lax.optimization_barrier((pieces, partial[0]))
-    mine = jnp.concatenate(pieces, axis=0)
+    mine, partial[0] = lax.optimization_barrier((mine, partial[0]))
     theirs = swap(mine, "pool", 1)
     summed = total_of(partial[0], gathered)
     returned = [
@@ -423,7 +422,7 @@
     moe = [moe_quarter] + [None] * (parts - 1)
     for k in order:
         moe[k] = swap(moe_quarter, "half", k)
-    keyvals = project(place, own, moe, norm_gain[None], w_kv, mine, theirs, eps)
+    keyvals = project(place, own, moe, norm_gain[None], mine, theirs, origins)
     block = swap(keyvals, "pool", 1)
 
     rows = queries.shape[1] // parts

time: 161 us -> 155 us (0.963)
  starting transfers between devices: 52.6 us -> 30.4 us
  waiting for transfers between devices: 49.5 us -> 66.1 us
    ppermute x9 -> x6, starting transfers between devices: 37.2 us -> 12.5 us  [shift(): lax.ppermute(shard, axis, [(i, (i + distance) % count) for i in range(cou...]
    ppermute x14 -> x16, waiting for transfers between devices: 24.1 us -> 48.5 us  [swap(): lax.ppermute(shard, axis, [(i, i ^ bits) for i in range(lax.axis_size(axi...]
    ppermute x9 -> x6, waiting for transfers between devices: 25.4 us -> 17.6 us  [shift(): lax.ppermute(shard, axis, [(i, (i + distance) % count) for i in range(cou...]
    ppermute x14 -> x16, starting transfers between devices: 15.5 us -> 17.9 us  [swap(): lax.ppermute(shard, axis, [(i, i ^ bits) for i in range(lax.axis_size(axi...]
  transfers between devices with their start and end apart: 23 -> 22, of which waited for: 15 -> 13; matrix products, arithmetic and copies ran while one was open for 0% -> 1% of each run, Pallas kernels for 32% -> 33%
where the time goes in v1:
time: 155 us
  waiting for transfers between devices  66.1 us (43%)
  Pallas kernels  54.1 us (35%)
  starting transfers between devices  30.4 us (20%)
  local copies, waits for them, and re-layouts  2.63 us (2%)
  other arithmetic  1.62 us (1%)
    ppermute x16, waiting for transfers between devices, swap(): lax.ppermute(shard, axis, [(i, i ^ bits) for i in range(lax.axis_size(axi...  48.5 us
    pallas_call x3, Pallas kernels, expand(): pl.pallas_call(kernel, out_shape=out_shape, grid_spec=pltpu.PrefetchScala...  27.9 us
    pallas_call x4, Pallas kernels, reduce(): pl.pallas_call(reduce_kernel, out_shape=jax.ShapeDtypeStruct((tokens, wid...  18 us
    ppermute x16, starting transfers between devices, swap(): lax.ppermute(shard, axis, [(i, i ^ bits) for i in range(lax.axis_size(axi...  17.9 us
    ppermute x6, waiting for transfers between devices, shift(): lax.ppermute(shard, axis, [(i, (i + distance) % count) for i in range(cou...  17.6 us
    ppermute x6, starting transfers between devices, shift(): lax.ppermute(shard, axis, [(i, (i + distance) % count) for i in range(cou...  12.5 us
    pallas_call x4, Pallas kernels, attend(): pl.pallas_call(functools.partial(attend_kernel, k, prompts), out_shape=ja...  6.48 us
  transfers between devices with their start and end apart: 22, of which 13 were waited for; matrix products, arithmetic and copies ran while one was open for 1% of the time, Pallas kernels for 33%

profile of v1, /device:TPU:0, one launch (start us, length us, event | category | flops | bytes accessed | tf_op | source)
XLA Modules:
  0.0 155.2 jit_solution(7371480168929296508)
XLA Ops:
  1.9 3.1 %collective-permute-start = (bf16[64,1152]{1,0:T(8,128)(2,1)S(1)}, bf16[64,1152]{1,0:T(8,128)(2,1)S(1)}, u32[]{:S(2)}, u32[]{:S(2)}) collective-permute-start(bf16[64,1152]{1,0:T(8,128)(2,1)S(1)} %pad_maximum_fusion.3), channel_id=1, source_target_pairs={{0,4},{4,8},{8,12},{12,0},{1,5},{5,9},{9,13},{13,1},{2,6},{6,10},{... | collective-permute-start | bytes 442376 | tf_op jit(solution)/shard_map/ppermute | solution.py:26
  5.0 2.6 %collective-permute-start.1 = (bf16[64,1152]{1,0:T(8,128)(2,1)S(1)}, bf16[64,1152]{1,0:T(8,128)(2,1)S(1)}, u32[]{:S(2)}, u32[]{:S(2)}) collective-permute-start(bf16[64,1152]{1,0:T(8,128)(2,1)S(1)} %pad_maximum_fusion.3), channel_id=1, source_target_pairs={{0,8},{4,12},{8,0},{12,4},{1,9},{5,13},{9,1},{13,5},{2,10},{6,14},... | collective-permute-start | bytes 442376 | tf_op jit(solution)/shard_map/ppermute | solution.py:26
  9.6 2.2 %collective-permute-done = bf16[64,1152]{1,0:T(8,128)(2,1)S(1)} collective-permute-done((bf16[64,1152]{1,0:T(8,128)(2,1)S(1)}, bf16[64,1152]{1,0:T(8,128)(2,1)S(1)}, u32[]{:S(2)}, u32[]{:S(2)}) %collective-permute-start) | collective-permute-done | bytes 147488 | tf_op jit(solution)/shard_map/ppermute | solution.py:26
  11.8 5.5 %collective-permute-done.1 = bf16[64,1152]{1,0:T(8,128)(2,1)S(1)} collective-permute-done((bf16[64,1152]{1,0:T(8,128)(2,1)S(1)}, bf16[64,1152]{1,0:T(8,128)(2,1)S(1)}, u32[]{:S(2)}, u32[]{:S(2)}) %collective-permute-start.1) | collective-permute-done | bytes 147488 | tf_op jit(solution)/shard_map/ppermute | solution.py:26
  17.4 2.6 %collective-permute-start.3 = (bf16[1024,256]{1,0:T(8,128)(2,1)S(1)}, bf16[1024,256]{1,0:T(8,128)(2,1)S(1)}, u32[]{:S(2)}, u32[]{:S(2)}) collective-permute-start(bf16[1024,256]{1,0:T(8,128)(2,1)S(1)} %constant_dynamic-slice_fusion), channel_id=1, source_target_pairs={{0,8},{4,12},{8,0},{12,4},{1,9},{5,13},{9,1},{13,5},{2,10},{6,14},... | collective-permute-start | bytes 1572872 | tf_op jit(solution)/shard_map/ppermute | solution.py:21
  21.6 1.5 collective-permute-start.7
  23.6 7.3 %expand.3 = (f32[8,256,768]{2,1,0:T(8,128)S(1)}, f32[256,32]{1,0:T(8,128)S(1)}) custom-call(s32[5]{0:T(128)S(1)} %pad_add_fusion.place, bf16[64,4096]{1,0:T(8,128)(2,1)S(1)} %bitcast.17, bf16[32,4096]{1,0:T(8,128)(2,1)S(1)} %bitcast.25, bf16[192,1024]{1,0:T(8,128)(2,1)S(1)} %pad_maximum_fusion.2.refs_0_, bf16[8,4096,384]{2,1,0:T(8,128)(2,1)} %refs_1_.3, ...), custom_call_target="tpu_custom_call" | custom-call | flops 3221225472 | bytes 12582912 | tf_op jit(solution)/shard_map/expand/pallas_call | solution.py:162
  31.0 12.4 %collective-permute-done.3 = bf16[1024,256]{1,0:T(8,128)(2,1)S(1)} collective-permute-done((bf16[1024,256]{1,0:T(8,128)(2,1)S(1)}, bf16[1024,256]{1,0:T(8,128)(2,1)S(1)}, u32[]{:S(2)}, u32[]{:S(2)}) %collective-permute-start.3) | collective-permute-done | bytes 524320 | tf_op jit(solution)/shard_map/ppermute | solution.py:21
  44.2 12.5 %expand.4 = (f32[8,256,768]{2,1,0:T(8,128)S(1)}, f32[256,32]{1,0:T(8,128)S(1)}) custom-call(s32[5]{0:T(128)S(1)} %pad_add_fusion.place, bf16[64,4096]{1,0:T(8,128)(2,1)S(1)} %bitcast.18, bf16[32,4096]{1,0:T(8,128)(2,1)S(1)} %bitcast.26, bf16[192,1024]{1,0:T(8,128)(2,1)S(1)} %collective-permute-done.6.refs_0_, ...), custom_call_target="tpu_custom_call", output_to_operand_aliasing={{0}: (9, {}), {1}: (10, {})} | custom-call | flops 6442450944 | bytes 25165824 | tf_op jit(solution)/shard_map/expand/pallas_call | solution.py:162
  56.7 8.1 %expand.5.hidden = bf16[256,3072]{1,0:T(8,128)(2,1)S(1)} custom-call(s32[5]{0:T(128)S(1)} %pad_add_fusion.place, bf16[64,4096]{1,0:T(8,128)(2,1)S(1)} %bitcast.19, bf16[32,4096]{1,0:T(8,128)(2,1)S(1)} %bitcast.27, bf16[192,1024]{1,0:T(8,128)(2,1)S(1)} %collective-permute-done.5.refs_0_, bf16[8,4096,384]{2,1,0:T(8,128)(2,1)} %refs_1_.3, ...), custom_call_target="tpu_custom_call" | custom-call | flops 3221225472 | bytes 12582912 | tf_op jit(solution)/shard_map/expand/pallas_call | solution.py:162
  64.8 4.5 %reduce.4 = bf16[256,1024]{1,0:T(8,128)(2,1)S(1)} custom-call(s32[5]{0:T(128)S(1)} %pad_add_fusion.place, bf16[256,3072]{1,0:T(8,128)(2,1)S(1)} %expand.5.hidden, bf16[8,384,4096]{2,1,0:T(8,128)(2,1)} %w_down.7), custom_call_target="tpu_custom_call" | custom-call | flops 1610612736 | bytes 6291456 | tf_op jit(solution)/shard_map/reduce/pallas_call | solution.py:194
  69.5 4.5 %reduce.5 = bf16[256,1024]{1,0:T(8,128)(2,1)S(1)} custom-call(s32[5]{0:T(128)S(1)} %pad_add_fusion.place, bf16[256,3072]{1,0:T(8,128)(2,1)S(1)} %expand.5.hidden, bf16[8,384,4096]{2,1,0:T(8,128)(2,1)} %w_down.7), custom_call_target="tpu_custom_call" | custom-call | flops 1610612736 | bytes 6291456 | tf_op jit(solution)/shard_map/reduce/pallas_call | solution.py:194
  74.0 4.5 %reduce.6 = bf16[256,1024]{1,0:T(8,128)(2,1)S(1)} custom-call(s32[5]{0:T(128)S(1)} %pad_add_fusion.place, bf16[256,3072]{1,0:T(8,128)(2,1)S(1)} %expand.5.hidden, bf16[8,384,4096]{2,1,0:T(8,128)(2,1)} %w_down.7), custom_call_target="tpu_custom_call" | custom-call | flops 1610612736 | bytes 6291456 | tf_op jit(solution)/shard_map/reduce/pallas_call | solution.py:194
  78.5 4.5 %reduce.7 = bf16[256,1024]{1,0:T(8,128)(2,1)S(1)} custom-call(s32[5]{0:T(128)S(1)} %pad_add_fusion.place, bf16[256,3072]{1,0:T(8,128)(2,1)S(1)} %expand.5.hidden, bf16[8,384,4096]{2,1,0:T(8,128)(2,1)} %w_down.7), custom_call_target="tpu_custom_call" | custom-call | flops 1610612736 | bytes 6291456 | tf_op jit(solution)/shard_map/reduce/pallas_call | solution.py:194
  83.1 2.5 %collective-permute-start.8 = (bf16[256,1024]{1,0:T(8,128)(2,1)S(1)}, bf16[256,1024]{1,0:T(8,128)(2,1)S(1)}, u32[]{:S(2)}, u32[]{:S(2)}) collective-permute-start(bf16[256,1024]{1,0:T(8,128)(2,1)S(1)} %reduce.5), channel_id=1, source_target_pairs={{0,3},{1,2},{2,1},{3,0},{4,7},{5,6},{6,5},{7,4},{8,11},{9,10},{10,... | collective-permute-start | bytes 1572872 | tf_op jit(solution)/shard_map/ppermute | solution.py:21
  86.6 12.2 %collective-permute-done.8 = bf16[256,1024]{1,0:T(8,128)(2,1)S(1)} collective-permute-done((bf16[256,1024]{1,0:T(8,128)(2,1)S(1)}, bf16[256,1024]{1,0:T(8,128)(2,1)S(1)}, u32[]{:S(2)}, u32[]{:S(2)}) %collective-permute-start.8) | collective-permute-done | bytes 524320 | tf_op jit(solution)/shard_map/ppermute | solution.py:21
  98.9 10.7 %collective-permute-done.9 = bf16[256,1024]{1,0:T(8,128)(2,1)S(1)} collective-permute-done((bf16[256,1024]{1,0:T(8,128)(2,1)S(1)}, bf16[256,1024]{1,0:T(8,128)(2,1)S(1)}, u32[]{:S(2)}, u32[]{:S(2)}) %collective-permute-start.9) | collective-permute-done | bytes 524320 | tf_op jit(solution)/shard_map/ppermute | solution.py:21
  110.1 2.9 %collective-permute-start.11 = (bf16[64,1024]{1,0:T(8,128)(2,1)S(1)}, bf16[64,1024]{1,0:T(8,128)(2,1)S(1)}, u32[]{:S(2)}, u32[]{:S(2)}) collective-permute-start(bf16[64,1024]{1,0:T(8,128)(2,1)S(1)} %get-tuple-element.23), channel_id=1, source_target_pairs={{0,12},{4,0},{8,4},{12,8},{1,13},{5,1},{9,5},{13,9},{2,14},{6,2},{... | collective-permute-start | bytes 393224 | tf_op jit(solution)/shard_map/ppermute | solution.py:26
  113.6 1.9 %collective-permute-start.13 = (bf16[64,1024]{1,0:T(8,128)(2,1)S(1)}, bf16[64,1024]{1,0:T(8,128)(2,1)S(1)}, u32[]{:S(2)}, u32[]{:S(2)}) collective-permute-start(bf16[64,1024]{1,0:T(8,128)(2,1)S(1)} %get-tuple-element.24), channel_id=1, source_target_pairs={{0,4},{4,8},{8,12},{12,0},{1,5},{5,9},{9,13},{13,1},{2,6},{6,10},{... | collective-permute-start | bytes 393224 | tf_op jit(solution)/shard_map/ppermute | solution.py:26
  116.9 8.6 %collective-permute-done.12 = bf16[64,1024]{1,0:T(8,128)(2,1)S(1)} collective-permute-done((bf16[64,1024]{1,0:T(8,128)(2,1)S(1)}, bf16[64,1024]{1,0:T(8,128)(2,1)S(1)}, u32[]{:S(2)}, u32[]{:S(2)}) %collective-permute-start.12) | collective-permute-done | bytes 131104 | tf_op jit(solution)/shard_map/ppermute | solution.py:26
  125.6 1.5 collective-permute-start.14
  127.4 1.8 %collective-permute-start.16 = (bf16[64,1024]{1,0:T(8,128)(2,1)S(1)}, bf16[64,1024]{1,0:T(8,128)(2,1)S(1)}, u32[]{:S(2)}, u32[]{:S(2)}) collective-permute-start(bf16[64,1024]{1,0:T(8,128)(2,1)S(1)} %fusion.3.refs_0_), channel_id=1, source_target_pairs={{0,3},{1,2},{2,1},{3,0},{4,7},{5,6},{6,5},{7,4},{8,11},{9,10},{10,... | collective-permute-start | bytes 393224 | tf_op jit(solution)/shard_map/ppermute | solution.py:21
  129.2 2.1 %collective-permute-done.14.refs_1_ = bf16[64,1024]{1,0:T(8,128)(2,1)S(1)} collective-permute-done((bf16[64,1024]{1,0:T(8,128)(2,1)S(1)}, bf16[64,1024]{1,0:T(8,128)(2,1)S(1)}, u32[]{:S(2)}, u32[]{:S(2)}) %collective-permute-start.14) | collective-permute-done | bytes 131104 | tf_op jit(solution)/shard_map/ppermute | solution.py:21
  131.3 3.3 %collective-permute-done.15.refs_2_ = bf16[64,1024]{1,0:T(8,128)(2,1)S(1)} collective-permute-done((bf16[64,1024]{1,0:T(8,128)(2,1)S(1)}, bf16[64,1024]{1,0:T(8,128)(2,1)S(1)}, u32[]{:S(2)}, u32[]{:S(2)}) %collective-permute-start.15) | collective-permute-done | bytes 131104 | tf_op jit(solution)/shard_map/ppermute | solution.py:21
  134.7 1.8 %project.1 = bf16[64,512]{1,0:T(8,128)(2,1)S(1)} custom-call(s32[5]{0:T(128)S(1)} %pad_add_fusion.place, bf16[64,4096]{1,0:T(8,128)(2,1)S(1)} %bitcast.20, bf16[64,1024]{1,0:T(8,128)(2,1)S(1)} %fusion.3.refs_0_, bf16[64,1024]{1,0:T(8,128)(2,1)S(1)} %collective-permute-done.14.refs_1_, bf16[64,1024]{1,0:T(8,128)(2,1)S(1)} %collective-permute-done.15.refs_2_, ...), custom_call_target="tpu_custom_call" | custom-call | tf_op jit(solution)/shard_map/project/pallas_call | solution.py:245
  137.8 1.6 %attend.5 = bf16[64,2048]{1,0:T(8,128)(2,1)S(1)} custom-call(s32[5]{0:T(128)S(1)} %pad_add_fusion.place, bf16[64,512]{1,0:T(8,128)(2,1)S(1)} %collective-permute-done.18.block, bf16[256,512]{1,0:T(8,128)(2,1)S(1)} %bitcast.21, bf16[256,256]{1,0:T(8,128)(2,1)S(1)} %bitcast.28, bf16[256,256]{1,0:T(8,128)(2,1)S(1)} %bitcast.32, bf16[512,2048]{1,0:T(8,128)(2,1)S(1)} %copy-done.2), custom_call_target="tpu_custom_call" | custom-call | flops 268435456 | bytes 2097152 | tf_op jit(solution)/shard_map/attend/pallas_call | solution.py:319
  139.4 1.6 %collective-permute-start.19 = (bf16[64,2048]{1,0:T(8,128)(2,1)S(1)}, bf16[64,2048]{1,0:T(8,128)(2,1)S(1)}, u32[]{:S(2)}, u32[]{:S(2)}) collective-permute-start(bf16[64,2048]{1,0:T(8,128)(2,1)S(1)} %attend.5), channel_id=1, source_target_pairs={{0,3},{1,2},{2,1},{3,0},{4,7},{5,6},{6,5},{7,4},{8,11},{9,10},{10,... | collective-permute-start | bytes 786440 | tf_op jit(solution)/shard_map/ppermute | solution.py:21
  141.0 1.6 %attend.6 = bf16[64,2048]{1,0:T(8,128)(2,1)S(1)} custom-call(s32[5]{0:T(128)S(1)} %pad_add_fusion.place, bf16[64,512]{1,0:T(8,128)(2,1)S(1)} %collective-permute-done.18.block, bf16[256,512]{1,0:T(8,128)(2,1)S(1)} %bitcast.22, bf16[256,256]{1,0:T(8,128)(2,1)S(1)} %bitcast.29, bf16[256,256]{1,0:T(8,128)(2,1)S(1)} %bitcast.33, bf16[512,2048]{1,0:T(8,128)(2,1)S(1)} %copy-done.2), custom_call_target="tpu_custom_call" | custom-call | flops 268435456 | bytes 2097152 | tf_op jit(solution)/shard_map/attend/pallas_call | solution.py:319
  143.5 1.6 %attend.7 = bf16[64,2048]{1,0:T(8,128)(2,1)S(1)} custom-call(s32[5]{0:T(128)S(1)} %pad_add_fusion.place, bf16[64,512]{1,0:T(8,128)(2,1)S(1)} %collective-permute-done.18.block, bf16[256,512]{1,0:T(8,128)(2,1)S(1)} %bitcast.23, bf16[256,256]{1,0:T(8,128)(2,1)S(1)} %bitcast.30, bf16[256,256]{1,0:T(8,128)(2,1)S(1)} %bitcast.34, bf16[512,2048]{1,0:T(8,128)(2,1)S(1)} %copy-done.2), custom_call_target="tpu_custom_call" | custom-call | flops 268435456 | bytes 2097152 | tf_op jit(solution)/shard_map/attend/pallas_call | solution.py:319
  146.4 1.6 %attend.4 = bf16[64,2048]{1,0:T(8,128)(2,1)S(1)} custom-call(s32[5]{0:T(128)S(1)} %pad_add_fusion.place, bf16[64,512]{1,0:T(8,128)(2,1)S(1)} %collective-permute-done.18.block, bf16[256,512]{1,0:T(8,128)(2,1)S(1)} %bitcast.24, bf16[256,256]{1,0:T(8,128)(2,1)S(1)} %bitcast.31, bf16[256,256]{1,0:T(8,128)(2,1)S(1)} %bitcast.35, bf16[512,2048]{1,0:T(8,128)(2,1)S(1)} %copy-done.2), custom_call_target="tpu_custom_call" | custom-call | flops 268435456 | bytes 2097152 | tf_op jit(solution)/shard_map/attend/pallas_call | solution.py:319
  148.0 1.6 %collective-permute-done.19 = bf16[64,2048]{1,0:T(8,128)(2,1)S(1)} collective-permute-done((bf16[64,2048]{1,0:T(8,128)(2,1)S(1)}, bf16[64,2048]{1,0:T(8,128)(2,1)S(1)}, u32[]{:S(2)}, u32[]{:S(2)}) %collective-permute-start.19) | collective-permute-done | bytes 262176 | tf_op jit(solution)/shard_map/ppermute | solution.py:21
  149.6 4.8 %collective-permute-done.20 = bf16[64,2048]{1,0:T(8,128)(2,1)S(1)} collective-permute-done((bf16[64,2048]{1,0:T(8,128)(2,1)S(1)}, bf16[64,2048]{1,0:T(8,128)(2,1)S(1)}, u32[]{:S(2)}, u32[]{:S(2)}) %collective-permute-start.20) | collective-permute-done | bytes 262176 | tf_op jit(solution)/shard_map/ppermute | solution.py:21
  (64 shorter events, 15.2 us)
Async XLA Ops:
  0.0 9.6 %copy-start = (bf16[1024,512]{1,0:T(8,128)(2,1)S(1)}, bf16[1024,512]{1,0:T(8,128)(2,1)}, u32[]{:S(2)}) copy-start(bf16[1024,512]{1,0:T(8,128)(2,1)} %param.20) | copy-start | bytes 3145732
  0.0 23.6 %copy-start.3 = (bf16[1,64,4096]{2,1,0:T(8,128)(2,1)S(1)}, bf16[1,64,4096]{2,1,0:T(8,128)(2,1)}, u32[]{:S(2)}) copy-start(bf16[1,64,4096]{2,1,0:T(8,128)(2,1)} %param.13) | copy-start | bytes 1572868
  0.0 23.6 %copy-start.5 = (bf16[4096,32]{0,1:T(8,128)(2,1)S(1)}, bf16[4096,32]{0,1:T(8,128)(2,1)}, u32[]{:S(2)}) copy-start(bf16[4096,32]{0,1:T(8,128)(2,1)} %param.15) | copy-start | bytes 786436
  1.9 9.9 %collective-permute-start = (bf16[64,1152]{1,0:T(8,128)(2,1)S(1)}, bf16[64,1152]{1,0:T(8,128)(2,1)S(1)}, u32[]{:S(2)}, u32[]{:S(2)}) collective-permute-start(bf16[64,1152]{1,0:T(8,128)(2,1)S(1)} %pad_maximum_fusion.3), channel_id=1, source_target_pairs={{0,4},{4,8},{8,12},{12,0},{1,5},{5,9},{9,13},{13,1},{2,6},{6,10},{... | collective-permute-start | bytes 442376 | tf_op jit(solution)/shard_map/ppermute | solution.py:26
  5.0 12.3 %collective-permute-start.1 = (bf16[64,1152]{1,0:T(8,128)(2,1)S(1)}, bf16[64,1152]{1,0:T(8,128)(2,1)S(1)}, u32[]{:S(2)}, u32[]{:S(2)}) collective-permute-start(bf16[64,1152]{1,0:T(8,128)(2,1)S(1)} %pad_maximum_fusion.3), channel_id=1, source_target_pairs={{0,8},{4,12},{8,0},{12,4},{1,9},{5,13},{9,1},{13,5},{2,10},{6,14},... | collective-permute-start | bytes 442376 | tf_op jit(solution)/shard_map/ppermute | solution.py:26
  7.6 9.7 %collective-permute-start.2 = (bf16[64,1152]{1,0:T(8,128)(2,1)S(1)}, bf16[64,1152]{1,0:T(8,128)(2,1)S(1)}, u32[]{:S(2)}, u32[]{:S(2)}) collective-permute-start(bf16[64,1152]{1,0:T(8,128)(2,1)S(1)} %pad_maximum_fusion.3), channel_id=1, source_target_pairs={{0,12},{4,0},{8,4},{12,8},{1,13},{5,1},{9,5},{13,9},{2,14},{6,2},{... | collective-permute-start | bytes 442376 | tf_op jit(solution)/shard_map/ppermute | solution.py:26
  17.4 26.0 %collective-permute-start.3 = (bf16[1024,256]{1,0:T(8,128)(2,1)S(1)}, bf16[1024,256]{1,0:T(8,128)(2,1)S(1)}, u32[]{:S(2)}, u32[]{:S(2)}) collective-permute-start(bf16[1024,256]{1,0:T(8,128)(2,1)S(1)} %constant_dynamic-slice_fusion), channel_id=1, source_target_pairs={{0,8},{4,12},{8,0},{12,4},{1,9},{5,13},{9,1},{13,5},{2,10},{6,14},... | collective-permute-start | bytes 1572872 | tf_op jit(solution)/shard_map/ppermute | solution.py:21
  20.1 24.1 %collective-permute-start.6 = (bf16[192,1024]{1,0:T(8,128)(2,1)S(1)}, bf16[192,1024]{1,0:T(8,128)(2,1)S(1)}, u32[]{:S(2)}, u32[]{:S(2)}) collective-permute-start(bf16[192,1024]{1,0:T(8,128)(2,1)S(1)} %pad_maximum_fusion.2.refs_0_), channel_id=1, source_target_pairs={{0,1},{1,0},{2,3},{3,2},{4,5},{5,4},{6,7},{7,6},{8,9},{9,8},{10,11... | collective-permute-start | bytes 1179656 | tf_op jit(solution)/shard_map/ppermute | solution.py:21
  21.6 22.6 %collective-permute-start.7 = (bf16[192,1024]{1,0:T(8,128)(2,1)S(1)}, bf16[192,1024]{1,0:T(8,128)(2,1)S(1)}, u32[]{:S(2)}, u32[]{:S(2)}) collective-permute-start(bf16[192,1024]{1,0:T(8,128)(2,1)S(1)} %pad_maximum_fusion.2.refs_0_), channel_id=1, source_target_pairs={{0,2},{1,3},{2,0},{3,1},{4,6},{5,7},{6,4},{7,5},{8,10},{9,11},{10,... | collective-permute-start | bytes 1179656 | tf_op jit(solution)/shard_map/ppermute | solution.py:21
  23.1 33.6 %collective-permute-start.5 = (bf16[192,1024]{1,0:T(8,128)(2,1)S(1)}, bf16[192,1024]{1,0:T(8,128)(2,1)S(1)}, u32[]{:S(2)}, u32[]{:S(2)}) collective-permute-start(bf16[192,1024]{1,0:T(8,128)(2,1)S(1)} %pad_maximum_fusion.2.refs_0_), channel_id=1, source_target_pairs={{0,3},{1,2},{2,1},{3,0},{4,7},{5,6},{6,5},{7,4},{8,11},{9,10},{10,... | collective-permute-start | bytes 1179656 | tf_op jit(solution)/shard_map/ppermute | solution.py:21
  43.4 25.9 %collective-permute-start.4 = (bf16[2048,256]{1,0:T(8,128)(2,1)S(1)}, bf16[2048,256]{1,0:T(8,128)(2,1)S(1)}, u32[]{:S(2)}, u32[]{:S(2)}) collective-permute-start(bf16[2048,256]{1,0:T(8,128)(2,1)S(1)} %pad_maximum_fusion.1), channel_id=1, source_target_pairs={{0,4},{4,0},{8,12},{12,8},{1,5},{5,1},{9,13},{13,9},{2,6},{6,2},{1... | collective-permute-start | bytes 3145736 | tf_op jit(solution)/shard_map/ppermute | solution.py:21
  69.5 65.2 %collective-permute-start.17 = (bf16[4096,256]{1,0:T(8,128)(2,1)S(1)}, bf16[4096,256]{1,0:T(8,128)(2,1)S(1)}, u32[]{:S(2)}, u32[]{:S(2)}) collective-permute-start(bf16[4096,256]{1,0:T(8,128)(2,1)S(1)} %pad_maximum_fusion.refs_5_), channel_id=1, source_target_pairs={{0,16},{16,0},{1,17},{17,1},{2,18},{18,2},{3,19},{19,3},{4,20},{20... | collective-permute-start | bytes 6291464 | tf_op jit(solution)/shard_map/ppermute | solution.py:21
  83.0 51.6 %copy-start.8 = (f32[4096]{0:T(1024)S(1)}, f32[4096]{0:T(1024)}, u32[]{:S(2)}) copy-start(f32[4096]{0:T(1024)} %param.19) | copy-start | bytes 49156
  83.1 15.8 %collective-permute-start.8 = (bf16[256,1024]{1,0:T(8,128)(2,1)S(1)}, bf16[256,1024]{1,0:T(8,128)(2,1)S(1)}, u32[]{:S(2)}, u32[]{:S(2)}) collective-permute-start(bf16[256,1024]{1,0:T(8,128)(2,1)S(1)} %reduce.5), channel_id=1, source_target_pairs={{0,3},{1,2},{2,1},{3,0},{4,7},{5,6},{6,5},{7,4},{8,11},{9,10},{10,... | collective-permute-start | bytes 1572872 | tf_op jit(solution)/shard_map/ppermute | solution.py:21
  85.6 24.0 %collective-permute-start.9 = (bf16[256,1024]{1,0:T(8,128)(2,1)S(1)}, bf16[256,1024]{1,0:T(8,128)(2,1)S(1)}, u32[]{:S(2)}, u32[]{:S(2)}) collective-permute-start(bf16[256,1024]{1,0:T(8,128)(2,1)S(1)} %reduce.6), channel_id=1, source_target_pairs={{0,2},{1,3},{2,0},{3,1},{4,6},{5,7},{6,4},{7,5},{8,10},{9,11},{10,... | collective-permute-start | bytes 1572872 | tf_op jit(solution)/shard_map/ppermute | solution.py:21
  86.1 23.6 %collective-permute-start.10 = (bf16[256,1024]{1,0:T(8,128)(2,1)S(1)}, bf16[256,1024]{1,0:T(8,128)(2,1)S(1)}, u32[]{:S(2)}, u32[]{:S(2)}) collective-permute-start(bf16[256,1024]{1,0:T(8,128)(2,1)S(1)} %reduce.7), channel_id=1, source_target_pairs={{0,1},{1,0},{2,3},{3,2},{4,5},{5,4},{6,7},{7,6},{8,9},{9,8},{10,11... | collective-permute-start | bytes 1572872 | tf_op jit(solution)/shard_map/ppermute | solution.py:21
  110.1 6.9 %collective-permute-start.11 = (bf16[64,1024]{1,0:T(8,128)(2,1)S(1)}, bf16[64,1024]{1,0:T(8,128)(2,1)S(1)}, u32[]{:S(2)}, u32[]{:S(2)}) collective-permute-start(bf16[64,1024]{1,0:T(8,128)(2,1)S(1)} %get-tuple-element.23), channel_id=1, source_target_pairs={{0,12},{4,0},{8,4},{12,8},{1,13},{5,1},{9,5},{13,9},{2,14},{6,2},{... | collective-permute-start | bytes 393224 | tf_op jit(solution)/shard_map/ppermute | solution.py:26
  113.0 12.6 %collective-permute-start.12 = (bf16[64,1024]{1,0:T(8,128)(2,1)S(1)}, bf16[64,1024]{1,0:T(8,128)(2,1)S(1)}, u32[]{:S(2)}, u32[]{:S(2)}) collective-permute-start(bf16[64,1024]{1,0:T(8,128)(2,1)S(1)} %get-tuple-element.25), channel_id=1, source_target_pairs={{0,8},{4,12},{8,0},{12,4},{1,9},{5,13},{9,1},{13,5},{2,10},{6,14},... | collective-permute-start | bytes 393224 | tf_op jit(solution)/shard_map/ppermute | solution.py:26
  113.6 11.9 %collective-permute-start.13 = (bf16[64,1024]{1,0:T(8,128)(2,1)S(1)}, bf16[64,1024]{1,0:T(8,128)(2,1)S(1)}, u32[]{:S(2)}, u32[]{:S(2)}) collective-permute-start(bf16[64,1024]{1,0:T(8,128)(2,1)S(1)} %get-tuple-element.24), channel_id=1, source_target_pairs={{0,4},{4,8},{8,12},{12,0},{1,5},{5,9},{9,13},{13,1},{2,6},{6,10},{... | collective-permute-start | bytes 393224 | tf_op jit(solution)/shard_map/ppermute | solution.py:26
  125.6 5.7 %collective-permute-start.14 = (bf16[64,1024]{1,0:T(8,128)(2,1)S(1)}, bf16[64,1024]{1,0:T(8,128)(2,1)S(1)}, u32[]{:S(2)}, u32[]{:S(2)}) collective-permute-start(bf16[64,1024]{1,0:T(8,128)(2,1)S(1)} %fusion.3.refs_0_), channel_id=1, source_target_pairs={{0,1},{1,0},{2,3},{3,2},{4,5},{5,4},{6,7},{7,6},{8,9},{9,8},{10,11... | collective-permute-start | bytes 393224 | tf_op jit(solution)/shard_map/ppermute | solution.py:21
  127.2 7.4 %collective-permute-start.15 = (bf16[64,1024]{1,0:T(8,128)(2,1)S(1)}, bf16[64,1024]{1,0:T(8,128)(2,1)S(1)}, u32[]{:S(2)}, u32[]{:S(2)}) collective-permute-start(bf16[64,1024]{1,0:T(8,128)(2,1)S(1)} %fusion.3.refs_0_), channel_id=1, source_target_pairs={{0,2},{1,3},{2,0},{3,1},{4,6},{5,7},{6,4},{7,5},{8,10},{9,11},{10,... | collective-permute-start | bytes 393224 | tf_op jit(solution)/shard_map/ppermute | solution.py:21
  127.4 7.2 %collective-permute-start.16 = (bf16[64,1024]{1,0:T(8,128)(2,1)S(1)}, bf16[64,1024]{1,0:T(8,128)(2,1)S(1)}, u32[]{:S(2)}, u32[]{:S(2)}) collective-permute-start(bf16[64,1024]{1,0:T(8,128)(2,1)S(1)} %fusion.3.refs_0_), channel_id=1, source_target_pairs={{0,3},{1,2},{2,1},{3,0},{4,7},{5,6},{6,5},{7,4},{8,11},{9,10},{10,... | collective-permute-start | bytes 393224 | tf_op jit(solution)/shard_map/ppermute | solution.py:21
  134.6 3.2 %copy-start.2 = (bf16[512,2048]{1,0:T(8,128)(2,1)S(1)}, bf16[512,2048]{1,0:T(8,128)(2,1)}, u32[]{:S(2)}) copy-start(bf16[512,2048]{1,0:T(8,128)(2,1)} %w_out.7) | copy-start | bytes 6291460
  134.6 3.1 %copy-start.4 = (bf16[1,256,512]{2,1,0:T(8,128)(2,1)S(1)}, bf16[1,256,512]{2,1,0:T(8,128)(2,1)}, u32[]{:S(2)}) copy-start(bf16[1,256,512]{2,1,0:T(8,128)(2,1)} %param.22) | copy-start | bytes 786436
  134.6 3.1 %copy-start.6 = (bf16[1,256,256]{2,1,0:T(8,128)(2,1)S(1)}, bf16[1,256,256]{2,1,0:T(8,128)(2,1)}, u32[]{:S(2)}) copy-start(bf16[1,256,256]{2,1,0:T(8,128)(2,1)} %param.23) | copy-start | bytes 393220
  134.7 3.1 %copy-start.7 = (bf16[1,256,256]{2,1,0:T(8,128)(2,1)S(1)}, bf16[1,256,256]{2,1,0:T(8,128)(2,1)}, u32[]{:S(2)}) copy-start(bf16[1,256,256]{2,1,0:T(8,128)(2,1)} %param.24) | copy-start | bytes 393220
  136.4 1.3 collective-permute-start.18
  139.4 10.1 %collective-permute-start.19 = (bf16[64,2048]{1,0:T(8,128)(2,1)S(1)}, bf16[64,2048]{1,0:T(8,128)(2,1)S(1)}, u32[]{:S(2)}, u32[]{:S(2)}) collective-permute-start(bf16[64,2048]{1,0:T(8,128)(2,1)S(1)} %attend.5), channel_id=1, source_target_pairs={{0,3},{1,2},{2,1},{3,0},{4,7},{5,6},{6,5},{7,4},{8,11},{9,10},{10,... | collective-permute-start | bytes 786440 | tf_op jit(solution)/shard_map/ppermute | solution.py:21
  142.6 11.8 %collective-permute-start.20 = (bf16[64,2048]{1,0:T(8,128)(2,1)S(1)}, bf16[64,2048]{1,0:T(8,128)(2,1)S(1)}, u32[]{:S(2)}, u32[]{:S(2)}) collective-permute-start(bf16[64,2048]{1,0:T(8,128)(2,1)S(1)} %attend.6), channel_id=1, source_target_pairs={{0,2},{1,3},{2,0},{3,1},{4,6},{5,7},{6,4},{7,5},{8,10},{9,11},{10,... | collective-permute-start | bytes 786440 | tf_op jit(solution)/shard_map/ppermute | solution.py:21
  143.5 11.7 %copy-start.1 = (bf16[1024,512]{1,0:T(8,128)(2,1)S(1)}, bf16[1024,512]{1,0:T(8,128)(2,1)}, u32[]{:S(2)}) copy-start(bf16[1024,512]{1,0:T(8,128)(2,1)} %param.20) | copy-start | bytes 3145732
  145.2 9.2 %collective-permute-start.21 = (bf16[64,2048]{1,0:T(8,128)(2,1)S(1)}, bf16[64,2048]{1,0:T(8,128)(2,1)S(1)}, u32[]{:S(2)}, u32[]{:S(2)}) collective-permute-start(bf16[64,2048]{1,0:T(8,128)(2,1)S(1)} %attend.7), channel_id=1, source_target_pairs={{0,1},{1,0},{2,3},{3,2},{4,5},{5,4},{6,7},{7,6},{8,9},{9,8},{10,11... | collective-permute-start | bytes 786440 | tf_op jit(solution)/shard_map/ppermute | solution.py:21

commit v2 on v1

--- a/solution.py
+++ b/solution.py
@@ -73,38 +73,52 @@
     return value
 
 
-def gather_kernel(quarters, first, place, own, router, *refs):
-    count = len(quarters)
-    nears, w_gates, w_ups, refs = (
-        refs[:count],
-        refs[count : 2 * count],
-        refs[2 * count : 3 * count],
-        refs[3 * count :],
-    )
+def with_weights(step, each, held, blocks, body):
+    if not held[0]:
+        body(*blocks, lambda i: i)
+        return
+    ready = held[0][0].shape[0] // each
+
+    @pl.when(step < ready)
+    def _():
+        body(*held, lambda i: step * each + i)
+
+    @pl.when(step >= ready)
+    def _():
+        body(*blocks, lambda i: i)
+
+
+def split_refs(count, fetched, refs):
+    groups = []
+    for _ in range(3 + 2 * fetched):
+        groups.append(refs[:count])
+        refs = refs[count:]
+    return groups[0], groups[1:3], groups[3:] if fetched else [(), ()], refs
+
+
+def gather_kernel(quarters, fetched, first, place, own, router, *refs):
+    nears, blocks, held, refs = split_refs(len(quarters), fetched, refs)
     totals, refs = ((None,) * 2, refs) if first else (refs[:2], refs[2:])
     out, logits_out, rows = refs
-    step, each = pl.program_id(0), w_gates[0].shape[0]
+    step, each = pl.program_id(0), blocks[0][0].shape[0]
 
     @pl.when(step == 0)
     def _():
         logits = take_rows(quarters, place, own, nears, router, rows)
         logits_out[...] = logits if first else logits + totals[1][...]
 
-    for i in range(each):
-        value = both(rows, w_gates, w_ups, i)
-        out[step * each + i] = value if first else value + totals[0][step * each + i]
-
-
-def finish_kernel(quarters, top, place, own, router, *refs):
-    count = len(quarters)
-    nears, w_gates, w_ups, refs = (
-        refs[:count],
-        refs[count : 2 * count],
-        refs[2 * count : 3 * count],
-        refs[3 * count :],
-    )
+    def body(w_gates, w_ups, at):
+        for i in range(each):
+            value = both(rows, w_gates, w_ups, at(i))
+            out[step * each + i] = value if first else value + totals[0][step * each + i]
+
+    with_weights(step, each, held, blocks, body)
+
+
+def finish_kernel(quarters, fetched, top, place, own, router, *refs):
+    nears, blocks, held, refs = split_refs(len(quarters), fetched, refs)
     total, logits_total, tags, hidden, rows, weights = refs
-    step, each, units = pl.program_id(0), w_gates[0].shape[0], w_gates[0].shape[2]
+    step, (each, _, units) = pl.program_id(0), blocks[0][0].shape
     expert = lax.broadcasted_iota(jnp.int32, weights.shape, 1)
 
     @pl.when(step == 0)
@@ -118,17 +132,57 @@
         spread = jnp.where(picked, jnp.exp(logits - most), 0.0)
         weights[...] = spread / jnp.sum(spread, axis=1, keepdims=True)
 
-    for i in range(each):
-        value = total[step * each + i] + both(rows, w_gates, w_ups, i)
-        gate, up = value[:, :units], value[:, units:]
-        mine = expert == (place[1] * pl.num_programs(0) + step) * each + i
-        scale = jnp.sum(jnp.where(mine, weights[...], 0.0), axis=1, keepdims=True)
-        hidden[:, i * units : (i + 1) * units] = (
-            gate / (1.0 + jnp.exp(-gate)) * up * scale
-        ).astype(BF16)
-
-
-def expand(quarters, place, own, nears, router, w_gate, w_up, totals, tags, top):
+    def body(w_gates, w_ups, at):
+        for i in range(each):
+            value = total[step * each + i] + both(rows, w_gates, w_ups, at(i))
+            gate, up = value[:, :units], value[:, units:]
+            mine = expert == (place[1] * pl.num_programs(0) + step) * each + i
+            scale = jnp.sum(jnp.where(mine, weights[...], 0.0), axis=1, keepdims=True)
+            hidden[:, i * units : (i + 1) * units] = (
+                gate / (1.0 + jnp.exp(-gate)) * up * scale
+            ).astype(BF16)
+
+    with_weights(step, each, held, blocks, body)
+
+
+def fetch_kernel(quarters, place, w_gate, w_up, *refs):
+    held, sems = refs[:-1], refs[-1]
+    experts, width = held[0].shape[:2]
+    copies = []
+    for i, k in enumerate(quarters):
+        rows = pl.ds(pl.multiple_of((place[0] ^ k) * width, width), width)
+        for j, weight in enumerate((w_gate, w_up)):
+            at = 2 * i + j
+            source = weight.at[pl.ds(0, experts), rows, :]
+            copies.append(pltpu.make_async_copy(source, held[at], sems.at[at]))
+    for copy in copies:
+        copy.start()
+    for copy in copies:
+        copy.wait()
+
+
+def fetch(quarters, place, w_gate, w_up, width):
+    experts, units = w_gate.shape[0] // 2, w_gate.shape[2]
+    if experts == 0 or experts % 4:
+        return {}
+    count = 2 * len(quarters)
+    held = pl.pallas_call(
+        functools.partial(fetch_kernel, quarters),
+        out_shape=[pltpu.VMEM((experts, width, units), BF16)] * count,
+        grid_spec=pltpu.PrefetchScalarGridSpec(
+            num_scalar_prefetch=1,
+            grid=(),
+            in_specs=[pl.BlockSpec(memory_space=pl.ANY)] * 2,
+            out_specs=[WHOLE] * count,
+            scratch_shapes=[pltpu.SemaphoreType.DMA((count,))],
+        ),
+        compiler_params=params(0, 2),
+        name="fetch",
+    )(place, in_hbm(w_gate), in_hbm(w_up))
+    return {k: held[2 * i : 2 * i + 2] for i, k in enumerate(quarters)}
+
+
+def expand(quarters, place, own, nears, router, w_gate, w_up, totals, tags, top, held):
     count = len(quarters)
     local, _ = own.shape
     tokens = local + nears[0].shape[0]
@@ -136,29 +190,36 @@
     each = math.gcd(experts, 4 // count)
     width = nears[0].shape[1]
     last = tags is not None
+    fetched = quarters[0] in held
+    ready = held[quarters[0]][0].shape[0] // each if fetched else 0
     weight = [
-        pl.BlockSpec((each, width, units), lambda e, place, k=k: (e, place[0] ^ k, 0))
+        pl.BlockSpec(
+            (each, width, units),
+            lambda e, place, k=k: (jnp.maximum(e, ready) if fetched else e, place[0] ^ k, 0),
+        )
         for k in quarters
     ]
     operands = [own, router] + [in_vmem(near) for near in nears]
     operands += [in_hbm(w_gate)] * count + [in_hbm(w_up)] * count
+    if fetched:
+        operands += [in_vmem(held[k][j]) for j in range(2) for k in quarters]
     operands += [in_vmem(t) for t in totals]
     scratch = [pltpu.VMEM((tokens, count * width), BF16)]
     if last:
         operands.append(tags)
-        kernel = functools.partial(finish_kernel, quarters, top)
+        kernel = functools.partial(finish_kernel, quarters, fetched, top)
         scratch.append(pltpu.VMEM((tokens, router.shape[0]), F32))
         out_shape = pltpu.VMEM((tokens, experts * units), BF16)
         out_specs = pl.BlockSpec((tokens, each * units), lambda e, place: (0, e))
         aliases = {}
     else:
-        kernel = functools.partial(gather_kernel, quarters, not totals)
+        kernel = functools.partial(gather_kernel, quarters, fetched, not totals)
         out_shape = [
             pltpu.VMEM((experts, tokens, 2 * units), F32),
             pltpu.VMEM((tokens, router.shape[0]), F32),
         ]
         out_specs = [WHOLE] * 2
-        aliases = {3 + 3 * count + i: i for i in range(len(totals))}
+        aliases = {3 + (3 + 2 * fetched) * count + i: i for i in range(len(totals))}
     return pl.pallas_call(
         kernel,
         out_shape=out_shape,
@@ -373,10 +434,11 @@
     tags = jnp.pad(chosen.astype(BF16), ((0, 0), (0, LANES - top)))
     quarter = lax.dynamic_slice_in_dim(own, half * width, width, axis=1)
     parcel = jnp.concatenate([quarter, tags], axis=1)
+    order = sorted(range(1, parts), key=lambda k: bin(k).count("1"))
     arrived = [shift(parcel, "ep", d) for d in range(1, eps)]
+    held = fetch([0] + order[:-1], place, w_gate, w_up, width)
     near = jnp.concatenate([a[:, :width] for a in arrived], axis=0)
     all_tags = jnp.concatenate([tags] + [a[:, width:] for a in arrived], axis=0)
-    order = sorted(range(1, parts), key=lambda k: bin(k).count("1"))
     far = order[::-1]
     others = {k: swap(near, "half", k) for k in order[:-1]}
     others[order[-1]] = swap(near, "half", order[-1])
@@ -404,6 +466,7 @@
             totals,
             all_tags if quarters is batches[-1] else None,
             top,
+            held,
         )
     hidden = totals
     partial = {}
@@ -412,12 +475,13 @@
     gathered = []
     for k in far:
         gathered.append(swap(partial[k], "half", k))
-    mine, partial[0] = lax.optimization_barrier((mine, partial[0]))
-    theirs = swap(mine, "pool", 1)
     summed = total_of(partial[0], gathered)
     returned = [
-        shift(summed[d * local : (d + 1) * local].astype(BF16), "ep", -d) for d in range(1, eps)
+        shift(summed[d * local : (d + 1) * local].astype(BF16), "ep", -d)
+        for d in range(1, eps)
     ]
+    mine, summed = lax.optimization_barrier((mine, summed))
+    theirs = swap(mine, "pool", 1)
     moe_quarter = total_of(summed[:local], returned).astype(BF16)
     moe = [moe_quarter] + [None] * (parts - 1)
     for k in order:

time: 155 us -> 137 us (0.88)
  waiting for transfers between devices: 66.1 us -> 40.8 us
  Pallas kernels: 54.1 us -> 61.2 us
    ppermute x16, waiting for transfers between devices: 48.5 us -> 29 us  [swap(): lax.ppermute(shard, axis, [(i, i ^ bits) for i in range(lax.axis_size(axi...]
    pallas_call x0 -> x1, Pallas kernels: none -> 7.04 us  [fetch(): pl.pallas_call(functools.partial(fetch_kernel, quarters), out_shape=[pltp...]
    ppermute x6, waiting for transfers between devices: 17.6 us -> 11.8 us  [shift(): lax.ppermute(shard, axis, [(i, (i + distance) % count) for i in range(cou...]
    ppermute x16, starting transfers between devices: 17.9 us -> 20.8 us  [swap(): lax.ppermute(shard, axis, [(i, i ^ bits) for i in range(lax.axis_size(axi...]
    ppermute x6, starting transfers between devices: 12.5 us -> 9.83 us  [shift(): lax.ppermute(shard, axis, [(i, (i + distance) % count) for i in range(cou...]
  transfers between devices with their start and end apart: 22 -> 22, of which waited for: 13 -> 12; matrix products, arithmetic and copies ran while one was open for 1% -> 1% of each run, Pallas kernels for 33% -> 42%
where the time goes in v2:
time: 137 us
  Pallas kernels  61.2 us (45%)
  waiting for transfers between devices  40.8 us (30%)
  starting transfers between devices  30.7 us (22%)
  local copies, waits for them, and re-layouts  2.6 us (2%)
  other arithmetic  1.62 us (1%)
    ppermute x16, waiting for transfers between devices, swap(): lax.ppermute(shard, axis, [(i, i ^ bits) for i in range(lax.axis_size(axi...  29 us
    pallas_call x3, Pallas kernels, expand(): pl.pallas_call(kernel, out_shape=out_shape, grid_spec=pltpu.PrefetchScala...  27.9 us
    ppermute x16, starting transfers between devices, swap(): lax.ppermute(shard, axis, [(i, i ^ bits) for i in range(lax.axis_size(axi...  20.8 us
    pallas_call x4, Pallas kernels, reduce(): pl.pallas_call(reduce_kernel, out_shape=jax.ShapeDtypeStruct((tokens, wid...  18 us
    ppermute x6, waiting for transfers between devices, shift(): lax.ppermute(shard, axis, [(i, (i + distance) % count) for i in range(cou...  11.8 us
    ppermute x6, starting transfers between devices, shift(): lax.ppermute(shard, axis, [(i, (i + distance) % count) for i in range(cou...  9.83 us
    pallas_call x1, Pallas kernels, fetch(): pl.pallas_call(functools.partial(fetch_kernel, quarters), out_shape=[pltp...  7.04 us
    pallas_call x4, Pallas kernels, attend(): pl.pallas_call(functools.partial(attend_kernel, k, prompts), out_shape=ja...  6.48 us
  transfers between devices with their start and end apart: 22, of which 12 were waited for; matrix products, arithmetic and copies ran while one was open for 1% of the time, Pallas kernels for 42%

profile of v2, /device:TPU:0, one launch (start us, length us, event | category | flops | bytes accessed | tf_op | source)
XLA Modules:
  0.0 137.3 jit_solution(13100331037520233473)
XLA Ops:
  1.8 3.1 %collective-permute-start = (bf16[64,1152]{1,0:T(8,128)(2,1)S(1)}, bf16[64,1152]{1,0:T(8,128)(2,1)S(1)}, u32[]{:S(2)}, u32[]{:S(2)}) collective-permute-start(bf16[64,1152]{1,0:T(8,128)(2,1)S(1)} %pad_maximum_fusion.3), channel_id=1, source_target_pairs={{0,4},{4,8},{8,12},{12,0},{1,5},{5,9},{9,13},{13,1},{2,6},{6,10},{... | collective-permute-start | bytes 442376 | tf_op jit(solution)/shard_map/ppermute | solution.py:26
  4.9 2.6 %collective-permute-start.1 = (bf16[64,1152]{1,0:T(8,128)(2,1)S(1)}, bf16[64,1152]{1,0:T(8,128)(2,1)S(1)}, u32[]{:S(2)}, u32[]{:S(2)}) collective-permute-start(bf16[64,1152]{1,0:T(8,128)(2,1)S(1)} %pad_maximum_fusion.3), channel_id=1, source_target_pairs={{0,8},{4,12},{8,0},{12,4},{1,9},{5,13},{9,1},{13,5},{2,10},{6,14},... | collective-permute-start | bytes 442376 | tf_op jit(solution)/shard_map/ppermute | solution.py:26
  7.5 1.3 collective-permute-start.2
  9.6 7.0 %fetch.1 = (bf16[4,1024,384]{2,1,0:T(8,128)(2,1)S(1)}, bf16[4,1024,384]{2,1,0:T(8,128)(2,1)S(1)}, bf16[4,1024,384]{2,1,0:T(8,128)(2,1)S(1)}, bf16[4,1024,384]{2,...) custom-call(s32[5]{0:T(128)S(1)} %pad_add_fusion.place, ...), custom_call_target="tpu_custom_call" | custom-call | tf_op jit(solution)/shard_map/fetch/pallas_call | solution.py:169
  17.3 1.6 %collective-permute-start.6 = (bf16[192,1024]{1,0:T(8,128)(2,1)S(1)}, bf16[192,1024]{1,0:T(8,128)(2,1)S(1)}, u32[]{:S(2)}, u32[]{:S(2)}) collective-permute-start(bf16[192,1024]{1,0:T(8,128)(2,1)S(1)} %pad_maximum_fusion.2.refs_0_), channel_id=1, source_target_pairs={{0,1},{1,0},{2,3},{3,2},{4,5},{5,4},{6,7},{7,6},{8,9},{9,8},{10,11... | collective-permute-start | bytes 1179656 | tf_op jit(solution)/shard_map/ppermute | solution.py:21
  18.9 1.5 %collective-permute-start.7 = (bf16[192,1024]{1,0:T(8,128)(2,1)S(1)}, bf16[192,1024]{1,0:T(8,128)(2,1)S(1)}, u32[]{:S(2)}, u32[]{:S(2)}) collective-permute-start(bf16[192,1024]{1,0:T(8,128)(2,1)S(1)} %pad_maximum_fusion.2.refs_0_), channel_id=1, source_target_pairs={{0,2},{1,3},{2,0},{3,1},{4,6},{5,7},{6,4},{7,5},{8,10},{9,11},{10,... | collective-permute-start | bytes 1179656 | tf_op jit(solution)/shard_map/ppermute | solution.py:21
  20.9 2.6 %collective-permute-start.3 = (bf16[1024,256]{1,0:T(8,128)(2,1)S(1)}, bf16[1024,256]{1,0:T(8,128)(2,1)S(1)}, u32[]{:S(2)}, u32[]{:S(2)}) collective-permute-start(bf16[1024,256]{1,0:T(8,128)(2,1)S(1)} %constant_dynamic-slice_fusion), channel_id=1, source_target_pairs={{0,8},{4,12},{8,0},{12,4},{1,9},{5,13},{9,1},{13,5},{2,10},{6,14},... | collective-permute-start | bytes 1572872 | tf_op jit(solution)/shard_map/ppermute | solution.py:21
  23.5 7.4 %expand.3 = (f32[8,256,768]{2,1,0:T(8,128)S(1)}, f32[256,32]{1,0:T(8,128)S(1)}) custom-call(s32[5]{0:T(128)S(1)} %pad_add_fusion.place, bf16[64,4096]{1,0:T(8,128)(2,1)S(1)} %bitcast.17, bf16[32,4096]{1,0:T(8,128)(2,1)S(1)} %bitcast.25, bf16[192,1024]{1,0:T(8,128)(2,1)S(1)} %pad_maximum_fusion.2.refs_0_, bf16[8,4096,384]{2,1,0:T(8,128)(2,1)} %refs_1_.3, ...), custom_call_target="tpu_custom_call" | custom-call | flops 3221225472 | bytes 12582912 | tf_op jit(solution)/shard_map/expand/pallas_call | solution.py:223
  30.9 7.1 %collective-permute-done.7.refs_1_ = bf16[192,1024]{1,0:T(8,128)(2,1)S(1)} collective-permute-done((bf16[192,1024]{1,0:T(8,128)(2,1)S(1)}, bf16[192,1024]{1,0:T(8,128)(2,1)S(1)}, u32[]{:S(2)}, u32[]{:S(2)}) %collective-permute-start.7) | collective-permute-done | bytes 393248 | tf_op jit(solution)/shard_map/ppermute | solution.py:21
  37.9 12.4 %expand.4 = (f32[8,256,768]{2,1,0:T(8,128)S(1)}, f32[256,32]{1,0:T(8,128)S(1)}) custom-call(s32[5]{0:T(128)S(1)} %pad_add_fusion.place, bf16[64,4096]{1,0:T(8,128)(2,1)S(1)} %bitcast.18, bf16[32,4096]{1,0:T(8,128)(2,1)S(1)} %bitcast.26, bf16[192,1024]{1,0:T(8,128)(2,1)S(1)} %collective-permute-done.6.refs_0_, ...), custom_call_target="tpu_custom_call", output_to_operand_aliasing={{0}: (13, {}), {1}: (14, {})} | custom-call | flops 6442450944 | bytes 25165824 | tf_op jit(solution)/shard_map/expand/pallas_call | solution.py:223
  50.4 8.1 %expand.5.hidden = bf16[256,3072]{1,0:T(8,128)(2,1)S(1)} custom-call(s32[5]{0:T(128)S(1)} %pad_add_fusion.place, bf16[64,4096]{1,0:T(8,128)(2,1)S(1)} %bitcast.19, bf16[32,4096]{1,0:T(8,128)(2,1)S(1)} %bitcast.27, bf16[192,1024]{1,0:T(8,128)(2,1)S(1)} %collective-permute-done.5.refs_0_, bf16[8,4096,384]{2,1,0:T(8,128)(2,1)} %refs_1_.3, ...), custom_call_target="tpu_custom_call" | custom-call | flops 3221225472 | bytes 12582912 | tf_op jit(solution)/shard_map/expand/pallas_call | solution.py:223
  58.5 4.5 %reduce.5 = bf16[256,1024]{1,0:T(8,128)(2,1)S(1)} custom-call(s32[5]{0:T(128)S(1)} %pad_add_fusion.place, bf16[256,3072]{1,0:T(8,128)(2,1)S(1)} %expand.5.hidden, bf16[8,384,4096]{2,1,0:T(8,128)(2,1)} %w_down.7), custom_call_target="tpu_custom_call" | custom-call | flops 1610612736 | bytes 6291456 | tf_op jit(solution)/shard_map/reduce/pallas_call | solution.py:255
  63.1 3.8 %collective-permute-start.4 = (bf16[2048,256]{1,0:T(8,128)(2,1)S(1)}, bf16[2048,256]{1,0:T(8,128)(2,1)S(1)}, u32[]{:S(2)}, u32[]{:S(2)}) collective-permute-start(bf16[2048,256]{1,0:T(8,128)(2,1)S(1)} %pad_maximum_fusion.1), channel_id=1, source_target_pairs={{0,4},{4,0},{8,12},{12,8},{1,5},{5,1},{9,13},{13,9},{2,6},{6,2},{1... | collective-permute-start | bytes 3145736 | tf_op jit(solution)/shard_map/ppermute | solution.py:21
  66.9 4.5 %reduce.6 = bf16[256,1024]{1,0:T(8,128)(2,1)S(1)} custom-call(s32[5]{0:T(128)S(1)} %pad_add_fusion.place, bf16[256,3072]{1,0:T(8,128)(2,1)S(1)} %expand.5.hidden, bf16[8,384,4096]{2,1,0:T(8,128)(2,1)} %w_down.7), custom_call_target="tpu_custom_call" | custom-call | flops 1610612736 | bytes 6291456 | tf_op jit(solution)/shard_map/reduce/pallas_call | solution.py:255
  71.4 4.5 %reduce.7 = bf16[256,1024]{1,0:T(8,128)(2,1)S(1)} custom-call(s32[5]{0:T(128)S(1)} %pad_add_fusion.place, bf16[256,3072]{1,0:T(8,128)(2,1)S(1)} %expand.5.hidden, bf16[8,384,4096]{2,1,0:T(8,128)(2,1)} %w_down.7), custom_call_target="tpu_custom_call" | custom-call | flops 1610612736 | bytes 6291456 | tf_op jit(solution)/shard_map/reduce/pallas_call | solution.py:255
  75.9 1.6 %collective-permute-start.8 = (bf16[256,1024]{1,0:T(8,128)(2,1)S(1)}, bf16[256,1024]{1,0:T(8,128)(2,1)S(1)}, u32[]{:S(2)}, u32[]{:S(2)}) collective-permute-start(bf16[256,1024]{1,0:T(8,128)(2,1)S(1)} %reduce.5), channel_id=1, source_target_pairs={{0,3},{1,2},{2,1},{3,0},{4,7},{5,6},{6,5},{7,4},{8,11},{9,10},{10,... | collective-permute-start | bytes 1572872 | tf_op jit(solution)/shard_map/ppermute | solution.py:21
  77.5 1.9 %collective-permute-start.10 = (bf16[256,1024]{1,0:T(8,128)(2,1)S(1)}, bf16[256,1024]{1,0:T(8,128)(2,1)S(1)}, u32[]{:S(2)}, u32[]{:S(2)}) collective-permute-start(bf16[256,1024]{1,0:T(8,128)(2,1)S(1)} %reduce.7), channel_id=1, source_target_pairs={{0,1},{1,0},{2,3},{3,2},{4,5},{5,4},{6,7},{7,6},{8,9},{9,8},{10,11... | collective-permute-start | bytes 1572872 | tf_op jit(solution)/shard_map/ppermute | solution.py:21
  79.4 4.5 %reduce.4 = bf16[256,1024]{1,0:T(8,128)(2,1)S(1)} custom-call(s32[5]{0:T(128)S(1)} %pad_add_fusion.place, bf16[256,3072]{1,0:T(8,128)(2,1)S(1)} %expand.5.hidden, bf16[8,384,4096]{2,1,0:T(8,128)(2,1)} %w_down.7), custom_call_target="tpu_custom_call" | custom-call | flops 1610612736 | bytes 6291456 | tf_op jit(solution)/shard_map/reduce/pallas_call | solution.py:255
  83.9 2.7 %collective-permute-done.8 = bf16[256,1024]{1,0:T(8,128)(2,1)S(1)} collective-permute-done((bf16[256,1024]{1,0:T(8,128)(2,1)S(1)}, bf16[256,1024]{1,0:T(8,128)(2,1)S(1)}, u32[]{:S(2)}, u32[]{:S(2)}) %collective-permute-start.8) | collective-permute-done | bytes 524320 | tf_op jit(solution)/shard_map/ppermute | solution.py:21
  86.6 5.5 %collective-permute-done.9 = bf16[256,1024]{1,0:T(8,128)(2,1)S(1)} collective-permute-done((bf16[256,1024]{1,0:T(8,128)(2,1)S(1)}, bf16[256,1024]{1,0:T(8,128)(2,1)S(1)}, u32[]{:S(2)}, u32[]{:S(2)}) %collective-permute-start.9) | collective-permute-done | bytes 524320 | tf_op jit(solution)/shard_map/ppermute | solution.py:21
  96.7 3.5 %collective-permute-done.11 = bf16[64,1024]{1,0:T(8,128)(2,1)S(1)} collective-permute-done((bf16[64,1024]{1,0:T(8,128)(2,1)S(1)}, bf16[64,1024]{1,0:T(8,128)(2,1)S(1)}, u32[]{:S(2)}, u32[]{:S(2)}) %collective-permute-start.11) | collective-permute-done | bytes 131104 | tf_op jit(solution)/shard_map/ppermute | solution.py:26
  100.2 7.8 %collective-permute-done.12 = bf16[64,1024]{1,0:T(8,128)(2,1)S(1)} collective-permute-done((bf16[64,1024]{1,0:T(8,128)(2,1)S(1)}, bf16[64,1024]{1,0:T(8,128)(2,1)S(1)}, u32[]{:S(2)}, u32[]{:S(2)}) %collective-permute-start.12) | collective-permute-done | bytes 131104 | tf_op jit(solution)/shard_map/ppermute | solution.py:26
  109.5 2.1 %collective-permute-start.16 = (bf16[64,1024]{1,0:T(8,128)(2,1)S(1)}, bf16[64,1024]{1,0:T(8,128)(2,1)S(1)}, u32[]{:S(2)}, u32[]{:S(2)}) collective-permute-start(bf16[64,1024]{1,0:T(8,128)(2,1)S(1)} %add_convert_fusion.1.refs_0_), channel_id=1, source_target_pairs={{0,3},{1,2},{2,1},{3,0},{4,7},{5,6},{6,5},{7,4},{8,11},{9,10},{10,... | collective-permute-start | bytes 393224 | tf_op jit(solution)/shard_map/ppermute | solution.py:21
  111.6 2.4 %collective-permute-done.14.refs_1_ = bf16[64,1024]{1,0:T(8,128)(2,1)S(1)} collective-permute-done((bf16[64,1024]{1,0:T(8,128)(2,1)S(1)}, bf16[64,1024]{1,0:T(8,128)(2,1)S(1)}, u32[]{:S(2)}, u32[]{:S(2)}) %collective-permute-start.14) | collective-permute-done | bytes 131104 | tf_op jit(solution)/shard_map/ppermute | solution.py:21
  114.1 2.7 %collective-permute-done.15.refs_2_ = bf16[64,1024]{1,0:T(8,128)(2,1)S(1)} collective-permute-done((bf16[64,1024]{1,0:T(8,128)(2,1)S(1)}, bf16[64,1024]{1,0:T(8,128)(2,1)S(1)}, u32[]{:S(2)}, u32[]{:S(2)}) %collective-permute-start.15) | collective-permute-done | bytes 131104 | tf_op jit(solution)/shard_map/ppermute | solution.py:21
  116.7 1.8 %project.1 = bf16[64,512]{1,0:T(8,128)(2,1)S(1)} custom-call(s32[5]{0:T(128)S(1)} %pad_add_fusion.place, bf16[64,4096]{1,0:T(8,128)(2,1)S(1)} %bitcast.20, bf16[64,1024]{1,0:T(8,128)(2,1)S(1)} %add_convert_fusion.1.refs_0_, bf16[64,1024]{1,0:T(8,128)(2,1)S(1)} %collective-permute-done.14.refs_1_, bf16[64,1024]{1,0:T(8,128)(2,1)S(1)} %collective-permute-done.15.refs_2_, ...), custom_call_target="tpu_custom_call" | custom-call | tf_op jit(solution)/shard_map/project/pallas_call | solution.py:306
  119.9 1.6 %attend.5 = bf16[64,2048]{1,0:T(8,128)(2,1)S(1)} custom-call(s32[5]{0:T(128)S(1)} %pad_add_fusion.place, bf16[64,512]{1,0:T(8,128)(2,1)S(1)} %collective-permute-done.18.block, bf16[256,512]{1,0:T(8,128)(2,1)S(1)} %bitcast.21, bf16[256,256]{1,0:T(8,128)(2,1)S(1)} %bitcast.28, bf16[256,256]{1,0:T(8,128)(2,1)S(1)} %bitcast.32, bf16[512,2048]{1,0:T(8,128)(2,1)S(1)} %copy-done.2), custom_call_target="tpu_custom_call" | custom-call | flops 268435456 | bytes 2097152 | tf_op jit(solution)/shard_map/attend/pallas_call | solution.py:380
  122.8 1.6 %attend.6 = bf16[64,2048]{1,0:T(8,128)(2,1)S(1)} custom-call(s32[5]{0:T(128)S(1)} %pad_add_fusion.place, bf16[64,512]{1,0:T(8,128)(2,1)S(1)} %collective-permute-done.18.block, bf16[256,512]{1,0:T(8,128)(2,1)S(1)} %bitcast.22, bf16[256,256]{1,0:T(8,128)(2,1)S(1)} %bitcast.29, bf16[256,256]{1,0:T(8,128)(2,1)S(1)} %bitcast.33, bf16[512,2048]{1,0:T(8,128)(2,1)S(1)} %copy-done.2), custom_call_target="tpu_custom_call" | custom-call | flops 268435456 | bytes 2097152 | tf_op jit(solution)/shard_map/attend/pallas_call | solution.py:380
  125.8 1.6 %attend.7 = bf16[64,2048]{1,0:T(8,128)(2,1)S(1)} custom-call(s32[5]{0:T(128)S(1)} %pad_add_fusion.place, bf16[64,512]{1,0:T(8,128)(2,1)S(1)} %collective-permute-done.18.block, bf16[256,512]{1,0:T(8,128)(2,1)S(1)} %bitcast.23, bf16[256,256]{1,0:T(8,128)(2,1)S(1)} %bitcast.30, bf16[256,256]{1,0:T(8,128)(2,1)S(1)} %bitcast.34, bf16[512,2048]{1,0:T(8,128)(2,1)S(1)} %copy-done.2), custom_call_target="tpu_custom_call" | custom-call | flops 268435456 | bytes 2097152 | tf_op jit(solution)/shard_map/attend/pallas_call | solution.py:380
  128.4 1.6 %attend.4 = bf16[64,2048]{1,0:T(8,128)(2,1)S(1)} custom-call(s32[5]{0:T(128)S(1)} %pad_add_fusion.place, bf16[64,512]{1,0:T(8,128)(2,1)S(1)} %collective-permute-done.18.block, bf16[256,512]{1,0:T(8,128)(2,1)S(1)} %bitcast.24, bf16[256,256]{1,0:T(8,128)(2,1)S(1)} %bitcast.31, bf16[256,256]{1,0:T(8,128)(2,1)S(1)} %bitcast.35, bf16[512,2048]{1,0:T(8,128)(2,1)S(1)} %copy-done.2), custom_call_target="tpu_custom_call" | custom-call | flops 268435456 | bytes 2097152 | tf_op jit(solution)/shard_map/attend/pallas_call | solution.py:380
  130.1 1.6 %collective-permute-done.19 = bf16[64,2048]{1,0:T(8,128)(2,1)S(1)} collective-permute-done((bf16[64,2048]{1,0:T(8,128)(2,1)S(1)}, bf16[64,2048]{1,0:T(8,128)(2,1)S(1)}, u32[]{:S(2)}, u32[]{:S(2)}) %collective-permute-start.19) | collective-permute-done | bytes 262176 | tf_op jit(solution)/shard_map/ppermute | solution.py:21
  131.7 4.8 %collective-permute-done.20 = bf16[64,2048]{1,0:T(8,128)(2,1)S(1)} collective-permute-done((bf16[64,2048]{1,0:T(8,128)(2,1)S(1)}, bf16[64,2048]{1,0:T(8,128)(2,1)S(1)}, u32[]{:S(2)}, u32[]{:S(2)}) %collective-permute-start.20) | collective-permute-done | bytes 262176 | tf_op jit(solution)/shard_map/ppermute | solution.py:21
  (65 shorter events, 15.7 us)
Async XLA Ops:
  0.0 16.7 %copy-start = (bf16[1024,512]{1,0:T(8,128)(2,1)S(1)}, bf16[1024,512]{1,0:T(8,128)(2,1)}, u32[]{:S(2)}) copy-start(bf16[1024,512]{1,0:T(8,128)(2,1)} %param.20) | copy-start | bytes 3145732
  1.8 14.9 %collective-permute-start = (bf16[64,1152]{1,0:T(8,128)(2,1)S(1)}, bf16[64,1152]{1,0:T(8,128)(2,1)S(1)}, u32[]{:S(2)}, u32[]{:S(2)}) collective-permute-start(bf16[64,1152]{1,0:T(8,128)(2,1)S(1)} %pad_maximum_fusion.3), channel_id=1, source_target_pairs={{0,4},{4,8},{8,12},{12,0},{1,5},{5,9},{9,13},{13,1},{2,6},{6,10},{... | collective-permute-start | bytes 442376 | tf_op jit(solution)/shard_map/ppermute | solution.py:26
  4.9 12.3 %collective-permute-start.1 = (bf16[64,1152]{1,0:T(8,128)(2,1)S(1)}, bf16[64,1152]{1,0:T(8,128)(2,1)S(1)}, u32[]{:S(2)}, u32[]{:S(2)}) collective-permute-start(bf16[64,1152]{1,0:T(8,128)(2,1)S(1)} %pad_maximum_fusion.3), channel_id=1, source_target_pairs={{0,8},{4,12},{8,0},{12,4},{1,9},{5,13},{9,1},{13,5},{2,10},{6,14},... | collective-permute-start | bytes 442376 | tf_op jit(solution)/shard_map/ppermute | solution.py:26
  7.5 9.7 %collective-permute-start.2 = (bf16[64,1152]{1,0:T(8,128)(2,1)S(1)}, bf16[64,1152]{1,0:T(8,128)(2,1)S(1)}, u32[]{:S(2)}, u32[]{:S(2)}) collective-permute-start(bf16[64,1152]{1,0:T(8,128)(2,1)S(1)} %pad_maximum_fusion.3), channel_id=1, source_target_pairs={{0,12},{4,0},{8,4},{12,8},{1,13},{5,1},{9,5},{13,9},{2,14},{6,2},{... | collective-permute-start | bytes 442376 | tf_op jit(solution)/shard_map/ppermute | solution.py:26
  9.6 13.8 %copy-start.5 = (bf16[4096,32]{0,1:T(8,128)(2,1)S(1)}, bf16[4096,32]{0,1:T(8,128)(2,1)}, u32[]{:S(2)}) copy-start(bf16[4096,32]{0,1:T(8,128)(2,1)} %param.15) | copy-start | bytes 786436
  16.7 6.8 %copy-start.3 = (bf16[1,64,4096]{2,1,0:T(8,128)(2,1)S(1)}, bf16[1,64,4096]{2,1,0:T(8,128)(2,1)}, u32[]{:S(2)}) copy-start(bf16[1,64,4096]{2,1,0:T(8,128)(2,1)} %param.13) | copy-start | bytes 1572868
  17.3 13.6 %collective-permute-start.6 = (bf16[192,1024]{1,0:T(8,128)(2,1)S(1)}, bf16[192,1024]{1,0:T(8,128)(2,1)S(1)}, u32[]{:S(2)}, u32[]{:S(2)}) collective-permute-start(bf16[192,1024]{1,0:T(8,128)(2,1)S(1)} %pad_maximum_fusion.2.refs_0_), channel_id=1, source_target_pairs={{0,1},{1,0},{2,3},{3,2},{4,5},{5,4},{6,7},{7,6},{8,9},{9,8},{10,11... | collective-permute-start | bytes 1179656 | tf_op jit(solution)/shard_map/ppermute | solution.py:21
  18.9 19.1 %collective-permute-start.7 = (bf16[192,1024]{1,0:T(8,128)(2,1)S(1)}, bf16[192,1024]{1,0:T(8,128)(2,1)S(1)}, u32[]{:S(2)}, u32[]{:S(2)}) collective-permute-start(bf16[192,1024]{1,0:T(8,128)(2,1)S(1)} %pad_maximum_fusion.2.refs_0_), channel_id=1, source_target_pairs={{0,2},{1,3},{2,0},{3,1},{4,6},{5,7},{6,4},{7,5},{8,10},{9,11},{10,... | collective-permute-start | bytes 1179656 | tf_op jit(solution)/shard_map/ppermute | solution.py:21
  20.4 30.0 %collective-permute-start.5 = (bf16[192,1024]{1,0:T(8,128)(2,1)S(1)}, bf16[192,1024]{1,0:T(8,128)(2,1)S(1)}, u32[]{:S(2)}, u32[]{:S(2)}) collective-permute-start(bf16[192,1024]{1,0:T(8,128)(2,1)S(1)} %pad_maximum_fusion.2.refs_0_), channel_id=1, source_target_pairs={{0,3},{1,2},{2,1},{3,0},{4,7},{5,6},{6,5},{7,4},{8,11},{9,10},{10,... | collective-permute-start | bytes 1179656 | tf_op jit(solution)/shard_map/ppermute | solution.py:21
  20.9 42.2 %collective-permute-start.3 = (bf16[1024,256]{1,0:T(8,128)(2,1)S(1)}, bf16[1024,256]{1,0:T(8,128)(2,1)S(1)}, u32[]{:S(2)}, u32[]{:S(2)}) collective-permute-start(bf16[1024,256]{1,0:T(8,128)(2,1)S(1)} %constant_dynamic-slice_fusion), channel_id=1, source_target_pairs={{0,8},{4,12},{8,0},{12,4},{1,9},{5,13},{9,1},{13,5},{2,10},{6,14},... | collective-permute-start | bytes 1572872 | tf_op jit(solution)/shard_map/ppermute | solution.py:21
  63.1 30.5 %collective-permute-start.4 = (bf16[2048,256]{1,0:T(8,128)(2,1)S(1)}, bf16[2048,256]{1,0:T(8,128)(2,1)S(1)}, u32[]{:S(2)}, u32[]{:S(2)}) collective-permute-start(bf16[2048,256]{1,0:T(8,128)(2,1)S(1)} %pad_maximum_fusion.1), channel_id=1, source_target_pairs={{0,4},{4,0},{8,12},{12,8},{1,5},{5,1},{9,13},{13,9},{2,6},{6,2},{1... | collective-permute-start | bytes 3145736 | tf_op jit(solution)/shard_map/ppermute | solution.py:21
  75.9 10.8 %collective-permute-start.8 = (bf16[256,1024]{1,0:T(8,128)(2,1)S(1)}, bf16[256,1024]{1,0:T(8,128)(2,1)S(1)}, u32[]{:S(2)}, u32[]{:S(2)}) collective-permute-start(bf16[256,1024]{1,0:T(8,128)(2,1)S(1)} %reduce.5), channel_id=1, source_target_pairs={{0,3},{1,2},{2,1},{3,0},{4,7},{5,6},{6,5},{7,4},{8,11},{9,10},{10,... | collective-permute-start | bytes 1572872 | tf_op jit(solution)/shard_map/ppermute | solution.py:21
  77.4 14.7 %collective-permute-start.9 = (bf16[256,1024]{1,0:T(8,128)(2,1)S(1)}, bf16[256,1024]{1,0:T(8,128)(2,1)S(1)}, u32[]{:S(2)}, u32[]{:S(2)}) collective-permute-start(bf16[256,1024]{1,0:T(8,128)(2,1)S(1)} %reduce.6), channel_id=1, source_target_pairs={{0,2},{1,3},{2,0},{3,1},{4,6},{5,7},{6,4},{7,5},{8,10},{9,11},{10,... | collective-permute-start | bytes 1572872 | tf_op jit(solution)/shard_map/ppermute | solution.py:21
  77.5 15.6 %collective-permute-start.10 = (bf16[256,1024]{1,0:T(8,128)(2,1)S(1)}, bf16[256,1024]{1,0:T(8,128)(2,1)S(1)}, u32[]{:S(2)}, u32[]{:S(2)}) collective-permute-start(bf16[256,1024]{1,0:T(8,128)(2,1)S(1)} %reduce.7), channel_id=1, source_target_pairs={{0,1},{1,0},{2,3},{3,2},{4,5},{5,4},{6,7},{7,6},{8,9},{9,8},{10,11... | collective-permute-start | bytes 1572872 | tf_op jit(solution)/shard_map/ppermute | solution.py:21
  93.6 23.2 %copy-start.8 = (f32[4096]{0:T(1024)S(1)}, f32[4096]{0:T(1024)}, u32[]{:S(2)}) copy-start(f32[4096]{0:T(1024)} %param.19) | copy-start | bytes 49156
  93.7 23.0 %collective-permute-start.17 = (bf16[4096,256]{1,0:T(8,128)(2,1)S(1)}, bf16[4096,256]{1,0:T(8,128)(2,1)S(1)}, u32[]{:S(2)}, u32[]{:S(2)}) collective-permute-start(bf16[4096,256]{1,0:T(8,128)(2,1)S(1)} %pad_maximum_fusion.refs_5_), channel_id=1, source_target_pairs={{0,16},{16,0},{1,17},{17,1},{2,18},{18,2},{3,19},{19,3},{4,20},{20... | collective-permute-start | bytes 6291464 | tf_op jit(solution)/shard_map/ppermute | solution.py:21
  93.9 26.0 %copy-start.2 = (bf16[512,2048]{1,0:T(8,128)(2,1)S(1)}, bf16[512,2048]{1,0:T(8,128)(2,1)}, u32[]{:S(2)}) copy-start(bf16[512,2048]{1,0:T(8,128)(2,1)} %w_out.7) | copy-start | bytes 6291460
  93.9 26.0 %copy-start.4 = (bf16[1,256,512]{2,1,0:T(8,128)(2,1)S(1)}, bf16[1,256,512]{2,1,0:T(8,128)(2,1)}, u32[]{:S(2)}) copy-start(bf16[1,256,512]{2,1,0:T(8,128)(2,1)} %param.22) | copy-start | bytes 786436
  93.9 26.0 %copy-start.6 = (bf16[1,256,256]{2,1,0:T(8,128)(2,1)S(1)}, bf16[1,256,256]{2,1,0:T(8,128)(2,1)}, u32[]{:S(2)}) copy-start(bf16[1,256,256]{2,1,0:T(8,128)(2,1)} %param.23) | copy-start | bytes 393220
  93.9 26.0 %copy-start.7 = (bf16[1,256,256]{2,1,0:T(8,128)(2,1)S(1)}, bf16[1,256,256]{2,1,0:T(8,128)(2,1)}, u32[]{:S(2)}) copy-start(bf16[1,256,256]{2,1,0:T(8,128)(2,1)} %param.24) | copy-start | bytes 393220
  93.9 6.3 %collective-permute-start.11 = (bf16[64,1024]{1,0:T(8,128)(2,1)S(1)}, bf16[64,1024]{1,0:T(8,128)(2,1)S(1)}, u32[]{:S(2)}, u32[]{:S(2)}) collective-permute-start(bf16[64,1024]{1,0:T(8,128)(2,1)S(1)} %get-tuple-element.35), channel_id=1, source_target_pairs={{0,12},{4,0},{8,4},{12,8},{1,13},{5,1},{9,5},{13,9},{2,14},{6,2},{... | collective-permute-start | bytes 393224 | tf_op jit(solution)/shard_map/ppermute | solution.py:26
  94.4 13.6 %collective-permute-start.12 = (bf16[64,1024]{1,0:T(8,128)(2,1)S(1)}, bf16[64,1024]{1,0:T(8,128)(2,1)S(1)}, u32[]{:S(2)}, u32[]{:S(2)}) collective-permute-start(bf16[64,1024]{1,0:T(8,128)(2,1)S(1)} %get-tuple-element.37), channel_id=1, source_target_pairs={{0,8},{4,12},{8,0},{12,4},{1,9},{5,13},{9,1},{13,5},{2,10},{6,14},... | collective-permute-start | bytes 393224 | tf_op jit(solution)/shard_map/ppermute | solution.py:26
  95.7 12.3 %collective-permute-start.13 = (bf16[64,1024]{1,0:T(8,128)(2,1)S(1)}, bf16[64,1024]{1,0:T(8,128)(2,1)S(1)}, u32[]{:S(2)}, u32[]{:S(2)}) collective-permute-start(bf16[64,1024]{1,0:T(8,128)(2,1)S(1)} %get-tuple-element.36), channel_id=1, source_target_pairs={{0,4},{4,8},{8,12},{12,0},{1,5},{5,9},{9,13},{13,1},{2,6},{6,10},{... | collective-permute-start | bytes 393224 | tf_op jit(solution)/shard_map/ppermute | solution.py:26
  108.1 6.0 %collective-permute-start.14 = (bf16[64,1024]{1,0:T(8,128)(2,1)S(1)}, bf16[64,1024]{1,0:T(8,128)(2,1)S(1)}, u32[]{:S(2)}, u32[]{:S(2)}) collective-permute-start(bf16[64,1024]{1,0:T(8,128)(2,1)S(1)} %add_convert_fusion.1.refs_0_), channel_id=1, source_target_pairs={{0,1},{1,0},{2,3},{3,2},{4,5},{5,4},{6,7},{7,6},{8,9},{9,8},{10,11... | collective-permute-start | bytes 393224 | tf_op jit(solution)/shard_map/ppermute | solution.py:21
  108.9 7.8 %collective-permute-start.15 = (bf16[64,1024]{1,0:T(8,128)(2,1)S(1)}, bf16[64,1024]{1,0:T(8,128)(2,1)S(1)}, u32[]{:S(2)}, u32[]{:S(2)}) collective-permute-start(bf16[64,1024]{1,0:T(8,128)(2,1)S(1)} %add_convert_fusion.1.refs_0_), channel_id=1, source_target_pairs={{0,2},{1,3},{2,0},{3,1},{4,6},{5,7},{6,4},{7,5},{8,10},{9,11},{10,... | collective-permute-start | bytes 393224 | tf_op jit(solution)/shard_map/ppermute | solution.py:21
  109.5 7.2 %collective-permute-start.16 = (bf16[64,1024]{1,0:T(8,128)(2,1)S(1)}, bf16[64,1024]{1,0:T(8,128)(2,1)S(1)}, u32[]{:S(2)}, u32[]{:S(2)}) collective-permute-start(bf16[64,1024]{1,0:T(8,128)(2,1)S(1)} %add_convert_fusion.1.refs_0_), channel_id=1, source_target_pairs={{0,3},{1,2},{2,1},{3,0},{4,7},{5,6},{6,5},{7,4},{8,11},{9,10},{10,... | collective-permute-start | bytes 393224 | tf_op jit(solution)/shard_map/ppermute | solution.py:21
  118.5 1.3 collective-permute-start.18
  121.5 10.2 %collective-permute-start.19 = (bf16[64,2048]{1,0:T(8,128)(2,1)S(1)}, bf16[64,2048]{1,0:T(8,128)(2,1)S(1)}, u32[]{:S(2)}, u32[]{:S(2)}) collective-permute-start(bf16[64,2048]{1,0:T(8,128)(2,1)S(1)} %attend.5), channel_id=1, source_target_pairs={{0,3},{1,2},{2,1},{3,0},{4,7},{5,6},{6,5},{7,4},{8,11},{9,10},{10,... | collective-permute-start | bytes 786440 | tf_op jit(solution)/shard_map/ppermute | solution.py:21
  122.8 14.5 %copy-start.1 = (bf16[1024,512]{1,0:T(8,128)(2,1)S(1)}, bf16[1024,512]{1,0:T(8,128)(2,1)}, u32[]{:S(2)}) copy-start(bf16[1024,512]{1,0:T(8,128)(2,1)} %param.20) | copy-start | bytes 3145732
  124.5 12.0 %collective-permute-start.20 = (bf16[64,2048]{1,0:T(8,128)(2,1)S(1)}, bf16[64,2048]{1,0:T(8,128)(2,1)S(1)}, u32[]{:S(2)}, u32[]{:S(2)}) collective-permute-start(bf16[64,2048]{1,0:T(8,128)(2,1)S(1)} %attend.6), channel_id=1, source_target_pairs={{0,2},{1,3},{2,0},{3,1},{4,6},{5,7},{6,4},{7,5},{8,10},{9,11},{10,... | collective-permute-start | bytes 786440 | tf_op jit(solution)/shard_map/ppermute | solution.py:21
  127.4 9.0 %collective-permute-start.21 = (bf16[64,2048]{1,0:T(8,128)(2,1)S(1)}, bf16[64,2048]{1,0:T(8,128)(2,1)S(1)}, u32[]{:S(2)}, u32[]{:S(2)}) collective-permute-start(bf16[64,2048]{1,0:T(8,128)(2,1)S(1)} %attend.7), channel_id=1, source_target_pairs={{0,1},{1,0},{2,3},{3,2},{4,5},{5,4},{6,7},{7,6},{8,9},{9,8},{10,11... | collective-permute-start | bytes 786440 | tf_op jit(solution)/shard_map/ppermute | solution.py:21

commit v3 on v2

--- a/solution.py
+++ b/solution.py
@@ -63,14 +63,14 @@
 
 
 def both(rows, w_gates, w_ups, i):
-    width = w_gates[0].shape[1]
-    value = 0.0
-    for j, (w_gate, w_up) in enumerate(zip(w_gates, w_ups)):
-        weight = jnp.concatenate([w_gate[i], w_up[i]], axis=1)
-        value += jnp.dot(
-            rows[:, j * width : (j + 1) * width], weight, preferred_element_type=F32
-        )
-    return value
+    weight = jnp.concatenate(
+        [
+            jnp.concatenate([w_gate[i], w_up[i]], axis=1)
+            for w_gate, w_up in zip(w_gates, w_ups)
+        ],
+        axis=0,
+    )
+    return jnp.dot(rows[...], weight, preferred_element_type=F32)
 
 
 def with_weights(step, each, held, blocks, body):
@@ -117,12 +117,16 @@
 
 def finish_kernel(quarters, fetched, top, place, own, router, *refs):
     nears, blocks, held, refs = split_refs(len(quarters), fetched, refs)
-    total, logits_total, tags, hidden, rows, weights = refs
+    total, logits_total, tags, w_down, hidden, ahead, rows, weights, sem = refs
     step, (each, _, units) = pl.program_id(0), blocks[0][0].shape
+    coming = pltpu.make_async_copy(
+        w_down.at[:, :, columns_of(place[0] ^ quarters[-1], ahead.shape[2])], ahead, sem
+    )
     expert = lax.broadcasted_iota(jnp.int32, weights.shape, 1)
 
     @pl.when(step == 0)
     def _():
+        coming.start()
         logits = logits_total[...] + take_rows(quarters, place, own, nears, router, rows)
         named = tags[...].astype(F32).astype(jnp.int32)
         picked = named[:, 0:1] == expert
@@ -143,6 +147,10 @@
             ).astype(BF16)
 
     with_weights(step, each, held, blocks, body)
+
+    @pl.when(step == pl.num_programs(0) - 1)
+    def _():
+        coming.wait()
 
 
 def fetch_kernel(quarters, place, w_gate, w_up, *refs):
@@ -182,7 +190,7 @@
     return {k: held[2 * i : 2 * i + 2] for i, k in enumerate(quarters)}
 
 
-def expand(quarters, place, own, nears, router, w_gate, w_up, totals, tags, top, held):
+def expand(quarters, place, own, nears, router, w_gate, w_up, totals, tags, top, held, w_down):
     count = len(quarters)
     local, _ = own.shape
     tokens = local + nears[0].shape[0]
@@ -206,11 +214,14 @@
     operands += [in_vmem(t) for t in totals]
     scratch = [pltpu.VMEM((tokens, count * width), BF16)]
     if last:
-        operands.append(tags)
+        operands += [tags, in_hbm(w_down)]
         kernel = functools.partial(finish_kernel, quarters, fetched, top)
-        scratch.append(pltpu.VMEM((tokens, router.shape[0]), F32))
-        out_shape = pltpu.VMEM((tokens, experts * units), BF16)
-        out_specs = pl.BlockSpec((tokens, each * units), lambda e, place: (0, e))
+        scratch += [pltpu.VMEM((tokens, router.shape[0]), F32), pltpu.SemaphoreType.DMA(())]
+        out_shape = [
+            pltpu.VMEM((tokens, experts * units), BF16),
+            pltpu.VMEM((experts, units, width), BF16),
+        ]
+        out_specs = [pl.BlockSpec((tokens, each * units), lambda e, place: (0, e)), WHOLE]
         aliases = {}
     else:
         kernel = functools.partial(gather_kernel, quarters, fetched, not totals)
@@ -228,7 +239,8 @@
             grid=(experts // each,),
             in_specs=[WHOLE] * (2 + count)
             + weight * 2
-            + [WHOLE] * (len(operands) - 2 - 3 * count),
+            + [WHOLE] * (len(operands) - 2 - 3 * count - last)
+            + [pl.BlockSpec(memory_space=pl.ANY)] * last,
             out_specs=out_specs,
             scratch_shapes=scratch,
         ),
@@ -246,6 +258,25 @@
 def reduce_kernel(place, hidden, w_down, out):
     weight = w_down[...].reshape(-1, w_down.shape[2])
     out[...] = jnp.dot(hidden[...], weight, preferred_element_type=F32).astype(BF16)
+
+
+def reduce_ahead_kernel(hidden, weight, out):
+    block = weight.shape[2] // 2
+    for i in range(2):
+        columns = slice(i * block, (i + 1) * block)
+        piece = weight[:, :, columns].reshape(-1, block)
+        out[:, columns] = jnp.dot(hidden[...], piece, preferred_element_type=F32).astype(BF16)
+
+
+def reduce_ahead(hidden, weight):
+    return pl.pallas_call(
+        reduce_ahead_kernel,
+        out_shape=jax.ShapeDtypeStruct((hidden.shape[0], weight.shape[2]), BF16),
+        in_specs=[WHOLE] * 2,
+        out_specs=WHOLE,
+        compiler_params=params(0, 12),
+        name="reduce",
+    )(in_vmem(hidden), in_vmem(weight))
 
 
 def reduce(k, place, hidden, w_down, width, block):
@@ -467,11 +498,15 @@
             all_tags if quarters is batches[-1] else None,
             top,
             held,
+            w_down,
         )
-    hidden = totals
+    hidden, ahead = totals
     partial = {}
     for k in far + [0]:
-        partial[k] = reduce(k, place, hidden, w_down, width, width // 2)
+        if k == order[-1]:
+            partial[k] = reduce_ahead(hidden, ahead)
+        else:
+            partial[k] = reduce(k, place, hidden, w_down, width, width // 2)
     gathered = []
     for k in far:
         gathered.append(swap(partial[k], "half", k))

time: 137 us -> 135 us (0.985)
  Pallas kernels: 61.2 us -> 58.8 us
    pallas_call x4 -> x3, Pallas kernels: 18 us -> 13.7 us  [reduce(): pl.pallas_call(reduce_kernel, out_shape=jax.ShapeDtypeStruct((tokens, wid...]
    pallas_call x0 -> x1, Pallas kernels: none -> 1.78 us  [reduce_ahead(): pl.pallas_call(reduce_ahead_kernel, out_shape=jax.ShapeDtypeStruct((hidde...]
  transfers between devices with their start and end apart: 22 -> 22, of which waited for: 12 -> 12; matrix products, arithmetic and copies ran while one was open for 1% -> 1% of each run, Pallas kernels for 42% -> 41%
where the time goes in v3:
time: 135 us
  Pallas kernels  58.8 us (44%)
  waiting for transfers between devices  40.6 us (30%)
  starting transfers between devices  30.7 us (23%)
  local copies, waits for them, and re-layouts  2.6 us (2%)
  other arithmetic  1.62 us (1%)
    ppermute x16, waiting for transfers between devices, swap(): lax.ppermute(shard, axis, [(i, i ^ bits) for i in range(lax.axis_size(axi...  28.9 us
    pallas_call x3, Pallas kernels, expand(): pl.pallas_call(kernel, out_shape=out_shape, grid_spec=pltpu.PrefetchScala...  28.1 us
    ppermute x16, starting transfers between devices, swap(): lax.ppermute(shard, axis, [(i, i ^ bits) for i in range(lax.axis_size(axi...  20.8 us
    pallas_call x3, Pallas kernels, reduce(): pl.pallas_call(reduce_kernel, out_shape=jax.ShapeDtypeStruct((tokens, wid...  13.7 us
    ppermute x6, waiting for transfers between devices, shift(): lax.ppermute(shard, axis, [(i, (i + distance) % count) for i in range(cou...  11.8 us
    ppermute x6, starting transfers between devices, shift(): lax.ppermute(shard, axis, [(i, (i + distance) % count) for i in range(cou...  9.84 us
    pallas_call x1, Pallas kernels, fetch(): pl.pallas_call(functools.partial(fetch_kernel, quarters), out_shape=[pltp...  7.04 us
    pallas_call x4, Pallas kernels, attend(): pl.pallas_call(functools.partial(attend_kernel, k, prompts), out_shape=ja...  6.48 us
  transfers between devices with their start and end apart: 22, of which 12 were waited for; matrix products, arithmetic and copies ran while one was open for 1% of the time, Pallas kernels for 41%

profile of v3, /device:TPU:0, one launch (start us, length us, event | category | flops | bytes accessed | tf_op | source)
XLA Modules:
  0.0 134.7 jit_solution(12171850185544484910)
XLA Ops:
  1.8 3.1 %collective-permute-start = (bf16[64,1152]{1,0:T(8,128)(2,1)S(1)}, bf16[64,1152]{1,0:T(8,128)(2,1)S(1)}, u32[]{:S(2)}, u32[]{:S(2)}) collective-permute-start(bf16[64,1152]{1,0:T(8,128)(2,1)S(1)} %pad_maximum_fusion.3), channel_id=1, source_target_pairs={{0,4},{4,8},{8,12},{12,0},{1,5},{5,9},{9,13},{13,1},{2,6},{6,10},{... | collective-permute-start | bytes 442376 | tf_op jit(solution)/shard_map/ppermute | solution.py:26
  4.9 2.6 %collective-permute-start.1 = (bf16[64,1152]{1,0:T(8,128)(2,1)S(1)}, bf16[64,1152]{1,0:T(8,128)(2,1)S(1)}, u32[]{:S(2)}, u32[]{:S(2)}) collective-permute-start(bf16[64,1152]{1,0:T(8,128)(2,1)S(1)} %pad_maximum_fusion.3), channel_id=1, source_target_pairs={{0,8},{4,12},{8,0},{12,4},{1,9},{5,13},{9,1},{13,5},{2,10},{6,14},... | collective-permute-start | bytes 442376 | tf_op jit(solution)/shard_map/ppermute | solution.py:26
  7.5 1.3 %collective-permute-start.2 = (bf16[64,1152]{1,0:T(8,128)(2,1)S(1)}, bf16[64,1152]{1,0:T(8,128)(2,1)S(1)}, u32[]{:S(2)}, u32[]{:S(2)}) collective-permute-start(bf16[64,1152]{1,0:T(8,128)(2,1)S(1)} %pad_maximum_fusion.3), channel_id=1, source_target_pairs={{0,12},{4,0},{8,4},{12,8},{1,13},{5,1},{9,5},{13,9},{2,14},{6,2},{... | collective-permute-start | bytes 442376 | tf_op jit(solution)/shard_map/ppermute | solution.py:26
  9.6 7.0 %fetch.1 = (bf16[4,1024,384]{2,1,0:T(8,128)(2,1)S(1)}, bf16[4,1024,384]{2,1,0:T(8,128)(2,1)S(1)}, bf16[4,1024,384]{2,1,0:T(8,128)(2,1)S(1)}, bf16[4,1024,384]{2,...) custom-call(s32[5]{0:T(128)S(1)} %pad_add_fusion.place, ...), custom_call_target="tpu_custom_call" | custom-call | tf_op jit(solution)/shard_map/fetch/pallas_call | solution.py:177
  17.3 1.6 %collective-permute-start.6 = (bf16[192,1024]{1,0:T(8,128)(2,1)S(1)}, bf16[192,1024]{1,0:T(8,128)(2,1)S(1)}, u32[]{:S(2)}, u32[]{:S(2)}) collective-permute-start(bf16[192,1024]{1,0:T(8,128)(2,1)S(1)} %pad_maximum_fusion.2.refs_0_), channel_id=1, source_target_pairs={{0,1},{1,0},{2,3},{3,2},{4,5},{5,4},{6,7},{7,6},{8,9},{9,8},{10,11... | collective-permute-start | bytes 1179656 | tf_op jit(solution)/shard_map/ppermute | solution.py:21
  18.9 1.5 %collective-permute-start.7 = (bf16[192,1024]{1,0:T(8,128)(2,1)S(1)}, bf16[192,1024]{1,0:T(8,128)(2,1)S(1)}, u32[]{:S(2)}, u32[]{:S(2)}) collective-permute-start(bf16[192,1024]{1,0:T(8,128)(2,1)S(1)} %pad_maximum_fusion.2.refs_0_), channel_id=1, source_target_pairs={{0,2},{1,3},{2,0},{3,1},{4,6},{5,7},{6,4},{7,5},{8,10},{9,11},{10,... | collective-permute-start | bytes 1179656 | tf_op jit(solution)/shard_map/ppermute | solution.py:21
  20.9 2.6 %collective-permute-start.3 = (bf16[1024,256]{1,0:T(8,128)(2,1)S(1)}, bf16[1024,256]{1,0:T(8,128)(2,1)S(1)}, u32[]{:S(2)}, u32[]{:S(2)}) collective-permute-start(bf16[1024,256]{1,0:T(8,128)(2,1)S(1)} %constant_dynamic-slice_fusion), channel_id=1, source_target_pairs={{0,8},{4,12},{8,0},{12,4},{1,9},{5,13},{9,1},{13,5},{2,10},{6,14},... | collective-permute-start | bytes 1572872 | tf_op jit(solution)/shard_map/ppermute | solution.py:21
  23.5 7.4 %expand.3 = (f32[8,256,768]{2,1,0:T(8,128)S(1)}, f32[256,32]{1,0:T(8,128)S(1)}) custom-call(s32[5]{0:T(128)S(1)} %pad_add_fusion.place, bf16[64,4096]{1,0:T(8,128)(2,1)S(1)} %bitcast.17, bf16[32,4096]{1,0:T(8,128)(2,1)S(1)} %bitcast.25, bf16[192,1024]{1,0:T(8,128)(2,1)S(1)} %pad_maximum_fusion.2.refs_0_, bf16[8,4096,384]{2,1,0:T(8,128)(2,1)} %refs_1_.3, ...), custom_call_target="tpu_custom_call" | custom-call | flops 3221225472 | bytes 12582912 | tf_op jit(solution)/shard_map/expand/pallas_call | solution.py:234
  30.9 7.1 %collective-permute-done.7.refs_1_ = bf16[192,1024]{1,0:T(8,128)(2,1)S(1)} collective-permute-done((bf16[192,1024]{1,0:T(8,128)(2,1)S(1)}, bf16[192,1024]{1,0:T(8,128)(2,1)S(1)}, u32[]{:S(2)}, u32[]{:S(2)}) %collective-permute-start.7) | collective-permute-done | bytes 393248 | tf_op jit(solution)/shard_map/ppermute | solution.py:21
  37.9 12.6 %expand.4 = (f32[8,256,768]{2,1,0:T(8,128)S(1)}, f32[256,32]{1,0:T(8,128)S(1)}) custom-call(s32[5]{0:T(128)S(1)} %pad_add_fusion.place, bf16[64,4096]{1,0:T(8,128)(2,1)S(1)} %bitcast.18, bf16[32,4096]{1,0:T(8,128)(2,1)S(1)} %bitcast.26, bf16[192,1024]{1,0:T(8,128)(2,1)S(1)} %collective-permute-done.6.refs_0_, ...), custom_call_target="tpu_custom_call", output_to_operand_aliasing={{0}: (13, {}), {1}: (14, {})} | custom-call | flops 6442450944 | bytes 25165824 | tf_op jit(solution)/shard_map/expand/pallas_call | solution.py:234
  50.5 8.1 %expand.5 = (bf16[256,3072]{1,0:T(8,128)(2,1)S(1)}, bf16[8,384,1024]{2,1,0:T(8,128)(2,1)S(1)}) custom-call(s32[5]{0:T(128)S(1)} %pad_add_fusion.place, bf16[64,4096]{1,0:T(8,128)(2,1)S(1)} %bitcast.19, bf16[32,4096]{1,0:T(8,128)(2,1)S(1)} %bitcast.27, bf16[192,1024]{1,0:T(8,128)(2,1)S(1)} %collective-permute-done.5.refs_0_, bf16[8,4096,384]{2,1,0:T(8,128)(2,1)} %refs_1_.3, ...), custom_call_target="tpu_custom_call" | custom-call | flops 3221225472 | bytes 12582912 | tf_op jit(solution)/shard_map/expand/pallas_call | solution.py:234
  58.8 3.8 %collective-permute-start.4 = (bf16[2048,256]{1,0:T(8,128)(2,1)S(1)}, bf16[2048,256]{1,0:T(8,128)(2,1)S(1)}, u32[]{:S(2)}, u32[]{:S(2)}) collective-permute-start(bf16[2048,256]{1,0:T(8,128)(2,1)S(1)} %pad_maximum_fusion.1), channel_id=1, source_target_pairs={{0,4},{4,0},{8,12},{12,8},{1,5},{5,1},{9,13},{13,9},{2,6},{6,2},{1... | collective-permute-start | bytes 3145736 | tf_op jit(solution)/shard_map/ppermute | solution.py:21
  62.5 4.5 %reduce.6 = bf16[256,1024]{1,0:T(8,128)(2,1)S(1)} custom-call(s32[5]{0:T(128)S(1)} %pad_add_fusion.place, bf16[256,3072]{1,0:T(8,128)(2,1)S(1)} %get-tuple-element.33.hidden, bf16[8,384,4096]{2,1,0:T(8,128)(2,1)} %w_down.5), custom_call_target="tpu_custom_call" | custom-call | flops 1610612736 | bytes 6291456 | tf_op jit(solution)/shard_map/reduce/pallas_call | solution.py:286
  67.0 1.8 %reduce.5 = bf16[256,1024]{1,0:T(8,128)(2,1)S(1)} custom-call(bf16[256,3072]{1,0:T(8,128)(2,1)S(1)} %get-tuple-element.33.hidden, bf16[8,384,1024]{2,1,0:T(8,128)(2,1)S(1)} %get-tuple-element.34.weight), custom_call_target="tpu_custom_call" | custom-call | tf_op jit(solution)/shard_map/reduce/pallas_call | solution.py:272
  68.8 4.5 %reduce.7 = bf16[256,1024]{1,0:T(8,128)(2,1)S(1)} custom-call(s32[5]{0:T(128)S(1)} %pad_add_fusion.place, bf16[256,3072]{1,0:T(8,128)(2,1)S(1)} %get-tuple-element.33.hidden, bf16[8,384,4096]{2,1,0:T(8,128)(2,1)} %w_down.5), custom_call_target="tpu_custom_call" | custom-call | flops 1610612736 | bytes 6291456 | tf_op jit(solution)/shard_map/reduce/pallas_call | solution.py:286
  73.3 1.6 %collective-permute-start.8 = (bf16[256,1024]{1,0:T(8,128)(2,1)S(1)}, bf16[256,1024]{1,0:T(8,128)(2,1)S(1)}, u32[]{:S(2)}, u32[]{:S(2)}) collective-permute-start(bf16[256,1024]{1,0:T(8,128)(2,1)S(1)} %reduce.5), channel_id=1, source_target_pairs={{0,3},{1,2},{2,1},{3,0},{4,7},{5,6},{6,5},{7,4},{8,11},{9,10},{10,... | collective-permute-start | bytes 1572872 | tf_op jit(solution)/shard_map/ppermute | solution.py:21
  75.0 1.9 %collective-permute-start.10 = (bf16[256,1024]{1,0:T(8,128)(2,1)S(1)}, bf16[256,1024]{1,0:T(8,128)(2,1)S(1)}, u32[]{:S(2)}, u32[]{:S(2)}) collective-permute-start(bf16[256,1024]{1,0:T(8,128)(2,1)S(1)} %reduce.7), channel_id=1, source_target_pairs={{0,1},{1,0},{2,3},{3,2},{4,5},{5,4},{6,7},{7,6},{8,9},{9,8},{10,11... | collective-permute-start | bytes 1572872 | tf_op jit(solution)/shard_map/ppermute | solution.py:21
  76.9 4.7 %reduce.4 = bf16[256,1024]{1,0:T(8,128)(2,1)S(1)} custom-call(s32[5]{0:T(128)S(1)} %pad_add_fusion.place, bf16[256,3072]{1,0:T(8,128)(2,1)S(1)} %get-tuple-element.33.hidden, bf16[8,384,4096]{2,1,0:T(8,128)(2,1)} %w_down.5), custom_call_target="tpu_custom_call" | custom-call | flops 1610612736 | bytes 6291456 | tf_op jit(solution)/shard_map/reduce/pallas_call | solution.py:286
  81.5 2.5 %collective-permute-done.8 = bf16[256,1024]{1,0:T(8,128)(2,1)S(1)} collective-permute-done((bf16[256,1024]{1,0:T(8,128)(2,1)S(1)}, bf16[256,1024]{1,0:T(8,128)(2,1)S(1)}, u32[]{:S(2)}, u32[]{:S(2)}) %collective-permute-start.8) | collective-permute-done | bytes 524320 | tf_op jit(solution)/shard_map/ppermute | solution.py:21
  84.0 5.5 %collective-permute-done.9 = bf16[256,1024]{1,0:T(8,128)(2,1)S(1)} collective-permute-done((bf16[256,1024]{1,0:T(8,128)(2,1)S(1)}, bf16[256,1024]{1,0:T(8,128)(2,1)S(1)}, u32[]{:S(2)}, u32[]{:S(2)}) %collective-permute-start.9) | collective-permute-done | bytes 524320 | tf_op jit(solution)/shard_map/ppermute | solution.py:21
  94.1 3.5 %collective-permute-done.11 = bf16[64,1024]{1,0:T(8,128)(2,1)S(1)} collective-permute-done((bf16[64,1024]{1,0:T(8,128)(2,1)S(1)}, bf16[64,1024]{1,0:T(8,128)(2,1)S(1)}, u32[]{:S(2)}, u32[]{:S(2)}) %collective-permute-start.11) | collective-permute-done | bytes 131104 | tf_op jit(solution)/shard_map/ppermute | solution.py:26
  97.7 7.8 %collective-permute-done.12 = bf16[64,1024]{1,0:T(8,128)(2,1)S(1)} collective-permute-done((bf16[64,1024]{1,0:T(8,128)(2,1)S(1)}, bf16[64,1024]{1,0:T(8,128)(2,1)S(1)}, u32[]{:S(2)}, u32[]{:S(2)}) %collective-permute-start.12) | collective-permute-done | bytes 131104 | tf_op jit(solution)/shard_map/ppermute | solution.py:26
  107.0 2.1 %collective-permute-start.16 = (bf16[64,1024]{1,0:T(8,128)(2,1)S(1)}, bf16[64,1024]{1,0:T(8,128)(2,1)S(1)}, u32[]{:S(2)}, u32[]{:S(2)}) collective-permute-start(bf16[64,1024]{1,0:T(8,128)(2,1)S(1)} %add_convert_fusion.1.refs_0_), channel_id=1, source_target_pairs={{0,3},{1,2},{2,1},{3,0},{4,7},{5,6},{6,5},{7,4},{8,11},{9,10},{10,... | collective-permute-start | bytes 393224 | tf_op jit(solution)/shard_map/ppermute | solution.py:21
  109.1 2.4 %collective-permute-done.14.refs_1_ = bf16[64,1024]{1,0:T(8,128)(2,1)S(1)} collective-permute-done((bf16[64,1024]{1,0:T(8,128)(2,1)S(1)}, bf16[64,1024]{1,0:T(8,128)(2,1)S(1)}, u32[]{:S(2)}, u32[]{:S(2)}) %collective-permute-start.14) | collective-permute-done | bytes 131104 | tf_op jit(solution)/shard_map/ppermute | solution.py:21
  111.5 2.7 %collective-permute-done.15.refs_2_ = bf16[64,1024]{1,0:T(8,128)(2,1)S(1)} collective-permute-done((bf16[64,1024]{1,0:T(8,128)(2,1)S(1)}, bf16[64,1024]{1,0:T(8,128)(2,1)S(1)}, u32[]{:S(2)}, u32[]{:S(2)}) %collective-permute-start.15) | collective-permute-done | bytes 131104 | tf_op jit(solution)/shard_map/ppermute | solution.py:21
  114.2 1.8 %project.1 = bf16[64,512]{1,0:T(8,128)(2,1)S(1)} custom-call(s32[5]{0:T(128)S(1)} %pad_add_fusion.place, bf16[64,4096]{1,0:T(8,128)(2,1)S(1)} %bitcast.20, bf16[64,1024]{1,0:T(8,128)(2,1)S(1)} %add_convert_fusion.1.refs_0_, bf16[64,1024]{1,0:T(8,128)(2,1)S(1)} %collective-permute-done.14.refs_1_, bf16[64,1024]{1,0:T(8,128)(2,1)S(1)} %collective-permute-done.15.refs_2_, ...), custom_call_target="tpu_custom_call" | custom-call | tf_op jit(solution)/shard_map/project/pallas_call | solution.py:337
  117.3 1.6 %attend.5 = bf16[64,2048]{1,0:T(8,128)(2,1)S(1)} custom-call(s32[5]{0:T(128)S(1)} %pad_add_fusion.place, bf16[64,512]{1,0:T(8,128)(2,1)S(1)} %collective-permute-done.18.block, bf16[256,512]{1,0:T(8,128)(2,1)S(1)} %bitcast.21, bf16[256,256]{1,0:T(8,128)(2,1)S(1)} %bitcast.28, bf16[256,256]{1,0:T(8,128)(2,1)S(1)} %bitcast.32, bf16[512,2048]{1,0:T(8,128)(2,1)S(1)} %copy-done.2), custom_call_target="tpu_custom_call" | custom-call | flops 268435456 | bytes 2097152 | tf_op jit(solution)/shard_map/attend/pallas_call | solution.py:411
  120.2 1.6 %attend.6 = bf16[64,2048]{1,0:T(8,128)(2,1)S(1)} custom-call(s32[5]{0:T(128)S(1)} %pad_add_fusion.place, bf16[64,512]{1,0:T(8,128)(2,1)S(1)} %collective-permute-done.18.block, bf16[256,512]{1,0:T(8,128)(2,1)S(1)} %bitcast.22, bf16[256,256]{1,0:T(8,128)(2,1)S(1)} %bitcast.29, bf16[256,256]{1,0:T(8,128)(2,1)S(1)} %bitcast.33, bf16[512,2048]{1,0:T(8,128)(2,1)S(1)} %copy-done.2), custom_call_target="tpu_custom_call" | custom-call | flops 268435456 | bytes 2097152 | tf_op jit(solution)/shard_map/attend/pallas_call | solution.py:411
  123.2 1.6 %attend.7 = bf16[64,2048]{1,0:T(8,128)(2,1)S(1)} custom-call(s32[5]{0:T(128)S(1)} %pad_add_fusion.place, bf16[64,512]{1,0:T(8,128)(2,1)S(1)} %collective-permute-done.18.block, bf16[256,512]{1,0:T(8,128)(2,1)S(1)} %bitcast.23, bf16[256,256]{1,0:T(8,128)(2,1)S(1)} %bitcast.30, bf16[256,256]{1,0:T(8,128)(2,1)S(1)} %bitcast.34, bf16[512,2048]{1,0:T(8,128)(2,1)S(1)} %copy-done.2), custom_call_target="tpu_custom_call" | custom-call | flops 268435456 | bytes 2097152 | tf_op jit(solution)/shard_map/attend/pallas_call | solution.py:411
  125.9 1.6 %attend.4 = bf16[64,2048]{1,0:T(8,128)(2,1)S(1)} custom-call(s32[5]{0:T(128)S(1)} %pad_add_fusion.place, bf16[64,512]{1,0:T(8,128)(2,1)S(1)} %collective-permute-done.18.block, bf16[256,512]{1,0:T(8,128)(2,1)S(1)} %bitcast.24, bf16[256,256]{1,0:T(8,128)(2,1)S(1)} %bitcast.31, bf16[256,256]{1,0:T(8,128)(2,1)S(1)} %bitcast.35, bf16[512,2048]{1,0:T(8,128)(2,1)S(1)} %copy-done.2), custom_call_target="tpu_custom_call" | custom-call | flops 268435456 | bytes 2097152 | tf_op jit(solution)/shard_map/attend/pallas_call | solution.py:411
  127.5 1.6 %collective-permute-done.19 = bf16[64,2048]{1,0:T(8,128)(2,1)S(1)} collective-permute-done((bf16[64,2048]{1,0:T(8,128)(2,1)S(1)}, bf16[64,2048]{1,0:T(8,128)(2,1)S(1)}, u32[]{:S(2)}, u32[]{:S(2)}) %collective-permute-start.19) | collective-permute-done | bytes 262176 | tf_op jit(solution)/shard_map/ppermute | solution.py:21
  129.1 4.8 %collective-permute-done.20 = bf16[64,2048]{1,0:T(8,128)(2,1)S(1)} collective-permute-done((bf16[64,2048]{1,0:T(8,128)(2,1)S(1)}, bf16[64,2048]{1,0:T(8,128)(2,1)S(1)}, u32[]{:S(2)}, u32[]{:S(2)}) %collective-permute-start.20) | collective-permute-done | bytes 262176 | tf_op jit(solution)/shard_map/ppermute | solution.py:21
  (65 shorter events, 15.7 us)
Async XLA Ops:
  0.0 16.7 %copy-start = (bf16[1024,512]{1,0:T(8,128)(2,1)S(1)}, bf16[1024,512]{1,0:T(8,128)(2,1)}, u32[]{:S(2)}) copy-start(bf16[1024,512]{1,0:T(8,128)(2,1)} %param.20) | copy-start | bytes 3145732
  1.8 14.9 %collective-permute-start = (bf16[64,1152]{1,0:T(8,128)(2,1)S(1)}, bf16[64,1152]{1,0:T(8,128)(2,1)S(1)}, u32[]{:S(2)}, u32[]{:S(2)}) collective-permute-start(bf16[64,1152]{1,0:T(8,128)(2,1)S(1)} %pad_maximum_fusion.3), channel_id=1, source_target_pairs={{0,4},{4,8},{8,12},{12,0},{1,5},{5,9},{9,13},{13,1},{2,6},{6,10},{... | collective-permute-start | bytes 442376 | tf_op jit(solution)/shard_map/ppermute | solution.py:26
  4.9 12.3 %collective-permute-start.1 = (bf16[64,1152]{1,0:T(8,128)(2,1)S(1)}, bf16[64,1152]{1,0:T(8,128)(2,1)S(1)}, u32[]{:S(2)}, u32[]{:S(2)}) collective-permute-start(bf16[64,1152]{1,0:T(8,128)(2,1)S(1)} %pad_maximum_fusion.3), channel_id=1, source_target_pairs={{0,8},{4,12},{8,0},{12,4},{1,9},{5,13},{9,1},{13,5},{2,10},{6,14},... | collective-permute-start | bytes 442376 | tf_op jit(solution)/shard_map/ppermute | solution.py:26
  7.5 9.7 %collective-permute-start.2 = (bf16[64,1152]{1,0:T(8,128)(2,1)S(1)}, bf16[64,1152]{1,0:T(8,128)(2,1)S(1)}, u32[]{:S(2)}, u32[]{:S(2)}) collective-permute-start(bf16[64,1152]{1,0:T(8,128)(2,1)S(1)} %pad_maximum_fusion.3), channel_id=1, source_target_pairs={{0,12},{4,0},{8,4},{12,8},{1,13},{5,1},{9,5},{13,9},{2,14},{6,2},{... | collective-permute-start | bytes 442376 | tf_op jit(solution)/shard_map/ppermute | solution.py:26
  9.6 13.8 %copy-start.5 = (bf16[4096,32]{0,1:T(8,128)(2,1)S(1)}, bf16[4096,32]{0,1:T(8,128)(2,1)}, u32[]{:S(2)}) copy-start(bf16[4096,32]{0,1:T(8,128)(2,1)} %param.15) | copy-start | bytes 786436
  16.7 6.8 %copy-start.3 = (bf16[1,64,4096]{2,1,0:T(8,128)(2,1)S(1)}, bf16[1,64,4096]{2,1,0:T(8,128)(2,1)}, u32[]{:S(2)}) copy-start(bf16[1,64,4096]{2,1,0:T(8,128)(2,1)} %param.13) | copy-start | bytes 1572868
  17.3 13.6 %collective-permute-start.6 = (bf16[192,1024]{1,0:T(8,128)(2,1)S(1)}, bf16[192,1024]{1,0:T(8,128)(2,1)S(1)}, u32[]{:S(2)}, u32[]{:S(2)}) collective-permute-start(bf16[192,1024]{1,0:T(8,128)(2,1)S(1)} %pad_maximum_fusion.2.refs_0_), channel_id=1, source_target_pairs={{0,1},{1,0},{2,3},{3,2},{4,5},{5,4},{6,7},{7,6},{8,9},{9,8},{10,11... | collective-permute-start | bytes 1179656 | tf_op jit(solution)/shard_map/ppermute | solution.py:21
  18.9 19.1 %collective-permute-start.7 = (bf16[192,1024]{1,0:T(8,128)(2,1)S(1)}, bf16[192,1024]{1,0:T(8,128)(2,1)S(1)}, u32[]{:S(2)}, u32[]{:S(2)}) collective-permute-start(bf16[192,1024]{1,0:T(8,128)(2,1)S(1)} %pad_maximum_fusion.2.refs_0_), channel_id=1, source_target_pairs={{0,2},{1,3},{2,0},{3,1},{4,6},{5,7},{6,4},{7,5},{8,10},{9,11},{10,... | collective-permute-start | bytes 1179656 | tf_op jit(solution)/shard_map/ppermute | solution.py:21
  20.4 30.2 %collective-permute-start.5 = (bf16[192,1024]{1,0:T(8,128)(2,1)S(1)}, bf16[192,1024]{1,0:T(8,128)(2,1)S(1)}, u32[]{:S(2)}, u32[]{:S(2)}) collective-permute-start(bf16[192,1024]{1,0:T(8,128)(2,1)S(1)} %pad_maximum_fusion.2.refs_0_), channel_id=1, source_target_pairs={{0,3},{1,2},{2,1},{3,0},{4,7},{5,6},{6,5},{7,4},{8,11},{9,10},{10,... | collective-permute-start | bytes 1179656 | tf_op jit(solution)/shard_map/ppermute | solution.py:21
  20.9 37.8 %collective-permute-start.3 = (bf16[1024,256]{1,0:T(8,128)(2,1)S(1)}, bf16[1024,256]{1,0:T(8,128)(2,1)S(1)}, u32[]{:S(2)}, u32[]{:S(2)}) collective-permute-start(bf16[1024,256]{1,0:T(8,128)(2,1)S(1)} %constant_dynamic-slice_fusion), channel_id=1, source_target_pairs={{0,8},{4,12},{8,0},{12,4},{1,9},{5,13},{9,1},{13,5},{2,10},{6,14},... | collective-permute-start | bytes 1572872 | tf_op jit(solution)/shard_map/ppermute | solution.py:21
  58.8 32.3 %collective-permute-start.4 = (bf16[2048,256]{1,0:T(8,128)(2,1)S(1)}, bf16[2048,256]{1,0:T(8,128)(2,1)S(1)}, u32[]{:S(2)}, u32[]{:S(2)}) collective-permute-start(bf16[2048,256]{1,0:T(8,128)(2,1)S(1)} %pad_maximum_fusion.1), channel_id=1, source_target_pairs={{0,4},{4,0},{8,12},{12,8},{1,5},{5,1},{9,13},{13,9},{2,6},{6,2},{1... | collective-permute-start | bytes 3145736 | tf_op jit(solution)/shard_map/ppermute | solution.py:21
  73.3 10.7 %collective-permute-start.8 = (bf16[256,1024]{1,0:T(8,128)(2,1)S(1)}, bf16[256,1024]{1,0:T(8,128)(2,1)S(1)}, u32[]{:S(2)}, u32[]{:S(2)}) collective-permute-start(bf16[256,1024]{1,0:T(8,128)(2,1)S(1)} %reduce.5), channel_id=1, source_target_pairs={{0,3},{1,2},{2,1},{3,0},{4,7},{5,6},{6,5},{7,4},{8,11},{9,10},{10,... | collective-permute-start | bytes 1572872 | tf_op jit(solution)/shard_map/ppermute | solution.py:21
  74.9 14.6 %collective-permute-start.9 = (bf16[256,1024]{1,0:T(8,128)(2,1)S(1)}, bf16[256,1024]{1,0:T(8,128)(2,1)S(1)}, u32[]{:S(2)}, u32[]{:S(2)}) collective-permute-start(bf16[256,1024]{1,0:T(8,128)(2,1)S(1)} %reduce.6), channel_id=1, source_target_pairs={{0,2},{1,3},{2,0},{3,1},{4,6},{5,7},{6,4},{7,5},{8,10},{9,11},{10,... | collective-permute-start | bytes 1572872 | tf_op jit(solution)/shard_map/ppermute | solution.py:21
  75.0 15.6 %collective-permute-start.10 = (bf16[256,1024]{1,0:T(8,128)(2,1)S(1)}, bf16[256,1024]{1,0:T(8,128)(2,1)S(1)}, u32[]{:S(2)}, u32[]{:S(2)}) collective-permute-start(bf16[256,1024]{1,0:T(8,128)(2,1)S(1)} %reduce.7), channel_id=1, source_target_pairs={{0,1},{1,0},{2,3},{3,2},{4,5},{5,4},{6,7},{7,6},{8,9},{9,8},{10,11... | collective-permute-start | bytes 1572872 | tf_op jit(solution)/shard_map/ppermute | solution.py:21
  91.0 23.2 %copy-start.8 = (f32[4096]{0:T(1024)S(1)}, f32[4096]{0:T(1024)}, u32[]{:S(2)}) copy-start(f32[4096]{0:T(1024)} %param.19) | copy-start | bytes 49156
  91.2 23.0 %collective-permute-start.17 = (bf16[4096,256]{1,0:T(8,128)(2,1)S(1)}, bf16[4096,256]{1,0:T(8,128)(2,1)S(1)}, u32[]{:S(2)}, u32[]{:S(2)}) collective-permute-start(bf16[4096,256]{1,0:T(8,128)(2,1)S(1)} %pad_maximum_fusion.refs_5_), channel_id=1, source_target_pairs={{0,16},{16,0},{1,17},{17,1},{2,18},{18,2},{3,19},{19,3},{4,20},{20... | collective-permute-start | bytes 6291464 | tf_op jit(solution)/shard_map/ppermute | solution.py:21
  91.3 26.0 %copy-start.2 = (bf16[512,2048]{1,0:T(8,128)(2,1)S(1)}, bf16[512,2048]{1,0:T(8,128)(2,1)}, u32[]{:S(2)}) copy-start(bf16[512,2048]{1,0:T(8,128)(2,1)} %w_out.7) | copy-start | bytes 6291460
  91.3 26.0 %copy-start.4 = (bf16[1,256,512]{2,1,0:T(8,128)(2,1)S(1)}, bf16[1,256,512]{2,1,0:T(8,128)(2,1)}, u32[]{:S(2)}) copy-start(bf16[1,256,512]{2,1,0:T(8,128)(2,1)} %param.22) | copy-start | bytes 786436
  91.3 26.0 %copy-start.6 = (bf16[1,256,256]{2,1,0:T(8,128)(2,1)S(1)}, bf16[1,256,256]{2,1,0:T(8,128)(2,1)}, u32[]{:S(2)}) copy-start(bf16[1,256,256]{2,1,0:T(8,128)(2,1)} %param.23) | copy-start | bytes 393220
  91.3 26.0 %copy-start.7 = (bf16[1,256,256]{2,1,0:T(8,128)(2,1)S(1)}, bf16[1,256,256]{2,1,0:T(8,128)(2,1)}, u32[]{:S(2)}) copy-start(bf16[1,256,256]{2,1,0:T(8,128)(2,1)} %param.24) | copy-start | bytes 393220
  91.3 6.3 %collective-permute-start.11 = (bf16[64,1024]{1,0:T(8,128)(2,1)S(1)}, bf16[64,1024]{1,0:T(8,128)(2,1)S(1)}, u32[]{:S(2)}, u32[]{:S(2)}) collective-permute-start(bf16[64,1024]{1,0:T(8,128)(2,1)S(1)} %get-tuple-element.39), channel_id=1, source_target_pairs={{0,12},{4,0},{8,4},{12,8},{1,13},{5,1},{9,5},{13,9},{2,14},{6,2},{... | collective-permute-start | bytes 393224 | tf_op jit(solution)/shard_map/ppermute | solution.py:26
  91.8 13.6 %collective-permute-start.12 = (bf16[64,1024]{1,0:T(8,128)(2,1)S(1)}, bf16[64,1024]{1,0:T(8,128)(2,1)S(1)}, u32[]{:S(2)}, u32[]{:S(2)}) collective-permute-start(bf16[64,1024]{1,0:T(8,128)(2,1)S(1)} %get-tuple-element.41), channel_id=1, source_target_pairs={{0,8},{4,12},{8,0},{12,4},{1,9},{5,13},{9,1},{13,5},{2,10},{6,14},... | collective-permute-start | bytes 393224 | tf_op jit(solution)/shard_map/ppermute | solution.py:26
  93.1 12.3 %collective-permute-start.13 = (bf16[64,1024]{1,0:T(8,128)(2,1)S(1)}, bf16[64,1024]{1,0:T(8,128)(2,1)S(1)}, u32[]{:S(2)}, u32[]{:S(2)}) collective-permute-start(bf16[64,1024]{1,0:T(8,128)(2,1)S(1)} %get-tuple-element.40), channel_id=1, source_target_pairs={{0,4},{4,8},{8,12},{12,0},{1,5},{5,9},{9,13},{13,1},{2,6},{6,10},{... | collective-permute-start | bytes 393224 | tf_op jit(solution)/shard_map/ppermute | solution.py:26
  105.5 6.0 %collective-permute-start.14 = (bf16[64,1024]{1,0:T(8,128)(2,1)S(1)}, bf16[64,1024]{1,0:T(8,128)(2,1)S(1)}, u32[]{:S(2)}, u32[]{:S(2)}) collective-permute-start(bf16[64,1024]{1,0:T(8,128)(2,1)S(1)} %add_convert_fusion.1.refs_0_), channel_id=1, source_target_pairs={{0,1},{1,0},{2,3},{3,2},{4,5},{5,4},{6,7},{7,6},{8,9},{9,8},{10,11... | collective-permute-start | bytes 393224 | tf_op jit(solution)/shard_map/ppermute | solution.py:21
  106.3 7.8 %collective-permute-start.15 = (bf16[64,1024]{1,0:T(8,128)(2,1)S(1)}, bf16[64,1024]{1,0:T(8,128)(2,1)S(1)}, u32[]{:S(2)}, u32[]{:S(2)}) collective-permute-start(bf16[64,1024]{1,0:T(8,128)(2,1)S(1)} %add_convert_fusion.1.refs_0_), channel_id=1, source_target_pairs={{0,2},{1,3},{2,0},{3,1},{4,6},{5,7},{6,4},{7,5},{8,10},{9,11},{10,... | collective-permute-start | bytes 393224 | tf_op jit(solution)/shard_map/ppermute | solution.py:21
  107.0 7.2 %collective-permute-start.16 = (bf16[64,1024]{1,0:T(8,128)(2,1)S(1)}, bf16[64,1024]{1,0:T(8,128)(2,1)S(1)}, u32[]{:S(2)}, u32[]{:S(2)}) collective-permute-start(bf16[64,1024]{1,0:T(8,128)(2,1)S(1)} %add_convert_fusion.1.refs_0_), channel_id=1, source_target_pairs={{0,3},{1,2},{2,1},{3,0},{4,7},{5,6},{6,5},{7,4},{8,11},{9,10},{10,... | collective-permute-start | bytes 393224 | tf_op jit(solution)/shard_map/ppermute | solution.py:21
  116.0 1.3 collective-permute-start.18
  118.9 10.2 %collective-permute-start.19 = (bf16[64,2048]{1,0:T(8,128)(2,1)S(1)}, bf16[64,2048]{1,0:T(8,128)(2,1)S(1)}, u32[]{:S(2)}, u32[]{:S(2)}) collective-permute-start(bf16[64,2048]{1,0:T(8,128)(2,1)S(1)} %attend.5), channel_id=1, source_target_pairs={{0,3},{1,2},{2,1},{3,0},{4,7},{5,6},{6,5},{7,4},{8,11},{9,10},{10,... | collective-permute-start | bytes 786440 | tf_op jit(solution)/shard_map/ppermute | solution.py:21
  120.2 14.5 %copy-start.1 = (bf16[1024,512]{1,0:T(8,128)(2,1)S(1)}, bf16[1024,512]{1,0:T(8,128)(2,1)}, u32[]{:S(2)}) copy-start(bf16[1024,512]{1,0:T(8,128)(2,1)} %param.20) | copy-start | bytes 3145732
  121.9 12.0 %collective-permute-start.20 = (bf16[64,2048]{1,0:T(8,128)(2,1)S(1)}, bf16[64,2048]{1,0:T(8,128)(2,1)S(1)}, u32[]{:S(2)}, u32[]{:S(2)}) collective-permute-start(bf16[64,2048]{1,0:T(8,128)(2,1)S(1)} %attend.6), channel_id=1, source_target_pairs={{0,2},{1,3},{2,0},{3,1},{4,6},{5,7},{6,4},{7,5},{8,10},{9,11},{10,... | collective-permute-start | bytes 786440 | tf_op jit(solution)/shard_map/ppermute | solution.py:21
  124.8 9.0 %collective-permute-start.21 = (bf16[64,2048]{1,0:T(8,128)(2,1)S(1)}, bf16[64,2048]{1,0:T(8,128)(2,1)S(1)}, u32[]{:S(2)}, u32[]{:S(2)}) collective-permute-start(bf16[64,2048]{1,0:T(8,128)(2,1)S(1)} %attend.7), channel_id=1, source_target_pairs={{0,1},{1,0},{2,3},{3,2},{4,5},{5,4},{6,7},{7,6},{8,9},{9,8},{10,11... | collective-permute-start | bytes 786440 | tf_op jit(solution)/shard_map/ppermute | solution.py:21

commit v4 on v1

--- a/solution.py
+++ b/solution.py
@@ -62,129 +62,222 @@
     return logits
 
 
-def both(rows, w_gates, w_ups, i):
-    width = w_gates[0].shape[1]
-    value = 0.0
-    for j, (w_gate, w_up) in enumerate(zip(w_gates, w_ups)):
-        weight = jnp.concatenate([w_gate[i], w_up[i]], axis=1)
-        value += jnp.dot(
-            rows[:, j * width : (j + 1) * width], weight, preferred_element_type=F32
+PAIR, DOWN = 0, 2
+
+
+def pair_copies(place, sources, k, low, high, out, sems):
+    rows, count = columns_of(place[0] ^ k, out.shape[1]), high - low
+    return [
+        pltpu.make_async_copy(
+            sources[j].at[pl.ds(low, count), rows, :], out.at[pl.ds(j * count, count)], sems.at[j]
         )
-    return value
-
-
-def gather_kernel(quarters, first, place, own, router, *refs):
+        for j in range(2)
+    ]
+
+
+def expert_copies(place, sources, k, low, e, out, sems):
+    rows, count = columns_of(place[0] ^ k, out.shape[1]), out.shape[0] // 2
+    return [
+        pltpu.make_async_copy(
+            sources[j].at[e, rows, :], out.at[j * count + e - low], sems.at[j, e - low]
+        )
+        for j in range(2)
+    ]
+
+
+def unpack_kernel(tags, *refs):
+    *arrived, near, all_tags = refs
+    local, width = tags.shape[0], near.shape[1]
+    all_tags[:local, :] = tags[...]
+    for d, parcel in enumerate(arrived):
+        near[d * local : (d + 1) * local, :] = parcel[:, :width]
+        all_tags[(d + 1) * local : (d + 2) * local, :] = parcel[:, width:]
+
+
+def unpack(tags, arrived, width):
+    local, extra = tags.shape
+    count = len(arrived)
+    return pl.pallas_call(
+        unpack_kernel,
+        out_shape=[
+            jax.ShapeDtypeStruct((count * local, width), BF16),
+            jax.ShapeDtypeStruct(((count + 1) * local, extra), BF16),
+        ],
+        in_specs=[WHOLE] * (1 + count),
+        out_specs=[WHOLE] * 2,
+        compiler_params=params(0, 4 if count < 8 else 32),
+        name="unpack",
+    )(tags, *arrived)
+
+
+def stage_kernel(items, quarters, parts, first, top, place, *refs):
+    refs = list(refs)
+
+    def take(count):
+        taken = refs[:count]
+        del refs[:count]
+        return taken
+
+    sources, count = take(3), len(quarters)
+    streams = [part for part in parts if part[3]]
+    if count:
+        (own, router), nears = take(2), take(count)
+        held = take(len(parts) - len(streams))
+        totals = [None, None] if first else take(2)
+        tags = take(1)[0] if top else None
+    ahead = take(len(items))
+    out = take(1)[0] if count else None
+    logits_out = take(1)[0] if count and not top else None
+    ahead_sems = take(1)[0]
+    rows = take(1)[0] if count else None
+    weights = take(1)[0] if top else None
+    buffers, buffer_sems = take(len(streams)), take(len(streams))
+
+    for (k, low, high, _), buffer, sems in zip(streams, buffers, buffer_sems):
+        for e in range(low, high):
+            for copy in expert_copies(place, sources, k, low, e, buffer, sems):
+                copy.start()
+    copies = []
+    for n, item in enumerate(items):
+        if item[0] == PAIR:
+            copies += pair_copies(place, sources, *item[1:], ahead[n], ahead_sems.at[n])
+        else:
+            columns = columns_of(place[0] ^ item[1], ahead[n].shape[2])
+            copies.append(
+                pltpu.make_async_copy(
+                    sources[DOWN].at[:, :, columns], ahead[n], ahead_sems.at[n, 0]
+                )
+            )
+    if not streams:
+        for copy in copies:
+            copy.start()
+    if count:
+        logits = take_rows(quarters, place, own, nears, router, rows)
+        if not first:
+            logits += totals[1][...]
+        if top:
+            expert = lax.broadcasted_iota(jnp.int32, logits.shape, 1)
+            named = tags[...].astype(F32).astype(jnp.int32)
+            picked = named[:, 0:1] == expert
+            for j in range(1, top):
+                picked = jnp.logical_or(picked, named[:, j : j + 1] == expert)
+            most = jnp.max(jnp.where(picked, logits, -1e30), axis=1, keepdims=True)
+            spread = jnp.where(picked, jnp.exp(logits - most), 0.0)
+            weights[...] = spread / jnp.sum(spread, axis=1, keepdims=True)
+        else:
+            logits_out[...] = logits
+        experts, (_, _, units) = sources[0].shape[0], sources[0].shape
+        width = nears[0].shape[1]
+        held, buffers, buffer_sems = list(held), list(buffers), list(buffer_sems)
+        for n, (k, low, high, streamed) in enumerate(parts):
+            weight = buffers.pop(0) if streamed else held.pop(0)
+            sems = buffer_sems.pop(0) if streamed else None
+            at = quarters.index(k) * width
+            begun = any(k != part[0] for part in parts[:n])
+
+            def body(e, carry, k=k, low=low, weight=weight, sems=sems, at=at, begun=begun):
+                if sems is not None:
+                    for copy in expert_copies(place, sources, k, low, e, weight, sems):
+                        copy.wait()
+                half = weight.shape[0] // 2
+                both = jnp.concatenate([weight[e - low], weight[half + e - low]], axis=1)
+                value = jnp.dot(rows[:, at : at + width], both, preferred_element_type=F32)
+                if begun:
+                    value += out[e]
+                elif not first:
+                    value += totals[0][e]
+                if not top:
+                    out[e] = value
+                    return carry
+                gate, up = value[:, :units], value[:, units:]
+                mine = expert == place[1] * experts + e
+                scale = jnp.sum(jnp.where(mine, weights[...], 0.0), axis=1, keepdims=True)
+                out[:, columns_of(e, units)] = (
+                    gate / (1.0 + jnp.exp(-gate)) * up * scale
+                ).astype(BF16)
+                return carry
+
+            lax.fori_loop(low, high, body, 0)
+            if streams and n == 0:
+                for copy in copies:
+                    copy.start()
+    for copy in copies:
+        copy.wait()
+
+
+def stage(place, sources, items, own=None, router=None, nears=None, parts=(), held=(),
+          totals=(), tags=None, top=0):
+    experts, model, units = sources[0].shape
+    nears = nears or {}
+    quarters = list(nears)
+    width = model // lax.axis_size("half")
     count = len(quarters)
-    nears, w_gates, w_ups, refs = (
-        refs[:count],
-        refs[count : 2 * count],
-        refs[2 * count : 3 * count],
-        refs[3 * count :],
-    )
-    totals, refs = ((None,) * 2, refs) if first else (refs[:2], refs[2:])
-    out, logits_out, rows = refs
-    step, each = pl.program_id(0), w_gates[0].shape[0]
-
-    @pl.when(step == 0)
-    def _():
-        logits = take_rows(quarters, place, own, nears, router, rows)
-        logits_out[...] = logits if first else logits + totals[1][...]
-
-    for i in range(each):
-        value = both(rows, w_gates, w_ups, i)
-        out[step * each + i] = value if first else value + totals[0][step * each + i]
-
-
-def finish_kernel(quarters, top, place, own, router, *refs):
-    count = len(quarters)
-    nears, w_gates, w_ups, refs = (
-        refs[:count],
-        refs[count : 2 * count],
-        refs[2 * count : 3 * count],
-        refs[3 * count :],
-    )
-    total, logits_total, tags, hidden, rows, weights = refs
-    step, each, units = pl.program_id(0), w_gates[0].shape[0], w_gates[0].shape[2]
-    expert = lax.broadcasted_iota(jnp.int32, weights.shape, 1)
-
-    @pl.when(step == 0)
-    def _():
-        logits = logits_total[...] + take_rows(quarters, place, own, nears, router, rows)
-        named = tags[...].astype(F32).astype(jnp.int32)
-        picked = named[:, 0:1] == expert
-        for j in range(1, top):
-            picked = jnp.logical_or(picked, named[:, j : j + 1] == expert)
-        most = jnp.max(jnp.where(picked, logits, -1e30), axis=1, keepdims=True)
-        spread = jnp.where(picked, jnp.exp(logits - most), 0.0)
-        weights[...] = spread / jnp.sum(spread, axis=1, keepdims=True)
-
-    for i in range(each):
-        value = total[step * each + i] + both(rows, w_gates, w_ups, i)
-        gate, up = value[:, :units], value[:, units:]
-        mine = expert == (place[1] * pl.num_programs(0) + step) * each + i
-        scale = jnp.sum(jnp.where(mine, weights[...], 0.0), axis=1, keepdims=True)
-        hidden[:, i * units : (i + 1) * units] = (
-            gate / (1.0 + jnp.exp(-gate)) * up * scale
-        ).astype(BF16)
-
-
-def expand(quarters, place, own, nears, router, w_gate, w_up, totals, tags, top):
-    count = len(quarters)
-    local, _ = own.shape
-    tokens = local + nears[0].shape[0]
-    experts, units = w_gate.shape[0], w_gate.shape[2]
-    each = math.gcd(experts, 4 // count)
-    width = nears[0].shape[1]
-    last = tags is not None
-    weight = [
-        pl.BlockSpec((each, width, units), lambda e, place, k=k: (e, place[0] ^ k, 0))
-        for k in quarters
+    operands = [in_hbm(array) for array in sources]
+    shapes = [
+        pltpu.VMEM((2 * (item[3] - item[2]), width, units), BF16)
+        if item[0] == PAIR
+        else pltpu.VMEM((experts, units, width), BF16)
+        for item in items
     ]
-    operands = [own, router] + [in_vmem(near) for near in nears]
-    operands += [in_hbm(w_gate)] * count + [in_hbm(w_up)] * count
-    operands += [in_vmem(t) for t in totals]
-    scratch = [pltpu.VMEM((tokens, count * width), BF16)]
-    if last:
-        operands.append(tags)
-        kernel = functools.partial(finish_kernel, quarters, top)
-        scratch.append(pltpu.VMEM((tokens, router.shape[0]), F32))
-        out_shape = pltpu.VMEM((tokens, experts * units), BF16)
-        out_specs = pl.BlockSpec((tokens, each * units), lambda e, place: (0, e))
-        aliases = {}
-    else:
-        kernel = functools.partial(gather_kernel, quarters, not totals)
-        out_shape = [
-            pltpu.VMEM((experts, tokens, 2 * units), F32),
-            pltpu.VMEM((tokens, router.shape[0]), F32),
-        ]
-        out_specs = [WHOLE] * 2
-        aliases = {3 + 3 * count + i: i for i in range(len(totals))}
-    return pl.pallas_call(
-        kernel,
-        out_shape=out_shape,
+    scratch, aliases, tokens = [pltpu.SemaphoreType.DMA((max(1, len(items)), 2))], {}, 0
+    streams = [part for part in parts if part[3]]
+    mebibytes = 1
+    if count:
+        tokens = own.shape[0] + nears[quarters[0]].shape[0]
+        mebibytes = 4 + -(-sum(4 * width * units * (p[2] - p[1]) for p in streams) >> 20)
+        operands += [own, router] + [in_vmem(nears[k]) for k in quarters]
+        operands += [in_vmem(array) for array in held]
+        aliases = {1 + len(operands) + i: len(items) + i for i in range(len(totals))}
+        operands += [in_vmem(total) for total in totals]
+        scratch.append(pltpu.VMEM((tokens, count * width), BF16))
+        if top:
+            operands.append(tags)
+            aliases = {}
+            scratch.append(pltpu.VMEM((tokens, router.shape[0]), F32))
+            shapes.append(pltpu.VMEM((tokens, experts * units), BF16))
+        else:
+            shapes.append(pltpu.VMEM((experts, tokens, 2 * units), F32))
+            shapes.append(pltpu.VMEM((tokens, router.shape[0]), F32))
+    scratch += [pltpu.VMEM((2 * (p[2] - p[1]), width, units), BF16) for p in streams]
+    scratch += [pltpu.SemaphoreType.DMA((2, p[2] - p[1])) for p in streams]
+    outs = pl.pallas_call(
+        functools.partial(stage_kernel, items, quarters, parts, not totals, top),
+        out_shape=shapes,
         grid_spec=pltpu.PrefetchScalarGridSpec(
             num_scalar_prefetch=1,
-            grid=(experts // each,),
-            in_specs=[WHOLE] * (2 + count)
-            + weight * 2
-            + [WHOLE] * (len(operands) - 2 - 3 * count),
-            out_specs=out_specs,
+            grid=(),
+            in_specs=[pl.BlockSpec(memory_space=pl.ANY)] * 3 + [WHOLE] * (len(operands) - 3),
+            out_specs=[WHOLE] * len(shapes),
             scratch_shapes=scratch,
         ),
         input_output_aliases=aliases,
-        compiler_params=params(1, 24 if tokens <= 1024 else 40),
-        cost_estimate=pl.CostEstimate(
-            flops=4 * tokens * width * experts * units * count,
-            transcendentals=0,
-            bytes_accessed=4 * experts * width * units * count,
-        ),
-        name="expand",
+        compiler_params=params(0, mebibytes if tokens <= 1024 else 32),
     )(place, *operands)
+    return outs[: len(items)], outs[len(items) :]
 
 
 def reduce_kernel(place, hidden, w_down, out):
     weight = w_down[...].reshape(-1, w_down.shape[2])
     out[...] = jnp.dot(hidden[...], weight, preferred_element_type=F32).astype(BF16)
+
+
+def reduce_ahead_kernel(hidden, weight, out):
+    block = weight.shape[2] // 2
+    for i in range(2):
+        columns = slice(i * block, (i + 1) * block)
+        piece = weight[:, :, columns].reshape(-1, block)
+        out[:, columns] = jnp.dot(hidden[...], piece, preferred_element_type=F32).astype(BF16)
+
+
+def reduce_ahead(hidden, weight):
+    return pl.pallas_call(
+        reduce_ahead_kernel,
+        out_shape=jax.ShapeDtypeStruct((hidden.shape[0], weight.shape[2]), BF16),
+        in_specs=[WHOLE] * 2,
+        out_specs=WHOLE,
+        compiler_params=params(0, 12),
+        name="reduce",
+    )(in_vmem(hidden), in_vmem(weight))
 
 
 def reduce(k, place, hidden, w_down, width, block):
@@ -373,10 +466,13 @@
     tags = jnp.pad(chosen.astype(BF16), ((0, 0), (0, LANES - top)))
     quarter = lax.dynamic_slice_in_dim(own, half * width, width, axis=1)
     parcel = jnp.concatenate([quarter, tags], axis=1)
+    order = sorted(range(1, parts), key=lambda k: bin(k).count("1"))
     arrived = [shift(parcel, "ep", d) for d in range(1, eps)]
-    near = jnp.concatenate([a[:, :width] for a in arrived], axis=0)
-    all_tags = jnp.concatenate([tags] + [a[:, width:] for a in arrived], axis=0)
-    order = sorted(range(1, parts), key=lambda k: bin(k).count("1"))
+    sources = (w_gate, w_up, w_down)
+    experts = w_gate.shape[0]
+    beside, last = order[:-1], order[-1]
+    got, _ = stage(place, sources, [(PAIR, 0, 0, experts)])
+    near, all_tags = unpack(tags, arrived, width)
     far = order[::-1]
     others = {k: swap(near, "half", k) for k in order[:-1]}
     others[order[-1]] = swap(near, "half", order[-1])
@@ -390,34 +486,38 @@
         mine = jnp.concatenate([mine, swap(mine, "ep", bit)], axis=0)
         origins += [origin ^ bit for origin in origins]
 
-    totals = ()
-    batches = [[0], order[:-1], order[-1:]]
-    for quarters in batches:
-        totals = expand(
-            quarters,
-            place,
-            own,
-            [others[k] for k in quarters],
-            router.T,
-            w_gate,
-            w_up,
-            totals,
-            all_tags if quarters is batches[-1] else None,
-            top,
-        )
-    hidden = totals
+    got, totals = stage(
+        place, sources, [(PAIR, beside[0], 0, experts)], own, router.T, {0: others[0]},
+        [(0, 0, experts, False)], got,
+    )
+    early = experts // 2
+    got, totals = stage(
+        place, sources, [(PAIR, last, 0, early)] if early else [], own, router.T,
+        {k: others[k] for k in beside},
+        [(k, 0, experts, k != beside[0]) for k in beside], got, totals,
+    )
+    pieces = [(last, 0, early, False)] if early else []
+    got, (hidden,) = stage(
+        place, sources, [(DOWN, far[0])], own, router.T, {last: others[last]},
+        pieces + [(last, early, experts, True)], got, totals, all_tags, top,
+    )
+    ahead = {far[0]: got[0]}
     partial = {}
     for k in far + [0]:
-        partial[k] = reduce(k, place, hidden, w_down, width, width // 2)
+        if k in ahead:
+            partial[k] = reduce_ahead(hidden, ahead[k])
+        else:
+            partial[k] = reduce(k, place, hidden, w_down, width, width // 2)
     gathered = []
     for k in far:
         gathered.append(swap(partial[k], "half", k))
-    mine, partial[0] = lax.optimization_barrier((mine, partial[0]))
-    theirs = swap(mine, "pool", 1)
     summed = total_of(partial[0], gathered)
     returned = [
-        shift(summed[d * local : (d + 1) * local].astype(BF16), "ep", -d) for d in range(1, eps)
+        shift(summed[d * local : (d + 1) * local].astype(BF16), "ep", -d)
+        for d in range(1, eps)
     ]
+    mine, summed = lax.optimization_barrier((mine, summed))
+    theirs = swap(mine, "pool", 1)
     moe_quarter = total_of(summed[:local], returned).astype(BF16)
     moe = [moe_quarter] + [None] * (parts - 1)
     for k in order:

time: 155 us -> 135 us (0.87)
  waiting for transfers between devices: 66.1 us -> 49.1 us
  Pallas kernels: 54.1 us -> 51 us
    ppermute x16, waiting for transfers between devices: 48.5 us -> 30.2 us  [swap(): lax.ppermute(shard, axis, [(i, i ^ bits) for i in range(lax.axis_size(axi...]
    pallas_call x4 -> x3, Pallas kernels: 18 us -> 13.5 us  [reduce(): pl.pallas_call(reduce_kernel, out_shape=jax.ShapeDtypeStruct((tokens, wid...]
    pallas_call x3 -> x6, Pallas kernels: 27.9 us -> 29.3 us  [the longest x4 27.4 us: stage(): pl.pallas_call(functools.partial(stage_kernel, items, quarters, parts, no...]
  transfers between devices with their start and end apart: 22 -> 22, of which waited for: 13 -> 13; matrix products, arithmetic and copies ran while one was open for 1% -> 1% of each run, Pallas kernels for 33% -> 35%
where the time goes in v4:
time: 135 us
  Pallas kernels  51 us (38%)
  waiting for transfers between devices  49.1 us (36%)
  starting transfers between devices  30.2 us (22%)
  local copies, waits for them, and re-layouts  2.55 us (2%)
  other arithmetic  1.59 us (1%)
    ppermute x16, waiting for transfers between devices, swap(): lax.ppermute(shard, axis, [(i, i ^ bits) for i in range(lax.axis_size(axi...  30.2 us
    pallas_call x4, Pallas kernels, stage(): pl.pallas_call(functools.partial(stage_kernel, items, quarters, parts, no...  27.4 us
    ppermute x6, waiting for transfers between devices, shift(): lax.ppermute(shard, axis, [(i, (i + distance) % count) for i in range(cou...  18.9 us
    ppermute x16, starting transfers between devices, swap(): lax.ppermute(shard, axis, [(i, i ^ bits) for i in range(lax.axis_size(axi...  18.8 us
    pallas_call x3, Pallas kernels, reduce(): pl.pallas_call(reduce_kernel, out_shape=jax.ShapeDtypeStruct((tokens, wid...  13.5 us
    ppermute x6, starting transfers between devices, shift(): lax.ppermute(shard, axis, [(i, (i + distance) % count) for i in range(cou...  11.5 us
    pallas_call x4, Pallas kernels, attend(): pl.pallas_call(functools.partial(attend_kernel, k, prompts), out_shape=ja...  6.48 us
  transfers between devices with their start and end apart: 22, of which 13 were waited for; matrix products, arithmetic and copies ran while one was open for 1% of the time, Pallas kernels for 35%

profile of v4, /device:TPU:0, one launch (start us, length us, event | category | flops | bytes accessed | tf_op | source)
XLA Modules:
  0.0 134.7 jit_solution(2872076710883841346)
XLA Ops:
  1.8 3.1 %collective-permute-start = (bf16[64,1152]{1,0:T(8,128)(2,1)S(1)}, bf16[64,1152]{1,0:T(8,128)(2,1)S(1)}, u32[]{:S(2)}, u32[]{:S(2)}) collective-permute-start(bf16[64,1152]{1,0:T(8,128)(2,1)S(1)} %pad_maximum_fusion.2), channel_id=1, source_target_pairs={{0,4},{4,8},{8,12},{12,0},{1,5},{5,9},{9,13},{13,1},{2,6},{6,10},{... | collective-permute-start | bytes 442376 | tf_op jit(solution)/shard_map/ppermute | solution.py:26
  4.9 2.6 %collective-permute-start.1 = (bf16[64,1152]{1,0:T(8,128)(2,1)S(1)}, bf16[64,1152]{1,0:T(8,128)(2,1)S(1)}, u32[]{:S(2)}, u32[]{:S(2)}) collective-permute-start(bf16[64,1152]{1,0:T(8,128)(2,1)S(1)} %pad_maximum_fusion.2), channel_id=1, source_target_pairs={{0,8},{4,12},{8,0},{12,4},{1,9},{5,13},{9,1},{13,5},{2,10},{6,14},... | collective-permute-start | bytes 442376 | tf_op jit(solution)/shard_map/ppermute | solution.py:26
  8.9 2.8 %collective-permute-done.refs_0_ = bf16[64,1152]{1,0:T(8,128)(2,1)S(1)} collective-permute-done((bf16[64,1152]{1,0:T(8,128)(2,1)S(1)}, bf16[64,1152]{1,0:T(8,128)(2,1)S(1)}, u32[]{:S(2)}, u32[]{:S(2)}) %collective-permute-start) | collective-permute-done | bytes 147488 | tf_op jit(solution)/shard_map/ppermute | solution.py:26
  11.8 5.5 %collective-permute-done.1.refs_1_ = bf16[64,1152]{1,0:T(8,128)(2,1)S(1)} collective-permute-done((bf16[64,1152]{1,0:T(8,128)(2,1)S(1)}, bf16[64,1152]{1,0:T(8,128)(2,1)S(1)}, u32[]{:S(2)}, u32[]{:S(2)}) %collective-permute-start.1) | collective-permute-done | bytes 147488 | tf_op jit(solution)/shard_map/ppermute | solution.py:26
  17.3 2.7 %collective-permute-start.3 = (bf16[1024,256]{1,0:T(8,128)(2,1)S(1)}, bf16[1024,256]{1,0:T(8,128)(2,1)S(1)}, u32[]{:S(2)}, u32[]{:S(2)}) collective-permute-start(bf16[1024,256]{1,0:T(8,128)(2,1)S(1)} %constant_dynamic-slice_fusion), channel_id=1, source_target_pairs={{0,8},{4,12},{8,0},{12,4},{1,9},{5,13},{9,1},{13,5},{2,10},{6,14},... | collective-permute-start | bytes 1572872 | tf_op jit(solution)/shard_map/ppermute | solution.py:21
  24.2 5.2 %shard_map.127.refs_6_ = bf16[16,1024,384]{2,1,0:T(8,128)(2,1)S(1)} custom-call(s32[5]{0:T(128)S(1)} %pad_add_fusion.place, bf16[8,4096,384]{2,1,0:T(8,128)(2,1)} %refs_0_.7, bf16[8,4096,384]{2,1,0:T(8,128)(2,1)} %refs_1_.7, bf16[8,384,4096]{2,1,0:T(8,128)(2,1)} %w_down.5), custom_call_target="tpu_custom_call" | custom-call | tf_op jit(solution)/shard_map/pallas_call | solution.py:243
  29.4 5.5 %shard_map.128 = (bf16[16,1024,384]{2,1,0:T(8,128)(2,1)S(1)}, f32[8,256,768]{2,1,0:T(8,128)S(1)}, f32[256,32]{1,0:T(8,128)S(1)}) custom-call(s32[5]{0:T(128)S(1)} %pad_add_fusion.place, bf16[8,4096,384]{2,1,0:T(8,128)(2,1)} %refs_0_.7, bf16[8,4096,384]{2,1,0:T(8,128)(2,1)} %refs_1_.7, bf16[8,384,4096]{2,1,0:T(8,128)(2,1)} %w_down.5, ...), custom_call_target="tpu_custom_call" | custom-call | tf_op jit(solution)/shard_map/pallas_call | solution.py:243
  34.9 5.4 %collective-permute-done.7.refs_6_ = bf16[192,1024]{1,0:T(8,128)(2,1)S(1)} collective-permute-done((bf16[192,1024]{1,0:T(8,128)(2,1)S(1)}, bf16[192,1024]{1,0:T(8,128)(2,1)S(1)}, u32[]{:S(2)}, u32[]{:S(2)}) %collective-permute-start.7) | collective-permute-done | bytes 393248 | tf_op jit(solution)/shard_map/ppermute | solution.py:21
  40.3 10.6 %shard_map.129 = (bf16[8,1024,384]{2,1,0:T(8,128)(2,1)S(1)}, f32[8,256,768]{2,1,0:T(8,128)S(1)}, f32[256,32]{1,0:T(8,128)S(1)}) custom-call(s32[5]{0:T(128)S(1)} %pad_add_fusion.place, bf16[8,4096,384]{2,1,0:T(8,128)(2,1)} %refs_0_.7, bf16[8,4096,384]{2,1,0:T(8,128)(2,1)} %refs_1_.7, ...), custom_call_target="tpu_custom_call", output_to_operand_aliasing={{1}: (9, {}), {2}: (10, {})} | custom-call | tf_op jit(solution)/shard_map/pallas_call | solution.py:243
  50.9 6.2 %shard_map.130 = (bf16[8,384,1024]{2,1,0:T(8,128)(2,1)S(1)}, bf16[256,3072]{1,0:T(8,128)(2,1)S(1)}) custom-call(s32[5]{0:T(128)S(1)} %pad_add_fusion.place, bf16[8,4096,384]{2,1,0:T(8,128)(2,1)} %refs_0_.7, bf16[8,4096,384]{2,1,0:T(8,128)(2,1)} %refs_1_.7, bf16[8,384,4096]{2,1,0:T(8,128)(2,1)} %w_down.5, bf16[64,4096]{1,0:T(8,128)(2,1)S(1)} %bitcast.19, ...), custom_call_target="tpu_custom_call" | custom-call | tf_op jit(solution)/shard_map/pallas_call | solution.py:243
  57.2 1.7 %collective-permute-start.4 = (bf16[2048,256]{1,0:T(8,128)(2,1)S(1)}, bf16[2048,256]{1,0:T(8,128)(2,1)S(1)}, u32[]{:S(2)}, u32[]{:S(2)}) collective-permute-start(bf16[2048,256]{1,0:T(8,128)(2,1)S(1)} %pad_maximum_fusion.1), channel_id=1, source_target_pairs={{0,4},{4,0},{8,12},{12,8},{1,5},{5,1},{9,13},{13,9},{2,6},{6,2},{1... | collective-permute-start | bytes 3145736 | tf_op jit(solution)/shard_map/ppermute | solution.py:21
  58.9 4.5 %reduce.6 = bf16[256,1024]{1,0:T(8,128)(2,1)S(1)} custom-call(s32[5]{0:T(128)S(1)} %pad_add_fusion.place, bf16[256,3072]{1,0:T(8,128)(2,1)S(1)} %get-tuple-element.29.hidden, bf16[8,384,4096]{2,1,0:T(8,128)(2,1)} %w_down.5), custom_call_target="tpu_custom_call" | custom-call | flops 1610612736 | bytes 6291456 | tf_op jit(solution)/shard_map/reduce/pallas_call | solution.py:287
  63.4 1.8 %reduce.5 = bf16[256,1024]{1,0:T(8,128)(2,1)S(1)} custom-call(bf16[256,3072]{1,0:T(8,128)(2,1)S(1)} %get-tuple-element.29.hidden, bf16[8,384,1024]{2,1,0:T(8,128)(2,1)S(1)} %get-tuple-element.30.weight), custom_call_target="tpu_custom_call" | custom-call | tf_op jit(solution)/shard_map/reduce/pallas_call | solution.py:273
  65.2 4.5 %reduce.7 = bf16[256,1024]{1,0:T(8,128)(2,1)S(1)} custom-call(s32[5]{0:T(128)S(1)} %pad_add_fusion.place, bf16[256,3072]{1,0:T(8,128)(2,1)S(1)} %get-tuple-element.29.hidden, bf16[8,384,4096]{2,1,0:T(8,128)(2,1)} %w_down.5), custom_call_target="tpu_custom_call" | custom-call | flops 1610612736 | bytes 6291456 | tf_op jit(solution)/shard_map/reduce/pallas_call | solution.py:287
  69.6 1.6 %collective-permute-start.8 = (bf16[256,1024]{1,0:T(8,128)(2,1)S(1)}, bf16[256,1024]{1,0:T(8,128)(2,1)S(1)}, u32[]{:S(2)}, u32[]{:S(2)}) collective-permute-start(bf16[256,1024]{1,0:T(8,128)(2,1)S(1)} %reduce.5), channel_id=1, source_target_pairs={{0,3},{1,2},{2,1},{3,0},{4,7},{5,6},{6,5},{7,4},{8,11},{9,10},{10,... | collective-permute-start | bytes 1572872 | tf_op jit(solution)/shard_map/ppermute | solution.py:21
  71.3 1.9 %collective-permute-start.10 = (bf16[256,1024]{1,0:T(8,128)(2,1)S(1)}, bf16[256,1024]{1,0:T(8,128)(2,1)S(1)}, u32[]{:S(2)}, u32[]{:S(2)}) collective-permute-start(bf16[256,1024]{1,0:T(8,128)(2,1)S(1)} %reduce.7), channel_id=1, source_target_pairs={{0,1},{1,0},{2,3},{3,2},{4,5},{5,4},{6,7},{7,6},{8,9},{9,8},{10,11... | collective-permute-start | bytes 1572872 | tf_op jit(solution)/shard_map/ppermute | solution.py:21
  73.2 4.5 %reduce.4 = bf16[256,1024]{1,0:T(8,128)(2,1)S(1)} custom-call(s32[5]{0:T(128)S(1)} %pad_add_fusion.place, bf16[256,3072]{1,0:T(8,128)(2,1)S(1)} %get-tuple-element.29.hidden, bf16[8,384,4096]{2,1,0:T(8,128)(2,1)} %w_down.5), custom_call_target="tpu_custom_call" | custom-call | flops 1610612736 | bytes 6291456 | tf_op jit(solution)/shard_map/reduce/pallas_call | solution.py:287
  77.7 5.7 %collective-permute-done.8 = bf16[256,1024]{1,0:T(8,128)(2,1)S(1)} collective-permute-done((bf16[256,1024]{1,0:T(8,128)(2,1)S(1)}, bf16[256,1024]{1,0:T(8,128)(2,1)S(1)}, u32[]{:S(2)}, u32[]{:S(2)}) %collective-permute-start.8) | collective-permute-done | bytes 524320 | tf_op jit(solution)/shard_map/ppermute | solution.py:21
  83.4 5.5 %collective-permute-done.9 = bf16[256,1024]{1,0:T(8,128)(2,1)S(1)} collective-permute-done((bf16[256,1024]{1,0:T(8,128)(2,1)S(1)}, bf16[256,1024]{1,0:T(8,128)(2,1)S(1)}, u32[]{:S(2)}, u32[]{:S(2)}) %collective-permute-start.9) | collective-permute-done | bytes 524320 | tf_op jit(solution)/shard_map/ppermute | solution.py:21
  89.7 2.1 %collective-permute-start.11 = (bf16[64,1024]{1,0:T(8,128)(2,1)S(1)}, bf16[64,1024]{1,0:T(8,128)(2,1)S(1)}, u32[]{:S(2)}, u32[]{:S(2)}) collective-permute-start(bf16[64,1024]{1,0:T(8,128)(2,1)S(1)} %get-tuple-element.35), channel_id=1, source_target_pairs={{0,12},{4,0},{8,4},{12,8},{1,13},{5,1},{9,5},{13,9},{2,14},{6,2},{... | collective-permute-start | bytes 393224 | tf_op jit(solution)/shard_map/ppermute | solution.py:26
  92.2 1.9 %collective-permute-start.13 = (bf16[64,1024]{1,0:T(8,128)(2,1)S(1)}, bf16[64,1024]{1,0:T(8,128)(2,1)S(1)}, u32[]{:S(2)}, u32[]{:S(2)}) collective-permute-start(bf16[64,1024]{1,0:T(8,128)(2,1)S(1)} %get-tuple-element.36), channel_id=1, source_target_pairs={{0,4},{4,8},{8,12},{12,0},{1,5},{5,9},{9,13},{13,1},{2,6},{6,10},{... | collective-permute-start | bytes 393224 | tf_op jit(solution)/shard_map/ppermute | solution.py:26
  94.2 1.7 %collective-permute-done.11 = bf16[64,1024]{1,0:T(8,128)(2,1)S(1)} collective-permute-done((bf16[64,1024]{1,0:T(8,128)(2,1)S(1)}, bf16[64,1024]{1,0:T(8,128)(2,1)S(1)}, u32[]{:S(2)}, u32[]{:S(2)}) %collective-permute-start.11) | collective-permute-done | bytes 131104 | tf_op jit(solution)/shard_map/ppermute | solution.py:26
  95.9 8.9 %collective-permute-done.12 = bf16[64,1024]{1,0:T(8,128)(2,1)S(1)} collective-permute-done((bf16[64,1024]{1,0:T(8,128)(2,1)S(1)}, bf16[64,1024]{1,0:T(8,128)(2,1)S(1)}, u32[]{:S(2)}, u32[]{:S(2)}) %collective-permute-start.12) | collective-permute-done | bytes 131104 | tf_op jit(solution)/shard_map/ppermute | solution.py:26
  108.3 2.2 %collective-permute-done.14.refs_1_ = bf16[64,1024]{1,0:T(8,128)(2,1)S(1)} collective-permute-done((bf16[64,1024]{1,0:T(8,128)(2,1)S(1)}, bf16[64,1024]{1,0:T(8,128)(2,1)S(1)}, u32[]{:S(2)}, u32[]{:S(2)}) %collective-permute-start.14) | collective-permute-done | bytes 131104 | tf_op jit(solution)/shard_map/ppermute | solution.py:21
  110.6 3.6 %collective-permute-done.15.refs_2_ = bf16[64,1024]{1,0:T(8,128)(2,1)S(1)} collective-permute-done((bf16[64,1024]{1,0:T(8,128)(2,1)S(1)}, bf16[64,1024]{1,0:T(8,128)(2,1)S(1)}, u32[]{:S(2)}, u32[]{:S(2)}) %collective-permute-start.15) | collective-permute-done | bytes 131104 | tf_op jit(solution)/shard_map/ppermute | solution.py:21
  114.2 1.8 %project.1 = bf16[64,512]{1,0:T(8,128)(2,1)S(1)} custom-call(s32[5]{0:T(128)S(1)} %pad_add_fusion.place, bf16[64,4096]{1,0:T(8,128)(2,1)S(1)} %bitcast.20, bf16[64,1024]{1,0:T(8,128)(2,1)S(1)} %add_convert_fusion.1.refs_0_, bf16[64,1024]{1,0:T(8,128)(2,1)S(1)} %collective-permute-done.14.refs_1_, bf16[64,1024]{1,0:T(8,128)(2,1)S(1)} %collective-permute-done.15.refs_2_, ...), custom_call_target="tpu_custom_call" | custom-call | tf_op jit(solution)/shard_map/project/pallas_call | solution.py:338
  117.3 1.6 %attend.5 = bf16[64,2048]{1,0:T(8,128)(2,1)S(1)} custom-call(s32[5]{0:T(128)S(1)} %pad_add_fusion.place, bf16[64,512]{1,0:T(8,128)(2,1)S(1)} %collective-permute-done.18.block, bf16[256,512]{1,0:T(8,128)(2,1)S(1)} %bitcast.21, bf16[256,256]{1,0:T(8,128)(2,1)S(1)} %bitcast.28, bf16[256,256]{1,0:T(8,128)(2,1)S(1)} %bitcast.32, bf16[512,2048]{1,0:T(8,128)(2,1)S(1)} %copy-done.2), custom_call_target="tpu_custom_call" | custom-call | flops 268435456 | bytes 2097152 | tf_op jit(solution)/shard_map/attend/pallas_call | solution.py:412
  120.4 1.6 %attend.6 = bf16[64,2048]{1,0:T(8,128)(2,1)S(1)} custom-call(s32[5]{0:T(128)S(1)} %pad_add_fusion.place, bf16[64,512]{1,0:T(8,128)(2,1)S(1)} %collective-permute-done.18.block, bf16[256,512]{1,0:T(8,128)(2,1)S(1)} %bitcast.22, bf16[256,256]{1,0:T(8,128)(2,1)S(1)} %bitcast.29, bf16[256,256]{1,0:T(8,128)(2,1)S(1)} %bitcast.33, bf16[512,2048]{1,0:T(8,128)(2,1)S(1)} %copy-done.2), custom_call_target="tpu_custom_call" | custom-call | flops 268435456 | bytes 2097152 | tf_op jit(solution)/shard_map/attend/pallas_call | solution.py:412
  122.7 1.6 %attend.7 = bf16[64,2048]{1,0:T(8,128)(2,1)S(1)} custom-call(s32[5]{0:T(128)S(1)} %pad_add_fusion.place, bf16[64,512]{1,0:T(8,128)(2,1)S(1)} %collective-permute-done.18.block, bf16[256,512]{1,0:T(8,128)(2,1)S(1)} %bitcast.23, bf16[256,256]{1,0:T(8,128)(2,1)S(1)} %bitcast.30, bf16[256,256]{1,0:T(8,128)(2,1)S(1)} %bitcast.34, bf16[512,2048]{1,0:T(8,128)(2,1)S(1)} %copy-done.2), custom_call_target="tpu_custom_call" | custom-call | flops 268435456 | bytes 2097152 | tf_op jit(solution)/shard_map/attend/pallas_call | solution.py:412
  125.9 1.6 %attend.4 = bf16[64,2048]{1,0:T(8,128)(2,1)S(1)} custom-call(s32[5]{0:T(128)S(1)} %pad_add_fusion.place, bf16[64,512]{1,0:T(8,128)(2,1)S(1)} %collective-permute-done.18.block, bf16[256,512]{1,0:T(8,128)(2,1)S(1)} %bitcast.24, bf16[256,256]{1,0:T(8,128)(2,1)S(1)} %bitcast.31, bf16[256,256]{1,0:T(8,128)(2,1)S(1)} %bitcast.35, bf16[512,2048]{1,0:T(8,128)(2,1)S(1)} %copy-done.2), custom_call_target="tpu_custom_call" | custom-call | flops 268435456 | bytes 2097152 | tf_op jit(solution)/shard_map/attend/pallas_call | solution.py:412
  127.5 1.6 %collective-permute-done.19 = bf16[64,2048]{1,0:T(8,128)(2,1)S(1)} collective-permute-done((bf16[64,2048]{1,0:T(8,128)(2,1)S(1)}, bf16[64,2048]{1,0:T(8,128)(2,1)S(1)}, u32[]{:S(2)}, u32[]{:S(2)}) %collective-permute-start.19) | collective-permute-done | bytes 262176 | tf_op jit(solution)/shard_map/ppermute | solution.py:21
  129.1 4.8 %collective-permute-done.20 = bf16[64,2048]{1,0:T(8,128)(2,1)S(1)} collective-permute-done((bf16[64,2048]{1,0:T(8,128)(2,1)S(1)}, bf16[64,2048]{1,0:T(8,128)(2,1)S(1)}, u32[]{:S(2)}, u32[]{:S(2)}) %collective-permute-start.20) | collective-permute-done | bytes 262176 | tf_op jit(solution)/shard_map/ppermute | solution.py:21
  (58 shorter events, 18.2 us)
Async XLA Ops:
  0.0 8.9 %copy-start = (bf16[1024,512]{1,0:T(8,128)(2,1)S(1)}, bf16[1024,512]{1,0:T(8,128)(2,1)}, u32[]{:S(2)}) copy-start(bf16[1024,512]{1,0:T(8,128)(2,1)} %param.20) | copy-start | bytes 3145732
  1.8 9.9 %collective-permute-start = (bf16[64,1152]{1,0:T(8,128)(2,1)S(1)}, bf16[64,1152]{1,0:T(8,128)(2,1)S(1)}, u32[]{:S(2)}, u32[]{:S(2)}) collective-permute-start(bf16[64,1152]{1,0:T(8,128)(2,1)S(1)} %pad_maximum_fusion.2), channel_id=1, source_target_pairs={{0,4},{4,8},{8,12},{12,0},{1,5},{5,9},{9,13},{13,1},{2,6},{6,10},{... | collective-permute-start | bytes 442376 | tf_op jit(solution)/shard_map/ppermute | solution.py:26
  4.9 12.3 %collective-permute-start.1 = (bf16[64,1152]{1,0:T(8,128)(2,1)S(1)}, bf16[64,1152]{1,0:T(8,128)(2,1)S(1)}, u32[]{:S(2)}, u32[]{:S(2)}) collective-permute-start(bf16[64,1152]{1,0:T(8,128)(2,1)S(1)} %pad_maximum_fusion.2), channel_id=1, source_target_pairs={{0,8},{4,12},{8,0},{12,4},{1,9},{5,13},{9,1},{13,5},{2,10},{6,14},... | collective-permute-start | bytes 442376 | tf_op jit(solution)/shard_map/ppermute | solution.py:26
  7.5 9.7 %collective-permute-start.2 = (bf16[64,1152]{1,0:T(8,128)(2,1)S(1)}, bf16[64,1152]{1,0:T(8,128)(2,1)S(1)}, u32[]{:S(2)}, u32[]{:S(2)}) collective-permute-start(bf16[64,1152]{1,0:T(8,128)(2,1)S(1)} %pad_maximum_fusion.2), channel_id=1, source_target_pairs={{0,12},{4,0},{8,4},{12,8},{1,13},{5,1},{9,5},{13,9},{2,14},{6,2},{... | collective-permute-start | bytes 442376 | tf_op jit(solution)/shard_map/ppermute | solution.py:26
  17.3 39.9 %collective-permute-start.3 = (bf16[1024,256]{1,0:T(8,128)(2,1)S(1)}, bf16[1024,256]{1,0:T(8,128)(2,1)S(1)}, u32[]{:S(2)}, u32[]{:S(2)}) collective-permute-start(bf16[1024,256]{1,0:T(8,128)(2,1)S(1)} %constant_dynamic-slice_fusion), channel_id=1, source_target_pairs={{0,8},{4,12},{8,0},{12,4},{1,9},{5,13},{9,1},{13,5},{2,10},{6,14},... | collective-permute-start | bytes 1572872 | tf_op jit(solution)/shard_map/ppermute | solution.py:21
  19.9 14.9 %collective-permute-start.6 = (bf16[192,1024]{1,0:T(8,128)(2,1)S(1)}, bf16[192,1024]{1,0:T(8,128)(2,1)S(1)}, u32[]{:S(2)}, u32[]{:S(2)}) collective-permute-start(bf16[192,1024]{1,0:T(8,128)(2,1)S(1)} %get-tuple-element.21.refs_5_), channel_id=1, source_target_pairs={{0,1},{1,0},{2,3},{3,2},{4,5},{5,4},{6,7},{7,6},{8,9},{9,8},{10,11... | collective-permute-start | bytes 1179656 | tf_op jit(solution)/shard_map/ppermute | solution.py:21
  21.4 18.9 %collective-permute-start.7 = (bf16[192,1024]{1,0:T(8,128)(2,1)S(1)}, bf16[192,1024]{1,0:T(8,128)(2,1)S(1)}, u32[]{:S(2)}, u32[]{:S(2)}) collective-permute-start(bf16[192,1024]{1,0:T(8,128)(2,1)S(1)} %get-tuple-element.21.refs_5_), channel_id=1, source_target_pairs={{0,2},{1,3},{2,0},{3,1},{4,6},{5,7},{6,4},{7,5},{8,10},{9,11},{10,... | collective-permute-start | bytes 1179656 | tf_op jit(solution)/shard_map/ppermute | solution.py:21
  22.9 28.0 %collective-permute-start.5 = (bf16[192,1024]{1,0:T(8,128)(2,1)S(1)}, bf16[192,1024]{1,0:T(8,128)(2,1)S(1)}, u32[]{:S(2)}, u32[]{:S(2)}) collective-permute-start(bf16[192,1024]{1,0:T(8,128)(2,1)S(1)} %get-tuple-element.21.refs_5_), channel_id=1, source_target_pairs={{0,3},{1,2},{2,1},{3,0},{4,7},{5,6},{6,5},{7,4},{8,11},{9,10},{10,... | collective-permute-start | bytes 1179656 | tf_op jit(solution)/shard_map/ppermute | solution.py:21
  24.2 5.2 %copy-start.3 = (bf16[1,64,4096]{2,1,0:T(8,128)(2,1)S(1)}, bf16[1,64,4096]{2,1,0:T(8,128)(2,1)}, u32[]{:S(2)}) copy-start(bf16[1,64,4096]{2,1,0:T(8,128)(2,1)} %param.13) | copy-start | bytes 1572868
  24.2 5.2 %copy-start.5 = (bf16[4096,32]{0,1:T(8,128)(2,1)S(1)}, bf16[4096,32]{0,1:T(8,128)(2,1)}, u32[]{:S(2)}) copy-start(bf16[4096,32]{0,1:T(8,128)(2,1)} %param.15) | copy-start | bytes 786436
  57.2 32.2 %collective-permute-start.4 = (bf16[2048,256]{1,0:T(8,128)(2,1)S(1)}, bf16[2048,256]{1,0:T(8,128)(2,1)S(1)}, u32[]{:S(2)}, u32[]{:S(2)}) collective-permute-start(bf16[2048,256]{1,0:T(8,128)(2,1)S(1)} %pad_maximum_fusion.1), channel_id=1, source_target_pairs={{0,4},{4,0},{8,12},{12,8},{1,5},{5,1},{9,13},{13,9},{2,6},{6,2},{1... | collective-permute-start | bytes 3145736 | tf_op jit(solution)/shard_map/ppermute | solution.py:21
  69.6 13.7 %collective-permute-start.8 = (bf16[256,1024]{1,0:T(8,128)(2,1)S(1)}, bf16[256,1024]{1,0:T(8,128)(2,1)S(1)}, u32[]{:S(2)}, u32[]{:S(2)}) collective-permute-start(bf16[256,1024]{1,0:T(8,128)(2,1)S(1)} %reduce.5), channel_id=1, source_target_pairs={{0,3},{1,2},{2,1},{3,0},{4,7},{5,6},{6,5},{7,4},{8,11},{9,10},{10,... | collective-permute-start | bytes 1572872 | tf_op jit(solution)/shard_map/ppermute | solution.py:21
  71.2 17.6 %collective-permute-start.9 = (bf16[256,1024]{1,0:T(8,128)(2,1)S(1)}, bf16[256,1024]{1,0:T(8,128)(2,1)S(1)}, u32[]{:S(2)}, u32[]{:S(2)}) collective-permute-start(bf16[256,1024]{1,0:T(8,128)(2,1)S(1)} %reduce.6), channel_id=1, source_target_pairs={{0,2},{1,3},{2,0},{3,1},{4,6},{5,7},{6,4},{7,5},{8,10},{9,11},{10,... | collective-permute-start | bytes 1572872 | tf_op jit(solution)/shard_map/ppermute | solution.py:21
  71.3 17.7 %collective-permute-start.10 = (bf16[256,1024]{1,0:T(8,128)(2,1)S(1)}, bf16[256,1024]{1,0:T(8,128)(2,1)S(1)}, u32[]{:S(2)}, u32[]{:S(2)}) collective-permute-start(bf16[256,1024]{1,0:T(8,128)(2,1)S(1)} %reduce.7), channel_id=1, source_target_pairs={{0,1},{1,0},{2,3},{3,2},{4,5},{5,4},{6,7},{7,6},{8,9},{9,8},{10,11... | collective-permute-start | bytes 1572872 | tf_op jit(solution)/shard_map/ppermute | solution.py:21
  77.7 36.5 %copy-start.8 = (f32[4096]{0:T(1024)S(1)}, f32[4096]{0:T(1024)}, u32[]{:S(2)}) copy-start(f32[4096]{0:T(1024)} %param.19) | copy-start | bytes 49156
  89.6 27.7 %copy-start.2 = (bf16[512,2048]{1,0:T(8,128)(2,1)S(1)}, bf16[512,2048]{1,0:T(8,128)(2,1)}, u32[]{:S(2)}) copy-start(bf16[512,2048]{1,0:T(8,128)(2,1)} %w_out.7) | copy-start | bytes 6291460
  89.6 27.7 %copy-start.4 = (bf16[1,256,512]{2,1,0:T(8,128)(2,1)S(1)}, bf16[1,256,512]{2,1,0:T(8,128)(2,1)}, u32[]{:S(2)}) copy-start(bf16[1,256,512]{2,1,0:T(8,128)(2,1)} %param.22) | copy-start | bytes 786436
  89.6 27.7 %copy-start.6 = (bf16[1,256,256]{2,1,0:T(8,128)(2,1)S(1)}, bf16[1,256,256]{2,1,0:T(8,128)(2,1)}, u32[]{:S(2)}) copy-start(bf16[1,256,256]{2,1,0:T(8,128)(2,1)} %param.23) | copy-start | bytes 393220
  89.6 27.7 %copy-start.7 = (bf16[1,256,256]{2,1,0:T(8,128)(2,1)S(1)}, bf16[1,256,256]{2,1,0:T(8,128)(2,1)}, u32[]{:S(2)}) copy-start(bf16[1,256,256]{2,1,0:T(8,128)(2,1)} %param.24) | copy-start | bytes 393220
  89.6 24.6 %collective-permute-start.17 = (bf16[4096,256]{1,0:T(8,128)(2,1)S(1)}, bf16[4096,256]{1,0:T(8,128)(2,1)S(1)}, u32[]{:S(2)}, u32[]{:S(2)}) collective-permute-start(bf16[4096,256]{1,0:T(8,128)(2,1)S(1)} %pad_maximum_fusion.refs_5_), channel_id=1, source_target_pairs={{0,16},{16,0},{1,17},{17,1},{2,18},{18,2},{3,19},{19,3},{4,20},{20... | collective-permute-start | bytes 6291464 | tf_op jit(solution)/shard_map/ppermute | solution.py:21
  89.7 6.1 %collective-permute-start.11 = (bf16[64,1024]{1,0:T(8,128)(2,1)S(1)}, bf16[64,1024]{1,0:T(8,128)(2,1)S(1)}, u32[]{:S(2)}, u32[]{:S(2)}) collective-permute-start(bf16[64,1024]{1,0:T(8,128)(2,1)S(1)} %get-tuple-element.35), channel_id=1, source_target_pairs={{0,12},{4,0},{8,4},{12,8},{1,13},{5,1},{9,5},{13,9},{2,14},{6,2},{... | collective-permute-start | bytes 393224 | tf_op jit(solution)/shard_map/ppermute | solution.py:26
  91.9 12.8 %collective-permute-start.12 = (bf16[64,1024]{1,0:T(8,128)(2,1)S(1)}, bf16[64,1024]{1,0:T(8,128)(2,1)S(1)}, u32[]{:S(2)}, u32[]{:S(2)}) collective-permute-start(bf16[64,1024]{1,0:T(8,128)(2,1)S(1)} %get-tuple-element.37), channel_id=1, source_target_pairs={{0,8},{4,12},{8,0},{12,4},{1,9},{5,13},{9,1},{13,5},{2,10},{6,14},... | collective-permute-start | bytes 393224 | tf_op jit(solution)/shard_map/ppermute | solution.py:26
  92.2 12.5 %collective-permute-start.13 = (bf16[64,1024]{1,0:T(8,128)(2,1)S(1)}, bf16[64,1024]{1,0:T(8,128)(2,1)S(1)}, u32[]{:S(2)}, u32[]{:S(2)}) collective-permute-start(bf16[64,1024]{1,0:T(8,128)(2,1)S(1)} %get-tuple-element.36), channel_id=1, source_target_pairs={{0,4},{4,8},{8,12},{12,0},{1,5},{5,9},{9,13},{13,1},{2,6},{6,10},{... | collective-permute-start | bytes 393224 | tf_op jit(solution)/shard_map/ppermute | solution.py:26
  104.8 5.8 %collective-permute-start.14 = (bf16[64,1024]{1,0:T(8,128)(2,1)S(1)}, bf16[64,1024]{1,0:T(8,128)(2,1)S(1)}, u32[]{:S(2)}, u32[]{:S(2)}) collective-permute-start(bf16[64,1024]{1,0:T(8,128)(2,1)S(1)} %add_convert_fusion.1.refs_0_), channel_id=1, source_target_pairs={{0,1},{1,0},{2,3},{3,2},{4,5},{5,4},{6,7},{7,6},{8,9},{9,8},{10,11... | collective-permute-start | bytes 393224 | tf_op jit(solution)/shard_map/ppermute | solution.py:21
  106.3 7.8 %collective-permute-start.15 = (bf16[64,1024]{1,0:T(8,128)(2,1)S(1)}, bf16[64,1024]{1,0:T(8,128)(2,1)S(1)}, u32[]{:S(2)}, u32[]{:S(2)}) collective-permute-start(bf16[64,1024]{1,0:T(8,128)(2,1)S(1)} %add_convert_fusion.1.refs_0_), channel_id=1, source_target_pairs={{0,2},{1,3},{2,0},{3,1},{4,6},{5,7},{6,4},{7,5},{8,10},{9,11},{10,... | collective-permute-start | bytes 393224 | tf_op jit(solution)/shard_map/ppermute | solution.py:21
  107.0 7.2 %collective-permute-start.16 = (bf16[64,1024]{1,0:T(8,128)(2,1)S(1)}, bf16[64,1024]{1,0:T(8,128)(2,1)S(1)}, u32[]{:S(2)}, u32[]{:S(2)}) collective-permute-start(bf16[64,1024]{1,0:T(8,128)(2,1)S(1)} %add_convert_fusion.1.refs_0_), channel_id=1, source_target_pairs={{0,3},{1,2},{2,1},{3,0},{4,7},{5,6},{6,5},{7,4},{8,11},{9,10},{10,... | collective-permute-start | bytes 393224 | tf_op jit(solution)/shard_map/ppermute | solution.py:21
  116.0 1.3 collective-permute-start.18
  118.9 10.2 %collective-permute-start.19 = (bf16[64,2048]{1,0:T(8,128)(2,1)S(1)}, bf16[64,2048]{1,0:T(8,128)(2,1)S(1)}, u32[]{:S(2)}, u32[]{:S(2)}) collective-permute-start(bf16[64,2048]{1,0:T(8,128)(2,1)S(1)} %attend.5), channel_id=1, source_target_pairs={{0,3},{1,2},{2,1},{3,0},{4,7},{5,6},{6,5},{7,4},{8,11},{9,10},{10,... | collective-permute-start | bytes 786440 | tf_op jit(solution)/shard_map/ppermute | solution.py:21
  120.4 14.4 %copy-start.1 = (bf16[1024,512]{1,0:T(8,128)(2,1)S(1)}, bf16[1024,512]{1,0:T(8,128)(2,1)}, u32[]{:S(2)}) copy-start(bf16[1024,512]{1,0:T(8,128)(2,1)} %param.20) | copy-start | bytes 3145732
  122.0 11.9 %collective-permute-start.20 = (bf16[64,2048]{1,0:T(8,128)(2,1)S(1)}, bf16[64,2048]{1,0:T(8,128)(2,1)S(1)}, u32[]{:S(2)}, u32[]{:S(2)}) collective-permute-start(bf16[64,2048]{1,0:T(8,128)(2,1)S(1)} %attend.6), channel_id=1, source_target_pairs={{0,2},{1,3},{2,0},{3,1},{4,6},{5,7},{6,4},{7,5},{8,10},{9,11},{10,... | collective-permute-start | bytes 786440 | tf_op jit(solution)/shard_map/ppermute | solution.py:21
  124.3 9.5 %collective-permute-start.21 = (bf16[64,2048]{1,0:T(8,128)(2,1)S(1)}, bf16[64,2048]{1,0:T(8,128)(2,1)S(1)}, u32[]{:S(2)}, u32[]{:S(2)}) collective-permute-start(bf16[64,2048]{1,0:T(8,128)(2,1)S(1)} %attend.7), channel_id=1, source_target_pairs={{0,1},{1,0},{2,3},{3,2},{4,5},{5,4},{6,7},{7,6},{8,9},{9,8},{10,11... | collective-permute-start | bytes 786440 | tf_op jit(solution)/shard_map/ppermute | solution.py:21

commit v5 on v4

--- a/solution.py
+++ b/solution.py
@@ -110,6 +110,10 @@
     )(tags, *arrived)
 
 
+def streams_of(parts):
+    return [(k, low, high) for low, high, ks in parts for k, streamed in ks if streamed]
+
+
 def stage_kernel(items, quarters, parts, first, top, place, *refs):
     refs = list(refs)
 
@@ -119,10 +123,10 @@
         return taken
 
     sources, count = take(3), len(quarters)
-    streams = [part for part in parts if part[3]]
+    streams = streams_of(parts)
     if count:
         (own, router), nears = take(2), take(count)
-        held = take(len(parts) - len(streams))
+        held = take(sum(len(part[2]) for part in parts) - len(streams))
         totals = [None, None] if first else take(2)
         tags = take(1)[0] if top else None
     ahead = take(len(items))
@@ -133,7 +137,7 @@
     weights = take(1)[0] if top else None
     buffers, buffer_sems = take(len(streams)), take(len(streams))
 
-    for (k, low, high, _), buffer, sems in zip(streams, buffers, buffer_sems):
+    for (k, low, high), buffer, sems in zip(streams, buffers, buffer_sems):
         for e in range(low, high):
             for copy in expert_copies(place, sources, k, low, e, buffer, sems):
                 copy.start()
@@ -167,24 +171,33 @@
         else:
             logits_out[...] = logits
         experts, (_, _, units) = sources[0].shape[0], sources[0].shape
-        width = nears[0].shape[1]
         held, buffers, buffer_sems = list(held), list(buffers), list(buffer_sems)
-        for n, (k, low, high, streamed) in enumerate(parts):
-            weight = buffers.pop(0) if streamed else held.pop(0)
-            sems = buffer_sems.pop(0) if streamed else None
-            at = quarters.index(k) * width
-            begun = any(k != part[0] for part in parts[:n])
-
-            def body(e, carry, k=k, low=low, weight=weight, sems=sems, at=at, begun=begun):
-                if sems is not None:
-                    for copy in expert_copies(place, sources, k, low, e, weight, sems):
-                        copy.wait()
-                half = weight.shape[0] // 2
-                both = jnp.concatenate([weight[e - low], weight[half + e - low]], axis=1)
-                value = jnp.dot(rows[:, at : at + width], both, preferred_element_type=F32)
-                if begun:
-                    value += out[e]
-                elif not first:
+        for n, (low, high, ks) in enumerate(parts):
+            sources_of = [
+                (k, buffers.pop(0), buffer_sems.pop(0)) if streamed else (k, held.pop(0), None)
+                for k, streamed in ks
+            ]
+
+            def body(e, carry, n=n, low=low, high=high, sources_of=sources_of):
+                both = []
+                for k, weight, sems in sources_of:
+                    if sems is not None:
+                        for copy in expert_copies(place, sources, k, low, e, weight, sems):
+                            copy.wait()
+                    half = weight.shape[0] // 2
+                    both.append(
+                        jnp.concatenate([weight[e - low], weight[half + e - low]], axis=1)
+                    )
+                if streams and n == 0:
+
+                    @pl.when(e == (low + high) // 2)
+                    def _():
+                        for copy in copies:
+                            copy.start()
+
+                both = jnp.concatenate(both, axis=0)
+                value = jnp.dot(rows[...], both, preferred_element_type=F32)
+                if not first:
                     value += totals[0][e]
                 if not top:
                     out[e] = value
@@ -197,10 +210,7 @@
                 ).astype(BF16)
                 return carry
 
-            lax.fori_loop(low, high, body, 0)
-            if streams and n == 0:
-                for copy in copies:
-                    copy.start()
+            lax.fori_loop(low, high, body, 0, unroll=math.gcd(2, high - low))
     for copy in copies:
         copy.wait()
 
@@ -220,11 +230,11 @@
         for item in items
     ]
     scratch, aliases, tokens = [pltpu.SemaphoreType.DMA((max(1, len(items)), 2))], {}, 0
-    streams = [part for part in parts if part[3]]
+    streams = streams_of(parts)
     mebibytes = 1
     if count:
         tokens = own.shape[0] + nears[quarters[0]].shape[0]
-        mebibytes = 4 + -(-sum(4 * width * units * (p[2] - p[1]) for p in streams) >> 20)
+        mebibytes = 8 + -(-sum(4 * width * units * (p[2] - p[1]) for p in streams) >> 20)
         operands += [own, router] + [in_vmem(nears[k]) for k in quarters]
         operands += [in_vmem(array) for array in held]
         aliases = {1 + len(operands) + i: len(items) + i for i in range(len(totals))}
@@ -475,31 +485,27 @@
     near, all_tags = unpack(tags, arrived, width)
     far = order[::-1]
     others = {k: swap(near, "half", k) for k in order[:-1]}
-    others[order[-1]] = swap(near, "half", order[-1])
-    mine, near = lax.optimization_barrier(
-        (lax.dynamic_slice_in_dim(w_kv, pool * narrow, narrow, axis=1), near)
-    )
+    again, others = lax.optimization_barrier((near, others))
+    others[order[-1]] = swap(again, "half", order[-1])
+    mine = lax.dynamic_slice_in_dim(w_kv, pool * narrow, narrow, axis=1)
     others[0] = near
-    origins = [0]
-    for i in range(eps.bit_length() - 1):
-        bit = eps >> i + 1
-        mine = jnp.concatenate([mine, swap(mine, "ep", bit)], axis=0)
-        origins += [origin ^ bit for origin in origins]
-
+    bits = [eps >> i + 1 for i in range(eps.bit_length() - 1)]
+    received = swap(mine, "ep", bits[0])
+    origins = [0, bits[0]]
     got, totals = stage(
         place, sources, [(PAIR, beside[0], 0, experts)], own, router.T, {0: others[0]},
-        [(0, 0, experts, False)], got,
+        [(0, experts, [(0, False)])], got,
     )
     early = experts // 2
     got, totals = stage(
         place, sources, [(PAIR, last, 0, early)] if early else [], own, router.T,
         {k: others[k] for k in beside},
-        [(k, 0, experts, k != beside[0]) for k in beside], got, totals,
-    )
-    pieces = [(last, 0, early, False)] if early else []
+        [(0, experts, [(k, k != beside[0]) for k in beside])], got, totals,
+    )
+    pieces = [(0, early, [(last, False)])] if early else []
     got, (hidden,) = stage(
         place, sources, [(DOWN, far[0])], own, router.T, {last: others[last]},
-        pieces + [(last, early, experts, True)], got, totals, all_tags, top,
+        pieces + [(early, experts, [(last, True)])], got, totals, all_tags, top,
     )
     ahead = {far[0]: got[0]}
     partial = {}
@@ -508,6 +514,11 @@
             partial[k] = reduce_ahead(hidden, ahead[k])
         else:
             partial[k] = reduce(k, place, hidden, w_down, width, width // 2)
+    received, partial[far[1]] = lax.optimization_barrier((received, partial[far[1]]))
+    mine = jnp.concatenate([mine, received], axis=0)
+    for bit in bits[1:]:
+        mine = jnp.concatenate([mine, swap(mine, "ep", bit)], axis=0)
+        origins += [origin ^ bit for origin in origins]
     gathered = []
     for k in far:
         gathered.append(swap(partial[k], "half", k))

time: 135 us -> 142 us (1.052)
  waiting for transfers between devices: 49.1 us -> 52.7 us
  Pallas kernels: 51 us -> 53.4 us
  starting transfers between devices: 30.2 us -> 31.7 us
    ppermute x16, waiting for transfers between devices: 30.2 us -> 33.8 us  [swap(): lax.ppermute(shard, axis, [(i, i ^ bits) for i in range(lax.axis_size(axi...]
    pallas_call x4, Pallas kernels: 27.4 us -> 29.9 us  [stage(): pl.pallas_call(functools.partial(stage_kernel, items, quarters, parts, no...]
where the time goes in v5:
time: 142 us
  Pallas kernels  53.4 us (38%)
  waiting for transfers between devices  52.7 us (37%)
  starting transfers between devices  31.7 us (22%)
  local copies, waits for them, and re-layouts  2.55 us (2%)
  other arithmetic  1.61 us (1%)
    ppermute x16, waiting for transfers between devices, swap(): lax.ppermute(shard, axis, [(i, i ^ bits) for i in range(lax.axis_size(axi...  33.8 us
    pallas_call x4, Pallas kernels, stage(): pl.pallas_call(functools.partial(stage_kernel, items, quarters, parts, no...  29.9 us
    ppermute x16, starting transfers between devices, swap(): lax.ppermute(shard, axis, [(i, i ^ bits) for i in range(lax.axis_size(axi...  20 us
    ppermute x6, waiting for transfers between devices, shift(): lax.ppermute(shard, axis, [(i, (i + distance) % count) for i in range(cou...  18.9 us
    pallas_call x3, Pallas kernels, reduce(): pl.pallas_call(reduce_kernel, out_shape=jax.ShapeDtypeStruct((tokens, wid...  13.5 us
    ppermute x6, starting transfers between devices, shift(): lax.ppermute(shard, axis, [(i, (i + distance) % count) for i in range(cou...  11.7 us
    pallas_call x4, Pallas kernels, attend(): pl.pallas_call(functools.partial(attend_kernel, k, prompts), out_shape=ja...  6.48 us
  transfers between devices with their start and end apart: 22, of which 13 were waited for; matrix products, arithmetic and copies ran while one was open for 1% of the time, Pallas kernels for 35%

profile of v5, /device:TPU:0, one launch (start us, length us, event | category | flops | bytes accessed | tf_op | source)
XLA Modules:
  0.0 142.2 jit_solution(7930162343695002454)
XLA Ops:
  1.8 3.1 %collective-permute-start.1 = (bf16[64,1152]{1,0:T(8,128)(2,1)S(1)}, bf16[64,1152]{1,0:T(8,128)(2,1)S(1)}, u32[]{:S(2)}, u32[]{:S(2)}) collective-permute-start(bf16[64,1152]{1,0:T(8,128)(2,1)S(1)} %pad_maximum_fusion.2), channel_id=1, source_target_pairs={{0,4},{4,8},{8,12},{12,0},{1,5},{5,9},{9,13},{13,1},{2,6},{6,10},{... | collective-permute-start | bytes 442376 | tf_op jit(solution)/shard_map/ppermute | solution.py:26
  4.9 2.6 %collective-permute-start.2 = (bf16[64,1152]{1,0:T(8,128)(2,1)S(1)}, bf16[64,1152]{1,0:T(8,128)(2,1)S(1)}, u32[]{:S(2)}, u32[]{:S(2)}) collective-permute-start(bf16[64,1152]{1,0:T(8,128)(2,1)S(1)} %pad_maximum_fusion.2), channel_id=1, source_target_pairs={{0,8},{4,12},{8,0},{12,4},{1,9},{5,13},{9,1},{13,5},{2,10},{6,14},... | collective-permute-start | bytes 442376 | tf_op jit(solution)/shard_map/ppermute | solution.py:26
  8.9 2.9 %collective-permute-done.1.refs_0_ = bf16[64,1152]{1,0:T(8,128)(2,1)S(1)} collective-permute-done((bf16[64,1152]{1,0:T(8,128)(2,1)S(1)}, bf16[64,1152]{1,0:T(8,128)(2,1)S(1)}, u32[]{:S(2)}, u32[]{:S(2)}) %collective-permute-start.1) | collective-permute-done | bytes 147488 | tf_op jit(solution)/shard_map/ppermute | solution.py:26
  11.8 5.5 %collective-permute-done.2.refs_1_ = bf16[64,1152]{1,0:T(8,128)(2,1)S(1)} collective-permute-done((bf16[64,1152]{1,0:T(8,128)(2,1)S(1)}, bf16[64,1152]{1,0:T(8,128)(2,1)S(1)}, u32[]{:S(2)}, u32[]{:S(2)}) %collective-permute-start.2) | collective-permute-done | bytes 147488 | tf_op jit(solution)/shard_map/ppermute | solution.py:26
  17.3 1.6 %collective-permute-start.4 = (bf16[192,1024]{1,0:T(8,128)(2,1)S(1)}, bf16[192,1024]{1,0:T(8,128)(2,1)S(1)}, u32[]{:S(2)}, u32[]{:S(2)}) collective-permute-start(bf16[192,1024]{1,0:T(8,128)(2,1)S(1)} %get-tuple-element.23.refs_5_), channel_id=1, source_target_pairs={{0,1},{1,0},{2,3},{3,2},{4,5},{5,4},{6,7},{7,6},{8,9},{9,8},{10,11... | collective-permute-start | bytes 1179656 | tf_op jit(solution)/shard_map/ppermute | solution.py:21
  20.3 7.9 %collective-permute-done.4.refs_5_ = bf16[192,1024]{1,0:T(8,128)(2,1)S(1)} collective-permute-done((bf16[192,1024]{1,0:T(8,128)(2,1)S(1)}, bf16[192,1024]{1,0:T(8,128)(2,1)S(1)}, u32[]{:S(2)}, u32[]{:S(2)}) %collective-permute-start.4) | collective-permute-done | bytes 393248 | tf_op jit(solution)/shard_map/ppermute | solution.py:21
  31.0 2.8 %collective-permute-start = (bf16[1024,256]{1,0:T(8,128)(2,1)S(1)}, bf16[1024,256]{1,0:T(8,128)(2,1)S(1)}, u32[]{:S(2)}, u32[]{:S(2)}) collective-permute-start(bf16[1024,256]{1,0:T(8,128)(2,1)S(1)} %constant_dynamic-slice_fusion), channel_id=1, source_target_pairs={{0,8},{4,12},{8,0},{12,4},{1,9},{5,13},{9,1},{13,5},{2,10},{6,14},... | collective-permute-start | bytes 1572872 | tf_op jit(solution)/shard_map/ppermute | solution.py:21
  34.5 5.2 %shard_map.127.refs_6_ = bf16[16,1024,384]{2,1,0:T(8,128)(2,1)S(1)} custom-call(s32[5]{0:T(128)S(1)} %pad_add_fusion.place, bf16[8,4096,384]{2,1,0:T(8,128)(2,1)} %refs_0_.7, bf16[8,4096,384]{2,1,0:T(8,128)(2,1)} %refs_1_.7, bf16[8,384,4096]{2,1,0:T(8,128)(2,1)} %w_down.5), custom_call_target="tpu_custom_call" | custom-call | tf_op jit(solution)/shard_map/pallas_call | solution.py:253
  39.7 5.3 %shard_map.128 = (bf16[16,1024,384]{2,1,0:T(8,128)(2,1)S(1)}, f32[8,256,768]{2,1,0:T(8,128)S(1)}, f32[256,32]{1,0:T(8,128)S(1)}) custom-call(s32[5]{0:T(128)S(1)} %pad_add_fusion.place, bf16[8,4096,384]{2,1,0:T(8,128)(2,1)} %refs_0_.7, bf16[8,4096,384]{2,1,0:T(8,128)(2,1)} %refs_1_.7, bf16[8,384,4096]{2,1,0:T(8,128)(2,1)} %w_down.5, ...), custom_call_target="tpu_custom_call" | custom-call | tf_op jit(solution)/shard_map/pallas_call | solution.py:253
  45.1 13.0 %shard_map.129 = (bf16[8,1024,384]{2,1,0:T(8,128)(2,1)S(1)}, f32[8,256,768]{2,1,0:T(8,128)S(1)}, f32[256,32]{1,0:T(8,128)S(1)}) custom-call(s32[5]{0:T(128)S(1)} %pad_add_fusion.place, bf16[8,4096,384]{2,1,0:T(8,128)(2,1)} %refs_0_.7, bf16[8,4096,384]{2,1,0:T(8,128)(2,1)} %refs_1_.7, ...), custom_call_target="tpu_custom_call", output_to_operand_aliasing={{1}: (9, {}), {2}: (10, {})} | custom-call | tf_op jit(solution)/shard_map/pallas_call | solution.py:253
  58.1 6.3 %shard_map.130 = (bf16[8,384,1024]{2,1,0:T(8,128)(2,1)S(1)}, bf16[256,3072]{1,0:T(8,128)(2,1)S(1)}) custom-call(s32[5]{0:T(128)S(1)} %pad_add_fusion.place, bf16[8,4096,384]{2,1,0:T(8,128)(2,1)} %refs_0_.7, bf16[8,4096,384]{2,1,0:T(8,128)(2,1)} %refs_1_.7, bf16[8,384,4096]{2,1,0:T(8,128)(2,1)} %w_down.5, bf16[64,4096]{1,0:T(8,128)(2,1)S(1)} %bitcast.19, ...), custom_call_target="tpu_custom_call" | custom-call | tf_op jit(solution)/shard_map/pallas_call | solution.py:253
  64.4 4.5 %reduce.4 = bf16[256,1024]{1,0:T(8,128)(2,1)S(1)} custom-call(s32[5]{0:T(128)S(1)} %pad_add_fusion.place, bf16[256,3072]{1,0:T(8,128)(2,1)S(1)} %get-tuple-element.33.hidden, bf16[8,384,4096]{2,1,0:T(8,128)(2,1)} %w_down.5), custom_call_target="tpu_custom_call" | custom-call | flops 1610612736 | bytes 6291456 | tf_op jit(solution)/shard_map/reduce/pallas_call | solution.py:297
  69.0 1.7 %collective-permute-start.7 = (bf16[2048,256]{1,0:T(8,128)(2,1)S(1)}, bf16[2048,256]{1,0:T(8,128)(2,1)S(1)}, u32[]{:S(2)}, u32[]{:S(2)}) collective-permute-start(bf16[2048,256]{1,0:T(8,128)(2,1)S(1)} %pad_maximum_fusion.1), channel_id=1, source_target_pairs={{0,4},{4,0},{8,12},{12,8},{1,5},{5,1},{9,13},{13,9},{2,6},{6,2},{1... | collective-permute-start | bytes 3145736 | tf_op jit(solution)/shard_map/ppermute | solution.py:21
  70.7 1.8 %reduce.6 = bf16[256,1024]{1,0:T(8,128)(2,1)S(1)} custom-call(bf16[256,3072]{1,0:T(8,128)(2,1)S(1)} %get-tuple-element.33.hidden, bf16[8,384,1024]{2,1,0:T(8,128)(2,1)S(1)} %get-tuple-element.35.weight), custom_call_target="tpu_custom_call" | custom-call | tf_op jit(solution)/shard_map/reduce/pallas_call | solution.py:283
  73.9 4.5 %reduce.7 = bf16[256,1024]{1,0:T(8,128)(2,1)S(1)} custom-call(s32[5]{0:T(128)S(1)} %pad_add_fusion.place, bf16[256,3072]{1,0:T(8,128)(2,1)S(1)} %get-tuple-element.33.hidden, bf16[8,384,4096]{2,1,0:T(8,128)(2,1)} %w_down.5), custom_call_target="tpu_custom_call" | custom-call | flops 1610612736 | bytes 6291456 | tf_op jit(solution)/shard_map/reduce/pallas_call | solution.py:297
  78.4 1.7 %collective-permute-start.9 = (bf16[256,1024]{1,0:T(8,128)(2,1)S(1)}, bf16[256,1024]{1,0:T(8,128)(2,1)S(1)}, u32[]{:S(2)}, u32[]{:S(2)}) collective-permute-start(bf16[256,1024]{1,0:T(8,128)(2,1)S(1)} %reduce.4), channel_id=1, source_target_pairs={{0,2},{1,3},{2,0},{3,1},{4,6},{5,7},{6,4},{7,5},{8,10},{9,11},{10,... | collective-permute-start | bytes 1572872 | tf_op jit(solution)/shard_map/ppermute | solution.py:21
  80.6 4.5 %reduce.5 = bf16[256,1024]{1,0:T(8,128)(2,1)S(1)} custom-call(s32[5]{0:T(128)S(1)} %pad_add_fusion.place, bf16[256,3072]{1,0:T(8,128)(2,1)S(1)} %get-tuple-element.33.hidden, bf16[8,384,4096]{2,1,0:T(8,128)(2,1)} %w_down.5), custom_call_target="tpu_custom_call" | custom-call | flops 1610612736 | bytes 6291456 | tf_op jit(solution)/shard_map/reduce/pallas_call | solution.py:297
  85.1 3.2 %collective-permute-done.8 = bf16[256,1024]{1,0:T(8,128)(2,1)S(1)} collective-permute-done((bf16[256,1024]{1,0:T(8,128)(2,1)S(1)}, bf16[256,1024]{1,0:T(8,128)(2,1)S(1)}, u32[]{:S(2)}, u32[]{:S(2)}) %collective-permute-start.8) | collective-permute-done | bytes 524320 | tf_op jit(solution)/shard_map/ppermute | solution.py:21
  88.3 8.0 %collective-permute-done.9 = bf16[256,1024]{1,0:T(8,128)(2,1)S(1)} collective-permute-done((bf16[256,1024]{1,0:T(8,128)(2,1)S(1)}, bf16[256,1024]{1,0:T(8,128)(2,1)S(1)}, u32[]{:S(2)}, u32[]{:S(2)}) %collective-permute-start.9) | collective-permute-done | bytes 524320 | tf_op jit(solution)/shard_map/ppermute | solution.py:21
  97.0 2.4 %collective-permute-start.11 = (bf16[64,1024]{1,0:T(8,128)(2,1)S(1)}, bf16[64,1024]{1,0:T(8,128)(2,1)S(1)}, u32[]{:S(2)}, u32[]{:S(2)}) collective-permute-start(bf16[64,1024]{1,0:T(8,128)(2,1)S(1)} %get-tuple-element.41), channel_id=1, source_target_pairs={{0,12},{4,0},{8,4},{12,8},{1,13},{5,1},{9,5},{13,9},{2,14},{6,2},{... | collective-permute-start | bytes 393224 | tf_op jit(solution)/shard_map/ppermute | solution.py:26
  99.7 1.9 %collective-permute-start.13 = (bf16[64,1024]{1,0:T(8,128)(2,1)S(1)}, bf16[64,1024]{1,0:T(8,128)(2,1)S(1)}, u32[]{:S(2)}, u32[]{:S(2)}) collective-permute-start(bf16[64,1024]{1,0:T(8,128)(2,1)S(1)} %get-tuple-element.42), channel_id=1, source_target_pairs={{0,4},{4,8},{8,12},{12,0},{1,5},{5,9},{9,13},{13,1},{2,6},{6,10},{... | collective-permute-start | bytes 393224 | tf_op jit(solution)/shard_map/ppermute | solution.py:26
  101.7 1.7 %collective-permute-done.11 = bf16[64,1024]{1,0:T(8,128)(2,1)S(1)} collective-permute-done((bf16[64,1024]{1,0:T(8,128)(2,1)S(1)}, bf16[64,1024]{1,0:T(8,128)(2,1)S(1)}, u32[]{:S(2)}, u32[]{:S(2)}) %collective-permute-start.11) | collective-permute-done | bytes 131104 | tf_op jit(solution)/shard_map/ppermute | solution.py:26
  103.4 8.9 %collective-permute-done.12 = bf16[64,1024]{1,0:T(8,128)(2,1)S(1)} collective-permute-done((bf16[64,1024]{1,0:T(8,128)(2,1)S(1)}, bf16[64,1024]{1,0:T(8,128)(2,1)S(1)}, u32[]{:S(2)}, u32[]{:S(2)}) %collective-permute-start.12) | collective-permute-done | bytes 131104 | tf_op jit(solution)/shard_map/ppermute | solution.py:26
  115.9 2.2 %collective-permute-done.14.refs_1_ = bf16[64,1024]{1,0:T(8,128)(2,1)S(1)} collective-permute-done((bf16[64,1024]{1,0:T(8,128)(2,1)S(1)}, bf16[64,1024]{1,0:T(8,128)(2,1)S(1)}, u32[]{:S(2)}, u32[]{:S(2)}) %collective-permute-start.14) | collective-permute-done | bytes 131104 | tf_op jit(solution)/shard_map/ppermute | solution.py:21
  118.1 3.6 %collective-permute-done.15.refs_2_ = bf16[64,1024]{1,0:T(8,128)(2,1)S(1)} collective-permute-done((bf16[64,1024]{1,0:T(8,128)(2,1)S(1)}, bf16[64,1024]{1,0:T(8,128)(2,1)S(1)}, u32[]{:S(2)}, u32[]{:S(2)}) %collective-permute-start.15) | collective-permute-done | bytes 131104 | tf_op jit(solution)/shard_map/ppermute | solution.py:21
  121.7 1.8 %project.1 = bf16[64,512]{1,0:T(8,128)(2,1)S(1)} custom-call(s32[5]{0:T(128)S(1)} %pad_add_fusion.place, bf16[64,4096]{1,0:T(8,128)(2,1)S(1)} %bitcast.20, bf16[64,1024]{1,0:T(8,128)(2,1)S(1)} %add_convert_fusion.1.refs_0_, bf16[64,1024]{1,0:T(8,128)(2,1)S(1)} %collective-permute-done.14.refs_1_, bf16[64,1024]{1,0:T(8,128)(2,1)S(1)} %collective-permute-done.15.refs_2_, ...), custom_call_target="tpu_custom_call" | custom-call | tf_op jit(solution)/shard_map/project/pallas_call | solution.py:348
  124.8 1.6 %attend.5 = bf16[64,2048]{1,0:T(8,128)(2,1)S(1)} custom-call(s32[5]{0:T(128)S(1)} %pad_add_fusion.place, bf16[64,512]{1,0:T(8,128)(2,1)S(1)} %collective-permute-done.18.block, bf16[256,512]{1,0:T(8,128)(2,1)S(1)} %bitcast.21, bf16[256,256]{1,0:T(8,128)(2,1)S(1)} %bitcast.28, bf16[256,256]{1,0:T(8,128)(2,1)S(1)} %bitcast.32, bf16[512,2048]{1,0:T(8,128)(2,1)S(1)} %copy-done.2), custom_call_target="tpu_custom_call" | custom-call | flops 268435456 | bytes 2097152 | tf_op jit(solution)/shard_map/attend/pallas_call | solution.py:422
  127.7 1.6 %attend.6 = bf16[64,2048]{1,0:T(8,128)(2,1)S(1)} custom-call(s32[5]{0:T(128)S(1)} %pad_add_fusion.place, bf16[64,512]{1,0:T(8,128)(2,1)S(1)} %collective-permute-done.18.block, bf16[256,512]{1,0:T(8,128)(2,1)S(1)} %bitcast.22, bf16[256,256]{1,0:T(8,128)(2,1)S(1)} %bitcast.29, bf16[256,256]{1,0:T(8,128)(2,1)S(1)} %bitcast.33, bf16[512,2048]{1,0:T(8,128)(2,1)S(1)} %copy-done.2), custom_call_target="tpu_custom_call" | custom-call | flops 268435456 | bytes 2097152 | tf_op jit(solution)/shard_map/attend/pallas_call | solution.py:422
  130.2 1.6 %attend.7 = bf16[64,2048]{1,0:T(8,128)(2,1)S(1)} custom-call(s32[5]{0:T(128)S(1)} %pad_add_fusion.place, bf16[64,512]{1,0:T(8,128)(2,1)S(1)} %collective-permute-done.18.block, bf16[256,512]{1,0:T(8,128)(2,1)S(1)} %bitcast.23, bf16[256,256]{1,0:T(8,128)(2,1)S(1)} %bitcast.30, bf16[256,256]{1,0:T(8,128)(2,1)S(1)} %bitcast.34, bf16[512,2048]{1,0:T(8,128)(2,1)S(1)} %copy-done.2), custom_call_target="tpu_custom_call" | custom-call | flops 268435456 | bytes 2097152 | tf_op jit(solution)/shard_map/attend/pallas_call | solution.py:422
  133.4 1.6 %attend.4 = bf16[64,2048]{1,0:T(8,128)(2,1)S(1)} custom-call(s32[5]{0:T(128)S(1)} %pad_add_fusion.place, bf16[64,512]{1,0:T(8,128)(2,1)S(1)} %collective-permute-done.18.block, bf16[256,512]{1,0:T(8,128)(2,1)S(1)} %bitcast.24, bf16[256,256]{1,0:T(8,128)(2,1)S(1)} %bitcast.31, bf16[256,256]{1,0:T(8,128)(2,1)S(1)} %bitcast.35, bf16[512,2048]{1,0:T(8,128)(2,1)S(1)} %copy-done.2), custom_call_target="tpu_custom_call" | custom-call | flops 268435456 | bytes 2097152 | tf_op jit(solution)/shard_map/attend/pallas_call | solution.py:422
  135.0 1.6 %collective-permute-done.19 = bf16[64,2048]{1,0:T(8,128)(2,1)S(1)} collective-permute-done((bf16[64,2048]{1,0:T(8,128)(2,1)S(1)}, bf16[64,2048]{1,0:T(8,128)(2,1)S(1)}, u32[]{:S(2)}, u32[]{:S(2)}) %collective-permute-start.19) | collective-permute-done | bytes 262176 | tf_op jit(solution)/shard_map/ppermute | solution.py:21
  136.6 4.8 %collective-permute-done.20 = bf16[64,2048]{1,0:T(8,128)(2,1)S(1)} collective-permute-done((bf16[64,2048]{1,0:T(8,128)(2,1)S(1)}, bf16[64,2048]{1,0:T(8,128)(2,1)S(1)}, u32[]{:S(2)}, u32[]{:S(2)}) %collective-permute-start.20) | collective-permute-done | bytes 262176 | tf_op jit(solution)/shard_map/ppermute | solution.py:21
  (58 shorter events, 20.7 us)
Async XLA Ops:
  0.0 31.0 %copy-start = (bf16[1024,512]{1,0:T(8,128)(2,1)S(1)}, bf16[1024,512]{1,0:T(8,128)(2,1)}, u32[]{:S(2)}) copy-start(bf16[1024,512]{1,0:T(8,128)(2,1)} %param.20) | copy-start | bytes 3145732
  1.8 9.9 %collective-permute-start.1 = (bf16[64,1152]{1,0:T(8,128)(2,1)S(1)}, bf16[64,1152]{1,0:T(8,128)(2,1)S(1)}, u32[]{:S(2)}, u32[]{:S(2)}) collective-permute-start(bf16[64,1152]{1,0:T(8,128)(2,1)S(1)} %pad_maximum_fusion.2), channel_id=1, source_target_pairs={{0,4},{4,8},{8,12},{12,0},{1,5},{5,9},{9,13},{13,1},{2,6},{6,10},{... | collective-permute-start | bytes 442376 | tf_op jit(solution)/shard_map/ppermute | solution.py:26
  4.9 12.3 %collective-permute-start.2 = (bf16[64,1152]{1,0:T(8,128)(2,1)S(1)}, bf16[64,1152]{1,0:T(8,128)(2,1)S(1)}, u32[]{:S(2)}, u32[]{:S(2)}) collective-permute-start(bf16[64,1152]{1,0:T(8,128)(2,1)S(1)} %pad_maximum_fusion.2), channel_id=1, source_target_pairs={{0,8},{4,12},{8,0},{12,4},{1,9},{5,13},{9,1},{13,5},{2,10},{6,14},... | collective-permute-start | bytes 442376 | tf_op jit(solution)/shard_map/ppermute | solution.py:26
  7.5 9.7 %collective-permute-start.3 = (bf16[64,1152]{1,0:T(8,128)(2,1)S(1)}, bf16[64,1152]{1,0:T(8,128)(2,1)S(1)}, u32[]{:S(2)}, u32[]{:S(2)}) collective-permute-start(bf16[64,1152]{1,0:T(8,128)(2,1)S(1)} %pad_maximum_fusion.2), channel_id=1, source_target_pairs={{0,12},{4,0},{8,4},{12,8},{1,13},{5,1},{9,5},{13,9},{2,14},{6,2},{... | collective-permute-start | bytes 442376 | tf_op jit(solution)/shard_map/ppermute | solution.py:26
  17.3 11.0 %collective-permute-start.4 = (bf16[192,1024]{1,0:T(8,128)(2,1)S(1)}, bf16[192,1024]{1,0:T(8,128)(2,1)S(1)}, u32[]{:S(2)}, u32[]{:S(2)}) collective-permute-start(bf16[192,1024]{1,0:T(8,128)(2,1)S(1)} %get-tuple-element.23.refs_5_), channel_id=1, source_target_pairs={{0,1},{1,0},{2,3},{3,2},{4,5},{5,4},{6,7},{7,6},{8,9},{9,8},{10,11... | collective-permute-start | bytes 1179656 | tf_op jit(solution)/shard_map/ppermute | solution.py:21
  18.8 10.7 %collective-permute-start.5 = (bf16[192,1024]{1,0:T(8,128)(2,1)S(1)}, bf16[192,1024]{1,0:T(8,128)(2,1)S(1)}, u32[]{:S(2)}, u32[]{:S(2)}) collective-permute-start(bf16[192,1024]{1,0:T(8,128)(2,1)S(1)} %get-tuple-element.23.refs_5_), channel_id=1, source_target_pairs={{0,2},{1,3},{2,0},{3,1},{4,6},{5,7},{6,4},{7,5},{8,10},{9,11},{10,... | collective-permute-start | bytes 1179656 | tf_op jit(solution)/shard_map/ppermute | solution.py:21
  29.5 28.6 %collective-permute-start.6 = (bf16[192,1024]{1,0:T(8,128)(2,1)S(1)}, bf16[192,1024]{1,0:T(8,128)(2,1)S(1)}, u32[]{:S(2)}, u32[]{:S(2)}) collective-permute-start(bf16[192,1024]{1,0:T(8,128)(2,1)S(1)} %get-tuple-element.23.refs_5_), channel_id=1, source_target_pairs={{0,3},{1,2},{2,1},{3,0},{4,7},{5,6},{6,5},{7,4},{8,11},{9,10},{10,... | collective-permute-start | bytes 1179656 | tf_op jit(solution)/shard_map/ppermute | solution.py:21
  31.0 37.9 %collective-permute-start = (bf16[1024,256]{1,0:T(8,128)(2,1)S(1)}, bf16[1024,256]{1,0:T(8,128)(2,1)S(1)}, u32[]{:S(2)}, u32[]{:S(2)}) collective-permute-start(bf16[1024,256]{1,0:T(8,128)(2,1)S(1)} %constant_dynamic-slice_fusion), channel_id=1, source_target_pairs={{0,8},{4,12},{8,0},{12,4},{1,9},{5,13},{9,1},{13,5},{2,10},{6,14},... | collective-permute-start | bytes 1572872 | tf_op jit(solution)/shard_map/ppermute | solution.py:21
  34.5 5.2 %copy-start.3 = (bf16[1,64,4096]{2,1,0:T(8,128)(2,1)S(1)}, bf16[1,64,4096]{2,1,0:T(8,128)(2,1)}, u32[]{:S(2)}) copy-start(bf16[1,64,4096]{2,1,0:T(8,128)(2,1)} %param.13) | copy-start | bytes 1572868
  34.5 5.2 %copy-start.5 = (bf16[4096,32]{0,1:T(8,128)(2,1)S(1)}, bf16[4096,32]{0,1:T(8,128)(2,1)}, u32[]{:S(2)}) copy-start(bf16[4096,32]{0,1:T(8,128)(2,1)} %param.15) | copy-start | bytes 786436
  69.0 27.6 %collective-permute-start.7 = (bf16[2048,256]{1,0:T(8,128)(2,1)S(1)}, bf16[2048,256]{1,0:T(8,128)(2,1)S(1)}, u32[]{:S(2)}, u32[]{:S(2)}) collective-permute-start(bf16[2048,256]{1,0:T(8,128)(2,1)S(1)} %pad_maximum_fusion.1), channel_id=1, source_target_pairs={{0,4},{4,0},{8,12},{12,8},{1,5},{5,1},{9,13},{13,9},{2,6},{6,2},{1... | collective-permute-start | bytes 3145736 | tf_op jit(solution)/shard_map/ppermute | solution.py:21
  72.5 15.8 %collective-permute-start.8 = (bf16[256,1024]{1,0:T(8,128)(2,1)S(1)}, bf16[256,1024]{1,0:T(8,128)(2,1)S(1)}, u32[]{:S(2)}, u32[]{:S(2)}) collective-permute-start(bf16[256,1024]{1,0:T(8,128)(2,1)S(1)} %reduce.6), channel_id=1, source_target_pairs={{0,3},{1,2},{2,1},{3,0},{4,7},{5,6},{6,5},{7,4},{8,11},{9,10},{10,... | collective-permute-start | bytes 1572872 | tf_op jit(solution)/shard_map/ppermute | solution.py:21
  78.4 17.9 %collective-permute-start.9 = (bf16[256,1024]{1,0:T(8,128)(2,1)S(1)}, bf16[256,1024]{1,0:T(8,128)(2,1)S(1)}, u32[]{:S(2)}, u32[]{:S(2)}) collective-permute-start(bf16[256,1024]{1,0:T(8,128)(2,1)S(1)} %reduce.4), channel_id=1, source_target_pairs={{0,2},{1,3},{2,0},{3,1},{4,6},{5,7},{6,4},{7,5},{8,10},{9,11},{10,... | collective-permute-start | bytes 1572872 | tf_op jit(solution)/shard_map/ppermute | solution.py:21
  80.0 16.2 %collective-permute-start.10 = (bf16[256,1024]{1,0:T(8,128)(2,1)S(1)}, bf16[256,1024]{1,0:T(8,128)(2,1)S(1)}, u32[]{:S(2)}, u32[]{:S(2)}) collective-permute-start(bf16[256,1024]{1,0:T(8,128)(2,1)S(1)} %reduce.7), channel_id=1, source_target_pairs={{0,1},{1,0},{2,3},{3,2},{4,5},{5,4},{6,7},{7,6},{8,9},{9,8},{10,11... | collective-permute-start | bytes 1572872 | tf_op jit(solution)/shard_map/ppermute | solution.py:21
  85.1 36.6 %copy-start.8 = (f32[4096]{0:T(1024)S(1)}, f32[4096]{0:T(1024)}, u32[]{:S(2)}) copy-start(f32[4096]{0:T(1024)} %param.19) | copy-start | bytes 49156
  96.8 28.0 %copy-start.2 = (bf16[512,2048]{1,0:T(8,128)(2,1)S(1)}, bf16[512,2048]{1,0:T(8,128)(2,1)}, u32[]{:S(2)}) copy-start(bf16[512,2048]{1,0:T(8,128)(2,1)} %w_out.7) | copy-start | bytes 6291460
  96.8 28.0 %copy-start.4 = (bf16[1,256,512]{2,1,0:T(8,128)(2,1)S(1)}, bf16[1,256,512]{2,1,0:T(8,128)(2,1)}, u32[]{:S(2)}) copy-start(bf16[1,256,512]{2,1,0:T(8,128)(2,1)} %param.22) | copy-start | bytes 786436
  96.8 28.0 %copy-start.6 = (bf16[1,256,256]{2,1,0:T(8,128)(2,1)S(1)}, bf16[1,256,256]{2,1,0:T(8,128)(2,1)}, u32[]{:S(2)}) copy-start(bf16[1,256,256]{2,1,0:T(8,128)(2,1)} %param.23) | copy-start | bytes 393220
  96.9 28.0 %copy-start.7 = (bf16[1,256,256]{2,1,0:T(8,128)(2,1)S(1)}, bf16[1,256,256]{2,1,0:T(8,128)(2,1)}, u32[]{:S(2)}) copy-start(bf16[1,256,256]{2,1,0:T(8,128)(2,1)} %param.24) | copy-start | bytes 393220
  96.9 24.8 %collective-permute-start.17 = (bf16[4096,256]{1,0:T(8,128)(2,1)S(1)}, bf16[4096,256]{1,0:T(8,128)(2,1)S(1)}, u32[]{:S(2)}, u32[]{:S(2)}) collective-permute-start(bf16[4096,256]{1,0:T(8,128)(2,1)S(1)} %pad_maximum_fusion.refs_5_), channel_id=1, source_target_pairs={{0,16},{16,0},{1,17},{17,1},{2,18},{18,2},{3,19},{19,3},{4,20},{20... | collective-permute-start | bytes 6291464 | tf_op jit(solution)/shard_map/ppermute | solution.py:21
  97.0 6.4 %collective-permute-start.11 = (bf16[64,1024]{1,0:T(8,128)(2,1)S(1)}, bf16[64,1024]{1,0:T(8,128)(2,1)S(1)}, u32[]{:S(2)}, u32[]{:S(2)}) collective-permute-start(bf16[64,1024]{1,0:T(8,128)(2,1)S(1)} %get-tuple-element.41), channel_id=1, source_target_pairs={{0,12},{4,0},{8,4},{12,8},{1,13},{5,1},{9,5},{13,9},{2,14},{6,2},{... | collective-permute-start | bytes 393224 | tf_op jit(solution)/shard_map/ppermute | solution.py:26
  99.4 12.8 %collective-permute-start.12 = (bf16[64,1024]{1,0:T(8,128)(2,1)S(1)}, bf16[64,1024]{1,0:T(8,128)(2,1)S(1)}, u32[]{:S(2)}, u32[]{:S(2)}) collective-permute-start(bf16[64,1024]{1,0:T(8,128)(2,1)S(1)} %get-tuple-element.43), channel_id=1, source_target_pairs={{0,8},{4,12},{8,0},{12,4},{1,9},{5,13},{9,1},{13,5},{2,10},{6,14},... | collective-permute-start | bytes 393224 | tf_op jit(solution)/shard_map/ppermute | solution.py:26
  99.7 12.5 %collective-permute-start.13 = (bf16[64,1024]{1,0:T(8,128)(2,1)S(1)}, bf16[64,1024]{1,0:T(8,128)(2,1)S(1)}, u32[]{:S(2)}, u32[]{:S(2)}) collective-permute-start(bf16[64,1024]{1,0:T(8,128)(2,1)S(1)} %get-tuple-element.42), channel_id=1, source_target_pairs={{0,4},{4,8},{8,12},{12,0},{1,5},{5,9},{9,13},{13,1},{2,6},{6,10},{... | collective-permute-start | bytes 393224 | tf_op jit(solution)/shard_map/ppermute | solution.py:26
  112.3 5.8 %collective-permute-start.14 = (bf16[64,1024]{1,0:T(8,128)(2,1)S(1)}, bf16[64,1024]{1,0:T(8,128)(2,1)S(1)}, u32[]{:S(2)}, u32[]{:S(2)}) collective-permute-start(bf16[64,1024]{1,0:T(8,128)(2,1)S(1)} %add_convert_fusion.1.refs_0_), channel_id=1, source_target_pairs={{0,1},{1,0},{2,3},{3,2},{4,5},{5,4},{6,7},{7,6},{8,9},{9,8},{10,11... | collective-permute-start | bytes 393224 | tf_op jit(solution)/shard_map/ppermute | solution.py:21
  113.9 7.8 %collective-permute-start.15 = (bf16[64,1024]{1,0:T(8,128)(2,1)S(1)}, bf16[64,1024]{1,0:T(8,128)(2,1)S(1)}, u32[]{:S(2)}, u32[]{:S(2)}) collective-permute-start(bf16[64,1024]{1,0:T(8,128)(2,1)S(1)} %add_convert_fusion.1.refs_0_), channel_id=1, source_target_pairs={{0,2},{1,3},{2,0},{3,1},{4,6},{5,7},{6,4},{7,5},{8,10},{9,11},{10,... | collective-permute-start | bytes 393224 | tf_op jit(solution)/shard_map/ppermute | solution.py:21
  114.5 7.2 %collective-permute-start.16 = (bf16[64,1024]{1,0:T(8,128)(2,1)S(1)}, bf16[64,1024]{1,0:T(8,128)(2,1)S(1)}, u32[]{:S(2)}, u32[]{:S(2)}) collective-permute-start(bf16[64,1024]{1,0:T(8,128)(2,1)S(1)} %add_convert_fusion.1.refs_0_), channel_id=1, source_target_pairs={{0,3},{1,2},{2,1},{3,0},{4,7},{5,6},{6,5},{7,4},{8,11},{9,10},{10,... | collective-permute-start | bytes 393224 | tf_op jit(solution)/shard_map/ppermute | solution.py:21
  123.5 1.3 collective-permute-start.18
  126.5 10.2 %collective-permute-start.19 = (bf16[64,2048]{1,0:T(8,128)(2,1)S(1)}, bf16[64,2048]{1,0:T(8,128)(2,1)S(1)}, u32[]{:S(2)}, u32[]{:S(2)}) collective-permute-start(bf16[64,2048]{1,0:T(8,128)(2,1)S(1)} %attend.5), channel_id=1, source_target_pairs={{0,3},{1,2},{2,1},{3,0},{4,7},{5,6},{6,5},{7,4},{8,11},{9,10},{10,... | collective-permute-start | bytes 786440 | tf_op jit(solution)/shard_map/ppermute | solution.py:21
  127.7 14.5 %copy-start.1 = (bf16[1024,512]{1,0:T(8,128)(2,1)S(1)}, bf16[1024,512]{1,0:T(8,128)(2,1)}, u32[]{:S(2)}) copy-start(bf16[1024,512]{1,0:T(8,128)(2,1)} %param.20) | copy-start | bytes 3145732
  129.3 12.1 %collective-permute-start.20 = (bf16[64,2048]{1,0:T(8,128)(2,1)S(1)}, bf16[64,2048]{1,0:T(8,128)(2,1)S(1)}, u32[]{:S(2)}, u32[]{:S(2)}) collective-permute-start(bf16[64,2048]{1,0:T(8,128)(2,1)S(1)} %attend.6), channel_id=1, source_target_pairs={{0,2},{1,3},{2,0},{3,1},{4,6},{5,7},{6,4},{7,5},{8,10},{9,11},{10,... | collective-permute-start | bytes 786440 | tf_op jit(solution)/shard_map/ppermute | solution.py:21
  131.9 9.5 %collective-permute-start.21 = (bf16[64,2048]{1,0:T(8,128)(2,1)S(1)}, bf16[64,2048]{1,0:T(8,128)(2,1)S(1)}, u32[]{:S(2)}, u32[]{:S(2)}) collective-permute-start(bf16[64,2048]{1,0:T(8,128)(2,1)S(1)} %attend.7), channel_id=1, source_target_pairs={{0,1},{1,0},{2,3},{3,2},{4,5},{5,4},{6,7},{7,6},{8,9},{9,8},{10,11... | collective-permute-start | bytes 786440 | tf_op jit(solution)/shard_map/ppermute | solution.py:21

commit v6 on v5

--- a/solution.py
+++ b/solution.py
@@ -171,6 +171,7 @@
         else:
             logits_out[...] = logits
         experts, (_, _, units) = sources[0].shape[0], sources[0].shape
+        near_width = nears[0].shape[1]
         held, buffers, buffer_sems = list(held), list(buffers), list(buffer_sems)
         for n, (low, high, ks) in enumerate(parts):
             sources_of = [
@@ -178,8 +179,11 @@
                 for k, streamed in ks
             ]
 
-            def body(e, carry, n=n, low=low, high=high, sources_of=sources_of):
+            begun = any(part[0] <= low < part[1] for part in parts[:n])
+
+            def body(e, carry, n=n, low=low, high=high, sources_of=sources_of, begun=begun):
                 both = []
+                at = quarters.index(sources_of[0][0]) * near_width
                 for k, weight, sems in sources_of:
                     if sems is not None:
                         for copy in expert_copies(place, sources, k, low, e, weight, sems):
@@ -196,8 +200,11 @@
                             copy.start()
 
                 both = jnp.concatenate(both, axis=0)
-                value = jnp.dot(rows[...], both, preferred_element_type=F32)
-                if not first:
+                used = rows[:, at : at + both.shape[0]]
+                value = jnp.dot(used, both, preferred_element_type=F32)
+                if begun:
+                    value += out[e]
+                elif not first:
                     value += totals[0][e]
                 if not top:
                     out[e] = value
@@ -319,7 +326,7 @@
     )(place, in_vmem(hidden), in_hbm(w_down))
 
 
-def project_kernel(parts, origins, place, own, *refs):
+def project_kernel(parts, eps, place, own, *refs):
     moe, refs = refs[:parts], refs[parts:]
     gain, mine, theirs, out, mixed, normed = refs
     half, ep, pool = place[0], place[1], place[2]
@@ -332,21 +339,21 @@
         square += jnp.sum(value * value, axis=1, keepdims=True)
     factor = lax.rsqrt(square / mixed.shape[1] + 1e-06)
     normed[...] = (mixed[...] * factor * gain[...]).astype(BF16)
-    depth, narrow = mine.shape[0] // len(origins), mine.shape[1]
+    depth, narrow = mine.shape[0] // eps, mine.shape[1]
     for side, pieces in ((pool, mine), (1 - pool, theirs)):
         total = 0.0
-        for i, origin in enumerate(origins):
+        for d in range(eps):
             total += jnp.dot(
-                normed[:, columns_of(ep ^ origin, depth)],
-                pieces[i * depth : (i + 1) * depth, :],
+                normed[:, columns_of(lax.rem(ep + eps - d, eps), depth)],
+                pieces[d * depth : (d + 1) * depth, :],
                 preferred_element_type=F32,
             )
         out[:, columns_of(side, narrow)] = total.astype(BF16)
 
 
-def project(place, own, moe, gain, mine, theirs, origins):
+def project(place, own, moe, gain, mine, theirs, eps):
     return pl.pallas_call(
-        functools.partial(project_kernel, len(moe), origins),
+        functools.partial(project_kernel, len(moe), eps),
         out_shape=jax.ShapeDtypeStruct((own.shape[0], 2 * mine.shape[1]), BF16),
         grid_spec=pltpu.PrefetchScalarGridSpec(
             num_scalar_prefetch=1,
@@ -489,9 +496,7 @@
     others[order[-1]] = swap(again, "half", order[-1])
     mine = lax.dynamic_slice_in_dim(w_kv, pool * narrow, narrow, axis=1)
     others[0] = near
-    bits = [eps >> i + 1 for i in range(eps.bit_length() - 1)]
-    received = swap(mine, "ep", bits[0])
-    origins = [0, bits[0]]
+    received = [shift(mine, "ep", d) for d in range(1, eps)]
     got, totals = stage(
         place, sources, [(PAIR, beside[0], 0, experts)], own, router.T, {0: others[0]},
         [(0, experts, [(0, False)])], got,
@@ -500,7 +505,7 @@
     got, totals = stage(
         place, sources, [(PAIR, last, 0, early)] if early else [], own, router.T,
         {k: others[k] for k in beside},
-        [(0, experts, [(k, k != beside[0]) for k in beside])], got, totals,
+        [(0, experts, [(k, k != beside[0])]) for k in beside], got, totals,
     )
     pieces = [(0, early, [(last, False)])] if early else []
     got, (hidden,) = stage(
@@ -514,11 +519,8 @@
             partial[k] = reduce_ahead(hidden, ahead[k])
         else:
             partial[k] = reduce(k, place, hidden, w_down, width, width // 2)
-    received, partial[far[1]] = lax.optimization_barrier((received, partial[far[1]]))
-    mine = jnp.concatenate([mine, received], axis=0)
-    for bit in bits[1:]:
-        mine = jnp.concatenate([mine, swap(mine, "ep", bit)], axis=0)
-        origins += [origin ^ bit for origin in origins]
+    received, partial[0] = lax.optimization_barrier((received, partial[0]))
+    mine = jnp.concatenate([mine] + received, axis=0)
     gathered = []
     for k in far:
         gathered.append(swap(partial[k], "half", k))
@@ -533,7 +535,7 @@
     moe = [moe_quarter] + [None] * (parts - 1)
     for k in order:
         moe[k] = swap(moe_quarter, "half", k)
-    keyvals = project(place, own, moe, norm_gain[None], mine, theirs, origins)
+    keyvals = project(place, own, moe, norm_gain[None], mine, theirs, eps)
     block = swap(keyvals, "pool", 1)
 
     rows = queries.shape[1] // parts

time: 142 us -> 136 us (0.958)
  waiting for transfers between devices: 52.7 us -> 47.7 us
  Pallas kernels: 53.4 us -> 51.5 us
    ppermute x16 -> x14, waiting for transfers between devices: 33.8 us -> 28.1 us  [swap(): lax.ppermute(shard, axis, [(i, i ^ bits) for i in range(lax.axis_size(axi...]
    ppermute x16 -> x14, starting transfers between devices: 20 us -> 15.6 us  [swap(): lax.ppermute(shard, axis, [(i, i ^ bits) for i in range(lax.axis_size(axi...]
    ppermute x6 -> x9, starting transfers between devices: 11.7 us -> 15.8 us  [shift(): lax.ppermute(shard, axis, [(i, (i + distance) % count) for i in range(cou...]
    pallas_call x4, Pallas kernels: 29.9 us -> 28.1 us  [stage(): pl.pallas_call(functools.partial(stage_kernel, items, quarters, parts, no...]
    ppermute x6 -> x9, waiting for transfers between devices: 18.9 us -> 19.6 us  [shift(): lax.ppermute(shard, axis, [(i, (i + distance) % count) for i in range(cou...]
  transfers between devices with their start and end apart: 22 -> 23, of which waited for: 13 -> 12; matrix products, arithmetic and copies ran while one was open for 1% -> 2% of each run, Pallas kernels for 35% -> 35%
where the time goes in v6:
time: 136 us
  Pallas kernels  51.5 us (38%)
  waiting for transfers between devices  47.7 us (35%)
  starting transfers between devices  31.5 us (23%)
  other arithmetic  2.57 us (2%)
  local copies, waits for them, and re-layouts  2.55 us (2%)
    ppermute x14, waiting for transfers between devices, swap(): lax.ppermute(shard, axis, [(i, i ^ bits) for i in range(lax.axis_size(axi...  28.1 us
    pallas_call x4, Pallas kernels, stage(): pl.pallas_call(functools.partial(stage_kernel, items, quarters, parts, no...  28.1 us
    ppermute x9, waiting for transfers between devices, shift(): lax.ppermute(shard, axis, [(i, (i + distance) % count) for i in range(cou...  19.6 us
    ppermute x9, starting transfers between devices, shift(): lax.ppermute(shard, axis, [(i, (i + distance) % count) for i in range(cou...  15.8 us
    ppermute x14, starting transfers between devices, swap(): lax.ppermute(shard, axis, [(i, i ^ bits) for i in range(lax.axis_size(axi...  15.6 us
    pallas_call x3, Pallas kernels, reduce(): pl.pallas_call(reduce_kernel, out_shape=jax.ShapeDtypeStruct((tokens, wid...  13.5 us
    pallas_call x4, Pallas kernels, attend(): pl.pallas_call(functools.partial(attend_kernel, k, prompts), out_shape=ja...  6.48 us
  transfers between devices with their start and end apart: 23, of which 12 were waited for; matrix products, arithmetic and copies ran while one was open for 2% of the time, Pallas kernels for 35%

profile of v6, /device:TPU:0, one launch (start us, length us, event | category | flops | bytes accessed | tf_op | source)
XLA Modules:
  0.0 136.1 jit_solution(5740658041734602443)
XLA Ops:
  1.8 3.1 %collective-permute-start.3 = (bf16[64,1152]{1,0:T(8,128)(2,1)S(1)}, bf16[64,1152]{1,0:T(8,128)(2,1)S(1)}, u32[]{:S(2)}, u32[]{:S(2)}) collective-permute-start(bf16[64,1152]{1,0:T(8,128)(2,1)S(1)} %pad_maximum_fusion.1), channel_id=1, source_target_pairs={{0,4},{4,8},{8,12},{12,0},{1,5},{5,9},{9,13},{13,1},{2,6},{6,10},{... | collective-permute-start | bytes 442376 | tf_op jit(solution)/shard_map/ppermute | solution.py:26
  4.9 2.6 %collective-permute-start.4 = (bf16[64,1152]{1,0:T(8,128)(2,1)S(1)}, bf16[64,1152]{1,0:T(8,128)(2,1)S(1)}, u32[]{:S(2)}, u32[]{:S(2)}) collective-permute-start(bf16[64,1152]{1,0:T(8,128)(2,1)S(1)} %pad_maximum_fusion.1), channel_id=1, source_target_pairs={{0,8},{4,12},{8,0},{12,4},{1,9},{5,13},{9,1},{13,5},{2,10},{6,14},... | collective-permute-start | bytes 442376 | tf_op jit(solution)/shard_map/ppermute | solution.py:26
  8.9 2.9 %collective-permute-done.3.refs_0_ = bf16[64,1152]{1,0:T(8,128)(2,1)S(1)} collective-permute-done((bf16[64,1152]{1,0:T(8,128)(2,1)S(1)}, bf16[64,1152]{1,0:T(8,128)(2,1)S(1)}, u32[]{:S(2)}, u32[]{:S(2)}) %collective-permute-start.3) | collective-permute-done | bytes 147488 | tf_op jit(solution)/shard_map/ppermute | solution.py:26
  11.8 5.5 %collective-permute-done.4.refs_1_ = bf16[64,1152]{1,0:T(8,128)(2,1)S(1)} collective-permute-done((bf16[64,1152]{1,0:T(8,128)(2,1)S(1)}, bf16[64,1152]{1,0:T(8,128)(2,1)S(1)}, u32[]{:S(2)}, u32[]{:S(2)}) %collective-permute-start.4) | collective-permute-done | bytes 147488 | tf_op jit(solution)/shard_map/ppermute | solution.py:26
  17.3 1.6 %collective-permute-start.6 = (bf16[192,1024]{1,0:T(8,128)(2,1)S(1)}, bf16[192,1024]{1,0:T(8,128)(2,1)S(1)}, u32[]{:S(2)}, u32[]{:S(2)}) collective-permute-start(bf16[192,1024]{1,0:T(8,128)(2,1)S(1)} %get-tuple-element.25.refs_5_), channel_id=1, source_target_pairs={{0,1},{1,0},{2,3},{3,2},{4,5},{5,4},{6,7},{7,6},{8,9},{9,8},{10,11... | collective-permute-start | bytes 1179656 | tf_op jit(solution)/shard_map/ppermute | solution.py:21
  18.8 1.5 %collective-permute-start.7 = (bf16[192,1024]{1,0:T(8,128)(2,1)S(1)}, bf16[192,1024]{1,0:T(8,128)(2,1)S(1)}, u32[]{:S(2)}, u32[]{:S(2)}) collective-permute-start(bf16[192,1024]{1,0:T(8,128)(2,1)S(1)} %get-tuple-element.25.refs_5_), channel_id=1, source_target_pairs={{0,2},{1,3},{2,0},{3,1},{4,6},{5,7},{6,4},{7,5},{8,10},{9,11},{10,... | collective-permute-start | bytes 1179656 | tf_op jit(solution)/shard_map/ppermute | solution.py:21
  20.3 7.9 %collective-permute-done.6.refs_5_ = bf16[192,1024]{1,0:T(8,128)(2,1)S(1)} collective-permute-done((bf16[192,1024]{1,0:T(8,128)(2,1)S(1)}, bf16[192,1024]{1,0:T(8,128)(2,1)S(1)}, u32[]{:S(2)}, u32[]{:S(2)}) %collective-permute-start.6) | collective-permute-done | bytes 393248 | tf_op jit(solution)/shard_map/ppermute | solution.py:21
  31.0 3.8 %collective-permute-start = (bf16[1024,256]{1,0:T(8,128)(2,1)S(1)}, bf16[1024,256]{1,0:T(8,128)(2,1)S(1)}, u32[]{:S(2)}, u32[]{:S(2)}) collective-permute-start(bf16[1024,256]{1,0:T(8,128)(2,1)S(1)} %constant_dynamic-slice_fusion), channel_id=1, source_target_pairs={{0,4},{4,8},{8,12},{12,0},{1,5},{5,9},{9,13},{13,1},{2,6},{6,10},{... | collective-permute-start | bytes 1572872 | tf_op jit(solution)/shard_map/ppermute | solution.py:26
  35.4 1.8 %collective-permute-start.2 = (bf16[1024,256]{1,0:T(8,128)(2,1)S(1)}, bf16[1024,256]{1,0:T(8,128)(2,1)}, u32[]{:S(2)}, u32[]{:S(2)}) collective-permute-start(bf16[1024,256]{1,0:T(8,128)(2,1)S(1)} %constant_dynamic-slice_fusion), channel_id=1, source_target_pairs={{0,12},{4,0},{8,4},{12,8},{1,13},{5,1},{9,5},{13,9},{2,14},{6,2},{... | collective-permute-start | bytes 1572872 | tf_op jit(solution)/shard_map/ppermute | solution.py:26
  38.0 5.2 %shard_map.127.refs_6_ = bf16[16,1024,384]{2,1,0:T(8,128)(2,1)S(1)} custom-call(s32[5]{0:T(128)S(1)} %pad_add_fusion.place, bf16[8,4096,384]{2,1,0:T(8,128)(2,1)} %refs_0_.7, bf16[8,4096,384]{2,1,0:T(8,128)(2,1)} %refs_1_.7, bf16[8,384,4096]{2,1,0:T(8,128)(2,1)} %w_down.5), custom_call_target="tpu_custom_call" | custom-call | tf_op jit(solution)/shard_map/pallas_call | solution.py:260
  43.2 5.3 %shard_map.128 = (bf16[16,1024,384]{2,1,0:T(8,128)(2,1)S(1)}, f32[8,256,768]{2,1,0:T(8,128)S(1)}, f32[256,32]{1,0:T(8,128)S(1)}) custom-call(s32[5]{0:T(128)S(1)} %pad_add_fusion.place, bf16[8,4096,384]{2,1,0:T(8,128)(2,1)} %refs_0_.7, bf16[8,4096,384]{2,1,0:T(8,128)(2,1)} %refs_1_.7, bf16[8,384,4096]{2,1,0:T(8,128)(2,1)} %w_down.5, ...), custom_call_target="tpu_custom_call" | custom-call | tf_op jit(solution)/shard_map/pallas_call | solution.py:260
  48.5 11.3 %shard_map.129 = (bf16[8,1024,384]{2,1,0:T(8,128)(2,1)S(1)}, f32[8,256,768]{2,1,0:T(8,128)S(1)}, f32[256,32]{1,0:T(8,128)S(1)}) custom-call(s32[5]{0:T(128)S(1)} %pad_add_fusion.place, bf16[8,4096,384]{2,1,0:T(8,128)(2,1)} %refs_0_.7, bf16[8,4096,384]{2,1,0:T(8,128)(2,1)} %refs_1_.7, ...), custom_call_target="tpu_custom_call", output_to_operand_aliasing={{1}: (9, {}), {2}: (10, {})} | custom-call | tf_op jit(solution)/shard_map/pallas_call | solution.py:260
  59.8 6.3 %shard_map.130 = (bf16[8,384,1024]{2,1,0:T(8,128)(2,1)S(1)}, bf16[256,3072]{1,0:T(8,128)(2,1)S(1)}) custom-call(s32[5]{0:T(128)S(1)} %pad_add_fusion.place, bf16[8,4096,384]{2,1,0:T(8,128)(2,1)} %refs_0_.7, bf16[8,4096,384]{2,1,0:T(8,128)(2,1)} %refs_1_.7, bf16[8,384,4096]{2,1,0:T(8,128)(2,1)} %w_down.5, bf16[64,4096]{1,0:T(8,128)(2,1)S(1)} %bitcast.19, ...), custom_call_target="tpu_custom_call" | custom-call | tf_op jit(solution)/shard_map/pallas_call | solution.py:260
  66.1 1.8 %reduce.5 = bf16[256,1024]{1,0:T(8,128)(2,1)S(1)} custom-call(bf16[256,3072]{1,0:T(8,128)(2,1)S(1)} %get-tuple-element.35.hidden, bf16[8,384,1024]{2,1,0:T(8,128)(2,1)S(1)} %get-tuple-element.40.weight), custom_call_target="tpu_custom_call" | custom-call | tf_op jit(solution)/shard_map/reduce/pallas_call | solution.py:290
  69.3 4.5 %reduce.6 = bf16[256,1024]{1,0:T(8,128)(2,1)S(1)} custom-call(s32[5]{0:T(128)S(1)} %pad_add_fusion.place, bf16[256,3072]{1,0:T(8,128)(2,1)S(1)} %get-tuple-element.35.hidden, bf16[8,384,4096]{2,1,0:T(8,128)(2,1)} %w_down.5), custom_call_target="tpu_custom_call" | custom-call | flops 1610612736 | bytes 6291456 | tf_op jit(solution)/shard_map/reduce/pallas_call | solution.py:304
  73.8 1.7 %collective-permute-start.10 = (bf16[256,1024]{1,0:T(8,128)(2,1)S(1)}, bf16[256,1024]{1,0:T(8,128)(2,1)S(1)}, u32[]{:S(2)}, u32[]{:S(2)}) collective-permute-start(bf16[256,1024]{1,0:T(8,128)(2,1)S(1)} %reduce.6), channel_id=1, source_target_pairs={{0,2},{1,3},{2,0},{3,1},{4,6},{5,7},{6,4},{7,5},{8,10},{9,11},{10,... | collective-permute-start | bytes 1572872 | tf_op jit(solution)/shard_map/ppermute | solution.py:21
  75.5 4.5 %reduce.7 = bf16[256,1024]{1,0:T(8,128)(2,1)S(1)} custom-call(s32[5]{0:T(128)S(1)} %pad_add_fusion.place, bf16[256,3072]{1,0:T(8,128)(2,1)S(1)} %get-tuple-element.35.hidden, bf16[8,384,4096]{2,1,0:T(8,128)(2,1)} %w_down.5), custom_call_target="tpu_custom_call" | custom-call | flops 1610612736 | bytes 6291456 | tf_op jit(solution)/shard_map/reduce/pallas_call | solution.py:304
  80.6 4.5 %reduce.4 = bf16[256,1024]{1,0:T(8,128)(2,1)S(1)} custom-call(s32[5]{0:T(128)S(1)} %pad_add_fusion.place, bf16[256,3072]{1,0:T(8,128)(2,1)S(1)} %get-tuple-element.35.hidden, bf16[8,384,4096]{2,1,0:T(8,128)(2,1)} %w_down.5), custom_call_target="tpu_custom_call" | custom-call | flops 1610612736 | bytes 6291456 | tf_op jit(solution)/shard_map/reduce/pallas_call | solution.py:304
  86.3 5.7 %collective-permute-done.10 = bf16[256,1024]{1,0:T(8,128)(2,1)S(1)} collective-permute-done((bf16[256,1024]{1,0:T(8,128)(2,1)S(1)}, bf16[256,1024]{1,0:T(8,128)(2,1)S(1)}, u32[]{:S(2)}, u32[]{:S(2)}) %collective-permute-start.10) | collective-permute-done | bytes 524320 | tf_op jit(solution)/shard_map/ppermute | solution.py:21
  92.5 1.7 %collective-permute-start.12 = (bf16[64,1024]{1,0:T(8,128)(2,1)S(1)}, bf16[64,1024]{1,0:T(8,128)(2,1)S(1)}, u32[]{:S(2)}, u32[]{:S(2)}) collective-permute-start(bf16[64,1024]{1,0:T(8,128)(2,1)S(1)} %get-tuple-element.45), channel_id=1, source_target_pairs={{0,12},{4,0},{8,4},{12,8},{1,13},{5,1},{9,5},{13,9},{2,14},{6,2},{... | collective-permute-start | bytes 393224 | tf_op jit(solution)/shard_map/ppermute | solution.py:26
  95.1 3.9 %collective-permute-done.12 = bf16[64,1024]{1,0:T(8,128)(2,1)S(1)} collective-permute-done((bf16[64,1024]{1,0:T(8,128)(2,1)S(1)}, bf16[64,1024]{1,0:T(8,128)(2,1)S(1)}, u32[]{:S(2)}, u32[]{:S(2)}) %collective-permute-start.12) | collective-permute-done | bytes 131104 | tf_op jit(solution)/shard_map/ppermute | solution.py:26
  99.0 7.4 %collective-permute-done.13 = bf16[64,1024]{1,0:T(8,128)(2,1)S(1)} collective-permute-done((bf16[64,1024]{1,0:T(8,128)(2,1)S(1)}, bf16[64,1024]{1,0:T(8,128)(2,1)S(1)}, u32[]{:S(2)}, u32[]{:S(2)}) %collective-permute-start.13) | collective-permute-done | bytes 131104 | tf_op jit(solution)/shard_map/ppermute | solution.py:26
  106.5 1.5 %collective-permute-start.15 = (bf16[64,1024]{1,0:T(8,128)(2,1)S(1)}, bf16[64,1024]{1,0:T(8,128)(2,1)S(1)}, u32[]{:S(2)}, u32[]{:S(2)}) collective-permute-start(bf16[64,1024]{1,0:T(8,128)(2,1)S(1)} %add_convert_fusion.1.refs_0_), channel_id=1, source_target_pairs={{0,1},{1,0},{2,3},{3,2},{4,5},{5,4},{6,7},{7,6},{8,9},{9,8},{10,11... | collective-permute-start | bytes 393224 | tf_op jit(solution)/shard_map/ppermute | solution.py:21
  110.0 2.1 %collective-permute-done.15.refs_1_ = bf16[64,1024]{1,0:T(8,128)(2,1)S(1)} collective-permute-done((bf16[64,1024]{1,0:T(8,128)(2,1)S(1)}, bf16[64,1024]{1,0:T(8,128)(2,1)S(1)}, u32[]{:S(2)}, u32[]{:S(2)}) %collective-permute-start.15) | collective-permute-done | bytes 131104 | tf_op jit(solution)/shard_map/ppermute | solution.py:21
  112.1 3.6 %collective-permute-done.16.refs_2_ = bf16[64,1024]{1,0:T(8,128)(2,1)S(1)} collective-permute-done((bf16[64,1024]{1,0:T(8,128)(2,1)S(1)}, bf16[64,1024]{1,0:T(8,128)(2,1)S(1)}, u32[]{:S(2)}, u32[]{:S(2)}) %collective-permute-start.16) | collective-permute-done | bytes 131104 | tf_op jit(solution)/shard_map/ppermute | solution.py:21
  115.7 1.6 %project.1 = bf16[64,512]{1,0:T(8,128)(2,1)S(1)} custom-call(s32[5]{0:T(128)S(1)} %pad_add_fusion.place, bf16[64,4096]{1,0:T(8,128)(2,1)S(1)} %bitcast.20, bf16[64,1024]{1,0:T(8,128)(2,1)S(1)} %add_convert_fusion.1.refs_0_, bf16[64,1024]{1,0:T(8,128)(2,1)S(1)} %collective-permute-done.15.refs_1_, bf16[64,1024]{1,0:T(8,128)(2,1)S(1)} %collective-permute-done.16.refs_2_, ...), custom_call_target="tpu_custom_call" | custom-call | tf_op jit(solution)/shard_map/project/pallas_call | solution.py:355
  118.7 1.6 %attend.5 = bf16[64,2048]{1,0:T(8,128)(2,1)S(1)} custom-call(s32[5]{0:T(128)S(1)} %pad_add_fusion.place, bf16[64,512]{1,0:T(8,128)(2,1)S(1)} %collective-permute-done.19.block, bf16[256,512]{1,0:T(8,128)(2,1)S(1)} %bitcast.21, bf16[256,256]{1,0:T(8,128)(2,1)S(1)} %bitcast.28, bf16[256,256]{1,0:T(8,128)(2,1)S(1)} %bitcast.32, bf16[512,2048]{1,0:T(8,128)(2,1)S(1)} %copy-done.2), custom_call_target="tpu_custom_call" | custom-call | flops 268435456 | bytes 2097152 | tf_op jit(solution)/shard_map/attend/pallas_call | solution.py:429
  121.5 1.6 %attend.6 = bf16[64,2048]{1,0:T(8,128)(2,1)S(1)} custom-call(s32[5]{0:T(128)S(1)} %pad_add_fusion.place, bf16[64,512]{1,0:T(8,128)(2,1)S(1)} %collective-permute-done.19.block, bf16[256,512]{1,0:T(8,128)(2,1)S(1)} %bitcast.22, bf16[256,256]{1,0:T(8,128)(2,1)S(1)} %bitcast.29, bf16[256,256]{1,0:T(8,128)(2,1)S(1)} %bitcast.33, bf16[512,2048]{1,0:T(8,128)(2,1)S(1)} %copy-done.2), custom_call_target="tpu_custom_call" | custom-call | flops 268435456 | bytes 2097152 | tf_op jit(solution)/shard_map/attend/pallas_call | solution.py:429
  124.1 1.6 %attend.7 = bf16[64,2048]{1,0:T(8,128)(2,1)S(1)} custom-call(s32[5]{0:T(128)S(1)} %pad_add_fusion.place, bf16[64,512]{1,0:T(8,128)(2,1)S(1)} %collective-permute-done.19.block, bf16[256,512]{1,0:T(8,128)(2,1)S(1)} %bitcast.23, bf16[256,256]{1,0:T(8,128)(2,1)S(1)} %bitcast.30, bf16[256,256]{1,0:T(8,128)(2,1)S(1)} %bitcast.34, bf16[512,2048]{1,0:T(8,128)(2,1)S(1)} %copy-done.2), custom_call_target="tpu_custom_call" | custom-call | flops 268435456 | bytes 2097152 | tf_op jit(solution)/shard_map/attend/pallas_call | solution.py:429
  127.2 1.6 %attend.4 = bf16[64,2048]{1,0:T(8,128)(2,1)S(1)} custom-call(s32[5]{0:T(128)S(1)} %pad_add_fusion.place, bf16[64,512]{1,0:T(8,128)(2,1)S(1)} %collective-permute-done.19.block, bf16[256,512]{1,0:T(8,128)(2,1)S(1)} %bitcast.24, bf16[256,256]{1,0:T(8,128)(2,1)S(1)} %bitcast.31, bf16[256,256]{1,0:T(8,128)(2,1)S(1)} %bitcast.35, bf16[512,2048]{1,0:T(8,128)(2,1)S(1)} %copy-done.2), custom_call_target="tpu_custom_call" | custom-call | flops 268435456 | bytes 2097152 | tf_op jit(solution)/shard_map/attend/pallas_call | solution.py:429
  128.9 1.6 %collective-permute-done.20 = bf16[64,2048]{1,0:T(8,128)(2,1)S(1)} collective-permute-done((bf16[64,2048]{1,0:T(8,128)(2,1)S(1)}, bf16[64,2048]{1,0:T(8,128)(2,1)S(1)}, u32[]{:S(2)}, u32[]{:S(2)}) %collective-permute-start.20) | collective-permute-done | bytes 262176 | tf_op jit(solution)/shard_map/ppermute | solution.py:21
  130.5 4.8 %collective-permute-done.21 = bf16[64,2048]{1,0:T(8,128)(2,1)S(1)} collective-permute-done((bf16[64,2048]{1,0:T(8,128)(2,1)S(1)}, bf16[64,2048]{1,0:T(8,128)(2,1)S(1)}, u32[]{:S(2)}, u32[]{:S(2)}) %collective-permute-start.21) | collective-permute-done | bytes 262176 | tf_op jit(solution)/shard_map/ppermute | solution.py:21
  (59 shorter events, 19.8 us)
Async XLA Ops:
  0.0 31.0 %copy-start = (bf16[1024,512]{1,0:T(8,128)(2,1)S(1)}, bf16[1024,512]{1,0:T(8,128)(2,1)}, u32[]{:S(2)}) copy-start(bf16[1024,512]{1,0:T(8,128)(2,1)} %param.20) | copy-start | bytes 3145732
  1.8 9.9 %collective-permute-start.3 = (bf16[64,1152]{1,0:T(8,128)(2,1)S(1)}, bf16[64,1152]{1,0:T(8,128)(2,1)S(1)}, u32[]{:S(2)}, u32[]{:S(2)}) collective-permute-start(bf16[64,1152]{1,0:T(8,128)(2,1)S(1)} %pad_maximum_fusion.1), channel_id=1, source_target_pairs={{0,4},{4,8},{8,12},{12,0},{1,5},{5,9},{9,13},{13,1},{2,6},{6,10},{... | collective-permute-start | bytes 442376 | tf_op jit(solution)/shard_map/ppermute | solution.py:26
  4.9 12.3 %collective-permute-start.4 = (bf16[64,1152]{1,0:T(8,128)(2,1)S(1)}, bf16[64,1152]{1,0:T(8,128)(2,1)S(1)}, u32[]{:S(2)}, u32[]{:S(2)}) collective-permute-start(bf16[64,1152]{1,0:T(8,128)(2,1)S(1)} %pad_maximum_fusion.1), channel_id=1, source_target_pairs={{0,8},{4,12},{8,0},{12,4},{1,9},{5,13},{9,1},{13,5},{2,10},{6,14},... | collective-permute-start | bytes 442376 | tf_op jit(solution)/shard_map/ppermute | solution.py:26
  7.5 9.7 %collective-permute-start.5 = (bf16[64,1152]{1,0:T(8,128)(2,1)S(1)}, bf16[64,1152]{1,0:T(8,128)(2,1)S(1)}, u32[]{:S(2)}, u32[]{:S(2)}) collective-permute-start(bf16[64,1152]{1,0:T(8,128)(2,1)S(1)} %pad_maximum_fusion.1), channel_id=1, source_target_pairs={{0,12},{4,0},{8,4},{12,8},{1,13},{5,1},{9,5},{13,9},{2,14},{6,2},{... | collective-permute-start | bytes 442376 | tf_op jit(solution)/shard_map/ppermute | solution.py:26
  17.3 11.0 %collective-permute-start.6 = (bf16[192,1024]{1,0:T(8,128)(2,1)S(1)}, bf16[192,1024]{1,0:T(8,128)(2,1)S(1)}, u32[]{:S(2)}, u32[]{:S(2)}) collective-permute-start(bf16[192,1024]{1,0:T(8,128)(2,1)S(1)} %get-tuple-element.25.refs_5_), channel_id=1, source_target_pairs={{0,1},{1,0},{2,3},{3,2},{4,5},{5,4},{6,7},{7,6},{8,9},{9,8},{10,11... | collective-permute-start | bytes 1179656 | tf_op jit(solution)/shard_map/ppermute | solution.py:21
  18.8 10.7 %collective-permute-start.7 = (bf16[192,1024]{1,0:T(8,128)(2,1)S(1)}, bf16[192,1024]{1,0:T(8,128)(2,1)S(1)}, u32[]{:S(2)}, u32[]{:S(2)}) collective-permute-start(bf16[192,1024]{1,0:T(8,128)(2,1)S(1)} %get-tuple-element.25.refs_5_), channel_id=1, source_target_pairs={{0,2},{1,3},{2,0},{3,1},{4,6},{5,7},{6,4},{7,5},{8,10},{9,11},{10,... | collective-permute-start | bytes 1179656 | tf_op jit(solution)/shard_map/ppermute | solution.py:21
  29.5 30.3 %collective-permute-start.8 = (bf16[192,1024]{1,0:T(8,128)(2,1)S(1)}, bf16[192,1024]{1,0:T(8,128)(2,1)S(1)}, u32[]{:S(2)}, u32[]{:S(2)}) collective-permute-start(bf16[192,1024]{1,0:T(8,128)(2,1)S(1)} %get-tuple-element.25.refs_5_), channel_id=1, source_target_pairs={{0,3},{1,2},{2,1},{3,0},{4,7},{5,6},{6,5},{7,4},{8,11},{9,10},{10,... | collective-permute-start | bytes 1179656 | tf_op jit(solution)/shard_map/ppermute | solution.py:21
  31.0 49.0 %collective-permute-start = (bf16[1024,256]{1,0:T(8,128)(2,1)S(1)}, bf16[1024,256]{1,0:T(8,128)(2,1)S(1)}, u32[]{:S(2)}, u32[]{:S(2)}) collective-permute-start(bf16[1024,256]{1,0:T(8,128)(2,1)S(1)} %constant_dynamic-slice_fusion), channel_id=1, source_target_pairs={{0,4},{4,8},{8,12},{12,0},{1,5},{5,9},{9,13},{13,1},{2,6},{6,10},{... | collective-permute-start | bytes 1572872 | tf_op jit(solution)/shard_map/ppermute | solution.py:26
  34.8 50.3 %collective-permute-start.1 = (bf16[1024,256]{1,0:T(8,128)(2,1)S(1)}, bf16[1024,256]{1,0:T(8,128)(2,1)S(1)}, u32[]{:S(2)}, u32[]{:S(2)}) collective-permute-start(bf16[1024,256]{1,0:T(8,128)(2,1)S(1)} %constant_dynamic-slice_fusion), channel_id=1, source_target_pairs={{0,8},{4,12},{8,0},{12,4},{1,9},{5,13},{9,1},{13,5},{2,10},{6,14},... | collective-permute-start | bytes 1572872 | tf_op jit(solution)/shard_map/ppermute | solution.py:26
  35.4 49.7 %collective-permute-start.2 = (bf16[1024,256]{1,0:T(8,128)(2,1)S(1)}, bf16[1024,256]{1,0:T(8,128)(2,1)}, u32[]{:S(2)}, u32[]{:S(2)}) collective-permute-start(bf16[1024,256]{1,0:T(8,128)(2,1)S(1)} %constant_dynamic-slice_fusion), channel_id=1, source_target_pairs={{0,12},{4,0},{8,4},{12,8},{1,13},{5,1},{9,5},{13,9},{2,14},{6,2},{... | collective-permute-start | bytes 1572872 | tf_op jit(solution)/shard_map/ppermute | solution.py:26
  38.0 5.2 %copy-start.3 = (bf16[1,64,4096]{2,1,0:T(8,128)(2,1)S(1)}, bf16[1,64,4096]{2,1,0:T(8,128)(2,1)}, u32[]{:S(2)}) copy-start(bf16[1,64,4096]{2,1,0:T(8,128)(2,1)} %param.13) | copy-start | bytes 1572868
  38.0 5.2 %copy-start.5 = (bf16[4096,32]{0,1:T(8,128)(2,1)S(1)}, bf16[4096,32]{0,1:T(8,128)(2,1)}, u32[]{:S(2)}) copy-start(bf16[4096,32]{0,1:T(8,128)(2,1)} %param.15) | copy-start | bytes 786436
  67.9 18.4 %collective-permute-start.9 = (bf16[256,1024]{1,0:T(8,128)(2,1)S(1)}, bf16[256,1024]{1,0:T(8,128)(2,1)S(1)}, u32[]{:S(2)}, u32[]{:S(2)}) collective-permute-start(bf16[256,1024]{1,0:T(8,128)(2,1)S(1)} %reduce.5), channel_id=1, source_target_pairs={{0,3},{1,2},{2,1},{3,0},{4,7},{5,6},{6,5},{7,4},{8,11},{9,10},{10,... | collective-permute-start | bytes 1572872 | tf_op jit(solution)/shard_map/ppermute | solution.py:21
  73.8 18.2 %collective-permute-start.10 = (bf16[256,1024]{1,0:T(8,128)(2,1)S(1)}, bf16[256,1024]{1,0:T(8,128)(2,1)S(1)}, u32[]{:S(2)}, u32[]{:S(2)}) collective-permute-start(bf16[256,1024]{1,0:T(8,128)(2,1)S(1)} %reduce.6), channel_id=1, source_target_pairs={{0,2},{1,3},{2,0},{3,1},{4,6},{5,7},{6,4},{7,5},{8,10},{9,11},{10,... | collective-permute-start | bytes 1572872 | tf_op jit(solution)/shard_map/ppermute | solution.py:21
  80.0 12.0 %collective-permute-start.11 = (bf16[256,1024]{1,0:T(8,128)(2,1)S(1)}, bf16[256,1024]{1,0:T(8,128)(2,1)S(1)}, u32[]{:S(2)}, u32[]{:S(2)}) collective-permute-start(bf16[256,1024]{1,0:T(8,128)(2,1)S(1)} %reduce.7), channel_id=1, source_target_pairs={{0,1},{1,0},{2,3},{3,2},{4,5},{5,4},{6,7},{7,6},{8,9},{9,8},{10,11... | collective-permute-start | bytes 1572872 | tf_op jit(solution)/shard_map/ppermute | solution.py:21
  85.1 30.6 %copy-start.8 = (f32[4096]{0:T(1024)S(1)}, f32[4096]{0:T(1024)}, u32[]{:S(2)}) copy-start(f32[4096]{0:T(1024)} %param.19) | copy-start | bytes 49156
  92.4 26.3 %copy-start.2 = (bf16[512,2048]{1,0:T(8,128)(2,1)S(1)}, bf16[512,2048]{1,0:T(8,128)(2,1)}, u32[]{:S(2)}) copy-start(bf16[512,2048]{1,0:T(8,128)(2,1)} %w_out.7) | copy-start | bytes 6291460
  92.4 26.2 %copy-start.4 = (bf16[1,256,512]{2,1,0:T(8,128)(2,1)S(1)}, bf16[1,256,512]{2,1,0:T(8,128)(2,1)}, u32[]{:S(2)}) copy-start(bf16[1,256,512]{2,1,0:T(8,128)(2,1)} %param.22) | copy-start | bytes 786436
  92.4 26.2 %copy-start.6 = (bf16[1,256,256]{2,1,0:T(8,128)(2,1)S(1)}, bf16[1,256,256]{2,1,0:T(8,128)(2,1)}, u32[]{:S(2)}) copy-start(bf16[1,256,256]{2,1,0:T(8,128)(2,1)} %param.23) | copy-start | bytes 393220
  92.4 26.2 %copy-start.7 = (bf16[1,256,256]{2,1,0:T(8,128)(2,1)S(1)}, bf16[1,256,256]{2,1,0:T(8,128)(2,1)}, u32[]{:S(2)}) copy-start(bf16[1,256,256]{2,1,0:T(8,128)(2,1)} %param.24) | copy-start | bytes 393220
  92.4 23.2 %collective-permute-start.18 = (bf16[4096,256]{1,0:T(8,128)(2,1)S(1)}, bf16[4096,256]{1,0:T(8,128)(2,1)S(1)}, u32[]{:S(2)}, u32[]{:S(2)}) collective-permute-start(bf16[4096,256]{1,0:T(8,128)(2,1)S(1)} %pad_maximum_fusion.refs_5_), channel_id=1, source_target_pairs={{0,16},{16,0},{1,17},{17,1},{2,18},{18,2},{3,19},{19,3},{4,20},{20... | collective-permute-start | bytes 6291464 | tf_op jit(solution)/shard_map/ppermute | solution.py:21
  92.5 6.4 %collective-permute-start.12 = (bf16[64,1024]{1,0:T(8,128)(2,1)S(1)}, bf16[64,1024]{1,0:T(8,128)(2,1)S(1)}, u32[]{:S(2)}, u32[]{:S(2)}) collective-permute-start(bf16[64,1024]{1,0:T(8,128)(2,1)S(1)} %get-tuple-element.45), channel_id=1, source_target_pairs={{0,12},{4,0},{8,4},{12,8},{1,13},{5,1},{9,5},{13,9},{2,14},{6,2},{... | collective-permute-start | bytes 393224 | tf_op jit(solution)/shard_map/ppermute | solution.py:26
  94.3 12.1 %collective-permute-start.13 = (bf16[64,1024]{1,0:T(8,128)(2,1)S(1)}, bf16[64,1024]{1,0:T(8,128)(2,1)S(1)}, u32[]{:S(2)}, u32[]{:S(2)}) collective-permute-start(bf16[64,1024]{1,0:T(8,128)(2,1)S(1)} %get-tuple-element.47), channel_id=1, source_target_pairs={{0,8},{4,12},{8,0},{12,4},{1,9},{5,13},{9,1},{13,5},{2,10},{6,14},... | collective-permute-start | bytes 393224 | tf_op jit(solution)/shard_map/ppermute | solution.py:26
  94.3 12.1 %collective-permute-start.14 = (bf16[64,1024]{1,0:T(8,128)(2,1)S(1)}, bf16[64,1024]{1,0:T(8,128)(2,1)S(1)}, u32[]{:S(2)}, u32[]{:S(2)}) collective-permute-start(bf16[64,1024]{1,0:T(8,128)(2,1)S(1)} %get-tuple-element.46), channel_id=1, source_target_pairs={{0,4},{4,8},{8,12},{12,0},{1,5},{5,9},{9,13},{13,1},{2,6},{6,10},{... | collective-permute-start | bytes 393224 | tf_op jit(solution)/shard_map/ppermute | solution.py:26
  106.5 5.6 %collective-permute-start.15 = (bf16[64,1024]{1,0:T(8,128)(2,1)S(1)}, bf16[64,1024]{1,0:T(8,128)(2,1)S(1)}, u32[]{:S(2)}, u32[]{:S(2)}) collective-permute-start(bf16[64,1024]{1,0:T(8,128)(2,1)S(1)} %add_convert_fusion.1.refs_0_), channel_id=1, source_target_pairs={{0,1},{1,0},{2,3},{3,2},{4,5},{5,4},{6,7},{7,6},{8,9},{9,8},{10,11... | collective-permute-start | bytes 393224 | tf_op jit(solution)/shard_map/ppermute | solution.py:21
  108.0 7.7 %collective-permute-start.16 = (bf16[64,1024]{1,0:T(8,128)(2,1)S(1)}, bf16[64,1024]{1,0:T(8,128)(2,1)S(1)}, u32[]{:S(2)}, u32[]{:S(2)}) collective-permute-start(bf16[64,1024]{1,0:T(8,128)(2,1)S(1)} %add_convert_fusion.1.refs_0_), channel_id=1, source_target_pairs={{0,2},{1,3},{2,0},{3,1},{4,6},{5,7},{6,4},{7,5},{8,10},{9,11},{10,... | collective-permute-start | bytes 393224 | tf_op jit(solution)/shard_map/ppermute | solution.py:21
  108.6 7.1 %collective-permute-start.17 = (bf16[64,1024]{1,0:T(8,128)(2,1)S(1)}, bf16[64,1024]{1,0:T(8,128)(2,1)S(1)}, u32[]{:S(2)}, u32[]{:S(2)}) collective-permute-start(bf16[64,1024]{1,0:T(8,128)(2,1)S(1)} %add_convert_fusion.1.refs_0_), channel_id=1, source_target_pairs={{0,3},{1,2},{2,1},{3,0},{4,7},{5,6},{6,5},{7,4},{8,11},{9,10},{10,... | collective-permute-start | bytes 393224 | tf_op jit(solution)/shard_map/ppermute | solution.py:21
  117.3 1.3 collective-permute-start.19
  120.3 10.2 %collective-permute-start.20 = (bf16[64,2048]{1,0:T(8,128)(2,1)S(1)}, bf16[64,2048]{1,0:T(8,128)(2,1)S(1)}, u32[]{:S(2)}, u32[]{:S(2)}) collective-permute-start(bf16[64,2048]{1,0:T(8,128)(2,1)S(1)} %attend.5), channel_id=1, source_target_pairs={{0,3},{1,2},{2,1},{3,0},{4,7},{5,6},{6,5},{7,4},{8,11},{9,10},{10,... | collective-permute-start | bytes 786440 | tf_op jit(solution)/shard_map/ppermute | solution.py:21
  121.5 14.6 %copy-start.1 = (bf16[1024,512]{1,0:T(8,128)(2,1)S(1)}, bf16[1024,512]{1,0:T(8,128)(2,1)}, u32[]{:S(2)}) copy-start(bf16[1024,512]{1,0:T(8,128)(2,1)} %param.20) | copy-start | bytes 3145732
  123.2 12.1 %collective-permute-start.21 = (bf16[64,2048]{1,0:T(8,128)(2,1)S(1)}, bf16[64,2048]{1,0:T(8,128)(2,1)S(1)}, u32[]{:S(2)}, u32[]{:S(2)}) collective-permute-start(bf16[64,2048]{1,0:T(8,128)(2,1)S(1)} %attend.6), channel_id=1, source_target_pairs={{0,2},{1,3},{2,0},{3,1},{4,6},{5,7},{6,4},{7,5},{8,10},{9,11},{10,... | collective-permute-start | bytes 786440 | tf_op jit(solution)/shard_map/ppermute | solution.py:21
  125.7 9.5 %collective-permute-start.22 = (bf16[64,2048]{1,0:T(8,128)(2,1)S(1)}, bf16[64,2048]{1,0:T(8,128)(2,1)S(1)}, u32[]{:S(2)}, u32[]{:S(2)}) collective-permute-start(bf16[64,2048]{1,0:T(8,128)(2,1)S(1)} %attend.7), channel_id=1, source_target_pairs={{0,1},{1,0},{2,3},{3,2},{4,5},{5,4},{6,7},{7,6},{8,9},{9,8},{10,11... | collective-permute-start | bytes 786440 | tf_op jit(solution)/shard_map/ppermute | solution.py:21

commit v7 on v6

--- a/solution.py
+++ b/solution.py
@@ -194,7 +194,7 @@
                     )
                 if streams and n == 0:
 
-                    @pl.when(e == (low + high) // 2)
+                    @pl.when(e == (low if top else (low + high) // 2))
                     def _():
                         for copy in copies:
                             copy.start()
@@ -270,7 +270,7 @@
         input_output_aliases=aliases,
         compiler_params=params(0, mebibytes if tokens <= 1024 else 32),
     )(place, *operands)
-    return outs[: len(items)], outs[len(items) :]
+    return list(outs[: len(items)]), outs[len(items) :]
 
 
 def reduce_kernel(place, hidden, w_down, out):
@@ -503,16 +503,17 @@
     )
     early = experts // 2
     got, totals = stage(
-        place, sources, [(PAIR, last, 0, early)] if early else [], own, router.T,
+        place, sources, [(PAIR, last, 0, early)] * (early > 0) + [(DOWN, far[0])], own, router.T,
         {k: others[k] for k in beside},
         [(0, experts, [(k, k != beside[0])]) for k in beside], got, totals,
     )
     pieces = [(0, early, [(last, False)])] if early else []
+    ahead = {far[0]: got.pop()}
     got, (hidden,) = stage(
-        place, sources, [(DOWN, far[0])], own, router.T, {last: others[last]},
+        place, sources, [(DOWN, far[1])], own, router.T, {last: others[last]},
         pieces + [(early, experts, [(last, True)])], got, totals, all_tags, top,
     )
-    ahead = {far[0]: got[0]}
+    ahead[far[1]] = got[0]
     partial = {}
     for k in far + [0]:
         if k in ahead:
@@ -533,7 +534,7 @@
     theirs = swap(mine, "pool", 1)
     moe_quarter = total_of(summed[:local], returned).astype(BF16)
     moe = [moe_quarter] + [None] * (parts - 1)
-    for k in order:
+    for k in far:
         moe[k] = swap(moe_quarter, "half", k)
     keyvals = project(place, own, moe, norm_gain[None], mine, theirs, eps)
     block = swap(keyvals, "pool", 1)

time: 136 us -> 141 us (1.037)
  waiting for transfers between devices: 47.7 us -> 53.9 us
  Pallas kernels: 51.5 us -> 48.8 us
    ppermute x14, waiting for transfers between devices: 28.1 us -> 36.3 us  [swap(): lax.ppermute(shard, axis, [(i, i ^ bits) for i in range(lax.axis_size(axi...]
    pallas_call x3 -> x2, Pallas kernels: 13.5 us -> 8.98 us  [reduce(): pl.pallas_call(reduce_kernel, out_shape=jax.ShapeDtypeStruct((tokens, wid...]
    ppermute x9, waiting for transfers between devices: 19.6 us -> 17.5 us  [shift(): lax.ppermute(shard, axis, [(i, (i + distance) % count) for i in range(cou...]
    pallas_call x1 -> x2, Pallas kernels: 1.78 us -> 3.56 us  [reduce_ahead(): pl.pallas_call(reduce_ahead_kernel, out_shape=jax.ShapeDtypeStruct((hidde...]
  transfers between devices with their start and end apart: 23 -> 23, of which waited for: 12 -> 12; matrix products, arithmetic and copies ran while one was open for 2% -> 1% of each run, Pallas kernels for 35% -> 32%
where the time goes in v7:
time: 141 us
  waiting for transfers between devices  53.9 us (38%)
  Pallas kernels  48.8 us (35%)
  starting transfers between devices  32.8 us (23%)
  other arithmetic  2.57 us (2%)
  local copies, waits for them, and re-layouts  2.55 us (2%)
    ppermute x14, waiting for transfers between devices, swap(): lax.ppermute(shard, axis, [(i, i ^ bits) for i in range(lax.axis_size(axi...  36.3 us
    pallas_call x4, Pallas kernels, stage(): pl.pallas_call(functools.partial(stage_kernel, items, quarters, parts, no...  28.1 us
    ppermute x9, waiting for transfers between devices, shift(): lax.ppermute(shard, axis, [(i, (i + distance) % count) for i in range(cou...  17.5 us
    ppermute x9, starting transfers between devices, shift(): lax.ppermute(shard, axis, [(i, (i + distance) % count) for i in range(cou...  17.1 us
    ppermute x14, starting transfers between devices, swap(): lax.ppermute(shard, axis, [(i, i ^ bits) for i in range(lax.axis_size(axi...  15.6 us
    pallas_call x2, Pallas kernels, reduce(): pl.pallas_call(reduce_kernel, out_shape=jax.ShapeDtypeStruct((tokens, wid...  8.98 us
    pallas_call x4, Pallas kernels, attend(): pl.pallas_call(functools.partial(attend_kernel, k, prompts), out_shape=ja...  6.49 us
    pallas_call x2, Pallas kernels, reduce_ahead(): pl.pallas_call(reduce_ahead_kernel, out_shape=jax.ShapeDtypeStruct((hidde...  3.56 us
  transfers between devices with their start and end apart: 23, of which 12 were waited for; matrix products, arithmetic and copies ran while one was open for 1% of the time, Pallas kernels for 32%

profile of v7, /device:TPU:0, one launch (start us, length us, event | category | flops | bytes accessed | tf_op | source)
XLA Modules:
  0.0 140.8 jit_solution(5644812724922136192)
XLA Ops:
  1.8 3.1 %collective-permute-start.3 = (bf16[64,1152]{1,0:T(8,128)(2,1)S(1)}, bf16[64,1152]{1,0:T(8,128)(2,1)S(1)}, u32[]{:S(2)}, u32[]{:S(2)}) collective-permute-start(bf16[64,1152]{1,0:T(8,128)(2,1)S(1)} %pad_maximum_fusion.1), channel_id=1, source_target_pairs={{0,4},{4,8},{8,12},{12,0},{1,5},{5,9},{9,13},{13,1},{2,6},{6,10},{... | collective-permute-start | bytes 442376 | tf_op jit(solution)/shard_map/ppermute | solution.py:26
  4.9 2.6 %collective-permute-start.4 = (bf16[64,1152]{1,0:T(8,128)(2,1)S(1)}, bf16[64,1152]{1,0:T(8,128)(2,1)S(1)}, u32[]{:S(2)}, u32[]{:S(2)}) collective-permute-start(bf16[64,1152]{1,0:T(8,128)(2,1)S(1)} %pad_maximum_fusion.1), channel_id=1, source_target_pairs={{0,8},{4,12},{8,0},{12,4},{1,9},{5,13},{9,1},{13,5},{2,10},{6,14},... | collective-permute-start | bytes 442376 | tf_op jit(solution)/shard_map/ppermute | solution.py:26
  8.9 2.9 %collective-permute-done.3.refs_0_ = bf16[64,1152]{1,0:T(8,128)(2,1)S(1)} collective-permute-done((bf16[64,1152]{1,0:T(8,128)(2,1)S(1)}, bf16[64,1152]{1,0:T(8,128)(2,1)S(1)}, u32[]{:S(2)}, u32[]{:S(2)}) %collective-permute-start.3) | collective-permute-done | bytes 147488 | tf_op jit(solution)/shard_map/ppermute | solution.py:26
  11.8 5.5 %collective-permute-done.4.refs_1_ = bf16[64,1152]{1,0:T(8,128)(2,1)S(1)} collective-permute-done((bf16[64,1152]{1,0:T(8,128)(2,1)S(1)}, bf16[64,1152]{1,0:T(8,128)(2,1)S(1)}, u32[]{:S(2)}, u32[]{:S(2)}) %collective-permute-start.4) | collective-permute-done | bytes 147488 | tf_op jit(solution)/shard_map/ppermute | solution.py:26
  20.3 7.9 %collective-permute-done.6.refs_5_ = bf16[192,1024]{1,0:T(8,128)(2,1)S(1)} collective-permute-done((bf16[192,1024]{1,0:T(8,128)(2,1)S(1)}, bf16[192,1024]{1,0:T(8,128)(2,1)S(1)}, u32[]{:S(2)}, u32[]{:S(2)}) %collective-permute-start.6) | collective-permute-done | bytes 393248 | tf_op jit(solution)/shard_map/ppermute | solution.py:21
  31.0 3.8 %collective-permute-start = (bf16[1024,256]{1,0:T(8,128)(2,1)S(1)}, bf16[1024,256]{1,0:T(8,128)(2,1)S(1)}, u32[]{:S(2)}, u32[]{:S(2)}) collective-permute-start(bf16[1024,256]{1,0:T(8,128)(2,1)S(1)} %constant_dynamic-slice_fusion), channel_id=1, source_target_pairs={{0,4},{4,8},{8,12},{12,0},{1,5},{5,9},{9,13},{13,1},{2,6},{6,10},{... | collective-permute-start | bytes 1572872 | tf_op jit(solution)/shard_map/ppermute | solution.py:26
  35.4 1.8 %collective-permute-start.2 = (bf16[1024,256]{1,0:T(8,128)(2,1)S(1)}, bf16[1024,256]{1,0:T(8,128)(2,1)}, u32[]{:S(2)}, u32[]{:S(2)}) collective-permute-start(bf16[1024,256]{1,0:T(8,128)(2,1)S(1)} %constant_dynamic-slice_fusion), channel_id=1, source_target_pairs={{0,12},{4,0},{8,4},{12,8},{1,13},{5,1},{9,5},{13,9},{2,14},{6,2},{... | collective-permute-start | bytes 1572872 | tf_op jit(solution)/shard_map/ppermute | solution.py:26
  38.0 5.2 %shard_map.127.refs_6_ = bf16[16,1024,384]{2,1,0:T(8,128)(2,1)S(1)} custom-call(s32[5]{0:T(128)S(1)} %pad_add_fusion.place, bf16[8,4096,384]{2,1,0:T(8,128)(2,1)} %refs_0_.7, bf16[8,4096,384]{2,1,0:T(8,128)(2,1)} %refs_1_.7, bf16[8,384,4096]{2,1,0:T(8,128)(2,1)} %w_down.3), custom_call_target="tpu_custom_call" | custom-call | tf_op jit(solution)/shard_map/pallas_call | solution.py:260
  43.2 5.3 %shard_map.128 = (bf16[16,1024,384]{2,1,0:T(8,128)(2,1)S(1)}, f32[8,256,768]{2,1,0:T(8,128)S(1)}, f32[256,32]{1,0:T(8,128)S(1)}) custom-call(s32[5]{0:T(128)S(1)} %pad_add_fusion.place, bf16[8,4096,384]{2,1,0:T(8,128)(2,1)} %refs_0_.7, bf16[8,4096,384]{2,1,0:T(8,128)(2,1)} %refs_1_.7, bf16[8,384,4096]{2,1,0:T(8,128)(2,1)} %w_down.3, ...), custom_call_target="tpu_custom_call" | custom-call | tf_op jit(solution)/shard_map/pallas_call | solution.py:260
  48.5 11.3 %shard_map.129 = (bf16[8,1024,384]{2,1,0:T(8,128)(2,1)S(1)}, bf16[8,384,1024]{2,1,0:T(8,128)(2,1)S(1)}, f32[8,256,768]{2,1,0:T(8,128)S(1)}, f32[256,32]{1,0:T(8,128)S(1)}) custom-call(s32[5]{0:T(128)S(1)} %pad_add_fusion.place, bf16[8,4096,384]{2,1,0:T(8,128)(2,1)} %refs_0_.7, ...), custom_call_target="tpu_custom_call", output_to_operand_aliasing={{2}: (9, {}), {3}: (10, {})} | custom-call | tf_op jit(solution)/shard_map/pallas_call | solution.py:260
  59.8 6.3 %shard_map.130 = (bf16[8,384,1024]{2,1,0:T(8,128)(2,1)S(1)}, bf16[256,3072]{1,0:T(8,128)(2,1)S(1)}) custom-call(s32[5]{0:T(128)S(1)} %pad_add_fusion.place, bf16[8,4096,384]{2,1,0:T(8,128)(2,1)} %refs_0_.7, bf16[8,4096,384]{2,1,0:T(8,128)(2,1)} %refs_1_.7, bf16[8,384,4096]{2,1,0:T(8,128)(2,1)} %w_down.3, bf16[64,4096]{1,0:T(8,128)(2,1)S(1)} %bitcast.19, ...), custom_call_target="tpu_custom_call" | custom-call | tf_op jit(solution)/shard_map/pallas_call | solution.py:260
  66.1 4.5 %reduce.7 = bf16[256,1024]{1,0:T(8,128)(2,1)S(1)} custom-call(s32[5]{0:T(128)S(1)} %pad_add_fusion.place, bf16[256,3072]{1,0:T(8,128)(2,1)S(1)} %get-tuple-element.36.hidden, bf16[8,384,4096]{2,1,0:T(8,128)(2,1)} %w_down.3), custom_call_target="tpu_custom_call" | custom-call | flops 1610612736 | bytes 6291456 | tf_op jit(solution)/shard_map/reduce/pallas_call | solution.py:304
  72.2 1.8 %reduce.6 = bf16[256,1024]{1,0:T(8,128)(2,1)S(1)} custom-call(bf16[256,3072]{1,0:T(8,128)(2,1)S(1)} %get-tuple-element.36.hidden, bf16[8,384,1024]{2,1,0:T(8,128)(2,1)S(1)} %get-tuple-element.42.weight), custom_call_target="tpu_custom_call" | custom-call | tf_op jit(solution)/shard_map/reduce/pallas_call | solution.py:290
  74.5 1.8 %reduce.5 = bf16[256,1024]{1,0:T(8,128)(2,1)S(1)} custom-call(bf16[256,3072]{1,0:T(8,128)(2,1)S(1)} %get-tuple-element.36.hidden, bf16[8,384,1024]{2,1,0:T(8,128)(2,1)S(1)} %get-tuple-element.41.weight), custom_call_target="tpu_custom_call" | custom-call | tf_op jit(solution)/shard_map/reduce/pallas_call | solution.py:290
  76.3 1.6 %collective-permute-start.9 = (bf16[256,1024]{1,0:T(8,128)(2,1)S(1)}, bf16[256,1024]{1,0:T(8,128)(2,1)S(1)}, u32[]{:S(2)}, u32[]{:S(2)}) collective-permute-start(bf16[256,1024]{1,0:T(8,128)(2,1)S(1)} %reduce.5), channel_id=1, source_target_pairs={{0,3},{1,2},{2,1},{3,0},{4,7},{5,6},{6,5},{7,4},{8,11},{9,10},{10,... | collective-permute-start | bytes 1572872 | tf_op jit(solution)/shard_map/ppermute | solution.py:21
  77.9 4.5 %reduce.4 = bf16[256,1024]{1,0:T(8,128)(2,1)S(1)} custom-call(s32[5]{0:T(128)S(1)} %pad_add_fusion.place, bf16[256,3072]{1,0:T(8,128)(2,1)S(1)} %get-tuple-element.36.hidden, bf16[8,384,4096]{2,1,0:T(8,128)(2,1)} %w_down.3), custom_call_target="tpu_custom_call" | custom-call | flops 1610612736 | bytes 6291456 | tf_op jit(solution)/shard_map/reduce/pallas_call | solution.py:304
  83.6 1.9 %collective-permute-done.11 = bf16[256,1024]{1,0:T(8,128)(2,1)S(1)} collective-permute-done((bf16[256,1024]{1,0:T(8,128)(2,1)S(1)}, bf16[256,1024]{1,0:T(8,128)(2,1)S(1)}, u32[]{:S(2)}, u32[]{:S(2)}) %collective-permute-start.11) | collective-permute-done | bytes 524320 | tf_op jit(solution)/shard_map/ppermute | solution.py:21
  85.5 11.4 %collective-permute-done.10 = bf16[256,1024]{1,0:T(8,128)(2,1)S(1)} collective-permute-done((bf16[256,1024]{1,0:T(8,128)(2,1)S(1)}, bf16[256,1024]{1,0:T(8,128)(2,1)S(1)}, u32[]{:S(2)}, u32[]{:S(2)}) %collective-permute-start.10) | collective-permute-done | bytes 524320 | tf_op jit(solution)/shard_map/ppermute | solution.py:21
  97.5 2.2 %collective-permute-start.13 = (bf16[64,1024]{1,0:T(8,128)(2,1)S(1)}, bf16[64,1024]{1,0:T(8,128)(2,1)S(1)}, u32[]{:S(2)}, u32[]{:S(2)}) collective-permute-start(bf16[64,1024]{1,0:T(8,128)(2,1)S(1)} %get-tuple-element.49), channel_id=1, source_target_pairs={{0,8},{4,12},{8,0},{12,4},{1,9},{5,13},{9,1},{13,5},{2,10},{6,14},... | collective-permute-start | bytes 393224 | tf_op jit(solution)/shard_map/ppermute | solution.py:26
  99.7 1.6 %collective-permute-start.12 = (bf16[64,1024]{1,0:T(8,128)(2,1)S(1)}, bf16[64,1024]{1,0:T(8,128)(2,1)S(1)}, u32[]{:S(2)}, u32[]{:S(2)}) collective-permute-start(bf16[64,1024]{1,0:T(8,128)(2,1)S(1)} %get-tuple-element.47), channel_id=1, source_target_pairs={{0,12},{4,0},{8,4},{12,8},{1,13},{5,1},{9,5},{13,9},{2,14},{6,2},{... | collective-permute-start | bytes 393224 | tf_op jit(solution)/shard_map/ppermute | solution.py:26
  101.3 4.5 %collective-permute-done.14 = bf16[64,1024]{1,0:T(8,128)(2,1)S(1)} collective-permute-done((bf16[64,1024]{1,0:T(8,128)(2,1)S(1)}, bf16[64,1024]{1,0:T(8,128)(2,1)S(1)}, u32[]{:S(2)}, u32[]{:S(2)}) %collective-permute-start.14) | collective-permute-done | bytes 131104 | tf_op jit(solution)/shard_map/ppermute | solution.py:26
  105.8 4.7 %collective-permute-done.13 = bf16[64,1024]{1,0:T(8,128)(2,1)S(1)} collective-permute-done((bf16[64,1024]{1,0:T(8,128)(2,1)S(1)}, bf16[64,1024]{1,0:T(8,128)(2,1)S(1)}, u32[]{:S(2)}, u32[]{:S(2)}) %collective-permute-start.13) | collective-permute-done | bytes 131104 | tf_op jit(solution)/shard_map/ppermute | solution.py:26
  111.6 2.5 %collective-permute-start.17 = (bf16[64,1024]{1,0:T(8,128)(2,1)S(1)}, bf16[64,1024]{1,0:T(8,128)(2,1)S(1)}, u32[]{:S(2)}, u32[]{:S(2)}) collective-permute-start(bf16[64,1024]{1,0:T(8,128)(2,1)S(1)} %add_convert_fusion.1.refs_0_), channel_id=1, source_target_pairs={{0,3},{1,2},{2,1},{3,0},{4,7},{5,6},{6,5},{7,4},{8,11},{9,10},{10,... | collective-permute-start | bytes 393224 | tf_op jit(solution)/shard_map/ppermute | solution.py:21
  114.1 2.5 %collective-permute-done.15.refs_1_ = bf16[64,1024]{1,0:T(8,128)(2,1)S(1)} collective-permute-done((bf16[64,1024]{1,0:T(8,128)(2,1)S(1)}, bf16[64,1024]{1,0:T(8,128)(2,1)S(1)}, u32[]{:S(2)}, u32[]{:S(2)}) %collective-permute-start.15) | collective-permute-done | bytes 131104 | tf_op jit(solution)/shard_map/ppermute | solution.py:21
  116.6 1.6 %collective-permute-done.16.refs_2_ = bf16[64,1024]{1,0:T(8,128)(2,1)S(1)} collective-permute-done((bf16[64,1024]{1,0:T(8,128)(2,1)S(1)}, bf16[64,1024]{1,0:T(8,128)(2,1)S(1)}, u32[]{:S(2)}, u32[]{:S(2)}) %collective-permute-start.16) | collective-permute-done | bytes 131104 | tf_op jit(solution)/shard_map/ppermute | solution.py:21
  118.3 1.6 %project.1 = bf16[64,512]{1,0:T(8,128)(2,1)S(1)} custom-call(s32[5]{0:T(128)S(1)} %pad_add_fusion.place, bf16[64,4096]{1,0:T(8,128)(2,1)S(1)} %bitcast.20, bf16[64,1024]{1,0:T(8,128)(2,1)S(1)} %add_convert_fusion.1.refs_0_, bf16[64,1024]{1,0:T(8,128)(2,1)S(1)} %collective-permute-done.15.refs_1_, bf16[64,1024]{1,0:T(8,128)(2,1)S(1)} %collective-permute-done.16.refs_2_, ...), custom_call_target="tpu_custom_call" | custom-call | tf_op jit(solution)/shard_map/project/pallas_call | solution.py:355
  121.3 1.6 %attend.7 = bf16[64,2048]{1,0:T(8,128)(2,1)S(1)} custom-call(s32[5]{0:T(128)S(1)} %pad_add_fusion.place, bf16[64,512]{1,0:T(8,128)(2,1)S(1)} %collective-permute-done.19.block, bf16[256,512]{1,0:T(8,128)(2,1)S(1)} %bitcast.21, bf16[256,256]{1,0:T(8,128)(2,1)S(1)} %bitcast.28, bf16[256,256]{1,0:T(8,128)(2,1)S(1)} %bitcast.32, bf16[512,2048]{1,0:T(8,128)(2,1)S(1)} %copy-done.2), custom_call_target="tpu_custom_call" | custom-call | flops 268435456 | bytes 2097152 | tf_op jit(solution)/shard_map/attend/pallas_call | solution.py:429
  122.9 1.7 %collective-permute-start.22 = (bf16[64,2048]{1,0:T(8,128)(2,1)S(1)}, bf16[64,2048]{1,0:T(8,128)(2,1)S(1)}, u32[]{:S(2)}, u32[]{:S(2)}) collective-permute-start(bf16[64,2048]{1,0:T(8,128)(2,1)S(1)} %attend.7), channel_id=1, source_target_pairs={{0,1},{1,0},{2,3},{3,2},{4,5},{5,4},{6,7},{7,6},{8,9},{9,8},{10,11... | collective-permute-start | bytes 786440 | tf_op jit(solution)/shard_map/ppermute | solution.py:21
  124.6 1.6 %attend.6 = bf16[64,2048]{1,0:T(8,128)(2,1)S(1)} custom-call(s32[5]{0:T(128)S(1)} %pad_add_fusion.place, bf16[64,512]{1,0:T(8,128)(2,1)S(1)} %collective-permute-done.19.block, bf16[256,512]{1,0:T(8,128)(2,1)S(1)} %bitcast.22, bf16[256,256]{1,0:T(8,128)(2,1)S(1)} %bitcast.29, bf16[256,256]{1,0:T(8,128)(2,1)S(1)} %bitcast.33, bf16[512,2048]{1,0:T(8,128)(2,1)S(1)} %copy-done.2), custom_call_target="tpu_custom_call" | custom-call | flops 268435456 | bytes 2097152 | tf_op jit(solution)/shard_map/attend/pallas_call | solution.py:429
  127.3 1.6 %attend.5 = bf16[64,2048]{1,0:T(8,128)(2,1)S(1)} custom-call(s32[5]{0:T(128)S(1)} %pad_add_fusion.place, bf16[64,512]{1,0:T(8,128)(2,1)S(1)} %collective-permute-done.19.block, bf16[256,512]{1,0:T(8,128)(2,1)S(1)} %bitcast.23, bf16[256,256]{1,0:T(8,128)(2,1)S(1)} %bitcast.30, bf16[256,256]{1,0:T(8,128)(2,1)S(1)} %bitcast.34, bf16[512,2048]{1,0:T(8,128)(2,1)S(1)} %copy-done.2), custom_call_target="tpu_custom_call" | custom-call | flops 268435456 | bytes 2097152 | tf_op jit(solution)/shard_map/attend/pallas_call | solution.py:429
  129.8 1.6 %attend.4 = bf16[64,2048]{1,0:T(8,128)(2,1)S(1)} custom-call(s32[5]{0:T(128)S(1)} %pad_add_fusion.place, bf16[64,512]{1,0:T(8,128)(2,1)S(1)} %collective-permute-done.19.block, bf16[256,512]{1,0:T(8,128)(2,1)S(1)} %bitcast.24, bf16[256,256]{1,0:T(8,128)(2,1)S(1)} %bitcast.31, bf16[256,256]{1,0:T(8,128)(2,1)S(1)} %bitcast.35, bf16[512,2048]{1,0:T(8,128)(2,1)S(1)} %copy-done.2), custom_call_target="tpu_custom_call" | custom-call | flops 268435456 | bytes 2097152 | tf_op jit(solution)/shard_map/attend/pallas_call | solution.py:429
  131.5 8.5 %collective-permute-done.21 = bf16[64,2048]{1,0:T(8,128)(2,1)S(1)} collective-permute-done((bf16[64,2048]{1,0:T(8,128)(2,1)S(1)}, bf16[64,2048]{1,0:T(8,128)(2,1)S(1)}, u32[]{:S(2)}, u32[]{:S(2)}) %collective-permute-start.21) | collective-permute-done | bytes 262176 | tf_op jit(solution)/shard_map/ppermute | solution.py:21
  (59 shorter events, 19.5 us)
Async XLA Ops:
  0.0 31.0 %copy-start = (bf16[1024,512]{1,0:T(8,128)(2,1)S(1)}, bf16[1024,512]{1,0:T(8,128)(2,1)}, u32[]{:S(2)}) copy-start(bf16[1024,512]{1,0:T(8,128)(2,1)} %param.20) | copy-start | bytes 3145732
  1.8 9.9 %collective-permute-start.3 = (bf16[64,1152]{1,0:T(8,128)(2,1)S(1)}, bf16[64,1152]{1,0:T(8,128)(2,1)S(1)}, u32[]{:S(2)}, u32[]{:S(2)}) collective-permute-start(bf16[64,1152]{1,0:T(8,128)(2,1)S(1)} %pad_maximum_fusion.1), channel_id=1, source_target_pairs={{0,4},{4,8},{8,12},{12,0},{1,5},{5,9},{9,13},{13,1},{2,6},{6,10},{... | collective-permute-start | bytes 442376 | tf_op jit(solution)/shard_map/ppermute | solution.py:26
  4.9 12.3 %collective-permute-start.4 = (bf16[64,1152]{1,0:T(8,128)(2,1)S(1)}, bf16[64,1152]{1,0:T(8,128)(2,1)S(1)}, u32[]{:S(2)}, u32[]{:S(2)}) collective-permute-start(bf16[64,1152]{1,0:T(8,128)(2,1)S(1)} %pad_maximum_fusion.1), channel_id=1, source_target_pairs={{0,8},{4,12},{8,0},{12,4},{1,9},{5,13},{9,1},{13,5},{2,10},{6,14},... | collective-permute-start | bytes 442376 | tf_op jit(solution)/shard_map/ppermute | solution.py:26
  7.5 9.7 %collective-permute-start.5 = (bf16[64,1152]{1,0:T(8,128)(2,1)S(1)}, bf16[64,1152]{1,0:T(8,128)(2,1)S(1)}, u32[]{:S(2)}, u32[]{:S(2)}) collective-permute-start(bf16[64,1152]{1,0:T(8,128)(2,1)S(1)} %pad_maximum_fusion.1), channel_id=1, source_target_pairs={{0,12},{4,0},{8,4},{12,8},{1,13},{5,1},{9,5},{13,9},{2,14},{6,2},{... | collective-permute-start | bytes 442376 | tf_op jit(solution)/shard_map/ppermute | solution.py:26
  17.3 11.0 %collective-permute-start.6 = (bf16[192,1024]{1,0:T(8,128)(2,1)S(1)}, bf16[192,1024]{1,0:T(8,128)(2,1)S(1)}, u32[]{:S(2)}, u32[]{:S(2)}) collective-permute-start(bf16[192,1024]{1,0:T(8,128)(2,1)S(1)} %get-tuple-element.26.refs_5_), channel_id=1, source_target_pairs={{0,1},{1,0},{2,3},{3,2},{4,5},{5,4},{6,7},{7,6},{8,9},{9,8},{10,11... | collective-permute-start | bytes 1179656 | tf_op jit(solution)/shard_map/ppermute | solution.py:21
  18.8 10.7 %collective-permute-start.7 = (bf16[192,1024]{1,0:T(8,128)(2,1)S(1)}, bf16[192,1024]{1,0:T(8,128)(2,1)S(1)}, u32[]{:S(2)}, u32[]{:S(2)}) collective-permute-start(bf16[192,1024]{1,0:T(8,128)(2,1)S(1)} %get-tuple-element.26.refs_5_), channel_id=1, source_target_pairs={{0,2},{1,3},{2,0},{3,1},{4,6},{5,7},{6,4},{7,5},{8,10},{9,11},{10,... | collective-permute-start | bytes 1179656 | tf_op jit(solution)/shard_map/ppermute | solution.py:21
  29.5 30.3 %collective-permute-start.8 = (bf16[192,1024]{1,0:T(8,128)(2,1)S(1)}, bf16[192,1024]{1,0:T(8,128)(2,1)S(1)}, u32[]{:S(2)}, u32[]{:S(2)}) collective-permute-start(bf16[192,1024]{1,0:T(8,128)(2,1)S(1)} %get-tuple-element.26.refs_5_), channel_id=1, source_target_pairs={{0,3},{1,2},{2,1},{3,0},{4,7},{5,6},{6,5},{7,4},{8,11},{9,10},{10,... | collective-permute-start | bytes 1179656 | tf_op jit(solution)/shard_map/ppermute | solution.py:21
  31.0 45.3 %collective-permute-start = (bf16[1024,256]{1,0:T(8,128)(2,1)S(1)}, bf16[1024,256]{1,0:T(8,128)(2,1)S(1)}, u32[]{:S(2)}, u32[]{:S(2)}) collective-permute-start(bf16[1024,256]{1,0:T(8,128)(2,1)S(1)} %constant_dynamic-slice_fusion), channel_id=1, source_target_pairs={{0,4},{4,8},{8,12},{12,0},{1,5},{5,9},{9,13},{13,1},{2,6},{6,10},{... | collective-permute-start | bytes 1572872 | tf_op jit(solution)/shard_map/ppermute | solution.py:26
  34.8 47.6 %collective-permute-start.1 = (bf16[1024,256]{1,0:T(8,128)(2,1)S(1)}, bf16[1024,256]{1,0:T(8,128)(2,1)S(1)}, u32[]{:S(2)}, u32[]{:S(2)}) collective-permute-start(bf16[1024,256]{1,0:T(8,128)(2,1)S(1)} %constant_dynamic-slice_fusion), channel_id=1, source_target_pairs={{0,8},{4,12},{8,0},{12,4},{1,9},{5,13},{9,1},{13,5},{2,10},{6,14},... | collective-permute-start | bytes 1572872 | tf_op jit(solution)/shard_map/ppermute | solution.py:26
  35.4 47.0 %collective-permute-start.2 = (bf16[1024,256]{1,0:T(8,128)(2,1)S(1)}, bf16[1024,256]{1,0:T(8,128)(2,1)}, u32[]{:S(2)}, u32[]{:S(2)}) collective-permute-start(bf16[1024,256]{1,0:T(8,128)(2,1)S(1)} %constant_dynamic-slice_fusion), channel_id=1, source_target_pairs={{0,12},{4,0},{8,4},{12,8},{1,13},{5,1},{9,5},{13,9},{2,14},{6,2},{... | collective-permute-start | bytes 1572872 | tf_op jit(solution)/shard_map/ppermute | solution.py:26
  38.0 5.2 %copy-start.3 = (bf16[1,64,4096]{2,1,0:T(8,128)(2,1)S(1)}, bf16[1,64,4096]{2,1,0:T(8,128)(2,1)}, u32[]{:S(2)}) copy-start(bf16[1,64,4096]{2,1,0:T(8,128)(2,1)} %param.13) | copy-start | bytes 1572868
  38.0 5.2 %copy-start.5 = (bf16[4096,32]{0,1:T(8,128)(2,1)S(1)}, bf16[4096,32]{0,1:T(8,128)(2,1)}, u32[]{:S(2)}) copy-start(bf16[4096,32]{0,1:T(8,128)(2,1)} %param.15) | copy-start | bytes 786436
  70.6 14.9 %collective-permute-start.11 = (bf16[256,1024]{1,0:T(8,128)(2,1)S(1)}, bf16[256,1024]{1,0:T(8,128)(2,1)S(1)}, u32[]{:S(2)}, u32[]{:S(2)}) collective-permute-start(bf16[256,1024]{1,0:T(8,128)(2,1)S(1)} %reduce.7), channel_id=1, source_target_pairs={{0,1},{1,0},{2,3},{3,2},{4,5},{5,4},{6,7},{7,6},{8,9},{9,8},{10,11... | collective-permute-start | bytes 1572872 | tf_op jit(solution)/shard_map/ppermute | solution.py:21
  74.0 22.9 %collective-permute-start.10 = (bf16[256,1024]{1,0:T(8,128)(2,1)S(1)}, bf16[256,1024]{1,0:T(8,128)(2,1)S(1)}, u32[]{:S(2)}, u32[]{:S(2)}) collective-permute-start(bf16[256,1024]{1,0:T(8,128)(2,1)S(1)} %reduce.6), channel_id=1, source_target_pairs={{0,2},{1,3},{2,0},{3,1},{4,6},{5,7},{6,4},{7,5},{8,10},{9,11},{10,... | collective-permute-start | bytes 1572872 | tf_op jit(solution)/shard_map/ppermute | solution.py:21
  76.3 20.6 %collective-permute-start.9 = (bf16[256,1024]{1,0:T(8,128)(2,1)S(1)}, bf16[256,1024]{1,0:T(8,128)(2,1)S(1)}, u32[]{:S(2)}, u32[]{:S(2)}) collective-permute-start(bf16[256,1024]{1,0:T(8,128)(2,1)S(1)} %reduce.5), channel_id=1, source_target_pairs={{0,3},{1,2},{2,1},{3,0},{4,7},{5,6},{6,5},{7,4},{8,11},{9,10},{10,... | collective-permute-start | bytes 1572872 | tf_op jit(solution)/shard_map/ppermute | solution.py:21
  82.4 35.9 %copy-start.8 = (f32[4096]{0:T(1024)S(1)}, f32[4096]{0:T(1024)}, u32[]{:S(2)}) copy-start(f32[4096]{0:T(1024)} %param.19) | copy-start | bytes 49156
  97.2 24.0 %copy-start.2 = (bf16[512,2048]{1,0:T(8,128)(2,1)S(1)}, bf16[512,2048]{1,0:T(8,128)(2,1)}, u32[]{:S(2)}) copy-start(bf16[512,2048]{1,0:T(8,128)(2,1)} %w_out.7) | copy-start | bytes 6291460
  97.3 24.0 %copy-start.4 = (bf16[1,256,512]{2,1,0:T(8,128)(2,1)S(1)}, bf16[1,256,512]{2,1,0:T(8,128)(2,1)}, u32[]{:S(2)}) copy-start(bf16[1,256,512]{2,1,0:T(8,128)(2,1)} %param.22) | copy-start | bytes 786436
  97.3 24.0 %copy-start.6 = (bf16[1,256,256]{2,1,0:T(8,128)(2,1)S(1)}, bf16[1,256,256]{2,1,0:T(8,128)(2,1)}, u32[]{:S(2)}) copy-start(bf16[1,256,256]{2,1,0:T(8,128)(2,1)} %param.23) | copy-start | bytes 393220
  97.3 24.0 %copy-start.7 = (bf16[1,256,256]{2,1,0:T(8,128)(2,1)S(1)}, bf16[1,256,256]{2,1,0:T(8,128)(2,1)}, u32[]{:S(2)}) copy-start(bf16[1,256,256]{2,1,0:T(8,128)(2,1)} %param.24) | copy-start | bytes 393220
  97.3 21.0 %collective-permute-start.18 = (bf16[4096,256]{1,0:T(8,128)(2,1)S(1)}, bf16[4096,256]{1,0:T(8,128)(2,1)S(1)}, u32[]{:S(2)}, u32[]{:S(2)}) collective-permute-start(bf16[4096,256]{1,0:T(8,128)(2,1)S(1)} %pad_maximum_fusion.refs_5_), channel_id=1, source_target_pairs={{0,16},{16,0},{1,17},{17,1},{2,18},{18,2},{3,19},{19,3},{4,20},{20... | collective-permute-start | bytes 6291464 | tf_op jit(solution)/shard_map/ppermute | solution.py:21
  97.4 8.4 %collective-permute-start.14 = (bf16[64,1024]{1,0:T(8,128)(2,1)S(1)}, bf16[64,1024]{1,0:T(8,128)(2,1)S(1)}, u32[]{:S(2)}, u32[]{:S(2)}) collective-permute-start(bf16[64,1024]{1,0:T(8,128)(2,1)S(1)} %get-tuple-element.48), channel_id=1, source_target_pairs={{0,4},{4,8},{8,12},{12,0},{1,5},{5,9},{9,13},{13,1},{2,6},{6,10},{... | collective-permute-start | bytes 393224 | tf_op jit(solution)/shard_map/ppermute | solution.py:26
  97.5 13.0 %collective-permute-start.13 = (bf16[64,1024]{1,0:T(8,128)(2,1)S(1)}, bf16[64,1024]{1,0:T(8,128)(2,1)S(1)}, u32[]{:S(2)}, u32[]{:S(2)}) collective-permute-start(bf16[64,1024]{1,0:T(8,128)(2,1)S(1)} %get-tuple-element.49), channel_id=1, source_target_pairs={{0,8},{4,12},{8,0},{12,4},{1,9},{5,13},{9,1},{13,5},{2,10},{6,14},... | collective-permute-start | bytes 393224 | tf_op jit(solution)/shard_map/ppermute | solution.py:26
  99.7 10.8 %collective-permute-start.12 = (bf16[64,1024]{1,0:T(8,128)(2,1)S(1)}, bf16[64,1024]{1,0:T(8,128)(2,1)S(1)}, u32[]{:S(2)}, u32[]{:S(2)}) collective-permute-start(bf16[64,1024]{1,0:T(8,128)(2,1)S(1)} %get-tuple-element.47), channel_id=1, source_target_pairs={{0,12},{4,0},{8,4},{12,8},{1,13},{5,1},{9,5},{13,9},{2,14},{6,2},{... | collective-permute-start | bytes 393224 | tf_op jit(solution)/shard_map/ppermute | solution.py:26
  110.6 6.1 %collective-permute-start.15 = (bf16[64,1024]{1,0:T(8,128)(2,1)S(1)}, bf16[64,1024]{1,0:T(8,128)(2,1)S(1)}, u32[]{:S(2)}, u32[]{:S(2)}) collective-permute-start(bf16[64,1024]{1,0:T(8,128)(2,1)S(1)} %add_convert_fusion.1.refs_0_), channel_id=1, source_target_pairs={{0,1},{1,0},{2,3},{3,2},{4,5},{5,4},{6,7},{7,6},{8,9},{9,8},{10,11... | collective-permute-start | bytes 393224 | tf_op jit(solution)/shard_map/ppermute | solution.py:21
  111.2 7.1 %collective-permute-start.16 = (bf16[64,1024]{1,0:T(8,128)(2,1)S(1)}, bf16[64,1024]{1,0:T(8,128)(2,1)S(1)}, u32[]{:S(2)}, u32[]{:S(2)}) collective-permute-start(bf16[64,1024]{1,0:T(8,128)(2,1)S(1)} %add_convert_fusion.1.refs_0_), channel_id=1, source_target_pairs={{0,2},{1,3},{2,0},{3,1},{4,6},{5,7},{6,4},{7,5},{8,10},{9,11},{10,... | collective-permute-start | bytes 393224 | tf_op jit(solution)/shard_map/ppermute | solution.py:21
  111.6 6.6 %collective-permute-start.17 = (bf16[64,1024]{1,0:T(8,128)(2,1)S(1)}, bf16[64,1024]{1,0:T(8,128)(2,1)S(1)}, u32[]{:S(2)}, u32[]{:S(2)}) collective-permute-start(bf16[64,1024]{1,0:T(8,128)(2,1)S(1)} %add_convert_fusion.1.refs_0_), channel_id=1, source_target_pairs={{0,3},{1,2},{2,1},{3,0},{4,7},{5,6},{6,5},{7,4},{8,11},{9,10},{10,... | collective-permute-start | bytes 393224 | tf_op jit(solution)/shard_map/ppermute | solution.py:21
  119.9 1.3 collective-permute-start.19
  122.9 8.6 %collective-permute-start.22 = (bf16[64,2048]{1,0:T(8,128)(2,1)S(1)}, bf16[64,2048]{1,0:T(8,128)(2,1)S(1)}, u32[]{:S(2)}, u32[]{:S(2)}) collective-permute-start(bf16[64,2048]{1,0:T(8,128)(2,1)S(1)} %attend.7), channel_id=1, source_target_pairs={{0,1},{1,0},{2,3},{3,2},{4,5},{5,4},{6,7},{7,6},{8,9},{9,8},{10,11... | collective-permute-start | bytes 786440 | tf_op jit(solution)/shard_map/ppermute | solution.py:21
  124.6 16.2 %copy-start.1 = (bf16[1024,512]{1,0:T(8,128)(2,1)S(1)}, bf16[1024,512]{1,0:T(8,128)(2,1)}, u32[]{:S(2)}) copy-start(bf16[1024,512]{1,0:T(8,128)(2,1)} %param.20) | copy-start | bytes 3145732
  126.2 13.8 %collective-permute-start.21 = (bf16[64,2048]{1,0:T(8,128)(2,1)S(1)}, bf16[64,2048]{1,0:T(8,128)(2,1)S(1)}, u32[]{:S(2)}, u32[]{:S(2)}) collective-permute-start(bf16[64,2048]{1,0:T(8,128)(2,1)S(1)} %attend.6), channel_id=1, source_target_pairs={{0,2},{1,3},{2,0},{3,1},{4,6},{5,7},{6,4},{7,5},{8,10},{9,11},{10,... | collective-permute-start | bytes 786440 | tf_op jit(solution)/shard_map/ppermute | solution.py:21
  128.9 11.1 %collective-permute-start.20 = (bf16[64,2048]{1,0:T(8,128)(2,1)S(1)}, bf16[64,2048]{1,0:T(8,128)(2,1)S(1)}, u32[]{:S(2)}, u32[]{:S(2)}) collective-permute-start(bf16[64,2048]{1,0:T(8,128)(2,1)S(1)} %attend.5), channel_id=1, source_target_pairs={{0,3},{1,2},{2,1},{3,0},{4,7},{5,6},{6,5},{7,4},{8,11},{9,10},{10,... | collective-permute-start | bytes 786440 | tf_op jit(solution)/shard_map/ppermute | solution.py:21

commit v8 on v7

--- a/solution.py
+++ b/solution.py
@@ -194,7 +194,7 @@
                     )
                 if streams and n == 0:
 
-                    @pl.when(e == (low if top else (low + high) // 2))
+                    @pl.when(e == (low + high) // 2)
                     def _():
                         for copy in copies:
                             copy.start()
@@ -484,7 +484,9 @@
     quarter = lax.dynamic_slice_in_dim(own, half * width, width, axis=1)
     parcel = jnp.concatenate([quarter, tags], axis=1)
     order = sorted(range(1, parts), key=lambda k: bin(k).count("1"))
-    arrived = [shift(parcel, "ep", d) for d in range(1, eps)]
+    arrived = []
+    for d in range(1, eps):
+        arrived.append(shift(parcel, "ep", d))
     sources = (w_gate, w_up, w_down)
     experts = w_gate.shape[0]
     beside, last = order[:-1], order[-1]
@@ -526,15 +528,15 @@
     for k in far:
         gathered.append(swap(partial[k], "half", k))
     summed = total_of(partial[0], gathered)
-    returned = [
-        shift(summed[d * local : (d + 1) * local].astype(BF16), "ep", -d)
-        for d in range(1, eps)
-    ]
+    returned = []
+    for d in range(1, eps):
+        block = summed[d * local : (d + 1) * local].astype(BF16)
+        returned.append(shift(block, "ep", -d))
     mine, summed = lax.optimization_barrier((mine, summed))
     theirs = swap(mine, "pool", 1)
     moe_quarter = total_of(summed[:local], returned).astype(BF16)
     moe = [moe_quarter] + [None] * (parts - 1)
-    for k in far:
+    for k in order:
         moe[k] = swap(moe_quarter, "half", k)
     keyvals = project(place, own, moe, norm_gain[None], mine, theirs, eps)
     block = swap(keyvals, "pool", 1)

time: 141 us -> 141 us (level)
  no operation moved by 1% of the time
where the time goes in v8:
time: 141 us
  waiting for transfers between devices  53.9 us (38%)
  Pallas kernels  48.8 us (35%)
  starting transfers between devices  32.8 us (23%)
  other arithmetic  2.57 us (2%)
  local copies, waits for them, and re-layouts  2.55 us (2%)
    ppermute x14, waiting for transfers between devices, swap(): lax.ppermute(shard, axis, [(i, i ^ bits) for i in range(lax.axis_size(axi...  36.3 us
    pallas_call x4, Pallas kernels, stage(): pl.pallas_call(functools.partial(stage_kernel, items, quarters, parts, no...  28.1 us
    ppermute x9, waiting for transfers between devices, shift(): lax.ppermute(shard, axis, [(i, (i + distance) % count) for i in range(cou...  17.5 us
    ppermute x9, starting transfers between devices, shift(): lax.ppermute(shard, axis, [(i, (i + distance) % count) for i in range(cou...  17.1 us
    ppermute x14, starting transfers between devices, swap(): lax.ppermute(shard, axis, [(i, i ^ bits) for i in range(lax.axis_size(axi...  15.6 us
    pallas_call x2, Pallas kernels, reduce(): pl.pallas_call(reduce_kernel, out_shape=jax.ShapeDtypeStruct((tokens, wid...  8.98 us
    pallas_call x4, Pallas kernels, attend(): pl.pallas_call(functools.partial(attend_kernel, k, prompts), out_shape=ja...  6.49 us
    pallas_call x2, Pallas kernels, reduce_ahead(): pl.pallas_call(reduce_ahead_kernel, out_shape=jax.ShapeDtypeStruct((hidde...  3.56 us
  transfers between devices with their start and end apart: 23, of which 12 were waited for; matrix products, arithmetic and copies ran while one was open for 1% of the time, Pallas kernels for 32%

profile of v8, /device:TPU:0, one launch (start us, length us, event | category | flops | bytes accessed | tf_op | source)
XLA Modules:
  0.0 140.8 jit_solution(13579726200406194691)
XLA Ops:
  1.8 3.1 %collective-permute-start.3 = (bf16[64,1152]{1,0:T(8,128)(2,1)S(1)}, bf16[64,1152]{1,0:T(8,128)(2,1)S(1)}, u32[]{:S(2)}, u32[]{:S(2)}) collective-permute-start(bf16[64,1152]{1,0:T(8,128)(2,1)S(1)} %pad_maximum_fusion.1), channel_id=1, source_target_pairs={{0,4},{4,8},{8,12},{12,0},{1,5},{5,9},{9,13},{13,1},{2,6},{6,10},{... | collective-permute-start | bytes 442376 | tf_op jit(solution)/shard_map/ppermute | solution.py:26
  4.9 2.6 %collective-permute-start.4 = (bf16[64,1152]{1,0:T(8,128)(2,1)S(1)}, bf16[64,1152]{1,0:T(8,128)(2,1)S(1)}, u32[]{:S(2)}, u32[]{:S(2)}) collective-permute-start(bf16[64,1152]{1,0:T(8,128)(2,1)S(1)} %pad_maximum_fusion.1), channel_id=1, source_target_pairs={{0,8},{4,12},{8,0},{12,4},{1,9},{5,13},{9,1},{13,5},{2,10},{6,14},... | collective-permute-start | bytes 442376 | tf_op jit(solution)/shard_map/ppermute | solution.py:26
  8.9 2.9 %collective-permute-done.3.refs_0_ = bf16[64,1152]{1,0:T(8,128)(2,1)S(1)} collective-permute-done((bf16[64,1152]{1,0:T(8,128)(2,1)S(1)}, bf16[64,1152]{1,0:T(8,128)(2,1)S(1)}, u32[]{:S(2)}, u32[]{:S(2)}) %collective-permute-start.3) | collective-permute-done | bytes 147488 | tf_op jit(solution)/shard_map/ppermute | solution.py:26
  11.8 5.5 %collective-permute-done.4.refs_1_ = bf16[64,1152]{1,0:T(8,128)(2,1)S(1)} collective-permute-done((bf16[64,1152]{1,0:T(8,128)(2,1)S(1)}, bf16[64,1152]{1,0:T(8,128)(2,1)S(1)}, u32[]{:S(2)}, u32[]{:S(2)}) %collective-permute-start.4) | collective-permute-done | bytes 147488 | tf_op jit(solution)/shard_map/ppermute | solution.py:26
  20.3 7.9 %collective-permute-done.6.refs_5_ = bf16[192,1024]{1,0:T(8,128)(2,1)S(1)} collective-permute-done((bf16[192,1024]{1,0:T(8,128)(2,1)S(1)}, bf16[192,1024]{1,0:T(8,128)(2,1)S(1)}, u32[]{:S(2)}, u32[]{:S(2)}) %collective-permute-start.6) | collective-permute-done | bytes 393248 | tf_op jit(solution)/shard_map/ppermute | solution.py:21
  31.0 3.8 %collective-permute-start = (bf16[1024,256]{1,0:T(8,128)(2,1)S(1)}, bf16[1024,256]{1,0:T(8,128)(2,1)S(1)}, u32[]{:S(2)}, u32[]{:S(2)}) collective-permute-start(bf16[1024,256]{1,0:T(8,128)(2,1)S(1)} %constant_dynamic-slice_fusion), channel_id=1, source_target_pairs={{0,4},{4,8},{8,12},{12,0},{1,5},{5,9},{9,13},{13,1},{2,6},{6,10},{... | collective-permute-start | bytes 1572872 | tf_op jit(solution)/shard_map/ppermute | solution.py:26
  35.4 1.8 %collective-permute-start.2 = (bf16[1024,256]{1,0:T(8,128)(2,1)S(1)}, bf16[1024,256]{1,0:T(8,128)(2,1)}, u32[]{:S(2)}, u32[]{:S(2)}) collective-permute-start(bf16[1024,256]{1,0:T(8,128)(2,1)S(1)} %constant_dynamic-slice_fusion), channel_id=1, source_target_pairs={{0,12},{4,0},{8,4},{12,8},{1,13},{5,1},{9,5},{13,9},{2,14},{6,2},{... | collective-permute-start | bytes 1572872 | tf_op jit(solution)/shard_map/ppermute | solution.py:26
  38.0 5.2 %shard_map.127.refs_6_ = bf16[16,1024,384]{2,1,0:T(8,128)(2,1)S(1)} custom-call(s32[5]{0:T(128)S(1)} %pad_add_fusion.place, bf16[8,4096,384]{2,1,0:T(8,128)(2,1)} %refs_0_.7, bf16[8,4096,384]{2,1,0:T(8,128)(2,1)} %refs_1_.7, bf16[8,384,4096]{2,1,0:T(8,128)(2,1)} %w_down.3), custom_call_target="tpu_custom_call" | custom-call | tf_op jit(solution)/shard_map/pallas_call | solution.py:260
  43.2 5.3 %shard_map.128 = (bf16[16,1024,384]{2,1,0:T(8,128)(2,1)S(1)}, f32[8,256,768]{2,1,0:T(8,128)S(1)}, f32[256,32]{1,0:T(8,128)S(1)}) custom-call(s32[5]{0:T(128)S(1)} %pad_add_fusion.place, bf16[8,4096,384]{2,1,0:T(8,128)(2,1)} %refs_0_.7, bf16[8,4096,384]{2,1,0:T(8,128)(2,1)} %refs_1_.7, bf16[8,384,4096]{2,1,0:T(8,128)(2,1)} %w_down.3, ...), custom_call_target="tpu_custom_call" | custom-call | tf_op jit(solution)/shard_map/pallas_call | solution.py:260
  48.5 11.3 %shard_map.129 = (bf16[8,1024,384]{2,1,0:T(8,128)(2,1)S(1)}, bf16[8,384,1024]{2,1,0:T(8,128)(2,1)S(1)}, f32[8,256,768]{2,1,0:T(8,128)S(1)}, f32[256,32]{1,0:T(8,128)S(1)}) custom-call(s32[5]{0:T(128)S(1)} %pad_add_fusion.place, bf16[8,4096,384]{2,1,0:T(8,128)(2,1)} %refs_0_.7, ...), custom_call_target="tpu_custom_call", output_to_operand_aliasing={{2}: (9, {}), {3}: (10, {})} | custom-call | tf_op jit(solution)/shard_map/pallas_call | solution.py:260
  59.8 6.3 %shard_map.130 = (bf16[8,384,1024]{2,1,0:T(8,128)(2,1)S(1)}, bf16[256,3072]{1,0:T(8,128)(2,1)S(1)}) custom-call(s32[5]{0:T(128)S(1)} %pad_add_fusion.place, bf16[8,4096,384]{2,1,0:T(8,128)(2,1)} %refs_0_.7, bf16[8,4096,384]{2,1,0:T(8,128)(2,1)} %refs_1_.7, bf16[8,384,4096]{2,1,0:T(8,128)(2,1)} %w_down.3, bf16[64,4096]{1,0:T(8,128)(2,1)S(1)} %bitcast.19, ...), custom_call_target="tpu_custom_call" | custom-call | tf_op jit(solution)/shard_map/pallas_call | solution.py:260
  66.1 4.5 %reduce.7 = bf16[256,1024]{1,0:T(8,128)(2,1)S(1)} custom-call(s32[5]{0:T(128)S(1)} %pad_add_fusion.place, bf16[256,3072]{1,0:T(8,128)(2,1)S(1)} %get-tuple-element.36.hidden, bf16[8,384,4096]{2,1,0:T(8,128)(2,1)} %w_down.3), custom_call_target="tpu_custom_call" | custom-call | flops 1610612736 | bytes 6291456 | tf_op jit(solution)/shard_map/reduce/pallas_call | solution.py:304
  72.2 1.8 %reduce.6 = bf16[256,1024]{1,0:T(8,128)(2,1)S(1)} custom-call(bf16[256,3072]{1,0:T(8,128)(2,1)S(1)} %get-tuple-element.36.hidden, bf16[8,384,1024]{2,1,0:T(8,128)(2,1)S(1)} %get-tuple-element.42.weight), custom_call_target="tpu_custom_call" | custom-call | tf_op jit(solution)/shard_map/reduce/pallas_call | solution.py:290
  74.5 1.8 %reduce.5 = bf16[256,1024]{1,0:T(8,128)(2,1)S(1)} custom-call(bf16[256,3072]{1,0:T(8,128)(2,1)S(1)} %get-tuple-element.36.hidden, bf16[8,384,1024]{2,1,0:T(8,128)(2,1)S(1)} %get-tuple-element.41.weight), custom_call_target="tpu_custom_call" | custom-call | tf_op jit(solution)/shard_map/reduce/pallas_call | solution.py:290
  76.3 1.6 %collective-permute-start.9 = (bf16[256,1024]{1,0:T(8,128)(2,1)S(1)}, bf16[256,1024]{1,0:T(8,128)(2,1)S(1)}, u32[]{:S(2)}, u32[]{:S(2)}) collective-permute-start(bf16[256,1024]{1,0:T(8,128)(2,1)S(1)} %reduce.5), channel_id=1, source_target_pairs={{0,3},{1,2},{2,1},{3,0},{4,7},{5,6},{6,5},{7,4},{8,11},{9,10},{10,... | collective-permute-start | bytes 1572872 | tf_op jit(solution)/shard_map/ppermute | solution.py:21
  77.9 4.5 %reduce.4 = bf16[256,1024]{1,0:T(8,128)(2,1)S(1)} custom-call(s32[5]{0:T(128)S(1)} %pad_add_fusion.place, bf16[256,3072]{1,0:T(8,128)(2,1)S(1)} %get-tuple-element.36.hidden, bf16[8,384,4096]{2,1,0:T(8,128)(2,1)} %w_down.3), custom_call_target="tpu_custom_call" | custom-call | flops 1610612736 | bytes 6291456 | tf_op jit(solution)/shard_map/reduce/pallas_call | solution.py:304
  83.6 1.9 %collective-permute-done.11 = bf16[256,1024]{1,0:T(8,128)(2,1)S(1)} collective-permute-done((bf16[256,1024]{1,0:T(8,128)(2,1)S(1)}, bf16[256,1024]{1,0:T(8,128)(2,1)S(1)}, u32[]{:S(2)}, u32[]{:S(2)}) %collective-permute-start.11) | collective-permute-done | bytes 524320 | tf_op jit(solution)/shard_map/ppermute | solution.py:21
  85.5 11.4 %collective-permute-done.10 = bf16[256,1024]{1,0:T(8,128)(2,1)S(1)} collective-permute-done((bf16[256,1024]{1,0:T(8,128)(2,1)S(1)}, bf16[256,1024]{1,0:T(8,128)(2,1)S(1)}, u32[]{:S(2)}, u32[]{:S(2)}) %collective-permute-start.10) | collective-permute-done | bytes 524320 | tf_op jit(solution)/shard_map/ppermute | solution.py:21
  97.5 2.2 %collective-permute-start.13 = (bf16[64,1024]{1,0:T(8,128)(2,1)S(1)}, bf16[64,1024]{1,0:T(8,128)(2,1)S(1)}, u32[]{:S(2)}, u32[]{:S(2)}) collective-permute-start(bf16[64,1024]{1,0:T(8,128)(2,1)S(1)} %get-tuple-element.49), channel_id=1, source_target_pairs={{0,8},{4,12},{8,0},{12,4},{1,9},{5,13},{9,1},{13,5},{2,10},{6,14},... | collective-permute-start | bytes 393224 | tf_op jit(solution)/shard_map/ppermute | solution.py:26
  99.7 1.6 %collective-permute-start.12 = (bf16[64,1024]{1,0:T(8,128)(2,1)S(1)}, bf16[64,1024]{1,0:T(8,128)(2,1)S(1)}, u32[]{:S(2)}, u32[]{:S(2)}) collective-permute-start(bf16[64,1024]{1,0:T(8,128)(2,1)S(1)} %get-tuple-element.47), channel_id=1, source_target_pairs={{0,12},{4,0},{8,4},{12,8},{1,13},{5,1},{9,5},{13,9},{2,14},{6,2},{... | collective-permute-start | bytes 393224 | tf_op jit(solution)/shard_map/ppermute | solution.py:26
  101.3 4.5 %collective-permute-done.14 = bf16[64,1024]{1,0:T(8,128)(2,1)S(1)} collective-permute-done((bf16[64,1024]{1,0:T(8,128)(2,1)S(1)}, bf16[64,1024]{1,0:T(8,128)(2,1)S(1)}, u32[]{:S(2)}, u32[]{:S(2)}) %collective-permute-start.14) | collective-permute-done | bytes 131104 | tf_op jit(solution)/shard_map/ppermute | solution.py:26
  105.8 4.7 %collective-permute-done.13 = bf16[64,1024]{1,0:T(8,128)(2,1)S(1)} collective-permute-done((bf16[64,1024]{1,0:T(8,128)(2,1)S(1)}, bf16[64,1024]{1,0:T(8,128)(2,1)S(1)}, u32[]{:S(2)}, u32[]{:S(2)}) %collective-permute-start.13) | collective-permute-done | bytes 131104 | tf_op jit(solution)/shard_map/ppermute | solution.py:26
  111.6 2.5 %collective-permute-start.17 = (bf16[64,1024]{1,0:T(8,128)(2,1)S(1)}, bf16[64,1024]{1,0:T(8,128)(2,1)S(1)}, u32[]{:S(2)}, u32[]{:S(2)}) collective-permute-start(bf16[64,1024]{1,0:T(8,128)(2,1)S(1)} %add_convert_fusion.1.refs_0_), channel_id=1, source_target_pairs={{0,3},{1,2},{2,1},{3,0},{4,7},{5,6},{6,5},{7,4},{8,11},{9,10},{10,... | collective-permute-start | bytes 393224 | tf_op jit(solution)/shard_map/ppermute | solution.py:21
  114.1 2.5 %collective-permute-done.15.refs_1_ = bf16[64,1024]{1,0:T(8,128)(2,1)S(1)} collective-permute-done((bf16[64,1024]{1,0:T(8,128)(2,1)S(1)}, bf16[64,1024]{1,0:T(8,128)(2,1)S(1)}, u32[]{:S(2)}, u32[]{:S(2)}) %collective-permute-start.15) | collective-permute-done | bytes 131104 | tf_op jit(solution)/shard_map/ppermute | solution.py:21
  116.6 1.6 %collective-permute-done.16.refs_2_ = bf16[64,1024]{1,0:T(8,128)(2,1)S(1)} collective-permute-done((bf16[64,1024]{1,0:T(8,128)(2,1)S(1)}, bf16[64,1024]{1,0:T(8,128)(2,1)S(1)}, u32[]{:S(2)}, u32[]{:S(2)}) %collective-permute-start.16) | collective-permute-done | bytes 131104 | tf_op jit(solution)/shard_map/ppermute | solution.py:21
  118.3 1.6 %project.1 = bf16[64,512]{1,0:T(8,128)(2,1)S(1)} custom-call(s32[5]{0:T(128)S(1)} %pad_add_fusion.place, bf16[64,4096]{1,0:T(8,128)(2,1)S(1)} %bitcast.20, bf16[64,1024]{1,0:T(8,128)(2,1)S(1)} %add_convert_fusion.1.refs_0_, bf16[64,1024]{1,0:T(8,128)(2,1)S(1)} %collective-permute-done.15.refs_1_, bf16[64,1024]{1,0:T(8,128)(2,1)S(1)} %collective-permute-done.16.refs_2_, ...), custom_call_target="tpu_custom_call" | custom-call | tf_op jit(solution)/shard_map/project/pallas_call | solution.py:355
  121.3 1.6 %attend.7 = bf16[64,2048]{1,0:T(8,128)(2,1)S(1)} custom-call(s32[5]{0:T(128)S(1)} %pad_add_fusion.place, bf16[64,512]{1,0:T(8,128)(2,1)S(1)} %collective-permute-done.19.block, bf16[256,512]{1,0:T(8,128)(2,1)S(1)} %bitcast.21, bf16[256,256]{1,0:T(8,128)(2,1)S(1)} %bitcast.28, bf16[256,256]{1,0:T(8,128)(2,1)S(1)} %bitcast.32, bf16[512,2048]{1,0:T(8,128)(2,1)S(1)} %copy-done.2), custom_call_target="tpu_custom_call" | custom-call | flops 268435456 | bytes 2097152 | tf_op jit(solution)/shard_map/attend/pallas_call | solution.py:429
  122.9 1.7 %collective-permute-start.22 = (bf16[64,2048]{1,0:T(8,128)(2,1)S(1)}, bf16[64,2048]{1,0:T(8,128)(2,1)S(1)}, u32[]{:S(2)}, u32[]{:S(2)}) collective-permute-start(bf16[64,2048]{1,0:T(8,128)(2,1)S(1)} %attend.7), channel_id=1, source_target_pairs={{0,1},{1,0},{2,3},{3,2},{4,5},{5,4},{6,7},{7,6},{8,9},{9,8},{10,11... | collective-permute-start | bytes 786440 | tf_op jit(solution)/shard_map/ppermute | solution.py:21
  124.6 1.6 %attend.6 = bf16[64,2048]{1,0:T(8,128)(2,1)S(1)} custom-call(s32[5]{0:T(128)S(1)} %pad_add_fusion.place, bf16[64,512]{1,0:T(8,128)(2,1)S(1)} %collective-permute-done.19.block, bf16[256,512]{1,0:T(8,128)(2,1)S(1)} %bitcast.22, bf16[256,256]{1,0:T(8,128)(2,1)S(1)} %bitcast.29, bf16[256,256]{1,0:T(8,128)(2,1)S(1)} %bitcast.33, bf16[512,2048]{1,0:T(8,128)(2,1)S(1)} %copy-done.2), custom_call_target="tpu_custom_call" | custom-call | flops 268435456 | bytes 2097152 | tf_op jit(solution)/shard_map/attend/pallas_call | solution.py:429
  127.3 1.6 %attend.5 = bf16[64,2048]{1,0:T(8,128)(2,1)S(1)} custom-call(s32[5]{0:T(128)S(1)} %pad_add_fusion.place, bf16[64,512]{1,0:T(8,128)(2,1)S(1)} %collective-permute-done.19.block, bf16[256,512]{1,0:T(8,128)(2,1)S(1)} %bitcast.23, bf16[256,256]{1,0:T(8,128)(2,1)S(1)} %bitcast.30, bf16[256,256]{1,0:T(8,128)(2,1)S(1)} %bitcast.34, bf16[512,2048]{1,0:T(8,128)(2,1)S(1)} %copy-done.2), custom_call_target="tpu_custom_call" | custom-call | flops 268435456 | bytes 2097152 | tf_op jit(solution)/shard_map/attend/pallas_call | solution.py:429
  129.8 1.6 %attend.4 = bf16[64,2048]{1,0:T(8,128)(2,1)S(1)} custom-call(s32[5]{0:T(128)S(1)} %pad_add_fusion.place, bf16[64,512]{1,0:T(8,128)(2,1)S(1)} %collective-permute-done.19.block, bf16[256,512]{1,0:T(8,128)(2,1)S(1)} %bitcast.24, bf16[256,256]{1,0:T(8,128)(2,1)S(1)} %bitcast.31, bf16[256,256]{1,0:T(8,128)(2,1)S(1)} %bitcast.35, bf16[512,2048]{1,0:T(8,128)(2,1)S(1)} %copy-done.2), custom_call_target="tpu_custom_call" | custom-call | flops 268435456 | bytes 2097152 | tf_op jit(solution)/shard_map/attend/pallas_call | solution.py:429
  131.5 8.5 %collective-permute-done.21 = bf16[64,2048]{1,0:T(8,128)(2,1)S(1)} collective-permute-done((bf16[64,2048]{1,0:T(8,128)(2,1)S(1)}, bf16[64,2048]{1,0:T(8,128)(2,1)S(1)}, u32[]{:S(2)}, u32[]{:S(2)}) %collective-permute-start.21) | collective-permute-done | bytes 262176 | tf_op jit(solution)/shard_map/ppermute | solution.py:21
  (59 shorter events, 19.5 us)
Async XLA Ops:
  0.0 31.0 %copy-start = (bf16[1024,512]{1,0:T(8,128)(2,1)S(1)}, bf16[1024,512]{1,0:T(8,128)(2,1)}, u32[]{:S(2)}) copy-start(bf16[1024,512]{1,0:T(8,128)(2,1)} %param.20) | copy-start | bytes 3145732
  1.8 9.9 %collective-permute-start.3 = (bf16[64,1152]{1,0:T(8,128)(2,1)S(1)}, bf16[64,1152]{1,0:T(8,128)(2,1)S(1)}, u32[]{:S(2)}, u32[]{:S(2)}) collective-permute-start(bf16[64,1152]{1,0:T(8,128)(2,1)S(1)} %pad_maximum_fusion.1), channel_id=1, source_target_pairs={{0,4},{4,8},{8,12},{12,0},{1,5},{5,9},{9,13},{13,1},{2,6},{6,10},{... | collective-permute-start | bytes 442376 | tf_op jit(solution)/shard_map/ppermute | solution.py:26
  4.9 12.3 %collective-permute-start.4 = (bf16[64,1152]{1,0:T(8,128)(2,1)S(1)}, bf16[64,1152]{1,0:T(8,128)(2,1)S(1)}, u32[]{:S(2)}, u32[]{:S(2)}) collective-permute-start(bf16[64,1152]{1,0:T(8,128)(2,1)S(1)} %pad_maximum_fusion.1), channel_id=1, source_target_pairs={{0,8},{4,12},{8,0},{12,4},{1,9},{5,13},{9,1},{13,5},{2,10},{6,14},... | collective-permute-start | bytes 442376 | tf_op jit(solution)/shard_map/ppermute | solution.py:26
  7.5 9.7 %collective-permute-start.5 = (bf16[64,1152]{1,0:T(8,128)(2,1)S(1)}, bf16[64,1152]{1,0:T(8,128)(2,1)S(1)}, u32[]{:S(2)}, u32[]{:S(2)}) collective-permute-start(bf16[64,1152]{1,0:T(8,128)(2,1)S(1)} %pad_maximum_fusion.1), channel_id=1, source_target_pairs={{0,12},{4,0},{8,4},{12,8},{1,13},{5,1},{9,5},{13,9},{2,14},{6,2},{... | collective-permute-start | bytes 442376 | tf_op jit(solution)/shard_map/ppermute | solution.py:26
  17.3 11.0 %collective-permute-start.6 = (bf16[192,1024]{1,0:T(8,128)(2,1)S(1)}, bf16[192,1024]{1,0:T(8,128)(2,1)S(1)}, u32[]{:S(2)}, u32[]{:S(2)}) collective-permute-start(bf16[192,1024]{1,0:T(8,128)(2,1)S(1)} %get-tuple-element.26.refs_5_), channel_id=1, source_target_pairs={{0,1},{1,0},{2,3},{3,2},{4,5},{5,4},{6,7},{7,6},{8,9},{9,8},{10,11... | collective-permute-start | bytes 1179656 | tf_op jit(solution)/shard_map/ppermute | solution.py:21
  18.8 10.7 %collective-permute-start.7 = (bf16[192,1024]{1,0:T(8,128)(2,1)S(1)}, bf16[192,1024]{1,0:T(8,128)(2,1)S(1)}, u32[]{:S(2)}, u32[]{:S(2)}) collective-permute-start(bf16[192,1024]{1,0:T(8,128)(2,1)S(1)} %get-tuple-element.26.refs_5_), channel_id=1, source_target_pairs={{0,2},{1,3},{2,0},{3,1},{4,6},{5,7},{6,4},{7,5},{8,10},{9,11},{10,... | collective-permute-start | bytes 1179656 | tf_op jit(solution)/shard_map/ppermute | solution.py:21
  29.5 30.3 %collective-permute-start.8 = (bf16[192,1024]{1,0:T(8,128)(2,1)S(1)}, bf16[192,1024]{1,0:T(8,128)(2,1)S(1)}, u32[]{:S(2)}, u32[]{:S(2)}) collective-permute-start(bf16[192,1024]{1,0:T(8,128)(2,1)S(1)} %get-tuple-element.26.refs_5_), channel_id=1, source_target_pairs={{0,3},{1,2},{2,1},{3,0},{4,7},{5,6},{6,5},{7,4},{8,11},{9,10},{10,... | collective-permute-start | bytes 1179656 | tf_op jit(solution)/shard_map/ppermute | solution.py:21
  31.0 45.3 %collective-permute-start = (bf16[1024,256]{1,0:T(8,128)(2,1)S(1)}, bf16[1024,256]{1,0:T(8,128)(2,1)S(1)}, u32[]{:S(2)}, u32[]{:S(2)}) collective-permute-start(bf16[1024,256]{1,0:T(8,128)(2,1)S(1)} %constant_dynamic-slice_fusion), channel_id=1, source_target_pairs={{0,4},{4,8},{8,12},{12,0},{1,5},{5,9},{9,13},{13,1},{2,6},{6,10},{... | collective-permute-start | bytes 1572872 | tf_op jit(solution)/shard_map/ppermute | solution.py:26
  34.8 47.6 %collective-permute-start.1 = (bf16[1024,256]{1,0:T(8,128)(2,1)S(1)}, bf16[1024,256]{1,0:T(8,128)(2,1)S(1)}, u32[]{:S(2)}, u32[]{:S(2)}) collective-permute-start(bf16[1024,256]{1,0:T(8,128)(2,1)S(1)} %constant_dynamic-slice_fusion), channel_id=1, source_target_pairs={{0,8},{4,12},{8,0},{12,4},{1,9},{5,13},{9,1},{13,5},{2,10},{6,14},... | collective-permute-start | bytes 1572872 | tf_op jit(solution)/shard_map/ppermute | solution.py:26
  35.4 47.0 %collective-permute-start.2 = (bf16[1024,256]{1,0:T(8,128)(2,1)S(1)}, bf16[1024,256]{1,0:T(8,128)(2,1)}, u32[]{:S(2)}, u32[]{:S(2)}) collective-permute-start(bf16[1024,256]{1,0:T(8,128)(2,1)S(1)} %constant_dynamic-slice_fusion), channel_id=1, source_target_pairs={{0,12},{4,0},{8,4},{12,8},{1,13},{5,1},{9,5},{13,9},{2,14},{6,2},{... | collective-permute-start | bytes 1572872 | tf_op jit(solution)/shard_map/ppermute | solution.py:26
  38.0 5.2 %copy-start.3 = (bf16[1,64,4096]{2,1,0:T(8,128)(2,1)S(1)}, bf16[1,64,4096]{2,1,0:T(8,128)(2,1)}, u32[]{:S(2)}) copy-start(bf16[1,64,4096]{2,1,0:T(8,128)(2,1)} %param.13) | copy-start | bytes 1572868
  38.0 5.2 %copy-start.5 = (bf16[4096,32]{0,1:T(8,128)(2,1)S(1)}, bf16[4096,32]{0,1:T(8,128)(2,1)}, u32[]{:S(2)}) copy-start(bf16[4096,32]{0,1:T(8,128)(2,1)} %param.15) | copy-start | bytes 786436
  70.6 14.9 %collective-permute-start.11 = (bf16[256,1024]{1,0:T(8,128)(2,1)S(1)}, bf16[256,1024]{1,0:T(8,128)(2,1)S(1)}, u32[]{:S(2)}, u32[]{:S(2)}) collective-permute-start(bf16[256,1024]{1,0:T(8,128)(2,1)S(1)} %reduce.7), channel_id=1, source_target_pairs={{0,1},{1,0},{2,3},{3,2},{4,5},{5,4},{6,7},{7,6},{8,9},{9,8},{10,11... | collective-permute-start | bytes 1572872 | tf_op jit(solution)/shard_map/ppermute | solution.py:21
  74.0 22.9 %collective-permute-start.10 = (bf16[256,1024]{1,0:T(8,128)(2,1)S(1)}, bf16[256,1024]{1,0:T(8,128)(2,1)S(1)}, u32[]{:S(2)}, u32[]{:S(2)}) collective-permute-start(bf16[256,1024]{1,0:T(8,128)(2,1)S(1)} %reduce.6), channel_id=1, source_target_pairs={{0,2},{1,3},{2,0},{3,1},{4,6},{5,7},{6,4},{7,5},{8,10},{9,11},{10,... | collective-permute-start | bytes 1572872 | tf_op jit(solution)/shard_map/ppermute | solution.py:21
  76.3 20.6 %collective-permute-start.9 = (bf16[256,1024]{1,0:T(8,128)(2,1)S(1)}, bf16[256,1024]{1,0:T(8,128)(2,1)S(1)}, u32[]{:S(2)}, u32[]{:S(2)}) collective-permute-start(bf16[256,1024]{1,0:T(8,128)(2,1)S(1)} %reduce.5), channel_id=1, source_target_pairs={{0,3},{1,2},{2,1},{3,0},{4,7},{5,6},{6,5},{7,4},{8,11},{9,10},{10,... | collective-permute-start | bytes 1572872 | tf_op jit(solution)/shard_map/ppermute | solution.py:21
  82.4 35.9 %copy-start.8 = (f32[4096]{0:T(1024)S(1)}, f32[4096]{0:T(1024)}, u32[]{:S(2)}) copy-start(f32[4096]{0:T(1024)} %param.19) | copy-start | bytes 49156
  97.2 24.0 %copy-start.2 = (bf16[512,2048]{1,0:T(8,128)(2,1)S(1)}, bf16[512,2048]{1,0:T(8,128)(2,1)}, u32[]{:S(2)}) copy-start(bf16[512,2048]{1,0:T(8,128)(2,1)} %w_out.7) | copy-start | bytes 6291460
  97.3 24.0 %copy-start.4 = (bf16[1,256,512]{2,1,0:T(8,128)(2,1)S(1)}, bf16[1,256,512]{2,1,0:T(8,128)(2,1)}, u32[]{:S(2)}) copy-start(bf16[1,256,512]{2,1,0:T(8,128)(2,1)} %param.22) | copy-start | bytes 786436
  97.3 24.0 %copy-start.6 = (bf16[1,256,256]{2,1,0:T(8,128)(2,1)S(1)}, bf16[1,256,256]{2,1,0:T(8,128)(2,1)}, u32[]{:S(2)}) copy-start(bf16[1,256,256]{2,1,0:T(8,128)(2,1)} %param.23) | copy-start | bytes 393220
  97.3 24.0 %copy-start.7 = (bf16[1,256,256]{2,1,0:T(8,128)(2,1)S(1)}, bf16[1,256,256]{2,1,0:T(8,128)(2,1)}, u32[]{:S(2)}) copy-start(bf16[1,256,256]{2,1,0:T(8,128)(2,1)} %param.24) | copy-start | bytes 393220
  97.3 21.0 %collective-permute-start.18 = (bf16[4096,256]{1,0:T(8,128)(2,1)S(1)}, bf16[4096,256]{1,0:T(8,128)(2,1)S(1)}, u32[]{:S(2)}, u32[]{:S(2)}) collective-permute-start(bf16[4096,256]{1,0:T(8,128)(2,1)S(1)} %pad_maximum_fusion.refs_5_), channel_id=1, source_target_pairs={{0,16},{16,0},{1,17},{17,1},{2,18},{18,2},{3,19},{19,3},{4,20},{20... | collective-permute-start | bytes 6291464 | tf_op jit(solution)/shard_map/ppermute | solution.py:21
  97.4 8.4 %collective-permute-start.14 = (bf16[64,1024]{1,0:T(8,128)(2,1)S(1)}, bf16[64,1024]{1,0:T(8,128)(2,1)S(1)}, u32[]{:S(2)}, u32[]{:S(2)}) collective-permute-start(bf16[64,1024]{1,0:T(8,128)(2,1)S(1)} %get-tuple-element.48), channel_id=1, source_target_pairs={{0,4},{4,8},{8,12},{12,0},{1,5},{5,9},{9,13},{13,1},{2,6},{6,10},{... | collective-permute-start | bytes 393224 | tf_op jit(solution)/shard_map/ppermute | solution.py:26
  97.5 13.0 %collective-permute-start.13 = (bf16[64,1024]{1,0:T(8,128)(2,1)S(1)}, bf16[64,1024]{1,0:T(8,128)(2,1)S(1)}, u32[]{:S(2)}, u32[]{:S(2)}) collective-permute-start(bf16[64,1024]{1,0:T(8,128)(2,1)S(1)} %get-tuple-element.49), channel_id=1, source_target_pairs={{0,8},{4,12},{8,0},{12,4},{1,9},{5,13},{9,1},{13,5},{2,10},{6,14},... | collective-permute-start | bytes 393224 | tf_op jit(solution)/shard_map/ppermute | solution.py:26
  99.7 10.8 %collective-permute-start.12 = (bf16[64,1024]{1,0:T(8,128)(2,1)S(1)}, bf16[64,1024]{1,0:T(8,128)(2,1)S(1)}, u32[]{:S(2)}, u32[]{:S(2)}) collective-permute-start(bf16[64,1024]{1,0:T(8,128)(2,1)S(1)} %get-tuple-element.47), channel_id=1, source_target_pairs={{0,12},{4,0},{8,4},{12,8},{1,13},{5,1},{9,5},{13,9},{2,14},{6,2},{... | collective-permute-start | bytes 393224 | tf_op jit(solution)/shard_map/ppermute | solution.py:26
  110.6 6.1 %collective-permute-start.15 = (bf16[64,1024]{1,0:T(8,128)(2,1)S(1)}, bf16[64,1024]{1,0:T(8,128)(2,1)S(1)}, u32[]{:S(2)}, u32[]{:S(2)}) collective-permute-start(bf16[64,1024]{1,0:T(8,128)(2,1)S(1)} %add_convert_fusion.1.refs_0_), channel_id=1, source_target_pairs={{0,1},{1,0},{2,3},{3,2},{4,5},{5,4},{6,7},{7,6},{8,9},{9,8},{10,11... | collective-permute-start | bytes 393224 | tf_op jit(solution)/shard_map/ppermute | solution.py:21
  111.2 7.1 %collective-permute-start.16 = (bf16[64,1024]{1,0:T(8,128)(2,1)S(1)}, bf16[64,1024]{1,0:T(8,128)(2,1)S(1)}, u32[]{:S(2)}, u32[]{:S(2)}) collective-permute-start(bf16[64,1024]{1,0:T(8,128)(2,1)S(1)} %add_convert_fusion.1.refs_0_), channel_id=1, source_target_pairs={{0,2},{1,3},{2,0},{3,1},{4,6},{5,7},{6,4},{7,5},{8,10},{9,11},{10,... | collective-permute-start | bytes 393224 | tf_op jit(solution)/shard_map/ppermute | solution.py:21
  111.6 6.6 %collective-permute-start.17 = (bf16[64,1024]{1,0:T(8,128)(2,1)S(1)}, bf16[64,1024]{1,0:T(8,128)(2,1)S(1)}, u32[]{:S(2)}, u32[]{:S(2)}) collective-permute-start(bf16[64,1024]{1,0:T(8,128)(2,1)S(1)} %add_convert_fusion.1.refs_0_), channel_id=1, source_target_pairs={{0,3},{1,2},{2,1},{3,0},{4,7},{5,6},{6,5},{7,4},{8,11},{9,10},{10,... | collective-permute-start | bytes 393224 | tf_op jit(solution)/shard_map/ppermute | solution.py:21
  119.9 1.3 collective-permute-start.19
  122.9 8.6 %collective-permute-start.22 = (bf16[64,2048]{1,0:T(8,128)(2,1)S(1)}, bf16[64,2048]{1,0:T(8,128)(2,1)S(1)}, u32[]{:S(2)}, u32[]{:S(2)}) collective-permute-start(bf16[64,2048]{1,0:T(8,128)(2,1)S(1)} %attend.7), channel_id=1, source_target_pairs={{0,1},{1,0},{2,3},{3,2},{4,5},{5,4},{6,7},{7,6},{8,9},{9,8},{10,11... | collective-permute-start | bytes 786440 | tf_op jit(solution)/shard_map/ppermute | solution.py:21
  124.6 16.2 %copy-start.1 = (bf16[1024,512]{1,0:T(8,128)(2,1)S(1)}, bf16[1024,512]{1,0:T(8,128)(2,1)}, u32[]{:S(2)}) copy-start(bf16[1024,512]{1,0:T(8,128)(2,1)} %param.20) | copy-start | bytes 3145732
  126.2 13.8 %collective-permute-start.21 = (bf16[64,2048]{1,0:T(8,128)(2,1)S(1)}, bf16[64,2048]{1,0:T(8,128)(2,1)S(1)}, u32[]{:S(2)}, u32[]{:S(2)}) collective-permute-start(bf16[64,2048]{1,0:T(8,128)(2,1)S(1)} %attend.6), channel_id=1, source_target_pairs={{0,2},{1,3},{2,0},{3,1},{4,6},{5,7},{6,4},{7,5},{8,10},{9,11},{10,... | collective-permute-start | bytes 786440 | tf_op jit(solution)/shard_map/ppermute | solution.py:21
  128.9 11.1 %collective-permute-start.20 = (bf16[64,2048]{1,0:T(8,128)(2,1)S(1)}, bf16[64,2048]{1,0:T(8,128)(2,1)S(1)}, u32[]{:S(2)}, u32[]{:S(2)}) collective-permute-start(bf16[64,2048]{1,0:T(8,128)(2,1)S(1)} %attend.5), channel_id=1, source_target_pairs={{0,3},{1,2},{2,1},{3,0},{4,7},{5,6},{6,5},{7,4},{8,11},{9,10},{10,... | collective-permute-start | bytes 786440 | tf_op jit(solution)/shard_map/ppermute | solution.py:21
